TPU v7x, 32 devices: a whole 2x2x4 slice. The times are simulated.
32 devices in a mesh: dp: 2 (over y), seq: 16 (over z, x, core).
Axes of the slice: x: 2, y: 2, z: 4, core: 2. Of those that a mesh axis runs over, the one named last changes fastest.
Arguments:
- patch_features: bfloat16 [4, 768, 1664], P('dp', 'seq'), may hold values from -6 to 6
- text_embeds: bfloat16 [4, 384, 1024], P('dp', 'seq'), may hold values from -6 to 6
- text_lengths: int32 [4, 3], P('dp'), may hold values from 1 to 192, 288 in all within a row
- w_in: bfloat16 [1664, 1024], P(None, ('dp', 'seq')), may hold values from -0.15625 to 0.15625
- b_in: bfloat16 [1024], P(('dp', 'seq')), may hold values from -3 to 3
- gain_attn: bfloat16 [1024], P(('dp', 'seq')), may hold values from 0.5 to 1.5
- w_query: bfloat16 [1024, 1024], P(None, ('dp', 'seq')), may hold values from -0.09375 to 0.09375
- w_key: bfloat16 [1024, 1024], P(None, ('dp', 'seq')), may hold values from -0.09375 to 0.09375
- w_value: bfloat16 [1024, 1024], P(None, ('dp', 'seq')), may hold values from -0.1875 to 0.1875
- w_out: bfloat16 [1024, 1024], P(None, ('dp', 'seq')), may hold values from -0.75 to 0.75
- gain_ffn: bfloat16 [1024], P(('dp', 'seq')), may hold values from 0.5 to 1.5
- w_gate: bfloat16 [1024, 2816], P(None, ('dp', 'seq')), may hold values from -0.1875 to 0.1875
- w_up: bfloat16 [1024, 2816], P(None, ('dp', 'seq')), may hold values from -0.1875 to 0.1875
- w_down: bfloat16 [2816, 1024], P(None, ('dp', 'seq')), may hold values from -0.109375 to 0.109375
- position_bias: bfloat16 [512], P(('dp', 'seq')), may hold values from -4 to 4
- d_patch: bfloat16 [4, 768, 1024], P('dp', 'seq'), may hold values from -6 to 6
- d_text: bfloat16 [4, 384, 1024], P('dp', 'seq'), may hold values from -6 to 6
Outputs:
- patch_out: bfloat16 [4, 768, 1024], P('dp', 'seq')
- text_out: bfloat16 [4, 384, 1024], P('dp', 'seq')
- feature_grad: float32 [4, 768, 1664], P('dp', 'seq')
- text_grad: float32 [4, 384, 1024], P('dp', 'seq')
- grad_w_in: float32 [1664, 1024], P(None, ('dp', 'seq'))
- grad_b_in: float32 [1024], P(('dp', 'seq'))
- grad_gain_attn: float32 [1024], P(('dp', 'seq'))
- grad_w_query: float32 [1024, 1024], P(None, ('dp', 'seq'))
- grad_w_key: float32 [1024, 1024], P(None, ('dp', 'seq'))
- grad_w_value: float32 [1024, 1024], P(None, ('dp', 'seq'))
- grad_w_out: float32 [1024, 1024], P(None, ('dp', 'seq'))
- grad_gain_ffn: float32 [1024], P(('dp', 'seq'))
- grad_w_gate: float32 [1024, 2816], P(None, ('dp', 'seq'))
- grad_w_up: float32 [1024, 2816], P(None, ('dp', 'seq'))
- grad_w_down: float32 [2816, 1024], P(None, ('dp', 'seq'))
- grad_position_bias: float32 [512], P(('dp', 'seq'))
Inputs may be any that keep to these rules, and one draw needn't show every extreme that they name: `text_lengths`: each row's 3 text lengths sum to 288, and the longest is exactly 192; the texts fill the slots in order of fill index, the rest are padding.
All inputs are finite; a program needn't handle non-finite values.
Results may differ from a plain program's by a relative error of at most 0.015.
Values may be sent and summed in bfloat16 or wider, within the bound.
No kernel may reach another device: no remote copies, remote signals or barrier semaphores. Data moves between devices by JAX's collectives and lax.ppermute only.
A program may use at most 384 MiB of HBM per device.

v0:
```python
import jax
import jax.numpy as jnp
from jax import lax
from jax.sharding import PartitionSpec as P

D = 1024
HEADS = 16
HEAD_DIM = 64
BUCKETS = 32
PATCHES_IMG = 256


EPSILON = 1e-06
BORDERS = (12, 16, 23, 32, 46, 64, 91)
MASKED = -1e30
GROUP = 4


def bucket_table(query_pos, key_pos):
    pos_delta = query_pos[:, None] - key_pos[None, :]
    magnitude = jnp.abs(pos_delta)
    far_bucket = jnp.full(magnitude.shape, 8, jnp.int32)
    for border in BORDERS:
        far_bucket = far_bucket + (magnitude >= border).astype(jnp.int32)
    near_bucket = jnp.where(magnitude < 8, magnitude, far_bucket)
    return jnp.where(pos_delta < 0, 16, 0) + near_bucket


def patch_layout(patch_count):
    patch_ids = jnp.arange(patch_count, dtype=jnp.int32)
    return (patch_ids // PATCHES_IMG + 1, patch_ids % PATCHES_IMG)


def text_layout(lengths, slot_count):
    image_count = lengths.shape[0]
    text_ends = jnp.cumsum(lengths)
    slot_ids = jnp.arange(slot_count, dtype=jnp.int32)
    fill_ids = (slot_ids + slot_count // 2) % slot_count
    text_index = jnp.sum((fill_ids[:, None] >= text_ends[None, :]).astype(jnp.int32), axis=1)
    text_starts = jnp.concatenate([text_ends - lengths, text_ends[image_count - 1 :]])
    matches = text_index[:, None] == jnp.arange(image_count + 1, dtype=jnp.int32)[None, :]
    text_begin = jnp.sum(jnp.where(matches, text_starts[None, :], 0), axis=1)
    segment = jnp.where(text_index < image_count, text_index + 1, 0)
    return (segment, PATCHES_IMG + fill_ids - text_begin)


def rms_norm(values, gain):
    return values * lax.rsqrt(jnp.mean(values * values, axis=-1, keepdims=True) + EPSILON) * gain


def gelu_tanh(values):
    return (
        0.5
        * values
        * (1.0 + jnp.tanh(0.7978845608 * (values + 0.044715 * values * values * values)))
    )


def gated_unit(gate_pre, up_pre):
    return gelu_tanh(gate_pre) * up_pre


def inner_rows(left, right):
    return lax.dot_general(
        left, right, (((0,), (0,)), ((), ())), preferred_element_type=jnp.float32
    )


def times_trans(left, right):
    return lax.dot_general(
        left, right, (((1,), (1,)), ((), ())), preferred_element_type=jnp.float32
    )


def bucket_onehot(bucket_mat):
    flat = bucket_mat.reshape(bucket_mat.shape[0] * bucket_mat.shape[1])
    return (flat[:, None] == jnp.arange(BUCKETS, dtype=jnp.int32)[None, :]).astype(jnp.bfloat16)


def bias_rows(table, onehot):
    return lax.dot_general(
        table, onehot, (((0,), (1,)), ((), ())), preferred_element_type=jnp.float32
    )


def bucket_sums(d_buffer, onehot):
    d_high = d_buffer.astype(jnp.bfloat16)
    d_rest = (d_buffer - d_high.astype(jnp.float32)).astype(jnp.bfloat16)
    upper = lax.dot_general(
        d_high, onehot, (((1,), (0,)), ((), ())), preferred_element_type=jnp.float32
    )
    lower = lax.dot_general(
        d_rest, onehot, (((1,), (0,)), ((), ())), preferred_element_type=jnp.float32
    )
    return upper + lower


def local(
    patch_features,
    text_embeds,
    text_lengths,
    w_in,
    b_in,
    gain_attn,
    w_query,
    w_key,
    w_value,
    w_out,
    gain_ffn,
    w_gate,
    w_up,
    w_down,
    position_bias,
    d_patch,
    d_text,
):
    seq_count = lax.axis_size("seq")
    seq_index = lax.axis_index("seq")
    micro_count = patch_features.shape[0]
    patch_dev = patch_features.shape[1]
    text_dev = text_embeds.shape[1]
    tok_dev = patch_dev + text_dev
    row_len = tok_dev * seq_count
    pair_count = tok_dev * row_len
    head_span = GROUP * HEAD_DIM
    group_count = HEADS // GROUP
    patch_seg, patch_pos = patch_layout(patch_dev * seq_count)
    grad_total = None
    outs_patch = []
    outs_text = []
    feat_grads = []
    text_grads = []
    for which_batch in range(micro_count):
        gathered = (
            lax.all_gather(w_in, ("dp", "seq"), axis=1, tiled=True),
            lax.all_gather(b_in, ("dp", "seq"), axis=0, tiled=True),
            lax.all_gather(gain_attn, ("dp", "seq"), axis=0, tiled=True),
            lax.all_gather(w_query, ("dp", "seq"), axis=1, tiled=True),
            lax.all_gather(w_key, ("dp", "seq"), axis=1, tiled=True),
            lax.all_gather(w_value, ("dp", "seq"), axis=1, tiled=True),
            lax.all_gather(w_out, ("dp", "seq"), axis=1, tiled=True),
            lax.all_gather(gain_ffn, ("dp", "seq"), axis=0, tiled=True),
            lax.all_gather(w_gate, ("dp", "seq"), axis=1, tiled=True),
            lax.all_gather(w_up, ("dp", "seq"), axis=1, tiled=True),
            lax.all_gather(w_down, ("dp", "seq"), axis=1, tiled=True),
            lax.all_gather(position_bias, ("dp", "seq"), axis=0, tiled=True),
        )
        (
            full_in,
            full_bias,
            full_gain_one,
            full_query,
            full_key,
            full_value,
            full_out,
            full_gain_two,
            full_gate,
            full_up,
            full_down,
            full_pos,
        ) = gathered
        bias_in = full_bias.astype(jnp.float32)
        gain_one = full_gain_one.astype(jnp.float32)
        gain_two = full_gain_two.astype(jnp.float32)
        table = full_pos.reshape(BUCKETS, HEADS)
        text_seg, text_pos = text_layout(text_lengths[which_batch], text_dev * seq_count)
        key_seg = jnp.concatenate(
            [patch_seg.reshape(seq_count, patch_dev), text_seg.reshape(seq_count, text_dev)], axis=1
        )
        key_pos = jnp.concatenate(
            [patch_pos.reshape(seq_count, patch_dev), text_pos.reshape(seq_count, text_dev)], axis=1
        )
        query_seg = lax.dynamic_index_in_dim(key_seg, seq_index, 0, keepdims=False)
        query_pos = lax.dynamic_index_in_dim(key_pos, seq_index, 0, keepdims=False)
        row_seg = key_seg.reshape(row_len)
        row_pos = key_pos.reshape(row_len)
        onehot = bucket_onehot(bucket_table(query_pos, row_pos))
        bias_all = bias_rows(table, onehot)
        allowed = query_seg[:, None] == row_seg[None, :]
        features = patch_features[which_batch]
        embeds = text_embeds[which_batch].astype(jnp.float32)
        resid = jnp.concatenate(
            [jnp.dot(features, full_in, preferred_element_type=jnp.float32) + bias_in, embeds],
            axis=0,
        )
        normed_one = rms_norm(resid, gain_one).astype(jnp.bfloat16)
        queries = jnp.dot(normed_one, full_query, preferred_element_type=jnp.float32).astype(
            jnp.bfloat16
        )
        keys_local = jnp.dot(normed_one, full_key, preferred_element_type=jnp.float32).astype(
            jnp.bfloat16
        )
        values_local = jnp.dot(normed_one, full_value, preferred_element_type=jnp.float32).astype(
            jnp.bfloat16
        )
        all_keys, all_values = (
            lax.all_gather(keys_local, "seq", axis=0, tiled=True),
            lax.all_gather(values_local, "seq", axis=0, tiled=True),
        )

        def group_scores(group_idx):
            start = group_idx * head_span
            query_part = lax.dynamic_slice_in_dim(queries, start, head_span, 1).reshape(
                tok_dev, GROUP, HEAD_DIM
            )
            key_part = lax.dynamic_slice_in_dim(all_keys, start, head_span, 1).reshape(
                row_len, GROUP, HEAD_DIM
            )
            value_part = lax.dynamic_slice_in_dim(all_values, start, head_span, 1).reshape(
                row_len, GROUP, HEAD_DIM
            )
            raw_scores = jnp.einsum(
                "qhd,khd->hqk", query_part, key_part, preferred_element_type=jnp.float32
            )
            extra = lax.dynamic_slice_in_dim(bias_all, group_idx * GROUP, GROUP, 0).reshape(
                GROUP, tok_dev, row_len
            )
            scores = jnp.where(allowed[None], raw_scores + extra, MASKED)
            return (scores, query_part, key_part, value_part)

        def forward_group(group_idx, carry):
            mixed, lse_all = carry
            scores, _, _, value_part = group_scores(group_idx)
            top_score = jnp.max(scores, axis=-1, keepdims=True)
            expd = jnp.exp(scores - top_score)
            total = jnp.sum(expd, axis=-1, keepdims=True)
            probs = (expd / total).astype(jnp.bfloat16)
            out_part = jnp.einsum(
                "hqk,khd->qhd", probs, value_part, preferred_element_type=jnp.float32
            ).reshape(tok_dev, head_span)
            mixed = lax.dynamic_update_slice_in_dim(mixed, out_part, group_idx * head_span, 1)
            lse_all = lax.dynamic_update_slice_in_dim(
                lse_all, (top_score + jnp.log(total))[..., 0], group_idx * GROUP, 0
            )
            return (mixed, lse_all)

        mixed, lse_all = lax.fori_loop(
            0,
            group_count,
            forward_group,
            (jnp.zeros((tok_dev, D), jnp.float32), jnp.zeros((HEADS, tok_dev), jnp.float32)),
        )
        attn_out = mixed.astype(jnp.bfloat16)
        resid_one = resid + jnp.dot(attn_out, full_out, preferred_element_type=jnp.float32)
        normed_two = rms_norm(resid_one, gain_two).astype(jnp.bfloat16)
        gate_pre = jnp.dot(normed_two, full_gate, preferred_element_type=jnp.float32)
        up_pre = jnp.dot(normed_two, full_up, preferred_element_type=jnp.float32)
        hidden = gated_unit(gate_pre, up_pre).astype(jnp.bfloat16)
        result = (
            resid_one + jnp.dot(hidden, full_down, preferred_element_type=jnp.float32)
        ).astype(jnp.bfloat16)
        outs_patch.append(result[:patch_dev])
        outs_text.append(result[patch_dev:])
        upstream = jnp.concatenate([d_patch[which_batch], d_text[which_batch]], axis=0)
        grad_down = inner_rows(hidden, upstream)
        d_hidden = times_trans(upstream, full_down)
        _, gated_back = jax.vjp(gated_unit, gate_pre, up_pre)
        d_gate, d_up = gated_back(d_hidden)
        d_gate = d_gate.astype(jnp.bfloat16)
        d_up = d_up.astype(jnp.bfloat16)
        grad_gate = inner_rows(normed_two, d_gate)
        grad_up = inner_rows(normed_two, d_up)
        d_normed_two = times_trans(d_gate, full_gate) + times_trans(d_up, full_up)
        _, norm_back_two = jax.vjp(rms_norm, resid_one, gain_two)
        d_resid_one, grad_gain_two = norm_back_two(d_normed_two)
        d_resid_one = d_resid_one + upstream.astype(jnp.float32)
        d_mix = d_resid_one.astype(jnp.bfloat16)
        grad_out = inner_rows(attn_out, d_mix)
        d_attn = times_trans(d_mix, full_out).astype(jnp.bfloat16)

        def backward_group(group_idx, carry):
            d_query_all, d_key_all, d_value_all, centre_all, d_buffer = carry
            start = group_idx * head_span
            scores, query_part, key_part, value_part = group_scores(group_idx)
            lse_part = lax.dynamic_slice_in_dim(lse_all, group_idx * GROUP, GROUP, 0)
            probs = jnp.exp(scores - lse_part[..., None])
            d_out_part = lax.dynamic_slice_in_dim(d_attn, start, head_span, 1).reshape(
                tok_dev, GROUP, HEAD_DIM
            )
            d_probs = jnp.einsum(
                "qhd,khd->hqk", d_out_part, value_part, preferred_element_type=jnp.float32
            )
            centre = jnp.sum(d_probs * probs, axis=-1, keepdims=True)
            d_scores = probs * (d_probs - centre)
            d_buffer = lax.dynamic_update_slice_in_dim(
                d_buffer, d_scores.reshape(GROUP, pair_count), group_idx * GROUP, 0
            )
            centre_all = lax.dynamic_update_slice_in_dim(
                centre_all, centre[..., 0], group_idx * GROUP, 0
            )
            d_scores_low = d_scores.astype(jnp.bfloat16)
            d_query_part = jnp.einsum(
                "hqk,khd->qhd", d_scores_low, key_part, preferred_element_type=jnp.float32
            ).reshape(tok_dev, head_span)
            d_query_all = lax.dynamic_update_slice_in_dim(d_query_all, d_query_part, start, 1)
            return (d_query_all, d_key_all, d_value_all, centre_all, d_buffer)

        zero_keys = jnp.zeros((1,), jnp.float32)
        d_query_all, d_key_all, d_value_all, centre_all, d_buffer = lax.fori_loop(
            0,
            group_count,
            backward_group,
            (
                jnp.zeros((tok_dev, D), jnp.float32),
                zero_keys,
                zero_keys,
                jnp.zeros((HEADS, tok_dev), jnp.float32),
                jnp.zeros((HEADS, pair_count), jnp.float32),
            ),
        )
        d_table = bucket_sums(d_buffer, onehot)
        row_queries, row_d_attn = (
            lax.all_gather(queries, "seq", axis=0, tiled=True),
            lax.all_gather(d_attn, "seq", axis=0, tiled=True),
        )
        row_lse, row_centre = (
            lax.all_gather(lse_all, "seq", axis=1, tiled=True),
            lax.all_gather(centre_all, "seq", axis=1, tiled=True),
        )
        bias_back = bias_rows(table, bucket_onehot(jnp.transpose(bucket_table(row_pos, query_pos))))
        allowed_back = query_seg[:, None] == row_seg[None, :]

        def owner_group(group_idx, carry):
            d_key_own, d_value_own = carry
            start = group_idx * head_span
            query_part = lax.dynamic_slice_in_dim(row_queries, start, head_span, 1).reshape(
                row_len, GROUP, HEAD_DIM
            )
            d_out_part = lax.dynamic_slice_in_dim(row_d_attn, start, head_span, 1).reshape(
                row_len, GROUP, HEAD_DIM
            )
            key_part = lax.dynamic_slice_in_dim(keys_local, start, head_span, 1).reshape(
                tok_dev, GROUP, HEAD_DIM
            )
            value_part = lax.dynamic_slice_in_dim(values_local, start, head_span, 1).reshape(
                tok_dev, GROUP, HEAD_DIM
            )
            raw_scores = jnp.einsum(
                "khd,qhd->hkq", key_part, query_part, preferred_element_type=jnp.float32
            )
            extra = lax.dynamic_slice_in_dim(bias_back, group_idx * GROUP, GROUP, 0).reshape(
                GROUP, tok_dev, row_len
            )
            scores = jnp.where(allowed_back[None], raw_scores + extra, MASKED)
            lse_part = lax.dynamic_slice_in_dim(row_lse, group_idx * GROUP, GROUP, 0)
            centre_part = lax.dynamic_slice_in_dim(row_centre, group_idx * GROUP, GROUP, 0)
            probs = jnp.exp(scores - lse_part[:, None, :])
            d_probs = jnp.einsum(
                "khd,qhd->hkq", value_part, d_out_part, preferred_element_type=jnp.float32
            )
            d_scores = probs * (d_probs - centre_part[:, None, :])
            d_key_part = jnp.einsum(
                "hkq,qhd->khd",
                d_scores.astype(jnp.bfloat16),
                query_part,
                preferred_element_type=jnp.float32,
            ).reshape(tok_dev, head_span)
            d_value_part = jnp.einsum(
                "hkq,qhd->khd",
                probs.astype(jnp.bfloat16),
                d_out_part,
                preferred_element_type=jnp.float32,
            ).reshape(tok_dev, head_span)
            d_key_own = lax.dynamic_update_slice_in_dim(d_key_own, d_key_part, start, 1)
            d_value_own = lax.dynamic_update_slice_in_dim(d_value_own, d_value_part, start, 1)
            return (d_key_own, d_value_own)

        zero_own = jnp.zeros((tok_dev, D), jnp.float32)
        d_key_own, d_value_own = lax.fori_loop(0, group_count, owner_group, (zero_own, zero_own))
        d_query_low = d_query_all.astype(jnp.bfloat16)
        d_key_low = d_key_own.astype(jnp.bfloat16)
        d_value_low = d_value_own.astype(jnp.bfloat16)
        grad_query = inner_rows(normed_one, d_query_low)
        grad_key = inner_rows(normed_one, d_key_low)
        grad_value = inner_rows(normed_one, d_value_low)
        d_normed_one = (
            times_trans(d_query_low, full_query)
            + times_trans(d_key_low, full_key)
            + times_trans(d_value_low, full_value)
        )
        _, norm_back_one = jax.vjp(rms_norm, resid, gain_one)
        d_resid, grad_gain_one = norm_back_one(d_normed_one)
        d_resid = d_resid + d_resid_one
        text_grads.append(d_resid[patch_dev:])
        d_patch_rows = d_resid[:patch_dev]
        grad_bias = jnp.sum(d_patch_rows, axis=0)
        d_patch_low = d_patch_rows.astype(jnp.bfloat16)
        grad_in = inner_rows(features, d_patch_low)
        feat_grads.append(times_trans(d_patch_low, full_in))
        grad_pos = jnp.transpose(d_table).reshape(BUCKETS * HEADS)
        shares = (
            lax.psum_scatter(grad_in, ("dp", "seq"), scatter_dimension=1, tiled=True),
            lax.psum_scatter(grad_bias, ("dp", "seq"), scatter_dimension=0, tiled=True),
            lax.psum_scatter(grad_gain_one, ("dp", "seq"), scatter_dimension=0, tiled=True),
            lax.psum_scatter(grad_query, ("dp", "seq"), scatter_dimension=1, tiled=True),
            lax.psum_scatter(grad_key, ("dp", "seq"), scatter_dimension=1, tiled=True),
            lax.psum_scatter(grad_value, ("dp", "seq"), scatter_dimension=1, tiled=True),
            lax.psum_scatter(grad_out, ("dp", "seq"), scatter_dimension=1, tiled=True),
            lax.psum_scatter(grad_gain_two, ("dp", "seq"), scatter_dimension=0, tiled=True),
            lax.psum_scatter(grad_gate, ("dp", "seq"), scatter_dimension=1, tiled=True),
            lax.psum_scatter(grad_up, ("dp", "seq"), scatter_dimension=1, tiled=True),
            lax.psum_scatter(grad_down, ("dp", "seq"), scatter_dimension=1, tiled=True),
            lax.psum_scatter(grad_pos, ("dp", "seq"), scatter_dimension=0, tiled=True),
        )
        if grad_total is None:
            grad_total = shares
        else:
            grad_total = tuple((older + newer for older, newer in zip(grad_total, shares)))
    return (
        jnp.stack(outs_patch),
        jnp.stack(outs_text),
        jnp.stack(feat_grads),
        jnp.stack(text_grads),
        grad_total[0],
        grad_total[1],
        grad_total[2],
        grad_total[3],
        grad_total[4],
        grad_total[5],
        grad_total[6],
        grad_total[7],
        grad_total[8],
        grad_total[9],
        grad_total[10],
        grad_total[11],
    )


def solution(mesh):
    return jax.shard_map(
        local,
        mesh=mesh,
        in_specs=(
            P("dp", "seq", None),
            P("dp", "seq", None),
            P("dp", None),
            P(None, ("dp", "seq")),
            P(("dp", "seq")),
            P(("dp", "seq")),
            P(None, ("dp", "seq")),
            P(None, ("dp", "seq")),
            P(None, ("dp", "seq")),
            P(None, ("dp", "seq")),
            P(("dp", "seq")),
            P(None, ("dp", "seq")),
            P(None, ("dp", "seq")),
            P(None, ("dp", "seq")),
            P(("dp", "seq")),
            P("dp", "seq", None),
            P("dp", "seq", None),
        ),
        out_specs=(
            P("dp", "seq", None),
            P("dp", "seq", None),
            P("dp", "seq", None),
            P("dp", "seq", None),
            P(None, ("dp", "seq")),
            P(("dp", "seq")),
            P(("dp", "seq")),
            P(None, ("dp", "seq")),
            P(None, ("dp", "seq")),
            P(None, ("dp", "seq")),
            P(None, ("dp", "seq")),
            P(("dp", "seq")),
            P(None, ("dp", "seq")),
            P(None, ("dp", "seq")),
            P(None, ("dp", "seq")),
            P(("dp", "seq")),
        ),
        check_vma=False,
    )
```

profile of v0, /device:TPU:0, one launch (start us, length us, event | category | flops | bytes accessed | tf_op | source)
XLA Modules:
  0.0 2102.1 jit_solution(12817903823437929154)
XLA Ops:
  13.4 42.2 %all-reduce.9 = (bf16[1024]{0:T(1024)(128)(2,1)S(1)}, bf16[1024]{0:T(1024)(128)(2,1)S(1)}, bf16[512]{0:T(512)(128)(2,1)S(1)}, bf16[1024]{0:T(1024)(128)(2,1)S(1)}) all-reduce(bf16[1024]{0:T(1024)(128)(2,1)S(1)} %dynamic-update-slice, bf16[1024]{0:T(1024)(128)(2,1)S(1)} %dynamic-update-slice.1, ...), channel_id=1, replica_groups=mesh['dp'=2,'seq'=16] {'dp','seq'}, use_global_device_ids=true, to_apply=%add | all-reduce | flops 3584 | bytes 14336
  57.1 16.2 all-gather.21.cloned.1.call-done
  73.4 3.2 convolution_add_fusion.24
  77.4 54.1 %all-gather.23.cloned.1.call-done = bf16[1024,1024]{0,1:T(8,128)(2,1)} async-done(((bf16[1024,32]{0,1:T(8,128)(2,1)}), bf16[1024,1024]{0,1:T(8,128)(2,1)}) %all-gather.23.cloned.1.call-update) | async-done | bytes 2097168 | tf_op jit(solution)/shard_map/all_gather | solution.py:140
  131.5 3.0 convolution_convert_fusion.7
  134.6 55.1 %all-gather.29.cloned.1.call-done = bf16[1024,1024]{0,1:T(8,128)(2,1)} async-done(((bf16[1024,32]{0,1:T(8,128)(2,1)}), bf16[1024,1024]{0,1:T(8,128)(2,1)}) %all-gather.29.cloned.1.call-update) | async-done | bytes 2097168 | tf_op jit(solution)/shard_map/all_gather | solution.py:139
  189.7 3.0 convolution_convert_fusion.5
  205.2 3.6 fusion.53
  209.1 4.5 fusion.54
  213.5 34.2 %all-gather.27.cloned.1.call-done = bf16[1024,1024]{0,1:T(8,128)(2,1)} async-done(((bf16[1024,32]{0,1:T(8,128)(2,1)}), bf16[1024,1024]{0,1:T(8,128)(2,1)}) %all-gather.27.cloned.1.call-update) | async-done | bytes 2097168 | tf_op jit(solution)/shard_map/all_gather | solution.py:138
  247.7 3.0 convolution_convert_fusion.6
  256.5 35.1 %all-gather.25.cloned.1.call-done = bf16[1152,1024]{1,0:T(8,128)(2,1)} async-done(((bf16[72,1024]{1,0:T(8,128)(2,1)}), bf16[1152,1024]{1,0:T(8,128)(2,1)}) %all-gather.25.cloned.1.call-update) | async-done | bytes 2359312 | tf_op jit(solution)/shard_map/all_gather | solution.py:198
  291.6 3.0 copy.215
  294.6 40.2 %all-gather.31.cloned.1.call-done = bf16[1152,1024]{1,0:T(8,128)(2,1)} async-done(((bf16[72,1024]{1,0:T(8,128)(2,1)}), bf16[1152,1024]{1,0:T(8,128)(2,1)}) %all-gather.31.cloned.1.call-update) | async-done | bytes 2359312 | tf_op jit(solution)/shard_map/all_gather | solution.py:197
  334.9 4.3 copy.217
  340.5 26.9 %while.100 = (s32[]{:T(128)}, bf16[72,1024]{0,1:T(8,128)(2,1)}, f32[16,72]{1,0:T(8,128)}, bf16[1152,1024]{0,1:T(8,128)(2,1)S(1)}, bf16[72,1024]{0,1:T(8,128)(2,1...) while((s32[]{:T(128)}, bf16[72,1024]{0,1:T(8,128)(2,1)}, ...), condition=%wide.region_7.8_spmd.clone, body=%wide.region_4.7_spmd.clone.sunk | while | flops 87671528 | bytes 11932581 | solution.py:237
  367.4 20.3 all-gather
  388.5 4.7 all-gather.33.cloned.1.call-done
  395.9 66.3 %all-gather.35.cloned.1.call-done = bf16[1024,2816]{0,1:T(8,128)(2,1)} async-done(((bf16[1024,88]{0,1:T(8,128)(2,1)}), bf16[1024,2816]{0,1:T(8,128)(2,1)}) %all-gather.35.cloned.1.call-update) | async-done | bytes 5767184 | tf_op jit(solution)/shard_map/all_gather | solution.py:143
  462.2 5.4 fusion.172
  467.6 63.8 %all-gather.37.cloned.1.call-done = bf16[1024,2816]{0,1:T(8,128)(2,1)} async-done(((bf16[1024,88]{0,1:T(8,128)(2,1)}), bf16[1024,2816]{0,1:T(8,128)(2,1)}) %all-gather.37.cloned.1.call-update) | async-done | bytes 5767184 | tf_op jit(solution)/shard_map/all_gather | solution.py:144
  531.4 5.5 fusion.173
  536.9 63.4 %all-gather.39.cloned.1.call-done = bf16[2816,1024]{0,1:T(8,128)(2,1)} async-done(((bf16[2816,32]{0,1:T(8,128)(2,1)}), bf16[2816,1024]{0,1:T(8,128)(2,1)}) %all-gather.39.cloned.1.call-update) | async-done | bytes 5767184 | tf_op jit(solution)/shard_map/all_gather | solution.py:145
  600.4 5.4 multiply_convert_fusion.1
  614.8 37.9 %while.102 = (s32[]{:T(128)}, bf16[72,1024]{0,1:T(8,128)(2,1)S(1)}, f32[16,72]{1,0:T(8,128)S(1)}, f32[16,82944]{1,0:T(8,128)}, bf16[1152,1024]{0,1:T(8,128)(2,1)...) while((s32[]{:T(128)}, bf16[72,1024]{0,1:T(8,128)(2,1)S(1)}, ...), condition=%wide.region_21.22_spmd.clone, body=%wide.region_19.21_spmd.clone.sunk | while | flops 130802408 | bytes 24680264 | solution.py:299
  652.7 20.6 all-gather.1
  674.1 2.8 fusion.184
  676.9 11.0 all-gather.47.cloned.1.call-done
  688.0 44.5 %while.103 = (s32[]{:T(128)}, bf16[72,1024]{0,1:T(8,128)(2,1)S(1)}, bf16[72,1024]{0,1:T(8,128)(2,1)S(1)}, bf16[1152,1024]{1,0:T(8,128)(2,1)}, bf16[72,1024]{1,0:...) while((s32[]{:T(128)}, bf16[72,1024]{0,1:T(8,128)(2,1)S(1)}, ...), condition=%wide.region_23.24_spmd.clone, body=%wide.region_22.23_spmd.clone.sunk | while | flops 172274688 | bytes 16026697 | solution.py:369
  741.8 3.6 fusion.50
  750.0 29.9 %all-gather.41.cloned.1.call-done = bf16[1152,1024]{1,0:T(8,128)(2,1)} async-done(((bf16[72,1024]{1,0:T(8,128)(2,1)}), bf16[1152,1024]{1,0:T(8,128)(2,1)}) %all-gather.41.cloned.1.call-update) | async-done | bytes 2359312 | tf_op jit(solution)/shard_map/all_gather | solution.py:198
  779.8 4.3 copy.218
  784.1 39.5 %all-gather.43.cloned.1.call-done = bf16[1152,1024]{1,0:T(8,128)(2,1)} async-done(((bf16[72,1024]{1,0:T(8,128)(2,1)}), bf16[1152,1024]{1,0:T(8,128)(2,1)}) %all-gather.43.cloned.1.call-update) | async-done | bytes 2359312 | tf_op jit(solution)/shard_map/all_gather | solution.py:197
  823.7 4.3 copy.220
  828.7 28.1 %while.101 = (s32[]{:T(128)}, bf16[72,1024]{0,1:T(8,128)(2,1)}, f32[16,72]{1,0:T(8,128)S(1)}, bf16[1152,1024]{0,1:T(8,128)(2,1)}, bf16[72,1024]{0,1:T(8,128)(2,1...) while((s32[]{:T(128)}, bf16[72,1024]{0,1:T(8,128)(2,1)}, ...), condition=%wide.region_16.17_spmd.clone, body=%wide.region_13.16_spmd.clone.sunk | while | flops 87671528 | bytes 11934373 | solution.py:237
  858.8 4.6 fusion.174
  863.4 4.7 fusion.175
  868.1 5.1 multiply_convert_fusion
  881.2 37.7 %while.104 = (s32[]{:T(128)}, bf16[72,1024]{0,1:T(8,128)(2,1)S(1)}, f32[16,72]{1,0:T(8,128)S(1)}, f32[16,82944]{1,0:T(8,128)}, bf16[1152,1024]{0,1:T(8,128)(2,1)...) while((s32[]{:T(128)}, bf16[72,1024]{0,1:T(8,128)(2,1)S(1)}, ...), condition=%wide.region_28.29_spmd.clone, body=%wide.region_26.28_spmd.clone.sunk | while | flops 130802408 | bytes 24680264 | solution.py:299
  918.8 5.0 convolution_add_fusion.12
  925.2 3.6 fusion.55
  928.8 2.8 fusion.131
  934.3 19.8 all-gather.2
  954.9 17.8 all-gather.3
  973.5 5.0 convolution_add_fusion.9
  979.3 44.3 %while.105 = (s32[]{:T(128)}, bf16[72,1024]{0,1:T(8,128)(2,1)S(1)}, bf16[72,1024]{0,1:T(8,128)(2,1)}, bf16[1152,1024]{1,0:T(8,128)(2,1)}, bf16[72,1024]{1,0:T(8,...) while((s32[]{:T(128)}, bf16[72,1024]{0,1:T(8,128)(2,1)S(1)}, ...), condition=%wide.region_30.31_spmd.clone, body=%wide.region_29.30_spmd.clone.sunk | while | flops 172274688 | bytes 16026697 | solution.py:369
  1023.6 4.9 convolution_add_fusion.11
  1030.1 2.8 convolution_add_fusion.10
  1038.6 3.9 add_bitcast_fusion
  1045.3 6.0 convolution_add_fusion.8
  1054.0 5.9 convolution_add_fusion.7
  1062.7 5.9 convolution_add_fusion.6
  1069.6 4.6 fusion.68
  1075.0 6.3 fusion.51
  1083.3 6.2 fusion.48
  1098.1 4.6 fusion.69
  1104.2 38.9 %all-reduce.8 = (f32[1024]{0:T(1024)S(1)}, f32[1024]{0:T(1024)S(1)}, f32[1024]{0:T(1024)S(1)}, f32[512]{0:T(512)S(1)}) all-reduce(f32[1024]{0:T(1024)S(1)} %add.865, f32[1024]{0:T(1024)S(1)} %add.866, f32[1024]{0:T(1024)} %add.871, f32[512]{0:T(512)} %reshape.690), channel_id=15, replica_groups=mesh['dp'=2,'seq'=16] {'dp','seq'}, use_global_device_ids=true, to_apply=%region_35.36.clone | all-reduce | flops 3584 | bytes 28672
  1149.5 55.5 %reduce-scatter.17.cloned.1.call-done = f32[1024,32]{0,1:T(8,128)} async-done(((f32[1024,1024]{0,1:T(8,128)}), f32[1024,32]{0,1:T(8,128)}) %reduce-scatter.17.cloned.1.call-update) | async-done | bytes 131088 | tf_op jit(solution)/shard_map/reduce_scatter | solution.py:398
  1205.0 140.7 %reduce-scatter.13.cloned.1.call-done = f32[1024,32]{0,1:T(8,128)} async-done(((f32[1024,1024]{0,1:T(8,128)}), f32[1024,32]{0,1:T(8,128)}) %reduce-scatter.13.cloned.1.call-update) | async-done | bytes 131088 | tf_op jit(solution)/shard_map/reduce_scatter | solution.py:396
  1345.7 140.4 %reduce-scatter.15.cloned.1.call-done = f32[1024,32]{0,1:T(8,128)} async-done(((f32[1024,1024]{0,1:T(8,128)}), f32[1024,32]{0,1:T(8,128)}) %reduce-scatter.15.cloned.1.call-update) | async-done | bytes 131088 | tf_op jit(solution)/shard_map/reduce_scatter | solution.py:397
  1486.1 145.1 %reduce-scatter.9.cloned.1.call-done = f32[1664,32]{0,1:T(8,128)} async-done(((f32[1664,1024]{0,1:T(8,128)}), f32[1664,32]{0,1:T(8,128)}) %reduce-scatter.9.cloned.1.call-update) | async-done | bytes 213008 | tf_op jit(solution)/shard_map/reduce_scatter | solution.py:392
  1631.2 154.2 %reduce-scatter.19.cloned.1.call-done = f32[1024,88]{0,1:T(8,128)} async-done(((f32[1024,2816]{0,1:T(8,128)}), f32[1024,88]{0,1:T(8,128)}) %reduce-scatter.19.cloned.1.call-update) | async-done | bytes 360464 | tf_op jit(solution)/shard_map/reduce_scatter | solution.py:400
  1785.4 154.7 %reduce-scatter.21.cloned.1.call-done = f32[1024,88]{0,1:T(8,128)} async-done(((f32[1024,2816]{0,1:T(8,128)}), f32[1024,88]{0,1:T(8,128)}) %reduce-scatter.21.cloned.1.call-update) | async-done | bytes 360464 | tf_op jit(solution)/shard_map/reduce_scatter | solution.py:401
  1940.1 154.9 %reduce-scatter.23.cloned.1.call-done = f32[2816,32]{0,1:T(8,128)} async-done(((f32[2816,1024]{0,1:T(8,128)}), f32[2816,32]{0,1:T(8,128)}) %reduce-scatter.23.cloned.1.call-update) | async-done | bytes 360464 | tf_op jit(solution)/shard_map/reduce_scatter | solution.py:402
  (764 shorter events, 325.1 us)
Async XLA Ops:
  7.2 66.2 %all-gather.21.cloned.1.call-start = ((), (), s32[]{:S(2)}) async-start(), calls=%async_computation.8 | async-start | bytes 3514368 | tf_op jit(solution)/shard_map/all_gather | solution.py:135
  7.9 123.6 %all-gather.23.cloned.1.call-start = ((), (), s32[]{:S(2)}) async-start(), calls=%async_computation.9 | async-start | bytes 2162688 | tf_op jit(solution)/shard_map/all_gather | solution.py:140
  8.7 181.0 %all-gather.29.cloned.1.call-start = ((), (), s32[]{:S(2)}) async-start(), calls=%async_computation.12 | async-start | bytes 2162688 | tf_op jit(solution)/shard_map/all_gather | solution.py:139
  9.4 238.3 %all-gather.27.cloned.1.call-start = ((), (), s32[]{:S(2)}) async-start(), calls=%async_computation.11 | async-start | bytes 2162688 | tf_op jit(solution)/shard_map/all_gather | solution.py:138
  10.0 281.6 %all-gather.25.cloned.1.call-start = ((), (), s32[]{:S(2)}) async-start(), calls=%async_computation.10 | async-start | bytes 2506752 | tf_op jit(solution)/shard_map/all_gather | solution.py:198
  55.6 21.7 %copy-start.86 = (f32[1024]{0:T(1024)}, f32[1024]{0:T(1024)S(1)}, u32[]{:S(2)}) copy-start(f32[1024]{0:T(1024)S(1)} %convert_element_type.423) | copy-start | bytes 12292
  55.6 21.8 %copy-start.90 = (f32[1024]{0:T(1024)}, f32[1024]{0:T(1024)S(1)}, u32[]{:S(2)}) copy-start(f32[1024]{0:T(1024)S(1)} %convert_element_type.420) | copy-start | bytes 12292
  57.1 77.4 %copy-start.33 = (f32[24,1024]{1,0:T(8,128)}, f32[24,1024]{1,0:T(8,128)S(1)}, u32[]{:S(2)}) copy-start(f32[24,1024]{1,0:T(8,128)S(1)} %get-tuple-element.1916) | copy-start | bytes 294916
  76.7 116.0 %copy-start.106 = (f32[72]{0:T(128)}, f32[72]{0:T(128)S(1)}, u32[]{:S(2)}) copy-start(f32[72]{0:T(128)S(1)} %multiply_reduce_fusion.13) | copy-start | bytes 868
  77.2 115.4 %copy-start.98 = (f32[72]{0:T(128)}, f32[72]{0:T(128)S(1)}, u32[]{:S(2)}) copy-start(f32[72]{0:T(128)S(1)} %fusion.162) | copy-start | bytes 868
  77.4 170.3 %copy-start.15 = (bf16[72,1024]{1,0:T(8,128)(2,1)}, bf16[72,1024]{1,0:T(8,128)(2,1)S(1)}, u32[]{:S(2)}) copy-start(bf16[72,1024]{1,0:T(8,128)(2,1)S(1)} %multiply_convert_fusion.7) | copy-start | bytes 442372
  77.4 118.3 %copy-start.102 = (s32[2,3]{1,0:T(2,128)S(1)}, s32[2,3]{1,0:T(2,128)}, u32[]{:S(2)}) copy-start(s32[2,3]{1,0:T(2,128)} %param.31) | copy-start | bytes 76
  134.5 200.3 %all-gather.31.cloned.1.call-start = ((), (), s32[]{:S(2)}) async-start(), calls=%async_computation.13 | async-start | bytes 2506752 | tf_op jit(solution)/shard_map/all_gather | solution.py:197
  192.7 200.5 %all-gather.33.cloned.1.call-start = ((), (), s32[]{:S(2)}) async-start(), calls=%async_computation.14 | async-start | bytes 2162688 | tf_op jit(solution)/shard_map/all_gather | solution.py:141
  193.5 268.8 %all-gather.35.cloned.1.call-start = ((), (), s32[]{:S(2)}) async-start(), calls=%async_computation.15 | async-start | bytes 5947392 | tf_op jit(solution)/shard_map/all_gather | solution.py:143
  194.2 9.3 copy-start.89
  194.2 337.1 %all-gather.37.cloned.1.call-start = ((), (), s32[]{:S(2)}) async-start(), calls=%async_computation.16 | async-start | bytes 5947392 | tf_op jit(solution)/shard_map/all_gather | solution.py:144
  195.0 9.2 copy-start.85
  195.0 405.4 %all-gather.39.cloned.1.call-start = ((), (), s32[]{:S(2)}) async-start(), calls=%async_computation.17 | async-start | bytes 5947392 | tf_op jit(solution)/shard_map/all_gather | solution.py:145
  195.6 481.4 %all-gather.45.cloned.1.call-start = ((), (), s32[]{:S(2)}) async-start(), calls=%async_computation.20 | async-start | bytes 2506752 | tf_op jit(solution)/shard_map/all_gather | solution.py:313
  195.7 9.5 copy-start.82
  209.0 43.5 %copy-start.1 = (bf16[1664,1024]{0,1:T(8,128)(2,1)S(1)}, bf16[1664,1024]{0,1:T(8,128)(2,1)}, u32[]{:S(2)}) copy-start(bf16[1664,1024]{0,1:T(8,128)(2,1)} %all-gather.21.cloned.1.call-done) | copy-start | bytes 10223620
  252.5 435.4 %all-gather.47.cloned.1.call-start = ((), (), s32[]{:S(2)}) async-start(), calls=%async_computation.21 | async-start | bytes 2506752 | tf_op jit(solution)/shard_map/all_gather | solution.py:314
  294.6 45.9 %copy-start.56 = (s32[1152]{0:T(1024)S(1)}, s32[1152]{0:T(1024)}, u32[]{:S(2)}) copy-start(s32[1152]{0:T(1024)} %eq.63) | copy-start | bytes 13828
  294.6 45.9 %copy-start.88 = (s32[72]{0:T(128)S(1)}, s32[72]{0:T(128)}, u32[]{:S(2)}) copy-start(s32[72]{0:T(128)} %get-tuple-element.2504) | copy-start | bytes 868
  367.4 100.2 %copy-start.11 = (bf16[1152,1024]{0,1:T(8,128)(2,1)}, bf16[1152,1024]{0,1:T(8,128)(2,1)S(1)}, u32[]{:S(2)}) copy-start(bf16[1152,1024]{0,1:T(8,128)(2,1)S(1)} %get-tuple-element.2739) | copy-start | bytes 7077892
  367.4 28.4 %copy-start.84 = (f32[1024]{0:T(1024)S(1)}, f32[1024]{0:T(1024)}, u32[]{:S(2)}) copy-start(f32[1024]{0:T(1024)} %convert_element_type.437) | copy-start | bytes 12292
  395.8 66.5 %copy-start.108 = (f32[72]{0:T(128)}, f32[72]{0:T(128)S(1)}, u32[]{:S(2)}) copy-start(f32[72]{0:T(128)S(1)} %get-tuple-element.1940) | copy-start | bytes 868
  395.8 214.8 %copy-start.12 = (f32[72,1024]{1,0:T(8,128)}, f32[72,1024]{1,0:T(8,128)S(1)}, u32[]{:S(2)}) copy-start(f32[72,1024]{1,0:T(8,128)S(1)} %get-tuple-element.1941) | copy-start | bytes 884740
  395.8 66.4 %copy-start.100 = (f32[72]{0:T(128)}, f32[72]{0:T(128)S(1)}, u32[]{:S(2)}) copy-start(f32[72]{0:T(128)S(1)} %fusion.163) | copy-start | bytes 868
  395.9 135.5 %copy-start.31 = (bf16[72,1024]{1,0:T(8,128)(2,1)}, bf16[72,1024]{1,0:T(8,128)(2,1)S(1)}, u32[]{:S(2)}) copy-start(bf16[72,1024]{1,0:T(8,128)(2,1)S(1)} %multiply_convert_fusion.6) | copy-start | bytes 442372
  467.6 132.8 %copy-start.71 = (bf16[48,1024]{1,0:T(8,128)(2,1)S(1)}, bf16[48,1024]{1,0:T(8,128)(2,1)}, u32[]{:S(2)}) copy-start(bf16[48,1024]{1,0:T(8,128)(2,1)} %get-tuple-element.1912) | copy-start | bytes 294916
  467.6 132.8 %copy-start.78 = (bf16[24,1024]{1,0:T(8,128)(2,1)S(1)}, bf16[24,1024]{1,0:T(8,128)(2,1)}, u32[]{:S(2)}) copy-start(bf16[24,1024]{1,0:T(8,128)(2,1)} %get-tuple-element.1914) | copy-start | bytes 147460
  531.4 74.4 %slice-start = ((s8[5767168]{0:T(1024)(128)(4,1)}), s8[1572864]{0:T(1024)(128)(4,1)S(1)}, s32[]{:S(2)}) async-start(s8[5767168]{0:T(1024)(128)(4,1)} %bitcast.434), calls=%async_computation.32 | async-start | bytes 3145728
  610.8 125.5 %copy-start.24 = (f32[72,1024]{1,0:T(8,128)}, f32[72,1024]{1,0:T(8,128)S(1)}, u32[]{:S(2)}) copy-start(f32[72,1024]{1,0:T(8,128)S(1)} %fusion.99) | copy-start | bytes 884740
  612.0 167.9 %all-gather.41.cloned.1.call-start = ((), (), s32[]{:S(2)}) async-start(), calls=%async_computation.18 | async-start | bytes 2506752 | tf_op jit(solution)/shard_map/all_gather | solution.py:198
  652.7 35.2 %copy-start.52 = (bf16[72,1024]{0,1:T(8,128)(2,1)}, bf16[72,1024]{0,1:T(8,128)(2,1)S(1)}, u32[]{:S(2)}) copy-start(bf16[72,1024]{0,1:T(8,128)(2,1)S(1)} %get-tuple-element.1041) | copy-start | bytes 442372
  737.1 11.0 copy-start.17
  738.6 85.1 %all-gather.43.cloned.1.call-start = ((), (), s32[]{:S(2)}) async-start(), calls=%async_computation.19 | async-start | bytes 2506752 | tf_op jit(solution)/shard_map/all_gather | solution.py:197
  740.1 238.4 %all-gather.49.cloned.1.call-start = ((), (), s32[]{:S(2)}) async-start(), calls=%async_computation.22 | async-start | bytes 2506752 | tf_op jit(solution)/shard_map/all_gather | solution.py:313
  749.7 228.8 %all-gather.51.cloned.1.call-start = ((), (), s32[]{:S(2)}) async-start(), calls=%async_computation.23 | async-start | bytes 2506752 | tf_op jit(solution)/shard_map/all_gather | solution.py:314
  828.7 28.1 %copy-start.10 = (bf16[1024,1024]{0,1:T(8,128)(2,1)S(1)}, bf16[1024,1024]{0,1:T(8,128)(2,1)}, u32[]{:S(2)}) copy-start(bf16[1024,1024]{0,1:T(8,128)(2,1)} %all-gather.33.cloned.1.call-done) | copy-start | bytes 6291460
  828.7 28.1 %copy-start.37 = (f32[24,1024]{1,0:T(8,128)S(1)}, f32[24,1024]{1,0:T(8,128)}, u32[]{:S(2)}) copy-start(f32[24,1024]{1,0:T(8,128)} %get-tuple-element.1917) | copy-start | bytes 294916
  858.6 17.5 copy-start.14
  863.3 9.8 slice-start.2
  863.4 11.0 slice-start.4
  878.2 271.3 %reduce-scatter.11.cloned.1.call-start = ((), (), s32[]{:S(2)}) async-start(), calls=%async_computation.25 | async-start | bytes 4325376 | tf_op jit(solution)/shard_map/reduce_scatter | solution.py:395
  881.2 37.7 %copy-start.18 = (bf16[72,1024]{1,0:T(8,128)(2,1)S(1)}, bf16[72,1024]{1,0:T(8,128)(2,1)}, u32[]{:S(2)}) copy-start(bf16[72,1024]{1,0:T(8,128)(2,1)} %copy-done.17) | copy-start | bytes 442372
  923.8 281.2 %reduce-scatter.17.cloned.1.call-start = ((), (), s32[]{:S(2)}) async-start(), calls=%async_computation.28 | async-start | bytes 4325376 | tf_op jit(solution)/shard_map/reduce_scatter | solution.py:398
  931.6 41.9 %copy-start.27 = (f32[72,1024]{1,0:T(8,128)S(1)}, f32[72,1024]{1,0:T(8,128)}, u32[]{:S(2)}) copy-start(f32[72,1024]{1,0:T(8,128)} %copy-done.26) | copy-start | bytes 884740
  931.6 41.9 %copy-start.51 = (bf16[72,1024]{0,1:T(8,128)(2,1)S(1)}, bf16[72,1024]{0,1:T(8,128)(2,1)}, u32[]{:S(2)}) copy-start(bf16[72,1024]{0,1:T(8,128)(2,1)} %get-tuple-element.1039) | copy-start | bytes 442372
  978.5 367.2 %reduce-scatter.13.cloned.1.call-start = ((), (), s32[]{:S(2)}) async-start(), calls=%async_computation.26 | async-start | bytes 4325376 | tf_op jit(solution)/shard_map/reduce_scatter | solution.py:396
  1028.5 457.6 %reduce-scatter.15.cloned.1.call-start = ((), (), s32[]{:S(2)}) async-start(), calls=%async_computation.27 | async-start | bytes 4325376 | tf_op jit(solution)/shard_map/reduce_scatter | solution.py:397
  1032.9 598.3 %reduce-scatter.9.cloned.1.call-start = ((), (), s32[]{:S(2)}) async-start(), calls=%async_computation.24 | async-start | bytes 7028736 | tf_op jit(solution)/shard_map/reduce_scatter | solution.py:392
  1042.5 742.9 %reduce-scatter.19.cloned.1.call-start = ((), (), s32[]{:S(2)}) async-start(), calls=%async_computation.29 | async-start | bytes 11894784 | tf_op jit(solution)/shard_map/reduce_scatter | solution.py:400
  1051.3 888.7 %reduce-scatter.21.cloned.1.call-start = ((), (), s32[]{:S(2)}) async-start(), calls=%async_computation.30 | async-start | bytes 11894784 | tf_op jit(solution)/shard_map/reduce_scatter | solution.py:401
  1060.0 1035.0 %reduce-scatter.23.cloned.1.call-start = ((), (), s32[]{:S(2)}) async-start(), calls=%async_computation.31 | async-start | bytes 11894784 | tf_op jit(solution)/shard_map/reduce_scatter | solution.py:402
  1069.6 19.9 slice-start.8
  1074.9 6.3 copy-start.30
  1075.0 6.9 copy-start.2
  1075.0 8.4 copy-start.44
  1075.0 14.6 slice-start.9
  1081.3 10.2 slice-start.6
  1083.3 8.1 slice-start.7
  (80 other events, 204.5 us)
Sparse Core Ops, SparseCore 0:
  10.8 62.4 all-gather.20
  76.2 55.2 all-gather.22
  134.3 55.2 all-gather.28
  192.3 55.2 all-gather.26
  250.4 41.1 all-gather.24
  293.7 41.0 all-gather.30
  337.7 55.4 all-gather.32
  396.1 66.0 all-gather.34
  465.2 66.1 all-gather.36
  534.1 66.1 all-gather.38
  603.2 41.2 all-gather.44
  646.7 41.1 all-gather.46
  738.7 41.0 all-gather.40
  782.5 41.0 all-gather.42
  825.8 41.0 all-gather.48
  878.3 41.3 all-gather.50
  924.0 140.0 reduce-scatter.10
  1066.7 138.2 reduce-scatter.16
  1207.9 137.7 reduce-scatter.12
  1348.4 137.6 reduce-scatter.14
  1489.0 142.1 reduce-scatter.8
  1634.2 151.1 reduce-scatter.18
  1788.4 151.6 reduce-scatter.20
  1942.9 152.0 reduce-scatter.22
where the time goes:
time: 2120 us; the launch traced here: 2100 us
  waiting for transfers between devices  1460 us (69%)
  local copies, waits for them, and re-layouts  222 us (10%)
  matrix products  203 us (10%)
  blocking collectives  160 us (8%)
  other arithmetic  34 us (2%)
    reduce_scatter x1, waiting for transfers between devices, local(): lax.psum_scatter(grad_down, ('dp', 'seq'), scatter_dimension=1, tiled=True)  155 us
    reduce_scatter x1, waiting for transfers between devices, local(): lax.psum_scatter(grad_up, ('dp', 'seq'), scatter_dimension=1, tiled=True)  155 us
    reduce_scatter x1, waiting for transfers between devices, local(): lax.psum_scatter(grad_gate, ('dp', 'seq'), scatter_dimension=1, tiled=True)  154 us
    reduce_scatter x1, waiting for transfers between devices, local(): lax.psum_scatter(grad_in, ('dp', 'seq'), scatter_dimension=1, tiled=True)  145 us
    reduce_scatter x1, waiting for transfers between devices, local(): lax.psum_scatter(grad_key, ('dp', 'seq'), scatter_dimension=1, tiled=True)  141 us
    reduce_scatter x1, waiting for transfers between devices, local(): lax.psum_scatter(grad_value, ('dp', 'seq'), scatter_dimension=1, tiled=True)  140 us
    unnamed x2, blocking collectives  81.1 us
    all_gather x2, waiting for transfers between devices, local(): lax.all_gather(keys_local, 'seq', axis=0, tiled=True)  79.8 us
  transfers between devices with their start and end apart: 24, of which 20 were waited for; matrix products, arithmetic and copies ran while one was open for 19% of the time, Pallas kernels for 0%

commit v1 on v0

v1 whole, which is shorter than its diff:
```python
import jax
import jax.numpy as jnp
from jax import lax
from jax.experimental import pallas as pl
from jax.experimental.pallas import tpu as pltpu
from jax.sharding import PartitionSpec as P

HEADS = 16
HEAD_DIM = 64
BUCKETS = 32
PATCHES_IMG = 256
TEXT_MOST = 192

EPSILON = 1e-06
MASKED = -1e30
STARTS = (0, 1, 2, 3, 4, 5, 6, 7, 8, 12, 16, 23, 32, 46, 64, 91)
BF16 = jnp.bfloat16
F32 = jnp.float32
INTERPRET = False

SEG_Q = PATCHES_IMG + TEXT_MOST
SEG_K = 2 * PATCHES_IMG
TEXT_K = SEG_K - PATCHES_IMG
TEXT_PITCH = 32


def dot_nt(left, right):
    return lax.dot_general(left, right, (((1,), (1,)), ((), ())), preferred_element_type=F32)


def dot_nn(left, right):
    return lax.dot_general(left, right, (((1,), (0,)), ((), ())), preferred_element_type=F32)


def dot_tn(left, right):
    return lax.dot_general(left, right, (((0,), (0,)), ((), ())), preferred_element_type=F32)


def rms_norm(values, gain):
    return values * lax.rsqrt(jnp.mean(values * values, axis=-1, keepdims=True) + EPSILON) * gain


def gelu_tanh(values):
    return (
        0.5
        * values
        * (1.0 + jnp.tanh(0.7978845608 * (values + 0.044715 * values * values * values)))
    )


def gated_unit(gate_pre, up_pre):
    return gelu_tanh(gate_pre) * up_pre


def swap(array, step):
    axis, bit = step
    count = lax.axis_size(axis)
    return lax.ppermute(array, axis, [(i, i ^ (1 << bit)) for i in range(count)])


def my_bit(step):
    axis, bit = step
    return (lax.axis_index(axis) >> bit) & 1


def rank(step):
    return (1000 if step[0] == "dp" else 0) + step[1]


def gather(block, order, absolute):
    rows, width = block.shape
    have = []
    for step in order:
        other = swap(block, step)
        at = sum(1 for done in have if rank(done) > rank(step))
        shape = [2] * len(have) + [rows, width]
        shape.insert(at, 1)
        mine, other = block.reshape(shape), other.reshape(shape)
        if absolute:
            bit = my_bit(step) == 1
            mine, other = jnp.where(bit, other, mine), jnp.where(bit, mine, other)
        have.append(step)
        block = jnp.concatenate([mine, other], axis=at).reshape((2 ** len(have)) * rows, width)
    return block


def scatter_add(grads, order, every, absolute, wide=()):
    every = sorted(every, key=rank, reverse=True)
    width = grads.shape[1]
    for step in order:
        at = every.index(step)
        rows = grads.shape[0] // 2
        view = grads.reshape(2**at, 2, rows // 2**at, width)
        if absolute:
            bit = my_bit(step)
            keep = lax.dynamic_slice_in_dim(view, bit, 1, 1)
            send = lax.dynamic_slice_in_dim(view, 1 - bit, 1, 1)
        else:
            keep = view[:, 0:1]
            send = view[:, 1:2]
        keep = keep.reshape(rows, width)
        send = send.reshape(rows, width)
        kind = F32 if step in wide else BF16
        got = swap(send.astype(kind), step)
        grads = keep.astype(F32) + got.astype(F32)
        every = [other for other in every if other != step]
    return grads


def bias_kernel(table_ref, out_ref):
    delta = lax.broadcasted_iota(jnp.int32, out_ref.shape, 0) - lax.broadcasted_iota(
        jnp.int32, out_ref.shape, 1
    )
    value = jnp.full(out_ref.shape, table_ref[0, BUCKETS - 1], F32)
    for which in range(14, 0, -1):
        value = jnp.where(delta > -STARTS[which + 1], table_ref[0, 16 + which], value)
    for which in range(16):
        value = jnp.where(delta >= STARTS[which], table_ref[0, which], value)
    out_ref[...] = value


def bucket_kernel(d_ref, out_ref):
    shape = d_ref.shape
    delta = lax.broadcasted_iota(jnp.int32, shape, 0) - lax.broadcasted_iota(jnp.int32, shape, 1)
    values = d_ref[...]
    rows = []
    for which in range(BUCKETS):
        low = STARTS[which % 16]
        high = STARTS[which % 16 + 1] if which % 16 < 15 else 1 << 20
        if which < 16:
            inside = (delta >= low) & (delta < high)
        else:
            inside = (delta <= -max(low, 1)) & (delta > -high)
        rows.append(jnp.sum(jnp.where(inside, values, 0.0), axis=0, keepdims=True))
    sums = jnp.sum(jnp.concatenate(rows, axis=0), axis=1, keepdims=True)
    out_ref[...] = jnp.broadcast_to(sums, out_ref.shape)


def unpack(source_ref, where, row, pat_ref, txt_ref, patch_dev, text_dev, lanes):
    tail = TEXT_PITCH - text_dev
    for place in range(source_ref.shape[0]):
        block = where(place)
        patches = block[0:patch_dev, lanes]
        text = block[patch_dev : patch_dev + text_dev, lanes]
        pat_ref[row, place * patch_dev : (place + 1) * patch_dev, :] = patches
        txt_ref[row, place * TEXT_PITCH : place * TEXT_PITCH + text_dev, :] = text
        if tail:
            txt_ref[row, place * TEXT_PITCH + text_dev : (place + 1) * TEXT_PITCH, :] = jnp.zeros(
                (tail, text.shape[1]), text.dtype
            )


def picker(count, text_rows, text_dev, slot_count, first, length):
    shape = (count, text_rows)
    column = lax.broadcasted_iota(jnp.int32, shape, 1)
    inner = column & (TEXT_PITCH - 1)
    slot = (column // TEXT_PITCH) * text_dev + inner
    fill = jnp.where(slot >= slot_count // 2, slot - slot_count // 2, slot + slot_count // 2)
    line = lax.broadcasted_iota(jnp.int32, shape, 0)
    hit = (fill == first + line) & (line < length) & (inner < text_dev)
    return hit.astype(F32).astype(BF16)


def softmax(scores):
    top = jnp.max(scores, axis=-1, keepdims=True)
    expd = jnp.exp(scores - top)
    return expd / jnp.sum(expd, axis=-1, keepdims=True)


def segment_start(len_ref, row, which):
    return lax.fori_loop(0, which, lambda at, total: total + len_ref[row, at], jnp.int32(0))


def forward_kernel(dims, me_ref, len_ref, bias_ref, qkv_ref, o_ref, pat, txt, opat, otxt):
    rows, images, patch_dev, text_dev, slots = dims
    seq_count = qkv_ref.shape[0]
    text_rows = seq_count * TEXT_PITCH
    for row in range(rows):
        unpack(
            qkv_ref,
            lambda place, row=row: qkv_ref.at[place ^ me_ref[0], row],
            row, pat, txt, patch_dev, text_dev, slice(None),
        )
    otxt[...] = jnp.zeros_like(otxt)

    def attend(compact, queries, keys, length):
        q = compact[:queries, :HEAD_DIM]
        k = compact[:keys, HEAD_DIM : 2 * HEAD_DIM]
        v = compact[:keys, 2 * HEAD_DIM :]
        scores = dot_nt(q, k) + bias_ref[:queries, :keys]
        column = lax.broadcasted_iota(jnp.int32, scores.shape, 1)
        probs = softmax(jnp.where(column < length, scores, MASKED)).astype(BF16)
        return dot_nn(probs, v).astype(BF16)

    def one_segment(step, carry):
        row, image = step // images, step % images
        length = len_ref[row, image]
        first = segment_start(len_ref, row, image)
        pick = picker(TEXT_K, text_rows, text_dev, slots, first, length)
        text = dot_nn(pick, txt[row]).astype(BF16)
        at = pl.multiple_of(image * PATCHES_IMG, PATCHES_IMG)
        compact = jnp.concatenate([pat[row, pl.ds(at, PATCHES_IMG), :], text], axis=0)
        out = attend(compact, SEG_Q, SEG_K, PATCHES_IMG + length)
        opat[row, pl.ds(at, PATCHES_IMG), :] = out[:PATCHES_IMG]
        otxt[row] = otxt[row] + dot_tn(pick[:TEXT_MOST], out[PATCHES_IMG:])
        return carry

    lax.fori_loop(0, rows * images, one_segment, 0)
    pad_q = slots // 4
    pad_k = -(-pad_q // 128) * 128
    for row in range(rows):
        first = segment_start(len_ref, row, images)
        pick = picker(pad_k, text_rows, text_dev, slots, first, pad_q)
        compact = dot_nn(pick, txt[row]).astype(BF16)
        out = attend(compact, pad_q, pad_k, pad_q)
        otxt[row] = otxt[row] + dot_tn(pick[:pad_q], out)
    for place in range(seq_count):
        o_ref[place, 0:patch_dev, :] = jnp.concatenate(
            [opat[row, place * patch_dev : (place + 1) * patch_dev, :] for row in range(rows)],
            axis=1,
        )
        low = place * TEXT_PITCH
        o_ref[place, patch_dev : patch_dev + text_dev, :] = jnp.concatenate(
            [otxt[row, low : low + text_dev, :].astype(BF16) for row in range(rows)], axis=1
        )


def backward_kernel(
    dims, me_ref, len_ref, bias_ref, qkv_ref, do_ref, dqkv_ref, dbias_ref,
    pat, txt, dpat, dtxt, gpat, gtxt,
):
    rows, images, patch_dev, text_dev, slots = dims
    seq_count = qkv_ref.shape[0]
    text_rows = seq_count * TEXT_PITCH
    for row in range(rows):
        unpack(
            qkv_ref,
            lambda place, row=row: qkv_ref.at[place ^ me_ref[0], row],
            row, pat, txt, patch_dev, text_dev, slice(None),
        )
        unpack(
            do_ref,
            lambda place: do_ref.at[place],
            row, dpat, dtxt, patch_dev, text_dev,
            slice(row * HEAD_DIM, (row + 1) * HEAD_DIM),
        )
    gtxt[...] = jnp.zeros_like(gtxt)
    dbias_ref[...] = jnp.zeros_like(dbias_ref)

    def attend_back(compact, d_out, queries, keys, length):
        q = compact[:queries, :HEAD_DIM]
        k = compact[:keys, HEAD_DIM : 2 * HEAD_DIM]
        v = compact[:keys, 2 * HEAD_DIM :]
        scores = dot_nt(q, k) + bias_ref[:queries, :keys]
        column = lax.broadcasted_iota(jnp.int32, scores.shape, 1)
        probs = softmax(jnp.where(column < length, scores, MASKED))
        d_probs = dot_nt(d_out, v)
        centre = jnp.sum(d_probs * probs, axis=-1, keepdims=True)
        d_scores = probs * (d_probs - centre)
        d_low = d_scores.astype(BF16)
        d_q = dot_nn(d_low, k).astype(BF16)
        d_k = dot_tn(d_low, q).astype(BF16)
        d_v = dot_tn(probs.astype(BF16), d_out).astype(BF16)
        return d_scores, jnp.concatenate([d_q, d_k[:queries], d_v[:queries]], axis=1)

    def one_segment(step, carry):
        row, image = step // images, step % images
        length = len_ref[row, image]
        first = segment_start(len_ref, row, image)
        pick = picker(TEXT_K, text_rows, text_dev, slots, first, length)
        at = pl.multiple_of(image * PATCHES_IMG, PATCHES_IMG)
        text = dot_nn(pick, txt[row]).astype(BF16)
        compact = jnp.concatenate([pat[row, pl.ds(at, PATCHES_IMG), :], text], axis=0)
        text_do = dot_nn(pick[:TEXT_MOST], dtxt[row]).astype(BF16)
        d_out = jnp.concatenate([dpat[row, pl.ds(at, PATCHES_IMG), :], text_do], axis=0)
        d_scores, grads = attend_back(compact, d_out, SEG_Q, SEG_K, PATCHES_IMG + length)
        dbias_ref[...] = dbias_ref[...] + d_scores
        gpat[row, pl.ds(at, PATCHES_IMG), :] = grads[:PATCHES_IMG]
        gtxt[row] = gtxt[row] + dot_tn(pick[:TEXT_MOST], grads[PATCHES_IMG:])
        return carry

    lax.fori_loop(0, rows * images, one_segment, 0)
    pad_q = slots // 4
    pad_k = -(-pad_q // 128) * 128
    for row in range(rows):
        first = segment_start(len_ref, row, images)
        pick = picker(pad_k, text_rows, text_dev, slots, first, pad_q)
        compact = dot_nn(pick, txt[row]).astype(BF16)
        d_out = dot_nn(pick[:pad_q], dtxt[row]).astype(BF16)
        d_scores, grads = attend_back(compact, d_out, pad_q, pad_k, pad_q)
        dbias_ref[:pad_q, :pad_k] = dbias_ref[:pad_q, :pad_k] + d_scores
        gtxt[row] = gtxt[row] + dot_tn(pick[:pad_q], grads)
    for row in range(rows):
        for place in range(seq_count):
            source = place ^ me_ref[0]
            dqkv_ref[source, row, 0:patch_dev, :] = gpat[
                row, place * patch_dev : (place + 1) * patch_dev, :
            ]
            low = place * TEXT_PITCH
            dqkv_ref[source, row, patch_dev : patch_dev + text_dev, :] = gtxt[
                row, low : low + text_dev, :
            ].astype(BF16)


SMEM = pl.BlockSpec(memory_space=pltpu.SMEM)
VMEM = pl.BlockSpec(memory_space=pltpu.VMEM)


def call(kernel, out_shape, in_specs, scratch=(), flops=0, bytes_accessed=0):
    single = not isinstance(out_shape, (tuple, list))
    return pl.pallas_call(
        kernel,
        out_shape=out_shape,
        in_specs=in_specs,
        out_specs=VMEM if single else [VMEM] * len(out_shape),
        scratch_shapes=list(scratch),
        cost_estimate=pl.CostEstimate(
            flops=flops, bytes_accessed=bytes_accessed, transcendentals=0
        ),
        compiler_params=pltpu.CompilerParams(vmem_limit_bytes=48 << 20),
        interpret=INTERPRET,
    )


def local(
    patch_features, text_embeds, text_lengths, w_in, b_in, gain_attn, w_query, w_key, w_value,
    w_out, gain_ffn, w_gate, w_up, w_down, position_bias, d_patch, d_text,
):
    seq_count, dp_count = lax.axis_size("seq"), lax.axis_size("dp")
    dev_count = seq_count * dp_count
    seq_index, dp_index = lax.axis_index("seq"), lax.axis_index("dp")
    rows, patch_dev, vit = patch_features.shape
    text_dev = text_embeds.shape[1]
    tok = patch_dev + text_dev
    mine = rows * tok
    d_model = text_embeds.shape[2]
    cols = w_in.shape[1]
    images = text_lengths.shape[1]
    slots = text_dev * seq_count
    seq_high = [("seq", bit) for bit in range(seq_count.bit_length() - 2, 1, -1)]
    near, core = ("seq", 1), ("seq", 0)
    dp_bits = [("dp", bit) for bit in range(dp_count.bit_length() - 1)]
    every = dp_bits + seq_high + [near, core]
    both = ("dp", "seq")

    bias_count = position_bias.shape[0]
    extra = jnp.zeros((cols, 128), BF16)
    extra = extra.at[:, 0].set(b_in).at[:, 1].set(gain_attn).at[:, 2].set(gain_ffn)
    extra = extra.at[:bias_count, 3].set(position_bias)
    pack = jnp.concatenate([w_in.T, extra], axis=1)
    wide = vit + 128
    half_in = wide // 256 * 128
    in_low = gather(pack[:, :half_in], seq_high + dp_bits + [near, core], True)
    in_high = gather(pack[:, half_in:], seq_high + [near] + dp_bits + [core], True)

    per_head = dev_count // HEADS
    twins = seq_count // HEADS
    head = seq_index // twins
    twin = seq_index % twins
    place_in_head = dp_index * twins + twin
    row_count = rows // twins
    three = jnp.concatenate([w_query.T, w_key.T, w_value.T], axis=0)

    def to_rank(which_head, place):
        return (place // twins) * seq_count + which_head * twins + place % twins

    def rounds(turn, back):
        pairs = []
        for which_head in range(HEADS):
            for i in range(per_head):
                owner = which_head * per_head + i
                user = to_rank(which_head, (i + turn) % per_head)
                pairs.append((user, owner) if back else (owner, user))
        return pairs

    pieces = jnp.stack([lax.ppermute(three, both, rounds(turn, False)) for turn in range(per_head)])
    pieces = pieces.reshape(per_head, 3, cols, d_model)
    ordered = [
        lax.dynamic_index_in_dim(pieces, (place_in_head - i) % per_head, 0, keepdims=False)
        for i in range(per_head)
    ]
    w_head = jnp.stack(ordered, axis=1).reshape(3 * HEAD_DIM, d_model)

    ff_order = seq_high + dp_bits
    units = w_gate.shape[1]
    down_out = jnp.transpose(w_down.reshape(dev_count, units, cols), (0, 2, 1))
    down_in = lax.all_to_all(down_out, both, 0, 0, tiled=True).reshape(d_model, units)
    full_gate = gather(w_gate.T, ff_order, False)
    full_up = gather(w_up.T, ff_order, False)
    full_down = gather(down_in.T, ff_order, False)
    full_out = gather(w_out.T, seq_high + [near] + dp_bits + [core], True)

    features = patch_features.reshape(rows * patch_dev, vit)
    ones = jnp.zeros((rows * patch_dev, 128), BF16).at[:, 0].set(1)
    features_more = jnp.concatenate([features, ones], axis=1)
    patch_rows = dot_nt(features_more[:, :half_in], in_low) + dot_nt(
        features_more[:, half_in:], in_high
    )
    units_eye = jnp.eye(8, 128, dtype=BF16)
    small = dot_nt(units_eye, in_high[:, wide - half_in - 128 :])
    gain_one, gain_two = small[1], small[2]
    table = small[3].reshape(dev_count, cols)[:, :bias_count].reshape(BUCKETS, HEADS)
    my_table = lax.dynamic_slice_in_dim(table, head, 1, 1).reshape(1, BUCKETS)
    resid = jnp.concatenate(
        [patch_rows.reshape(rows, patch_dev, d_model), text_embeds.astype(F32)], axis=1
    ).reshape(mine, d_model)
    normed_one = rms_norm(resid, gain_one).astype(BF16)
    half = d_model // 2
    order_low = seq_high + [near, core]
    order_high = [near] + seq_high + [core]
    all_low = gather(normed_one[:, :half], order_low, False)
    all_high = gather(normed_one[:, half:], order_high, False)

    def my_rows(array):
        view = array.reshape(seq_count, rows, tok, array.shape[1])
        view = lax.dynamic_slice_in_dim(view, twin * row_count, row_count, 1)
        return view.reshape(seq_count * row_count * tok, array.shape[1])

    if twins > 1:
        all_low, all_high = my_rows(all_low), my_rows(all_high)
    qkv = (dot_nt(all_low, w_head[:, :half]) + dot_nt(all_high, w_head[:, half:])).astype(BF16)
    qkv = qkv.reshape(seq_count, row_count, tok, 3 * HEAD_DIM)
    lengths = lax.dynamic_slice_in_dim(text_lengths, twin * row_count, row_count, 0)
    me = seq_index.reshape(1).astype(jnp.int32)
    dims = (row_count, images, patch_dev, text_dev, slots)
    bias = call(
        bias_kernel, jax.ShapeDtypeStruct((SEG_Q, SEG_K), F32), [SMEM], (), 1 << 24, 1 << 20
    )(my_table)
    text_rows = seq_count * TEXT_PITCH
    patches = seq_count * patch_dev
    packed_shape = jax.ShapeDtypeStruct((seq_count, tok, row_count * HEAD_DIM), BF16)
    mixed = call(
        lambda *refs: forward_kernel(dims, *refs),
        packed_shape,
        [SMEM, SMEM, VMEM, VMEM],
        (
            pltpu.VMEM((row_count, patches, 3 * HEAD_DIM), BF16),
            pltpu.VMEM((row_count, text_rows, 3 * HEAD_DIM), BF16),
            pltpu.VMEM((row_count, patches, HEAD_DIM), BF16),
            pltpu.VMEM((row_count, text_rows, HEAD_DIM), F32),
        ),
        1 << 30,
        4 << 20,
    )(me, lengths, bias, qkv)
    mixed = lax.all_to_all(mixed, "seq", 0, 0, tiled=True)
    mixed = mixed.reshape(HEADS, twins, tok, row_count, HEAD_DIM)
    attn_out = jnp.transpose(mixed, (1, 3, 2, 0, 4)).reshape(mine, d_model)
    resid_one = resid + dot_nt(attn_out, full_out)
    normed_two = rms_norm(resid_one, gain_two).astype(BF16)
    team = [near, core]
    upstream = jnp.concatenate([d_patch, d_text], axis=1).reshape(mine, d_model)
    team_up = gather(upstream, team, False)
    team_normed = gather(normed_two, team, False)
    gate_pre = dot_nt(team_normed, full_gate)
    up_pre = dot_nt(team_normed, full_up)
    hidden, gated_back = jax.vjp(gated_unit, gate_pre, up_pre)
    hidden = hidden.astype(BF16)
    out_part = dot_nn(hidden, full_down)
    result = resid_one + scatter_add(out_part, [core, near], team, False, (core,))
    result = result.astype(BF16).reshape(rows, tok, d_model)

    d_hidden = dot_nt(team_up, full_down)
    d_gate, d_up = gated_back(d_hidden)
    d_gate, d_up = d_gate.astype(BF16), d_up.astype(BF16)
    d_normed_two = scatter_add(
        dot_nn(d_gate, full_gate) + dot_nn(d_up, full_up), [core, near], team, False, (core,)
    )
    back = ff_order[::-1]
    grad_down = scatter_add(dot_tn(hidden, team_up), back, ff_order, False)
    grad_gate = scatter_add(dot_tn(d_gate, team_normed), back, ff_order, False)
    grad_up = scatter_add(dot_tn(d_up, team_normed), back, ff_order, False)
    down_back = grad_down.T.reshape(dev_count, cols, units)
    down_back = lax.all_to_all(down_back, both, 0, 0, tiled=True)
    grad_down = jnp.transpose(down_back, (0, 2, 1)).reshape(dev_count * units, cols)

    _, norm_back_two = jax.vjp(rms_norm, resid_one, gain_two)
    d_resid_one, grad_gain_two = norm_back_two(d_normed_two)
    d_resid_one = d_resid_one + upstream.astype(F32)
    d_mix = d_resid_one.astype(BF16)
    grad_out = scatter_add(
        dot_tn(d_mix, attn_out), [core] + dp_bits[::-1] + [near] + seq_high[::-1], every, True
    )
    d_attn = dot_nn(d_mix, full_out).astype(BF16)
    d_attn = d_attn.reshape(twins, row_count, tok, HEADS, HEAD_DIM)
    d_attn = jnp.transpose(d_attn, (3, 0, 2, 1, 4)).reshape(packed_shape.shape)
    d_attn = lax.all_to_all(d_attn, "seq", 0, 0, tiled=True)
    d_qkv, d_bias = call(
        lambda *refs: backward_kernel(dims, *refs),
        (
            jax.ShapeDtypeStruct(qkv.shape, BF16),
            jax.ShapeDtypeStruct((SEG_Q, SEG_K), F32),
        ),
        [SMEM, SMEM, VMEM, VMEM, VMEM],
        (
            pltpu.VMEM((row_count, patches, 3 * HEAD_DIM), BF16),
            pltpu.VMEM((row_count, text_rows, 3 * HEAD_DIM), BF16),
            pltpu.VMEM((row_count, patches, HEAD_DIM), BF16),
            pltpu.VMEM((row_count, text_rows, HEAD_DIM), BF16),
            pltpu.VMEM((row_count, patches, 3 * HEAD_DIM), BF16),
            pltpu.VMEM((row_count, text_rows, 3 * HEAD_DIM), F32),
        ),
        3 << 30,
        8 << 20,
    )(me, lengths, bias, qkv, d_attn)
    d_table = call(
        bucket_kernel, jax.ShapeDtypeStruct((BUCKETS, 128), F32), [VMEM], (), 1 << 25, 1 << 20
    )(d_bias)[:, 0]
    d_qkv = d_qkv.reshape(seq_count * row_count * tok, 3 * HEAD_DIM)
    d_head = jnp.concatenate([dot_tn(d_qkv, all_low), dot_tn(d_qkv, all_high)], axis=1)
    d_head = d_head.reshape(3, per_head, cols, d_model).astype(BF16)
    d_three = 0.0
    for turn in range(per_head):
        piece = lax.dynamic_index_in_dim(
            d_head, (place_in_head - turn) % per_head, 1, keepdims=False
        )
        got = lax.ppermute(piece.reshape(3 * cols, d_model), both, rounds(turn, True))
        d_three = d_three + got.astype(F32)

    def all_rows(array):
        if twins == 1:
            return array
        view = array.reshape(seq_count, row_count, tok, array.shape[1])
        zero = jnp.zeros((seq_count, rows, tok, array.shape[1]), array.dtype)
        view = lax.dynamic_update_slice_in_dim(zero, view, twin * row_count, 1)
        return view.reshape(seq_count * mine, array.shape[1])

    seq_bits = seq_high + [near, core]
    d_normed_one = jnp.concatenate(
        [
            scatter_add(
                all_rows(dot_nn(d_qkv, w_head[:, :half])), order_low[::-1], seq_bits, False
            ),
            scatter_add(
                all_rows(dot_nn(d_qkv, w_head[:, half:])), order_high[::-1], seq_bits, False
            ),
        ],
        axis=1,
    )
    _, norm_back_one = jax.vjp(rms_norm, resid, gain_one)
    d_resid, grad_gain_one = norm_back_one(d_normed_one)
    d_resid = (d_resid + d_resid_one).reshape(rows, tok, d_model)
    text_grad = d_resid[:, patch_dev:]
    d_patch_rows = d_resid[:, :patch_dev].reshape(rows * patch_dev, d_model)
    d_low = d_patch_rows.astype(BF16)
    feature_grad = jnp.concatenate(
        [dot_nn(d_low, in_low), dot_nn(d_low, in_high[:, : vit - half_in])], axis=1
    ).reshape(rows, patch_dev, vit)
    pos_grads = d_table[:, None] * (jnp.arange(HEADS)[None, :] == head).astype(F32)
    pos_grads = jnp.pad(
        pos_grads.reshape(dev_count, bias_count), ((0, 0), (0, cols - bias_count))
    ).reshape(1, d_model)
    small_grads = jnp.concatenate(
        [
            jnp.sum(d_patch_rows, axis=0)[None],
            grad_gain_one[None],
            grad_gain_two[None],
            pos_grads,
            jnp.zeros((12, d_model), F32),
        ],
        axis=0,
    ).astype(BF16)
    left = jnp.concatenate([d_low, small_grads], axis=0)
    right = jnp.concatenate(
        [
            jnp.pad(features, ((0, 0), (0, 128))),
            jnp.pad(jnp.eye(16, 128, dtype=BF16), ((0, 0), (vit, 0))),
        ],
        axis=0,
    )
    in_grads = jnp.concatenate(
        [
            scatter_add(
                dot_tn(left, right[:, :half_in]),
                [core, near] + dp_bits[::-1] + seq_high[::-1],
                every,
                True,
            ),
            scatter_add(
                dot_tn(left, right[:, half_in:]),
                [core] + dp_bits[::-1] + [near] + seq_high[::-1],
                every,
                True,
            ),
        ],
        axis=1,
    )
    small_out = in_grads[:, vit:]
    d_three = d_three.reshape(3, cols, d_model)
    return (
        result[:, :patch_dev],
        result[:, patch_dev:],
        feature_grad,
        text_grad,
        in_grads[:, :vit].T,
        small_out[:, 0],
        small_out[:, 1],
        d_three[0].T,
        d_three[1].T,
        d_three[2].T,
        grad_out.T,
        small_out[:, 2],
        grad_gate.T,
        grad_up.T,
        grad_down,
        small_out[:bias_count, 3],
    )


def solution(mesh):
    token = P("dp", "seq", None)
    matrix = P(None, ("dp", "seq"))
    vector = P(("dp", "seq"))
    return jax.shard_map(
        local,
        mesh=mesh,
        in_specs=(
            token, token, P("dp", None), matrix, vector, vector, matrix, matrix, matrix, matrix,
            vector, matrix, matrix, matrix, vector, token, token,
        ),
        out_specs=(
            token, token, token, token, matrix, vector, vector, matrix, matrix, matrix, matrix,
            vector, matrix, matrix, matrix, vector,
        ),
        check_vma=False,
    )
```

time: 2120 us -> 550 us (0.26)
  waiting for transfers between devices: 1460 us -> 212 us
  matrix products: 203 us -> 35.9 us
  blocking collectives: 160 us -> 0 us
  local copies, waits for them, and re-layouts: 222 us -> 94.6 us
  starting transfers between devices: 1.93 us -> 90.8 us
  other arithmetic: 34 us -> 79.1 us
  Pallas kernels: 0 us -> 28.3 us
    reduce_scatter x8 -> x0, waiting for transfers between devices: 945 us -> none  [the longest x1 155 us: local(): lax.psum_scatter(grad_down, ('dp', 'seq'), scatter_dimension=1, tiled=True)]
    all_gather x16 -> x0, waiting for transfers between devices: 514 us -> none  [the longest x2 79.8 us: local(): lax.all_gather(keys_local, 'seq', axis=0, tiled=True)]
    ppermute x0 -> x76, waiting for transfers between devices: none -> 209 us  [the longest x72 209 us: swap(): return lax.ppermute(array, axis, [(i, i ^ 1 << bit) for i in range(count)])]
    dot_general x120 -> x25, matrix products: 203 us -> 35.9 us  [the longest x9 14.5 us: dot_nt(): lax.dot_general(left, right, (((1,), (1,)), ((), ())), preferred_element_...]
    dynamic_slice x152 -> x11, local copies, waits for them, and re-layouts: 143 us -> 2.07 us  [the longest x9 1.96 us: scatter_add(): keep = lax.dynamic_slice_in_dim(view, bit, 1, 1)]
    unnamed x2 -> x0, blocking collectives: 81.1 us -> none
    all_gather x4 -> x0, blocking collectives: 78.5 us -> none  [the longest x2 40.1 us: local(): lax.all_gather(lse_all, 'seq', axis=1, tiled=True)]
    ppermute x0 -> x76, starting transfers between devices: none -> 73 us  [the longest x72 63.7 us: swap(): return lax.ppermute(array, axis, [(i, i ^ 1 << bit) for i in range(count)])]
  transfers between devices with their start and end apart: 24 -> 80, of which waited for: 20 -> 41; matrix products, arithmetic and copies ran while one was open for 19% -> 32% of each run, Pallas kernels for 0% -> 5%
where the time goes in v1:
time: 550 us; the launch traced here: 545 us
  waiting for transfers between devices  212 us (39%)
  local copies, waits for them, and re-layouts  94.6 us (17%)
  starting transfers between devices  90.8 us (17%)
  other arithmetic  79.1 us (14%)
  matrix products  35.9 us (7%)
  Pallas kernels  28.3 us (5%)
    ppermute x72, waiting for transfers between devices, swap(): return lax.ppermute(array, axis, [(i, i ^ 1 << bit) for i in range(count)])  209 us
    ppermute x72, starting transfers between devices, swap(): return lax.ppermute(array, axis, [(i, i ^ 1 << bit) for i in range(count)])  63.7 us
    another operation x14, other arithmetic, gather(): mine, other = (block.reshape(shape), other.reshape(shape))  18.6 us
    concatenate x31, other arithmetic, gather(): jnp.concatenate([mine, other], axis=at)  16.5 us
    concatenate x20, local copies, waits for them, and re-layouts, gather(): jnp.concatenate([mine, other], axis=at)  16.1 us
    unnamed x142, local copies, waits for them, and re-layouts  15 us
    dot_general x9, matrix products, dot_nt(): lax.dot_general(left, right, (((1,), (1,)), ((), ())), preferred_element_...  14.5 us
    pallas_call x1, Pallas kernels, local(): call(lambda *refs: backward_kernel(dims, *refs), (jax.ShapeDtypeStruct(qk...  14 us
  transfers between devices with their start and end apart: 80, of which 41 were waited for; matrix products, arithmetic and copies ran while one was open for 32% of the time, Pallas kernels for 5%

profile of v1, /device:TPU:0, one launch (start us, length us, event | category | flops | bytes accessed | tf_op | source)
XLA Modules:
  0.0 544.7 jit_solution(17245505109872413907)
XLA Ops:
  3.1 6.1 %collective-permute-start.15 = (bf16[96,1024]{1,0:T(8,128)(2,1)S(1)}, bf16[96,1024]{1,0:T(8,128)(2,1)}, u32[]{:S(2)}, u32[]{:S(2)}) collective-permute-start(bf16[96,1024]{1,0:T(8,128)(2,1)S(1)} %pad_maximum_fusion.48), channel_id=1, source_target_pairs={{0,16},{1,0},{2,17},{3,1},{4,18},{5,2},{6,19},{7,3},{8,20},{9,4},{... | collective-permute-start | bytes 589832 | tf_op jit(solution)/shard_map/ppermute | solution.py:376
  10.0 2.4 collective-permute-start
  13.0 2.4 collective-permute-start.30
  17.7 3.4 all-to-all-start.1
  31.9 4.8 collective-permute-done
  38.8 8.5 %collective-permute-done.5 = bf16[32,896]{1,0:T(8,128)(2,1)S(1)} collective-permute-done((bf16[32,896]{1,0:T(8,128)(2,1)S(1)}, bf16[32,896]{1,0:T(8,128)(2,1)S(1)}, u32[]{:S(2)}, u32[]{:S(2)}) %collective-permute-start.5) | collective-permute-done | bytes 57376 | tf_op jit(solution)/shard_map/ppermute | solution.py:58
  47.3 5.1 collective-permute-done.1
  53.8 9.2 %collective-permute-done.27 = bf16[88,1024]{1,0:T(8,128)(2,1)S(1)} collective-permute-done((bf16[88,1024]{1,0:T(8,128)(2,1)S(1)}, bf16[88,1024]{1,0:T(8,128)(2,1)S(1)}, u32[]{:S(2)}, u32[]{:S(2)}) %collective-permute-start.27) | collective-permute-done | bytes 180256 | tf_op jit(solution)/shard_map/ppermute | solution.py:58
  65.6 2.4 collective-permute-done.6
  72.7 3.4 collective-permute-done.7
  76.4 8.2 %collective-permute-done.3 = bf16[256,896]{1,0:T(8,128)(2,1)S(1)} collective-permute-done((bf16[256,896]{1,0:T(8,128)(2,1)S(1)}, bf16[256,896]{1,0:T(8,128)(2,1)S(1)}, u32[]{:S(2)}, u32[]{:S(2)}) %collective-permute-start.3) | collective-permute-done | bytes 458784 | tf_op jit(solution)/shard_map/ppermute | solution.py:58
  100.7 6.4 %collective-permute-done.10 = bf16[144,512]{1,0:T(8,128)(2,1)S(1)} collective-permute-done((bf16[144,512]{1,0:T(8,128)(2,1)S(1)}, bf16[144,512]{1,0:T(8,128)(2,1)S(1)}, u32[]{:S(2)}, u32[]{:S(2)}) %collective-permute-start.10) | collective-permute-done | bytes 147488 | tf_op jit(solution)/shard_map/ppermute | solution.py:58
  108.3 3.3 collective-permute-start.11
  112.6 3.4 collective-permute-start.17
  116.1 6.0 %collective-permute-done.11 = bf16[288,512]{1,0:T(8,128)(2,1)S(1)} collective-permute-done((bf16[288,512]{1,0:T(8,128)(2,1)S(1)}, bf16[288,512]{1,0:T(8,128)(2,1)S(1)}, u32[]{:S(2)}, u32[]{:S(2)}) %collective-permute-start.11) | collective-permute-done | bytes 294944 | tf_op jit(solution)/shard_map/ppermute | solution.py:58
  125.1 3.3 collective-permute-done.17
  129.4 7.8 %collective-permute-done.12 = bf16[576,512]{1,0:T(8,128)(2,1)} collective-permute-done((bf16[576,512]{1,0:T(8,128)(2,1)}, bf16[576,512]{1,0:T(8,128)(2,1)}, u32[]{:S(2)}, u32[]{:S(2)}) %collective-permute-start.12) | collective-permute-done | bytes 589856 | tf_op jit(solution)/shard_map/ppermute | solution.py:58
  139.6 10.6 %collective-permute-done.33 = bf16[88,1024]{0,1:T(8,128)(2,1)S(1)} collective-permute-done((bf16[88,1024]{0,1:T(8,128)(2,1)}, bf16[88,1024]{0,1:T(8,128)(2,1)S(1)}, u32[]{:S(2)}, u32[]{:S(2)}) %collective-permute-start.33) | collective-permute-done | bytes 180256 | tf_op jit(solution)/shard_map/ppermute | solution.py:58
  153.1 2.2 fusion.140
  158.3 2.3 fusion.137
  184.5 11.8 %shard_map.289 = bf16[16,72,128]{2,1,0:T(8,128)(2,1)} custom-call(s32[1]{0:T(128)} %bitcast.58.refs_0_, s32[2,3]{1,0:T(2,128)S(1)} %copy-done, f32[448,512]{1,0:T(8,128)S(1)} %shard_map.288.refs_2_, bf16[16,2,72,192]{3,2,1,0:T(8,128)(2,1)S(1)} %bitcast.618), custom_call_target="tpu_custom_call" | custom-call | flops 1073741824 | bytes 4194304 | tf_op jit(solution)/shard_map/pallas_call | solution.py:432
  196.3 4.2 all-to-all-start
  200.5 2.7 fusion.139
  215.5 2.7 multiply_reduce_fusion.4
  218.4 2.4 pad_maximum_fusion.7
  220.9 6.2 %collective-permute-done.25 = bf16[144,1024]{1,0:T(8,128)(2,1)S(1)} collective-permute-done((bf16[144,1024]{1,0:T(8,128)(2,1)S(1)}, bf16[144,1024]{1,0:T(8,128)(2,1)S(1)}, u32[]{:S(2)}, u32[]{:S(2)}) %collective-permute-start.25) | collective-permute-done | bytes 294944 | tf_op jit(solution)/shard_map/ppermute | solution.py:58
  228.3 2.4 pad_maximum_fusion.6
  230.7 2.2 copy.198
  232.9 3.3 pad_maximum_fusion.3
  236.2 3.9 copy.199
  240.1 4.0 fusion.149
  250.9 2.3 multiply_convert_fusion.1
  254.5 3.9 fusion.13
  258.4 2.4 convolution_add_fusion.1
  262.9 3.5 reshape.2539
  266.4 2.9 convolution_bitcast_fusion.2
  272.2 3.4 reshape.2545
  275.5 2.9 convolution_bitcast_fusion.1
  282.7 3.4 reshape.2551
  286.1 3.0 convolution_bitcast_fusion
  295.2 11.5 %collective-permute-done.70 = bf16[352,1024]{1,0:T(8,128)(2,1)} collective-permute-done((bf16[352,1024]{1,0:T(8,128)(2,1)}, bf16[352,1024]{1,0:T(8,128)(2,1)}, u32[]{:S(2)}, u32[]{:S(2)}) %collective-permute-start.70) | collective-permute-done | bytes 720928 | tf_op jit(solution)/shard_map/ppermute | solution.py:58
  308.2 12.8 %collective-permute-done.73 = bf16[352,1024]{1,0:T(8,128)(2,1)S(1)} collective-permute-done((bf16[352,1024]{1,0:T(8,128)(2,1)S(1)}, bf16[352,1024]{1,0:T(8,128)(2,1)S(1)}, u32[]{:S(2)}, u32[]{:S(2)}) %collective-permute-start.73) | collective-permute-done | bytes 720928 | tf_op jit(solution)/shard_map/ppermute | solution.py:58
  325.3 11.4 %collective-permute-done.71 = bf16[176,1024]{1,0:T(8,128)(2,1)S(1)} collective-permute-done((bf16[176,1024]{1,0:T(8,128)(2,1)S(1)}, bf16[176,1024]{1,0:T(8,128)(2,1)S(1)}, u32[]{:S(2)}, u32[]{:S(2)}) %collective-permute-start.71) | collective-permute-done | bytes 360480 | tf_op jit(solution)/shard_map/ppermute | solution.py:58
  337.5 6.7 %collective-permute-done.74 = bf16[176,1024]{1,0:T(8,128)(2,1)S(1)} collective-permute-done((bf16[176,1024]{1,0:T(8,128)(2,1)S(1)}, bf16[176,1024]{1,0:T(8,128)(2,1)S(1)}, u32[]{:S(2)}, u32[]{:S(2)}) %collective-permute-start.74) | collective-permute-done | bytes 360480 | tf_op jit(solution)/shard_map/ppermute | solution.py:58
  350.9 5.8 %collective-permute-done.75 = bf16[88,1024]{1,0:T(8,128)(2,1)S(1)} collective-permute-done((bf16[88,1024]{1,0:T(8,128)(2,1)S(1)}, bf16[88,1024]{1,0:T(8,128)(2,1)S(1)}, u32[]{:S(2)}, u32[]{:S(2)}) %collective-permute-start.75) | collective-permute-done | bytes 180256 | tf_op jit(solution)/shard_map/ppermute | solution.py:58
  359.4 4.2 all-to-all-start.3
  368.7 2.2 convert_bitcast_fusion
  380.4 6.0 %all-to-all-start.2 = ((bf16[16,72,128]{2,1,0:T(8,128)(2,1)}), bf16[16,72,128]{2,1,0:T(8,128)(2,1)S(1)}, u32[]{:S(2)}, u32[]{:S(2)}) async-start(bf16[16,72,128]{2,1,0:T(8,128)(2,1)} %reshape.2487), calls=%async_computation.2 | async-start | bytes 589824 | tf_op jit(solution)/shard_map/all_to_all | solution.py:486
  397.1 14.0 %shard_map.290 = (bf16[16,2,72,192]{3,2,1,0:T(8,128)(2,1)S(1)}, f32[448,512]{1,0:T(8,128)S(1)}) custom-call(s32[1]{0:T(128)} %bitcast.58.refs_0_, s32[2,3]{1,0:T(2,128)S(1)} %copy-done, f32[448,512]{1,0:T(8,128)S(1)} %shard_map.288.refs_2_, bf16[16,2,72,192]{3,2,1,0:T(8,128)(2,1)S(1)} %bitcast.619, bf16[16,72,128]{2,1,0:T(8,128)(2,1)S(1)} %all-to-all-done.2.refs_4_), custom_call_target="tpu_custom_call" | custom-call | flops 3221225472 | bytes 8388608 | tf_op jit(solution)/shard_map/pallas_call | solution.py:487
  426.1 2.5 collective-permute-start.63
  430.5 11.9 %collective-permute-done.63 = bf16[256,1024]{1,0:T(8,128)(2,1)} collective-permute-done((bf16[256,1024]{1,0:T(8,128)(2,1)}, bf16[256,1024]{1,0:T(8,128)(2,1)}, u32[]{:S(2)}, u32[]{:S(2)}) %collective-permute-start.63) | collective-permute-done | bytes 524320 | tf_op jit(solution)/shard_map/ppermute | solution.py:58
  443.7 2.3 collective-permute-start.64
  449.7 3.0 collective-permute-done.64
  456.9 9.2 %collective-permute-done.65 = bf16[64,1024]{1,0:T(8,128)(2,1)S(1)} collective-permute-done((bf16[64,1024]{1,0:T(8,128)(2,1)S(1)}, bf16[64,1024]{1,0:T(8,128)(2,1)S(1)}, u32[]{:S(2)}, u32[]{:S(2)}) %collective-permute-start.65) | collective-permute-done | bytes 131104 | tf_op jit(solution)/shard_map/ppermute | solution.py:58
  466.1 2.5 collective-permute-start.66
  469.3 2.7 collective-permute-done.66
  474.7 8.1 %collective-permute-done.43 = bf16[576,512]{1,0:T(8,128)(2,1)S(1)} collective-permute-done((bf16[576,512]{1,0:T(8,128)(2,1)S(1)}, bf16[576,512]{1,0:T(8,128)(2,1)S(1)}, u32[]{:S(2)}, u32[]{:S(2)}) %collective-permute-start.43) | collective-permute-done | bytes 589856 | tf_op jit(solution)/shard_map/ppermute | solution.py:58
  483.4 2.4 collective-permute-done.48
  487.3 4.7 collective-permute-done.44
  492.9 8.0 %collective-permute-done.45 = bf16[144,512]{1,0:T(8,128)(2,1)S(1)} collective-permute-done((bf16[144,512]{1,0:T(8,128)(2,1)S(1)}, bf16[144,512]{1,0:T(8,128)(2,1)S(1)}, u32[]{:S(2)}, u32[]{:S(2)}) %collective-permute-start.45) | collective-permute-done | bytes 147488 | tf_op jit(solution)/shard_map/ppermute | solution.py:58
  514.0 9.6 %collective-permute-done.56 = bf16[256,896]{1,0:T(8,128)(2,1)S(1)} collective-permute-done((bf16[256,896]{1,0:T(8,128)(2,1)S(1)}, bf16[256,896]{1,0:T(8,128)(2,1)S(1)}, u32[]{:S(2)}, u32[]{:S(2)}) %collective-permute-start.56) | collective-permute-done | bytes 458784 | tf_op jit(solution)/shard_map/ppermute | solution.py:58
  526.4 4.2 collective-permute-done.57
  533.0 2.6 collective-permute-done.58
  538.8 2.6 collective-permute-done.59
  (522 shorter events, 215.3 us)
Async XLA Ops:
  1.7 85.0 %collective-permute-start.14 = (bf16[96,1024]{1,0:T(8,128)(2,1)S(1)}, bf16[96,1024]{1,0:T(8,128)(2,1)}, u32[]{:S(2)}, u32[]{:S(2)}) collective-permute-start(bf16[96,1024]{1,0:T(8,128)(2,1)S(1)} %pad_maximum_fusion.48), channel_id=1, source_target_pairs={{0,0},{1,16},{2,1},{3,17},{4,2},{5,18},{6,3},{7,19},{8,4},{9,20},{... | collective-permute-start | bytes 589832 | tf_op jit(solution)/shard_map/ppermute | solution.py:376
  3.1 84.6 %collective-permute-start.15 = (bf16[96,1024]{1,0:T(8,128)(2,1)S(1)}, bf16[96,1024]{1,0:T(8,128)(2,1)}, u32[]{:S(2)}, u32[]{:S(2)}) collective-permute-start(bf16[96,1024]{1,0:T(8,128)(2,1)S(1)} %pad_maximum_fusion.48), channel_id=1, source_target_pairs={{0,16},{1,0},{2,17},{3,1},{4,18},{5,2},{6,19},{7,3},{8,20},{9,4},{... | collective-permute-start | bytes 589832 | tf_op jit(solution)/shard_map/ppermute | solution.py:376
  10.0 26.7 %collective-permute-start = (bf16[32,896]{1,0:T(8,128)(2,1)S(1)}, bf16[32,896]{1,0:T(8,128)(2,1)S(1)}, u32[]{:S(2)}, u32[]{:S(2)}) collective-permute-start(bf16[32,896]{1,0:T(8,128)(2,1)S(1)} %slice.398), channel_id=1, source_target_pairs={{0,8},{1,9},{2,10},{3,11},{4,12},{5,13},{6,14},{7,15},{8,0},{9,1},... | collective-permute-start | bytes 172040 | tf_op jit(solution)/shard_map/ppermute | solution.py:58
  12.4 26.3 %collective-permute-start.20 = (bf16[32,1024]{1,0:T(8,128)(2,1)}, bf16[32,1024]{1,0:T(8,128)(2,1)S(1)}, u32[]{:S(2)}, u32[]{:S(2)}) collective-permute-start(bf16[32,1024]{1,0:T(8,128)(2,1)} %bitcast.819), channel_id=1, source_target_pairs={{0,8},{1,9},{2,10},{3,11},{4,12},{5,13},{6,14},{7,15},{8,0},{9,1},... | collective-permute-start | bytes 196616 | tf_op jit(solution)/shard_map/ppermute | solution.py:58
  13.0 39.6 %collective-permute-start.30 = (bf16[88,1024]{1,0:T(8,128)(2,1)}, bf16[88,1024]{1,0:T(8,128)(2,1)S(1)}, u32[]{:S(2)}, u32[]{:S(2)}) collective-permute-start(bf16[88,1024]{1,0:T(8,128)(2,1)} %bitcast.792), channel_id=1, source_target_pairs={{0,8},{1,9},{2,10},{3,11},{4,12},{5,13},{6,14},{7,15},{8,0},{9,1},... | collective-permute-start | bytes 540680 | tf_op jit(solution)/shard_map/ppermute | solution.py:58
  17.7 111.7 %all-to-all-start.1 = ((bf16[32,32,88]{2,1,0:T(8,128)(2,1)}), bf16[32,32,88]{2,1,0:T(8,128)(2,1)}, u32[]{:S(2)}, u32[]{:S(2)}) async-start(bf16[32,32,88]{2,1,0:T(8,128)(2,1)} %bitcast.612), calls=%async_computation.1 | async-start | bytes 524288 | tf_op jit(solution)/shard_map/all_to_all | solution.py:387
  36.7 61.9 %collective-permute-start.38 = (bf16[144,1024]{1,0:T(8,128)(2,1)S(1)}, bf16[144,1024]{1,0:T(8,128)(2,1)}, u32[]{:S(2)}, u32[]{:S(2)}) collective-permute-start(bf16[144,1024]{1,0:T(8,128)(2,1)S(1)} %bitcast.704), channel_id=1, source_target_pairs={{0,2},{1,3},{2,0},{3,1},{4,6},{5,7},{6,4},{7,5},{8,10},{9,11},{10,... | collective-permute-start | bytes 884744 | tf_op jit(solution)/shard_map/ppermute | solution.py:58
  38.8 8.5 %collective-permute-start.5 = (bf16[32,896]{1,0:T(8,128)(2,1)S(1)}, bf16[32,896]{1,0:T(8,128)(2,1)S(1)}, u32[]{:S(2)}, u32[]{:S(2)}) collective-permute-start(bf16[32,896]{1,0:T(8,128)(2,1)S(1)} %get-tuple-element.174), channel_id=1, source_target_pairs={{0,8},{1,9},{2,10},{3,11},{4,12},{5,13},{6,14},{7,15},{8,0},{9,1},... | collective-permute-start | bytes 172040 | tf_op jit(solution)/shard_map/ppermute | solution.py:58
  52.4 10.5 %collective-permute-start.27 = (bf16[88,1024]{1,0:T(8,128)(2,1)S(1)}, bf16[88,1024]{1,0:T(8,128)(2,1)S(1)}, u32[]{:S(2)}, u32[]{:S(2)}) collective-permute-start(bf16[88,1024]{1,0:T(8,128)(2,1)S(1)} %bitcast.794), channel_id=1, source_target_pairs={{0,8},{1,9},{2,10},{3,11},{4,12},{5,13},{6,14},{7,15},{8,0},{9,1},... | collective-permute-start | bytes 540680 | tf_op jit(solution)/shard_map/ppermute | solution.py:58
  52.5 11.4 %collective-permute-start.21 = (bf16[64,1024]{1,0:T(8,128)(2,1)S(1)}, bf16[64,1024]{1,0:T(8,128)(2,1)S(1)}, u32[]{:S(2)}, u32[]{:S(2)}) collective-permute-start(bf16[64,1024]{1,0:T(8,128)(2,1)S(1)} %bitcast.800), channel_id=1, source_target_pairs={{0,4},{1,5},{2,6},{3,7},{4,0},{5,1},{6,2},{7,3},{8,12},{9,13},{10,... | collective-permute-start | bytes 393224 | tf_op jit(solution)/shard_map/ppermute | solution.py:58
  68.1 8.1 %collective-permute-start.7 = (bf16[128,896]{1,0:T(8,128)(2,1)S(1)}, bf16[128,896]{1,0:T(8,128)(2,1)S(1)}, u32[]{:S(2)}, u32[]{:S(2)}) collective-permute-start(bf16[128,896]{1,0:T(8,128)(2,1)S(1)} %bitcast.786), channel_id=1, source_target_pairs={{0,2},{1,3},{2,0},{3,1},{4,6},{5,7},{6,4},{7,5},{8,10},{9,11},{10,... | collective-permute-start | bytes 688136 | tf_op jit(solution)/shard_map/ppermute | solution.py:58
  71.5 13.1 %collective-permute-start.3 = (bf16[256,896]{1,0:T(8,128)(2,1)S(1)}, bf16[256,896]{1,0:T(8,128)(2,1)S(1)}, u32[]{:S(2)}, u32[]{:S(2)}) collective-permute-start(bf16[256,896]{1,0:T(8,128)(2,1)S(1)} %bitcast.769), channel_id=1, source_target_pairs={{0,2},{1,3},{2,0},{3,1},{4,6},{5,7},{6,4},{7,5},{8,10},{9,11},{10,... | collective-permute-start | bytes 1376264 | tf_op jit(solution)/shard_map/ppermute | solution.py:58
  76.3 9.3 %collective-permute-start.8 = (bf16[256,896]{1,0:T(8,128)(2,1)S(1)}, bf16[256,896]{1,0:T(8,128)(2,1)S(1)}, u32[]{:S(2)}, u32[]{:S(2)}) collective-permute-start(bf16[256,896]{1,0:T(8,128)(2,1)S(1)} %bitcast.768), channel_id=1, source_target_pairs={{0,16},{16,0},{1,17},{17,1},{2,18},{18,2},{3,19},{19,3},{4,20},{20... | collective-permute-start | bytes 1376264 | tf_op jit(solution)/shard_map/ppermute | solution.py:58
  86.8 69.6 %collective-permute-start.31 = (bf16[176,1024]{1,0:T(8,128)(2,1)}, bf16[176,1024]{1,0:T(8,128)(2,1)}, u32[]{:S(2)}, u32[]{:S(2)}) collective-permute-start(bf16[176,1024]{1,0:T(8,128)(2,1)} %bitcast.144), channel_id=1, source_target_pairs={{0,4},{1,5},{2,6},{3,7},{4,0},{5,1},{6,2},{7,3},{8,12},{9,13},{10,... | collective-permute-start | bytes 1081352 | tf_op jit(solution)/shard_map/ppermute | solution.py:58
  87.7 70.6 %collective-permute-start.28 = (bf16[176,1024]{1,0:T(8,128)(2,1)}, bf16[176,1024]{1,0:T(8,128)(2,1)}, u32[]{:S(2)}, u32[]{:S(2)}) collective-permute-start(bf16[176,1024]{1,0:T(8,128)(2,1)} %bitcast.134), channel_id=1, source_target_pairs={{0,4},{1,5},{2,6},{3,7},{4,0},{5,1},{6,2},{7,3},{8,12},{9,13},{10,... | collective-permute-start | bytes 1081352 | tf_op jit(solution)/shard_map/ppermute | solution.py:58
  90.8 17.5 %collective-permute-start.22 = (bf16[128,1024]{1,0:T(8,128)(2,1)}, bf16[128,1024]{1,0:T(8,128)(2,1)S(1)}, u32[]{:S(2)}, u32[]{:S(2)}) collective-permute-start(bf16[128,1024]{1,0:T(8,128)(2,1)} %bitcast.107), channel_id=1, source_target_pairs={{0,2},{1,3},{2,0},{3,1},{4,6},{5,7},{6,4},{7,5},{8,10},{9,11},{10,... | collective-permute-start | bytes 786440 | tf_op jit(solution)/shard_map/ppermute | solution.py:58
  96.1 11.0 %collective-permute-start.10 = (bf16[144,512]{1,0:T(8,128)(2,1)S(1)}, bf16[144,512]{1,0:T(8,128)(2,1)S(1)}, u32[]{:S(2)}, u32[]{:S(2)}) collective-permute-start(bf16[144,512]{1,0:T(8,128)(2,1)S(1)} %get-tuple-element.153), channel_id=1, source_target_pairs={{0,8},{1,9},{2,10},{3,11},{4,12},{5,13},{6,14},{7,15},{8,0},{9,1},... | collective-permute-start | bytes 442376 | tf_op jit(solution)/shard_map/ppermute | solution.py:58
  100.7 62.1 %collective-permute-start.39 = (bf16[288,1024]{1,0:T(8,128)(2,1)}, bf16[288,1024]{1,0:T(8,128)(2,1)}, u32[]{:S(2)}, u32[]{:S(2)}) collective-permute-start(bf16[288,1024]{1,0:T(8,128)(2,1)} %bitcast.176), channel_id=1, source_target_pairs={{0,1},{1,0},{2,3},{3,2},{4,5},{5,4},{6,7},{7,6},{8,9},{9,8},{10,11... | collective-permute-start | bytes 1769480 | tf_op jit(solution)/shard_map/ppermute | solution.py:58
  108.3 13.8 %collective-permute-start.11 = (bf16[288,512]{1,0:T(8,128)(2,1)S(1)}, bf16[288,512]{1,0:T(8,128)(2,1)S(1)}, u32[]{:S(2)}, u32[]{:S(2)}) collective-permute-start(bf16[288,512]{1,0:T(8,128)(2,1)S(1)} %bitcast.778), channel_id=1, source_target_pairs={{0,4},{1,5},{2,6},{3,7},{4,0},{5,1},{6,2},{7,3},{8,12},{9,13},{10,... | collective-permute-start | bytes 884744 | tf_op jit(solution)/shard_map/ppermute | solution.py:58
  112.6 15.8 %collective-permute-start.17 = (bf16[288,512]{1,0:T(8,128)(2,1)S(1)}, bf16[288,512]{1,0:T(8,128)(2,1)S(1)}, u32[]{:S(2)}, u32[]{:S(2)}) collective-permute-start(bf16[288,512]{1,0:T(8,128)(2,1)S(1)} %bitcast.779), channel_id=1, source_target_pairs={{0,8},{1,9},{2,10},{3,11},{4,12},{5,13},{6,14},{7,15},{8,0},{9,1},... | collective-permute-start | bytes 884744 | tf_op jit(solution)/shard_map/ppermute | solution.py:58
  123.0 14.2 %collective-permute-start.12 = (bf16[576,512]{1,0:T(8,128)(2,1)}, bf16[576,512]{1,0:T(8,128)(2,1)}, u32[]{:S(2)}, u32[]{:S(2)}) collective-permute-start(bf16[576,512]{1,0:T(8,128)(2,1)} %bitcast.67), channel_id=1, source_target_pairs={{0,2},{1,3},{2,0},{3,1},{4,6},{5,7},{6,4},{7,5},{8,10},{9,11},{10,... | collective-permute-start | bytes 1769480 | tf_op jit(solution)/shard_map/ppermute | solution.py:58
  129.3 23.7 %collective-permute-start.18 = (bf16[576,512]{1,0:T(8,128)(2,1)}, bf16[576,512]{1,0:T(8,128)(2,1)}, u32[]{:S(2)}, u32[]{:S(2)}) collective-permute-start(bf16[576,512]{1,0:T(8,128)(2,1)} %bitcast.87), channel_id=1, source_target_pairs={{0,4},{1,5},{2,6},{3,7},{4,0},{5,1},{6,2},{7,3},{8,12},{9,13},{10,... | collective-permute-start | bytes 1769480 | tf_op jit(solution)/shard_map/ppermute | solution.py:58
  137.2 13.0 %collective-permute-start.33 = (bf16[88,1024]{0,1:T(8,128)(2,1)}, bf16[88,1024]{0,1:T(8,128)(2,1)S(1)}, u32[]{:S(2)}, u32[]{:S(2)}) collective-permute-start(bf16[88,1024]{0,1:T(8,128)(2,1)} %bitcast.153), channel_id=1, source_target_pairs={{0,8},{1,9},{2,10},{3,11},{4,12},{5,13},{6,14},{7,15},{8,0},{9,1},... | collective-permute-start | bytes 540680 | tf_op jit(solution)/shard_map/ppermute | solution.py:58
  150.2 25.2 %collective-permute-start.13 = (bf16[1152,512]{1,0:T(8,128)(2,1)}, bf16[1152,512]{1,0:T(8,128)(2,1)}, u32[]{:S(2)}, u32[]{:S(2)}) collective-permute-start(bf16[1152,512]{1,0:T(8,128)(2,1)} %bitcast.70), channel_id=1, source_target_pairs={{0,1},{1,0},{2,3},{3,2},{4,5},{5,4},{6,7},{7,6},{8,9},{9,8},{10,11... | collective-permute-start | bytes 3538952 | tf_op jit(solution)/shard_map/ppermute | solution.py:58
  153.0 18.7 %collective-permute-start.23 = (bf16[256,1024]{1,0:T(8,128)(2,1)}, bf16[256,1024]{1,0:T(8,128)(2,1)}, u32[]{:S(2)}, u32[]{:S(2)}) collective-permute-start(bf16[256,1024]{1,0:T(8,128)(2,1)} %bitcast.765), channel_id=1, source_target_pairs={{0,16},{16,0},{1,17},{17,1},{2,18},{18,2},{3,19},{19,3},{4,20},{20... | collective-permute-start | bytes 1572872 | tf_op jit(solution)/shard_map/ppermute | solution.py:58
  156.4 10.8 %collective-permute-start.34 = (bf16[176,1024]{1,0:T(8,128)(2,1)S(1)}, bf16[176,1024]{1,0:T(8,128)(2,1)S(1)}, u32[]{:S(2)}, u32[]{:S(2)}) collective-permute-start(bf16[176,1024]{1,0:T(8,128)(2,1)S(1)} %bitcast.772), channel_id=1, source_target_pairs={{0,4},{1,5},{2,6},{3,7},{4,0},{5,1},{6,2},{7,3},{8,12},{9,13},{10,... | collective-permute-start | bytes 1081352 | tf_op jit(solution)/shard_map/ppermute | solution.py:58
  158.3 18.6 %collective-permute-start.19 = (bf16[1152,512]{1,0:T(8,128)(2,1)}, bf16[1152,512]{1,0:T(8,128)(2,1)}, u32[]{:S(2)}, u32[]{:S(2)}) collective-permute-start(bf16[1152,512]{1,0:T(8,128)(2,1)} %bitcast.90), channel_id=1, source_target_pairs={{0,1},{1,0},{2,3},{3,2},{4,5},{5,4},{6,7},{7,6},{8,9},{9,8},{10,11... | collective-permute-start | bytes 3538952 | tf_op jit(solution)/shard_map/ppermute | solution.py:58
  162.8 55.6 %collective-permute-start.32 = (bf16[352,1024]{1,0:T(8,128)(2,1)}, bf16[352,1024]{1,0:T(8,128)(2,1)}, u32[]{:S(2)}, u32[]{:S(2)}) collective-permute-start(bf16[352,1024]{1,0:T(8,128)(2,1)} %bitcast.147), channel_id=1, source_target_pairs={{0,16},{16,0},{1,17},{17,1},{2,18},{18,2},{3,19},{19,3},{4,20},{20... | collective-permute-start | bytes 2162696 | tf_op jit(solution)/shard_map/ppermute | solution.py:58
  168.0 60.3 %collective-permute-start.29 = (bf16[352,1024]{1,0:T(8,128)(2,1)}, bf16[352,1024]{1,0:T(8,128)(2,1)}, u32[]{:S(2)}, u32[]{:S(2)}) collective-permute-start(bf16[352,1024]{1,0:T(8,128)(2,1)} %bitcast.137), channel_id=1, source_target_pairs={{0,16},{16,0},{1,17},{17,1},{2,18},{18,2},{3,19},{19,3},{4,20},{20... | collective-permute-start | bytes 2162696 | tf_op jit(solution)/shard_map/ppermute | solution.py:58
  174.1 31.6 %collective-permute-start.24 = (bf16[512,1024]{1,0:T(8,128)(2,1)}, bf16[512,1024]{1,0:T(8,128)(2,1)}, u32[]{:S(2)}, u32[]{:S(2)}) collective-permute-start(bf16[512,1024]{1,0:T(8,128)(2,1)} %bitcast.118), channel_id=1, source_target_pairs={{0,1},{1,0},{2,3},{3,2},{4,5},{5,4},{6,7},{7,6},{8,9},{9,8},{10,11... | collective-permute-start | bytes 3145736 | tf_op jit(solution)/shard_map/ppermute | solution.py:58
  196.3 14.8 %all-to-all-start = ((bf16[16,72,128]{2,1,0:T(8,128)(2,1)}), bf16[16,72,128]{2,1,0:T(8,128)(2,1)}, u32[]{:S(2)}, u32[]{:S(2)}) async-start(bf16[16,72,128]{2,1,0:T(8,128)(2,1)} %shard_map.289), calls=%async_computation | async-start | bytes 589824 | tf_op jit(solution)/shard_map/all_to_all | solution.py:445
  205.4 25.3 %collective-permute-start.35 = (bf16[352,1024]{1,0:T(8,128)(2,1)}, bf16[352,1024]{1,0:T(8,128)(2,1)}, u32[]{:S(2)}, u32[]{:S(2)}) collective-permute-start(bf16[352,1024]{1,0:T(8,128)(2,1)} %bitcast.757), channel_id=1, source_target_pairs={{0,16},{16,0},{1,17},{17,1},{2,18},{18,2},{3,19},{19,3},{4,20},{20... | collective-permute-start | bytes 2162696 | tf_op jit(solution)/shard_map/ppermute | solution.py:58
  218.3 8.8 %collective-permute-start.25 = (bf16[144,1024]{1,0:T(8,128)(2,1)S(1)}, bf16[144,1024]{1,0:T(8,128)(2,1)S(1)}, u32[]{:S(2)}, u32[]{:S(2)}) collective-permute-start(bf16[144,1024]{1,0:T(8,128)(2,1)S(1)} %multiply_convert_fusion.3), channel_id=1, source_target_pairs={{0,2},{1,3},{2,0},{3,1},{4,6},{5,7},{6,4},{7,5},{8,10},{9,11},{10,... | collective-permute-start | bytes 884744 | tf_op jit(solution)/shard_map/ppermute | solution.py:58
  228.2 18.1 %collective-permute-start.26 = (bf16[288,1024]{1,0:T(8,128)(2,1)}, bf16[288,1024]{1,0:T(8,128)(2,1)}, u32[]{:S(2)}, u32[]{:S(2)}) collective-permute-start(bf16[288,1024]{1,0:T(8,128)(2,1)} %bitcast.127), channel_id=1, source_target_pairs={{0,1},{1,0},{2,3},{3,2},{4,5},{5,4},{6,7},{7,6},{8,9},{9,8},{10,11... | collective-permute-start | bytes 1769480 | tf_op jit(solution)/shard_map/ppermute | solution.py:58
  262.4 82.1 %collective-permute-start.40 = (f32[288,1024]{1,0:T(8,128)}, f32[288,1024]{1,0:T(8,128)}, u32[]{:S(2)}, u32[]{:S(2)}) collective-permute-start(f32[288,1024]{1,0:T(8,128)} %bitcast.181), channel_id=1, source_target_pairs={{0,1},{1,0},{2,3},{3,2},{4,5},{5,4},{6,7},{7,6},{8,9},{9,8},{10,11... | collective-permute-start | bytes 3538952 | tf_op jit(solution)/shard_map/ppermute | solution.py:58
  271.9 19.3 %collective-permute-start.67 = (bf16[352,1024]{1,0:T(8,128)(2,1)}, bf16[352,1024]{1,0:T(8,128)(2,1)}, u32[]{:S(2)}, u32[]{:S(2)}) collective-permute-start(bf16[352,1024]{1,0:T(8,128)(2,1)} %fusion.33), channel_id=1, source_target_pairs={{0,16},{16,0},{1,17},{17,1},{2,18},{18,2},{3,19},{19,3},{4,20},{20... | collective-permute-start | bytes 2162696 | tf_op jit(solution)/shard_map/ppermute | solution.py:58
  281.0 25.6 %collective-permute-start.70 = (bf16[352,1024]{1,0:T(8,128)(2,1)}, bf16[352,1024]{1,0:T(8,128)(2,1)}, u32[]{:S(2)}, u32[]{:S(2)}) collective-permute-start(bf16[352,1024]{1,0:T(8,128)(2,1)} %fusion.34), channel_id=1, source_target_pairs={{0,16},{16,0},{1,17},{17,1},{2,18},{18,2},{3,19},{19,3},{4,20},{20... | collective-permute-start | bytes 2162696 | tf_op jit(solution)/shard_map/ppermute | solution.py:58
  289.2 31.8 %collective-permute-start.73 = (bf16[352,1024]{1,0:T(8,128)(2,1)S(1)}, bf16[352,1024]{1,0:T(8,128)(2,1)S(1)}, u32[]{:S(2)}, u32[]{:S(2)}) collective-permute-start(bf16[352,1024]{1,0:T(8,128)(2,1)S(1)} %fusion.35), channel_id=1, source_target_pairs={{0,16},{16,0},{1,17},{17,1},{2,18},{18,2},{3,19},{19,3},{4,20},{20... | collective-permute-start | bytes 2162696 | tf_op jit(solution)/shard_map/ppermute | solution.py:58
  291.0 57.2 %collective-permute-start.36 = (f32[288,1024]{1,0:T(8,128)S(1)}, f32[288,1024]{1,0:T(8,128)S(1)}, u32[]{:S(2)}, u32[]{:S(2)}) collective-permute-start(f32[288,1024]{1,0:T(8,128)S(1)} %bitcast.744), channel_id=1, source_target_pairs={{0,1},{1,0},{2,3},{3,2},{4,5},{5,4},{6,7},{7,6},{8,9},{9,8},{10,11... | collective-permute-start | bytes 3538952 | tf_op jit(solution)/shard_map/ppermute | solution.py:58
  293.9 29.6 %collective-permute-start.68 = (bf16[176,1024]{1,0:T(8,128)(2,1)S(1)}, bf16[176,1024]{1,0:T(8,128)(2,1)S(1)}, u32[]{:S(2)}, u32[]{:S(2)}) collective-permute-start(bf16[176,1024]{1,0:T(8,128)(2,1)S(1)} %bitcast.774), channel_id=1, source_target_pairs={{0,4},{1,5},{2,6},{3,7},{4,0},{5,1},{6,2},{7,3},{8,12},{9,13},{10,... | collective-permute-start | bytes 1081352 | tf_op jit(solution)/shard_map/ppermute | solution.py:58
  321.4 15.3 %collective-permute-start.71 = (bf16[176,1024]{1,0:T(8,128)(2,1)S(1)}, bf16[176,1024]{1,0:T(8,128)(2,1)S(1)}, u32[]{:S(2)}, u32[]{:S(2)}) collective-permute-start(bf16[176,1024]{1,0:T(8,128)(2,1)S(1)} %bitcast.776), channel_id=1, source_target_pairs={{0,4},{1,5},{2,6},{3,7},{4,0},{5,1},{6,2},{7,3},{8,12},{9,13},{10,... | collective-permute-start | bytes 1081352 | tf_op jit(solution)/shard_map/ppermute | solution.py:58
  322.5 21.8 %collective-permute-start.74 = (bf16[176,1024]{1,0:T(8,128)(2,1)S(1)}, bf16[176,1024]{1,0:T(8,128)(2,1)S(1)}, u32[]{:S(2)}, u32[]{:S(2)}) collective-permute-start(bf16[176,1024]{1,0:T(8,128)(2,1)S(1)} %bitcast.775), channel_id=1, source_target_pairs={{0,4},{1,5},{2,6},{3,7},{4,0},{5,1},{6,2},{7,3},{8,12},{9,13},{10,... | collective-permute-start | bytes 1081352 | tf_op jit(solution)/shard_map/ppermute | solution.py:58
  324.4 39.3 %collective-permute-start.69 = (bf16[88,1024]{1,0:T(8,128)(2,1)}, bf16[88,1024]{1,0:T(8,128)(2,1)}, u32[]{:S(2)}, u32[]{:S(2)}) collective-permute-start(bf16[88,1024]{1,0:T(8,128)(2,1)} %fusion.78), channel_id=1, source_target_pairs={{0,8},{1,9},{2,10},{3,11},{4,12},{5,13},{6,14},{7,15},{8,0},{9,1},... | collective-permute-start | bytes 540680 | tf_op jit(solution)/shard_map/ppermute | solution.py:58
  337.5 28.1 %collective-permute-start.72 = (bf16[88,1024]{1,0:T(8,128)(2,1)}, bf16[88,1024]{1,0:T(8,128)(2,1)}, u32[]{:S(2)}, u32[]{:S(2)}) collective-permute-start(bf16[88,1024]{1,0:T(8,128)(2,1)} %fusion.79), channel_id=1, source_target_pairs={{0,8},{1,9},{2,10},{3,11},{4,12},{5,13},{6,14},{7,15},{8,0},{9,1},... | collective-permute-start | bytes 540680 | tf_op jit(solution)/shard_map/ppermute | solution.py:58
  344.4 12.3 %collective-permute-start.75 = (bf16[88,1024]{1,0:T(8,128)(2,1)S(1)}, bf16[88,1024]{1,0:T(8,128)(2,1)S(1)}, u32[]{:S(2)}, u32[]{:S(2)}) collective-permute-start(bf16[88,1024]{1,0:T(8,128)(2,1)S(1)} %fusion.80), channel_id=1, source_target_pairs={{0,8},{1,9},{2,10},{3,11},{4,12},{5,13},{6,14},{7,15},{8,0},{9,1},... | collective-permute-start | bytes 540680 | tf_op jit(solution)/shard_map/ppermute | solution.py:58
  346.8 20.7 %collective-permute-start.41 = (bf16[144,1024]{1,0:T(8,128)(2,1)}, bf16[144,1024]{1,0:T(8,128)(2,1)}, u32[]{:S(2)}, u32[]{:S(2)}) collective-permute-start(bf16[144,1024]{1,0:T(8,128)(2,1)} %fusion.56), channel_id=1, source_target_pairs={{0,2},{1,3},{2,0},{3,1},{4,6},{5,7},{6,4},{7,5},{8,10},{9,11},{10,... | collective-permute-start | bytes 884744 | tf_op jit(solution)/shard_map/ppermute | solution.py:58
  350.2 18.5 %collective-permute-start.37 = (bf16[144,1024]{1,0:T(8,128)(2,1)}, bf16[144,1024]{1,0:T(8,128)(2,1)}, u32[]{:S(2)}, u32[]{:S(2)}) collective-permute-start(bf16[144,1024]{1,0:T(8,128)(2,1)} %fusion.55), channel_id=1, source_target_pairs={{0,2},{1,3},{2,0},{3,1},{4,6},{5,7},{6,4},{7,5},{8,10},{9,11},{10,... | collective-permute-start | bytes 884744 | tf_op jit(solution)/shard_map/ppermute | solution.py:58
  359.4 21.0 %all-to-all-start.3 = ((f32[32,32,88]{2,1,0:T(8,128)}), f32[32,32,88]{2,1,0:T(8,128)}, u32[]{:S(2)}, u32[]{:S(2)}) async-start(f32[32,32,88]{2,1,0:T(8,128)} %bitcast.707), calls=%async_computation.3 | async-start | bytes 1048576 | tf_op jit(solution)/shard_map/all_to_all | solution.py:473
  380.4 16.6 %all-to-all-start.2 = ((bf16[16,72,128]{2,1,0:T(8,128)(2,1)}), bf16[16,72,128]{2,1,0:T(8,128)(2,1)S(1)}, u32[]{:S(2)}, u32[]{:S(2)}) async-start(bf16[16,72,128]{2,1,0:T(8,128)(2,1)} %reshape.2487), calls=%async_computation.2 | async-start | bytes 589824 | tf_op jit(solution)/shard_map/all_to_all | solution.py:486
  389.4 34.1 %collective-permute-start.62 = (bf16[512,1024]{1,0:T(8,128)(2,1)}, bf16[512,1024]{1,0:T(8,128)(2,1)}, u32[]{:S(2)}, u32[]{:S(2)}) collective-permute-start(bf16[512,1024]{1,0:T(8,128)(2,1)} %bitcast.260), channel_id=1, source_target_pairs={{0,1},{1,0},{2,3},{3,2},{4,5},{5,4},{6,7},{7,6},{8,9},{9,8},{10,11... | collective-permute-start | bytes 3145736 | tf_op jit(solution)/shard_map/ppermute | solution.py:58
  417.0 29.1 %collective-permute-start.46 = (bf16[1152,512]{1,0:T(8,128)(2,1)}, bf16[1152,512]{1,0:T(8,128)(2,1)}, u32[]{:S(2)}, u32[]{:S(2)}) collective-permute-start(bf16[1152,512]{1,0:T(8,128)(2,1)} %bitcast.203), channel_id=1, source_target_pairs={{0,1},{1,0},{2,3},{3,2},{4,5},{5,4},{6,7},{7,6},{8,9},{9,8},{10,11... | collective-permute-start | bytes 3538952 | tf_op jit(solution)/shard_map/ppermute | solution.py:58
  417.0 38.0 %collective-permute-start.42 = (bf16[1152,512]{1,0:T(8,128)(2,1)}, bf16[1152,512]{1,0:T(8,128)(2,1)}, u32[]{:S(2)}, u32[]{:S(2)}) collective-permute-start(bf16[1152,512]{1,0:T(8,128)(2,1)} %bitcast.190), channel_id=1, source_target_pairs={{0,1},{1,0},{2,3},{3,2},{4,5},{5,4},{6,7},{7,6},{8,9},{9,8},{10,11... | collective-permute-start | bytes 3538952 | tf_op jit(solution)/shard_map/ppermute | solution.py:58
  420.3 8.5 %collective-permute-start.61 = (bf16[96,1024]{1,0:T(8,128)(2,1)S(1)}, bf16[96,1024]{1,0:T(8,128)(2,1)S(1)}, u32[]{:S(2)}, u32[]{:S(2)}) collective-permute-start(bf16[96,1024]{1,0:T(8,128)(2,1)S(1)} %bitcast.791), channel_id=1, source_target_pairs={{16,0},{0,1},{17,2},{1,3},{18,4},{2,5},{19,6},{3,7},{20,8},{4,9},{... | collective-permute-start | bytes 589832 | tf_op jit(solution)/shard_map/ppermute | solution.py:516
  420.3 8.5 %collective-permute-start.60 = (bf16[96,1024]{1,0:T(8,128)(2,1)S(1)}, bf16[96,1024]{1,0:T(8,128)(2,1)}, u32[]{:S(2)}, u32[]{:S(2)}) collective-permute-start(bf16[96,1024]{1,0:T(8,128)(2,1)S(1)} %bitcast.790), channel_id=1, source_target_pairs={{0,0},{16,1},{1,2},{17,3},{2,4},{18,5},{3,6},{19,7},{4,8},{20,9},{... | collective-permute-start | bytes 589832 | tf_op jit(solution)/shard_map/ppermute | solution.py:516
  426.1 16.3 %collective-permute-start.63 = (bf16[256,1024]{1,0:T(8,128)(2,1)}, bf16[256,1024]{1,0:T(8,128)(2,1)}, u32[]{:S(2)}, u32[]{:S(2)}) collective-permute-start(bf16[256,1024]{1,0:T(8,128)(2,1)} %fusion.46), channel_id=1, source_target_pairs={{0,16},{16,0},{1,17},{17,1},{2,18},{18,2},{3,19},{19,3},{4,20},{20... | collective-permute-start | bytes 1572872 | tf_op jit(solution)/shard_map/ppermute | solution.py:58
  443.7 8.9 %collective-permute-start.64 = (bf16[128,1024]{1,0:T(8,128)(2,1)S(1)}, bf16[128,1024]{1,0:T(8,128)(2,1)S(1)}, u32[]{:S(2)}, u32[]{:S(2)}) collective-permute-start(bf16[128,1024]{1,0:T(8,128)(2,1)S(1)} %bitcast.783), channel_id=1, source_target_pairs={{0,2},{1,3},{2,0},{3,1},{4,6},{5,7},{6,4},{7,5},{8,10},{9,11},{10,... | collective-permute-start | bytes 786440 | tf_op jit(solution)/shard_map/ppermute | solution.py:58
  448.1 24.6 %collective-permute-start.47 = (bf16[576,512]{1,0:T(8,128)(2,1)S(1)}, bf16[576,512]{1,0:T(8,128)(2,1)S(1)}, u32[]{:S(2)}, u32[]{:S(2)}) collective-permute-start(bf16[576,512]{1,0:T(8,128)(2,1)S(1)} %bitcast.763), channel_id=1, source_target_pairs={{0,4},{1,5},{2,6},{3,7},{4,0},{5,1},{6,2},{7,3},{8,12},{9,13},{10,... | collective-permute-start | bytes 1769480 | tf_op jit(solution)/shard_map/ppermute | solution.py:58
  452.8 13.3 %collective-permute-start.65 = (bf16[64,1024]{1,0:T(8,128)(2,1)S(1)}, bf16[64,1024]{1,0:T(8,128)(2,1)S(1)}, u32[]{:S(2)}, u32[]{:S(2)}) collective-permute-start(bf16[64,1024]{1,0:T(8,128)(2,1)S(1)} %bitcast.801), channel_id=1, source_target_pairs={{0,4},{1,5},{2,6},{3,7},{4,0},{5,1},{6,2},{7,3},{8,12},{9,13},{10,... | collective-permute-start | bytes 393224 | tf_op jit(solution)/shard_map/ppermute | solution.py:58
  468.9 13.9 %collective-permute-start.43 = (bf16[576,512]{1,0:T(8,128)(2,1)S(1)}, bf16[576,512]{1,0:T(8,128)(2,1)S(1)}, u32[]{:S(2)}, u32[]{:S(2)}) collective-permute-start(bf16[576,512]{1,0:T(8,128)(2,1)S(1)} %bitcast.764), channel_id=1, source_target_pairs={{0,2},{1,3},{2,0},{3,1},{4,6},{5,7},{6,4},{7,5},{8,10},{9,11},{10,... | collective-permute-start | bytes 1769480 | tf_op jit(solution)/shard_map/ppermute | solution.py:58
  472.9 12.8 %collective-permute-start.48 = (bf16[288,512]{1,0:T(8,128)(2,1)S(1)}, bf16[288,512]{1,0:T(8,128)(2,1)S(1)}, u32[]{:S(2)}, u32[]{:S(2)}) collective-permute-start(bf16[288,512]{1,0:T(8,128)(2,1)S(1)} %fusion.57), channel_id=1, source_target_pairs={{0,8},{1,9},{2,10},{3,11},{4,12},{5,13},{6,14},{7,15},{8,0},{9,1},... | collective-permute-start | bytes 884744 | tf_op jit(solution)/shard_map/ppermute | solution.py:58
  483.1 8.9 %collective-permute-start.44 = (bf16[288,512]{1,0:T(8,128)(2,1)S(1)}, bf16[288,512]{1,0:T(8,128)(2,1)S(1)}, u32[]{:S(2)}, u32[]{:S(2)}) collective-permute-start(bf16[288,512]{1,0:T(8,128)(2,1)S(1)} %bitcast.782), channel_id=1, source_target_pairs={{0,4},{1,5},{2,6},{3,7},{4,0},{5,1},{6,2},{7,3},{8,12},{9,13},{10,... | collective-permute-start | bytes 884744 | tf_op jit(solution)/shard_map/ppermute | solution.py:58
  492.1 8.9 %collective-permute-start.45 = (bf16[144,512]{1,0:T(8,128)(2,1)S(1)}, bf16[144,512]{1,0:T(8,128)(2,1)S(1)}, u32[]{:S(2)}, u32[]{:S(2)}) collective-permute-start(bf16[144,512]{1,0:T(8,128)(2,1)S(1)} %fusion.88), channel_id=1, source_target_pairs={{0,8},{1,9},{2,10},{3,11},{4,12},{5,13},{6,14},{7,15},{8,0},{9,1},... | collective-permute-start | bytes 442376 | tf_op jit(solution)/shard_map/ppermute | solution.py:58
  510.8 12.7 %collective-permute-start.56 = (bf16[256,896]{1,0:T(8,128)(2,1)S(1)}, bf16[256,896]{1,0:T(8,128)(2,1)S(1)}, u32[]{:S(2)}, u32[]{:S(2)}) collective-permute-start(bf16[256,896]{1,0:T(8,128)(2,1)S(1)} %fusion.47), channel_id=1, source_target_pairs={{0,16},{16,0},{1,17},{17,1},{2,18},{18,2},{3,19},{19,3},{4,20},{20... | collective-permute-start | bytes 1376264 | tf_op jit(solution)/shard_map/ppermute | solution.py:58
  513.1 12.7 %collective-permute-start.51 = (bf16[256,896]{1,0:T(8,128)(2,1)S(1)}, bf16[256,896]{1,0:T(8,128)(2,1)S(1)}, u32[]{:S(2)}, u32[]{:S(2)}) collective-permute-start(bf16[256,896]{1,0:T(8,128)(2,1)S(1)} %bitcast.770), channel_id=1, source_target_pairs={{0,2},{1,3},{2,0},{3,1},{4,6},{5,7},{6,4},{7,5},{8,10},{9,11},{10,... | collective-permute-start | bytes 1376264 | tf_op jit(solution)/shard_map/ppermute | solution.py:58
  (87 other events, 741.7 us)

commit v2 on v1

--- a/solution.py
+++ b/solution.py
@@ -67,44 +67,58 @@
     return (1000 if step[0] == "dp" else 0) + step[1]
 
 
-def gather(block, order, absolute):
-    rows, width = block.shape
+def after(value, signal):
+    return value + (signal[(0,) * signal.ndim] * 0).astype(value.dtype)
+
+
+def gather(block, order, absolute, hold=None):
     have = []
-    for step in order:
+    stages = []
+    for number, step in enumerate(order):
+        if hold and number in hold:
+            block = after(block, hold[number])
         other = swap(block, step)
         at = sum(1 for done in have if rank(done) > rank(step))
-        shape = [2] * len(have) + [rows, width]
-        shape.insert(at, 1)
-        mine, other = block.reshape(shape), other.reshape(shape)
+        mine = block
         if absolute:
             bit = my_bit(step) == 1
             mine, other = jnp.where(bit, other, mine), jnp.where(bit, mine, other)
+        outer = 2**at
+        size = block.shape[0] // outer
+        parts = []
+        for which in range(outer):
+            parts += [mine[which * size : (which + 1) * size], other[which * size : (which + 1) * size]]
         have.append(step)
-        block = jnp.concatenate([mine, other], axis=at).reshape((2 ** len(have)) * rows, width)
-    return block
-
-
-def scatter_add(grads, order, every, absolute, wide=()):
+        block = jnp.concatenate(parts, axis=0)
+        stages.append(block)
+    return stages
+
+
+def scatter_add(grads, order, every, absolute, wide=(), hold=None):
     every = sorted(every, key=rank, reverse=True)
     width = grads.shape[1]
-    for step in order:
+    stages = []
+    for number, step in enumerate(order):
         at = every.index(step)
         rows = grads.shape[0] // 2
-        view = grads.reshape(2**at, 2, rows // 2**at, width)
         if absolute:
+            view = grads.reshape(2**at, 2, rows // 2**at, width)
             bit = my_bit(step)
-            keep = lax.dynamic_slice_in_dim(view, bit, 1, 1)
-            send = lax.dynamic_slice_in_dim(view, 1 - bit, 1, 1)
+            keep = lax.dynamic_slice_in_dim(view, bit, 1, 1).reshape(rows, width)
+            send = lax.dynamic_slice_in_dim(view, 1 - bit, 1, 1).reshape(rows, width)
+        elif at == 0:
+            keep, send = grads[:rows], grads[rows:]
         else:
-            keep = view[:, 0:1]
-            send = view[:, 1:2]
-        keep = keep.reshape(rows, width)
-        send = send.reshape(rows, width)
+            view = grads.reshape(2**at, 2, rows // 2**at, width)
+            keep, send = view[:, 0].reshape(rows, width), view[:, 1].reshape(rows, width)
+        if hold and number in hold:
+            send = after(send, hold[number])
         kind = F32 if step in wide else BF16
         got = swap(send.astype(kind), step)
         grads = keep.astype(F32) + got.astype(F32)
         every = [other for other in every if other != step]
-    return grads
+        stages.append(grads)
+    return stages
 
 
 def bias_kernel(table_ref, out_ref):
@@ -136,9 +150,9 @@
     out_ref[...] = jnp.broadcast_to(sums, out_ref.shape)
 
 
-def unpack(source_ref, where, row, pat_ref, txt_ref, patch_dev, text_dev, lanes):
+def unpack(seq_count, where, row, pat_ref, txt_ref, patch_dev, text_dev, lanes):
     tail = TEXT_PITCH - text_dev
-    for place in range(source_ref.shape[0]):
+    for place in range(seq_count):
         block = where(place)
         patches = block[0:patch_dev, lanes]
         text = block[patch_dev : patch_dev + text_dev, lanes]
@@ -171,14 +185,26 @@
     return lax.fori_loop(0, which, lambda at, total: total + len_ref[row, at], jnp.int32(0))
 
 
-def forward_kernel(dims, me_ref, len_ref, bias_ref, qkv_ref, o_ref, pat, txt, opat, otxt):
+class Halves:
+    def __init__(self, me, own_ref, other_ref, row):
+        self.me, self.own, self.other, self.row = me, own_ref, other_ref, row
+
+    def at(self, place):
+        apart = place ^ self.me
+        return apart & 1, apart >> 1
+
+    def __call__(self, place):
+        odd, index = self.at(place)
+        return jnp.where(odd == 1, self.other[index, self.row], self.own[index, self.row])
+
+
+def forward_kernel(dims, me_ref, len_ref, bias_ref, own_ref, other_ref, o_ref, pat, txt, opat, otxt):
     rows, images, patch_dev, text_dev, slots = dims
-    seq_count = qkv_ref.shape[0]
+    seq_count = 2 * own_ref.shape[0]
     text_rows = seq_count * TEXT_PITCH
     for row in range(rows):
         unpack(
-            qkv_ref,
-            lambda place, row=row: qkv_ref.at[place ^ me_ref[0], row],
+            seq_count, Halves(me_ref[0], own_ref, other_ref, row),
             row, pat, txt, patch_dev, text_dev, slice(None),
         )
     otxt[...] = jnp.zeros_like(otxt)
@@ -226,21 +252,19 @@
 
 
 def backward_kernel(
-    dims, me_ref, len_ref, bias_ref, qkv_ref, do_ref, dqkv_ref, dbias_ref,
+    dims, me_ref, len_ref, bias_ref, own_ref, other_ref, do_ref, down_ref, dother_ref, dbias_ref,
     pat, txt, dpat, dtxt, gpat, gtxt,
 ):
     rows, images, patch_dev, text_dev, slots = dims
-    seq_count = qkv_ref.shape[0]
+    seq_count = 2 * own_ref.shape[0]
     text_rows = seq_count * TEXT_PITCH
     for row in range(rows):
         unpack(
-            qkv_ref,
-            lambda place, row=row: qkv_ref.at[place ^ me_ref[0], row],
+            seq_count, Halves(me_ref[0], own_ref, other_ref, row),
             row, pat, txt, patch_dev, text_dev, slice(None),
         )
         unpack(
-            do_ref,
-            lambda place: do_ref.at[place],
+            seq_count, lambda place: do_ref.at[place],
             row, dpat, dtxt, patch_dev, text_dev,
             slice(row * HEAD_DIM, (row + 1) * HEAD_DIM),
         )
@@ -292,21 +316,24 @@
         gtxt[row] = gtxt[row] + dot_tn(pick[:pad_q], grads)
     for row in range(rows):
         for place in range(seq_count):
-            source = place ^ me_ref[0]
-            dqkv_ref[source, row, 0:patch_dev, :] = gpat[
-                row, place * patch_dev : (place + 1) * patch_dev, :
-            ]
+            odd, index = Halves(me_ref[0], own_ref, other_ref, row).at(place)
             low = place * TEXT_PITCH
-            dqkv_ref[source, row, patch_dev : patch_dev + text_dev, :] = gtxt[
-                row, low : low + text_dev, :
-            ].astype(BF16)
+            patches = gpat[row, place * patch_dev : (place + 1) * patch_dev, :]
+            text = gtxt[row, low : low + text_dev, :].astype(BF16)
+
+            def put(target):
+                target[index, row, 0:patch_dev, :] = patches
+                target[index, row, patch_dev : patch_dev + text_dev, :] = text
+
+            pl.when(odd == 0)(lambda: put(down_ref))
+            pl.when(odd == 1)(lambda: put(dother_ref))
 
 
 SMEM = pl.BlockSpec(memory_space=pltpu.SMEM)
 VMEM = pl.BlockSpec(memory_space=pltpu.VMEM)
 
 
-def call(kernel, out_shape, in_specs, scratch=(), flops=0, bytes_accessed=0):
+def call(kernel, out_shape, in_specs, scratch=(), flops=0, bytes_accessed=0, vmem=16):
     single = not isinstance(out_shape, (tuple, list))
     return pl.pallas_call(
         kernel,
@@ -317,7 +344,7 @@
         cost_estimate=pl.CostEstimate(
             flops=flops, bytes_accessed=bytes_accessed, transcendentals=0
         ),
-        compiler_params=pltpu.CompilerParams(vmem_limit_bytes=48 << 20),
+        compiler_params=pltpu.CompilerParams(vmem_limit_bytes=vmem << 20),
         interpret=INTERPRET,
     )
 
@@ -337,21 +364,30 @@
     cols = w_in.shape[1]
     images = text_lengths.shape[1]
     slots = text_dev * seq_count
+    core, near, team_bit = ("seq", 0), ("seq", 1), ("seq", 2)
     seq_high = [("seq", bit) for bit in range(seq_count.bit_length() - 2, 1, -1)]
-    near, core = ("seq", 1), ("seq", 0)
     dp_bits = [("dp", bit) for bit in range(dp_count.bit_length() - 1)]
     every = dp_bits + seq_high + [near, core]
     both = ("dp", "seq")
 
     bias_count = position_bias.shape[0]
-    extra = jnp.zeros((cols, 128), BF16)
-    extra = extra.at[:, 0].set(b_in).at[:, 1].set(gain_attn).at[:, 2].set(gain_ffn)
-    extra = extra.at[:bias_count, 3].set(position_bias)
-    pack = jnp.concatenate([w_in.T, extra], axis=1)
+    pack = jnp.concatenate(
+        [
+            w_in,
+            b_in[None],
+            gain_attn[None],
+            gain_ffn[None],
+            jnp.pad(position_bias, (0, cols - bias_count))[None],
+            jnp.zeros((124, cols), BF16),
+        ],
+        axis=0,
+    ).T
     wide = vit + 128
     half_in = wide // 256 * 128
-    in_low = gather(pack[:, :half_in], seq_high + dp_bits + [near, core], True)
-    in_high = gather(pack[:, half_in:], seq_high + [near] + dp_bits + [core], True)
+    in_low_stages = gather(pack[:, :half_in], seq_high + dp_bits + [near, core], True)
+    in_high_stages = gather(pack[:, half_in:], seq_high + [near] + dp_bits + [core], True)
+    in_low, in_high = in_low_stages[-1], in_high_stages[-1]
+    in_part = in_low_stages[len(seq_high) - 1]
 
     per_head = dev_count // HEADS
     twins = seq_count // HEADS
@@ -360,6 +396,7 @@
     place_in_head = dp_index * twins + twin
     row_count = rows // twins
     three = jnp.concatenate([w_query.T, w_key.T, w_value.T], axis=0)
+    three = after(three, in_part)
 
     def to_rank(which_head, place):
         return (place // twins) * seq_count + which_head * twins + place % twins
@@ -381,14 +418,16 @@
     ]
     w_head = jnp.stack(ordered, axis=1).reshape(3 * HEAD_DIM, d_model)
 
-    ff_order = seq_high + dp_bits
+    team = [team_bit, core]
+    ff_high = [step for step in seq_high if step != team_bit]
+    ff_order = ff_high + [near] + dp_bits
+    ff_other = ff_high + dp_bits + [near]
     units = w_gate.shape[1]
+    full_gate = gather(w_gate.T, ff_order, False, {0: in_low})[-1]
+    full_up = gather(w_up.T, ff_order, False, {0: in_low})[-1]
     down_out = jnp.transpose(w_down.reshape(dev_count, units, cols), (0, 2, 1))
-    down_in = lax.all_to_all(down_out, both, 0, 0, tiled=True).reshape(d_model, units)
-    full_gate = gather(w_gate.T, ff_order, False)
-    full_up = gather(w_up.T, ff_order, False)
-    full_down = gather(down_in.T, ff_order, False)
-    full_out = gather(w_out.T, seq_high + [near] + dp_bits + [core], True)
+    down_in = lax.all_to_all(after(down_out, in_low), both, 0, 0, tiled=True)
+    full_down = gather(down_in.reshape(d_model, units).T, ff_other, False)[-1]
 
     features = patch_features.reshape(rows * patch_dev, vit)
     ones = jnp.zeros((rows * patch_dev, 128), BF16).at[:, 0].set(1)
@@ -406,25 +445,38 @@
     ).reshape(mine, d_model)
     normed_one = rms_norm(resid, gain_one).astype(BF16)
     half = d_model // 2
-    order_low = seq_high + [near, core]
-    order_high = [near] + seq_high + [core]
-    all_low = gather(normed_one[:, :half], order_low, False)
-    all_high = gather(normed_one[:, half:], order_high, False)
+    order_low = seq_high + [near]
+    order_high = [near] + seq_high
+    low_stages = gather(normed_one[:, :half], order_low, False)
+    high_stages = gather(normed_one[:, half:], order_high, False)
+    chips = seq_count // 2
 
     def my_rows(array):
-        view = array.reshape(seq_count, rows, tok, array.shape[1])
+        if twins == 1:
+            return array
+        view = array.reshape(chips, rows, tok, array.shape[1])
         view = lax.dynamic_slice_in_dim(view, twin * row_count, row_count, 1)
-        return view.reshape(seq_count * row_count * tok, array.shape[1])
-
-    if twins > 1:
-        all_low, all_high = my_rows(all_low), my_rows(all_high)
-    qkv = (dot_nt(all_low, w_head[:, :half]) + dot_nt(all_high, w_head[:, half:])).astype(BF16)
-    qkv = qkv.reshape(seq_count, row_count, tok, 3 * HEAD_DIM)
+        return view.reshape(chips * row_count * tok, array.shape[1])
+
+    own_low, own_high = low_stages[-1], high_stages[-1]
+    normed_pairs = [
+        (my_rows(own_low), my_rows(own_high)),
+        (my_rows(swap(own_low, core)), my_rows(swap(own_high, core))),
+    ]
+    qkv = [
+        (dot_nt(low, w_head[:, :half]) + dot_nt(high, w_head[:, half:]))
+        .astype(BF16)
+        .reshape(chips, row_count, tok, 3 * HEAD_DIM)
+        for low, high in normed_pairs
+    ]
+    full_out = gather(
+        w_out.T, seq_high + [near] + dp_bits + [core], True, {0: low_stages[len(seq_high) - 1]}
+    )[-1]
     lengths = lax.dynamic_slice_in_dim(text_lengths, twin * row_count, row_count, 0)
     me = seq_index.reshape(1).astype(jnp.int32)
     dims = (row_count, images, patch_dev, text_dev, slots)
     bias = call(
-        bias_kernel, jax.ShapeDtypeStruct((SEG_Q, SEG_K), F32), [SMEM], (), 1 << 24, 1 << 20
+        bias_kernel, jax.ShapeDtypeStruct((SEG_Q, SEG_K), F32), [SMEM], (), 1 << 24, 1 << 20, 8
     )(my_table)
     text_rows = seq_count * TEXT_PITCH
     patches = seq_count * patch_dev
@@ -432,7 +484,7 @@
     mixed = call(
         lambda *refs: forward_kernel(dims, *refs),
         packed_shape,
-        [SMEM, SMEM, VMEM, VMEM],
+        [SMEM, SMEM, VMEM, VMEM, VMEM],
         (
             pltpu.VMEM((row_count, patches, 3 * HEAD_DIM), BF16),
             pltpu.VMEM((row_count, text_rows, 3 * HEAD_DIM), BF16),
@@ -441,56 +493,39 @@
         ),
         1 << 30,
         4 << 20,
-    )(me, lengths, bias, qkv)
+        20,
+    )(me, lengths, bias, *qkv)
     mixed = lax.all_to_all(mixed, "seq", 0, 0, tiled=True)
     mixed = mixed.reshape(HEADS, twins, tok, row_count, HEAD_DIM)
     attn_out = jnp.transpose(mixed, (1, 3, 2, 0, 4)).reshape(mine, d_model)
     resid_one = resid + dot_nt(attn_out, full_out)
     normed_two = rms_norm(resid_one, gain_two).astype(BF16)
-    team = [near, core]
     upstream = jnp.concatenate([d_patch, d_text], axis=1).reshape(mine, d_model)
-    team_up = gather(upstream, team, False)
-    team_normed = gather(normed_two, team, False)
+    team_up = gather(upstream, team, False, {0: own_low})[-1]
+    team_normed = gather(normed_two, team, False)[-1]
     gate_pre = dot_nt(team_normed, full_gate)
     up_pre = dot_nt(team_normed, full_up)
     hidden, gated_back = jax.vjp(gated_unit, gate_pre, up_pre)
     hidden = hidden.astype(BF16)
-    out_part = dot_nn(hidden, full_down)
-    result = resid_one + scatter_add(out_part, [core, near], team, False, (core,))
-    result = result.astype(BF16).reshape(rows, tok, d_model)
 
     d_hidden = dot_nt(team_up, full_down)
     d_gate, d_up = gated_back(d_hidden)
     d_gate, d_up = d_gate.astype(BF16), d_up.astype(BF16)
-    d_normed_two = scatter_add(
-        dot_nn(d_gate, full_gate) + dot_nn(d_up, full_up), [core, near], team, False, (core,)
-    )
-    back = ff_order[::-1]
-    grad_down = scatter_add(dot_tn(hidden, team_up), back, ff_order, False)
-    grad_gate = scatter_add(dot_tn(d_gate, team_normed), back, ff_order, False)
-    grad_up = scatter_add(dot_tn(d_up, team_normed), back, ff_order, False)
-    down_back = grad_down.T.reshape(dev_count, cols, units)
-    down_back = lax.all_to_all(down_back, both, 0, 0, tiled=True)
-    grad_down = jnp.transpose(down_back, (0, 2, 1)).reshape(dev_count * units, cols)
-
+    d_normed_part = dot_nn(d_gate, full_gate) + dot_nn(d_up, full_up)
+    d_normed_two = scatter_add(d_normed_part, [core, team_bit], team, False, (core,))[-1]
     _, norm_back_two = jax.vjp(rms_norm, resid_one, gain_two)
     d_resid_one, grad_gain_two = norm_back_two(d_normed_two)
     d_resid_one = d_resid_one + upstream.astype(F32)
     d_mix = d_resid_one.astype(BF16)
-    grad_out = scatter_add(
-        dot_tn(d_mix, attn_out), [core] + dp_bits[::-1] + [near] + seq_high[::-1], every, True
-    )
     d_attn = dot_nn(d_mix, full_out).astype(BF16)
     d_attn = d_attn.reshape(twins, row_count, tok, HEADS, HEAD_DIM)
     d_attn = jnp.transpose(d_attn, (3, 0, 2, 1, 4)).reshape(packed_shape.shape)
     d_attn = lax.all_to_all(d_attn, "seq", 0, 0, tiled=True)
-    d_qkv, d_bias = call(
+    half_shape = jax.ShapeDtypeStruct(qkv[0].shape, BF16)
+    d_own, d_other, d_bias = call(
         lambda *refs: backward_kernel(dims, *refs),
-        (
-            jax.ShapeDtypeStruct(qkv.shape, BF16),
-            jax.ShapeDtypeStruct((SEG_Q, SEG_K), F32),
-        ),
-        [SMEM, SMEM, VMEM, VMEM, VMEM],
+        (half_shape, half_shape, jax.ShapeDtypeStruct((SEG_Q, SEG_K), F32)),
+        [SMEM, SMEM, VMEM, VMEM, VMEM, VMEM],
         (
             pltpu.VMEM((row_count, patches, 3 * HEAD_DIM), BF16),
             pltpu.VMEM((row_count, text_rows, 3 * HEAD_DIM), BF16),
@@ -501,13 +536,72 @@
         ),
         3 << 30,
         8 << 20,
-    )(me, lengths, bias, qkv, d_attn)
+        28,
+    )(me, lengths, bias, *qkv, d_attn)
+    d_qkv = [
+        array.reshape(chips * row_count * tok, 3 * HEAD_DIM) for array in (d_own, d_other)
+    ]
+
+    ff_hold = {1: d_own}
+    grad_gate = scatter_add(
+        dot_tn(after(d_gate, d_normed_part), team_normed).astype(BF16),
+        ff_order[::-1], ff_order, False, (), ff_hold,
+    )[-1]
+    grad_up = scatter_add(
+        dot_tn(after(d_up, d_normed_part), team_normed).astype(BF16),
+        ff_order[::-1], ff_order, False, (), ff_hold,
+    )[-1]
+    grad_down = scatter_add(
+        dot_tn(after(hidden, d_normed_part), team_up).astype(BF16),
+        ff_other[::-1], ff_order, False, (), ff_hold,
+    )[-1]
+    down_back = grad_down.T.reshape(dev_count, cols, units)
+    down_back = lax.all_to_all(down_back, both, 0, 0, tiled=True)
+    grad_down = jnp.transpose(down_back, (0, 2, 1)).reshape(dev_count * units, cols)
+    out_part = dot_nn(after(hidden, d_normed_part), full_down)
+    result = scatter_add(
+        out_part, [core, team_bit], team, False, (core,), {0: d_normed_two, 1: d_own}
+    )[-1]
+    result = (resid_one + result).astype(BF16).reshape(rows, tok, d_model)
+
     d_table = call(
-        bucket_kernel, jax.ShapeDtypeStruct((BUCKETS, 128), F32), [VMEM], (), 1 << 25, 1 << 20
+        bucket_kernel, jax.ShapeDtypeStruct((BUCKETS, 128), F32), [VMEM], (), 1 << 25, 1 << 20, 8
     )(d_bias)[:, 0]
-    d_qkv = d_qkv.reshape(seq_count * row_count * tok, 3 * HEAD_DIM)
-    d_head = jnp.concatenate([dot_tn(d_qkv, all_low), dot_tn(d_qkv, all_high)], axis=1)
+
+    def all_rows(array):
+        if twins == 1:
+            return array
+        view = array.reshape(chips, row_count, tok, array.shape[1])
+        zero = jnp.zeros((chips, rows, tok, array.shape[1]), array.dtype)
+        view = lax.dynamic_update_slice_in_dim(zero, view, twin * row_count, 1)
+        return view.reshape(chips * mine, array.shape[1])
+
+    chip_bits = seq_high + [near]
+
+    def d_normed(weights, order):
+        other = all_rows(dot_nn(d_qkv[1], weights).astype(BF16))
+        own = all_rows(dot_nn(d_qkv[0], weights))
+        return scatter_add(
+            own + swap(other, core).astype(F32), order, chip_bits, False
+        )
+
+    low_sums = d_normed(w_head[:, :half], order_low[::-1])
+    high_sums = d_normed(w_head[:, half:], order_high[::-1])
+    d_normed_one = jnp.concatenate([low_sums[-1], high_sums[-1]], axis=1)
+    out_order = [core] + dp_bits[::-1] + [near] + seq_high[::-1]
+    grad_out = scatter_add(
+        dot_tn(after(d_mix, d_attn), attn_out).astype(BF16), out_order, every, True, (), {1: d_own}
+    )[-1]
+
+    d_head = jnp.concatenate(
+        [
+            sum(dot_tn(grads, pair[which]) for grads, pair in zip(d_qkv, normed_pairs))
+            for which in range(2)
+        ],
+        axis=1,
+    )
     d_head = d_head.reshape(3, per_head, cols, d_model).astype(BF16)
+    d_head = after(d_head, low_sums[-1])
     d_three = 0.0
     for turn in range(per_head):
         piece = lax.dynamic_index_in_dim(
@@ -516,26 +610,6 @@
         got = lax.ppermute(piece.reshape(3 * cols, d_model), both, rounds(turn, True))
         d_three = d_three + got.astype(F32)
 
-    def all_rows(array):
-        if twins == 1:
-            return array
-        view = array.reshape(seq_count, row_count, tok, array.shape[1])
-        zero = jnp.zeros((seq_count, rows, tok, array.shape[1]), array.dtype)
-        view = lax.dynamic_update_slice_in_dim(zero, view, twin * row_count, 1)
-        return view.reshape(seq_count * mine, array.shape[1])
-
-    seq_bits = seq_high + [near, core]
-    d_normed_one = jnp.concatenate(
-        [
-            scatter_add(
-                all_rows(dot_nn(d_qkv, w_head[:, :half])), order_low[::-1], seq_bits, False
-            ),
-            scatter_add(
-                all_rows(dot_nn(d_qkv, w_head[:, half:])), order_high[::-1], seq_bits, False
-            ),
-        ],
-        axis=1,
-    )
     _, norm_back_one = jax.vjp(rms_norm, resid, gain_one)
     d_resid, grad_gain_one = norm_back_one(d_normed_one)
     d_resid = (d_resid + d_resid_one).reshape(rows, tok, d_model)
@@ -570,17 +644,17 @@
     in_grads = jnp.concatenate(
         [
             scatter_add(
-                dot_tn(left, right[:, :half_in]),
+                dot_tn(left, right[:, :half_in]).astype(BF16),
                 [core, near] + dp_bits[::-1] + seq_high[::-1],
                 every,
                 True,
-            ),
+            )[-1],
             scatter_add(
-                dot_tn(left, right[:, half_in:]),
+                dot_tn(left, right[:, half_in:]).astype(BF16),
                 [core] + dp_bits[::-1] + [near] + seq_high[::-1],
                 every,
                 True,
-            ),
+            )[-1],
         ],
         axis=1,
     )

time: 550 us -> 548 us (level)
  waiting for transfers between devices: 212 us -> 178 us
  starting transfers between devices: 90.8 us -> 112 us
  other arithmetic: 79.1 us -> 64.2 us
  matrix products: 35.9 us -> 47 us
  local copies, waits for them, and re-layouts: 94.6 us -> 103 us
  between operations: 3.68 us -> 9.36 us
    ppermute x72, waiting for transfers between devices: 209 us -> 166 us  [swap(): return lax.ppermute(array, axis, [(i, i ^ 1 << bit) for i in range(count)])]
    unnamed x142 -> x311, local copies, waits for them, and re-layouts: 15 us -> 46.8 us
    another operation x23 -> x2, other arithmetic: 24.6 us -> 0.71 us  [the longest x14 18.6 us: gather(): mine, other = (block.reshape(shape), other.reshape(shape))]
    ppermute x72, starting transfers between devices: 63.7 us -> 83.1 us  [swap(): return lax.ppermute(array, axis, [(i, i ^ 1 << bit) for i in range(count)])]
    slice x20 -> x38, local copies, waits for them, and re-layouts: 6.36 us -> 20.6 us  [the longest x7 7.18 us: gather(): other[which * size:(which + 1) * size]]
    another operation x8 -> x0, local copies, waits for them, and re-layouts: 11.3 us -> none
    convert_element_type x26 -> x11, local copies, waits for them, and re-layouts: 7.87 us -> 0.35 us  [scatter_add(): got = swap(send.astype(kind), step)]
    reshape x5 -> x0, local copies, waits for them, and re-layouts: 6.6 us -> none  [the longest x3 4.27 us: gather(): mine, other = (block.reshape(shape), other.reshape(shape))]
  transfers between devices with their start and end apart: 80 -> 80, of which waited for: 41 -> 29; matrix products, arithmetic and copies ran while one was open for 32% -> 34% of each run, Pallas kernels for 5% -> 5%
where the time goes in v2:
time: 548 us; the launch traced here: 541 us
  waiting for transfers between devices  178 us (32%)
  starting transfers between devices  112 us (20%)
  local copies, waits for them, and re-layouts  103 us (19%)
  other arithmetic  64.2 us (12%)
  matrix products  47 us (9%)
  Pallas kernels  28.3 us (5%)
  between operations  9.36 us (2%)
    ppermute x72, waiting for transfers between devices, swap(): return lax.ppermute(array, axis, [(i, i ^ 1 << bit) for i in range(count)])  166 us
    ppermute x72, starting transfers between devices, swap(): return lax.ppermute(array, axis, [(i, i ^ 1 << bit) for i in range(count)])  83.1 us
    unnamed x311, local copies, waits for them, and re-layouts  46.8 us
    dot_general x11, matrix products, dot_nt(): lax.dot_general(left, right, (((1,), (1,)), ((), ())), preferred_element_...  19.3 us
    concatenate x21, other arithmetic, gather(): block = jnp.concatenate(parts, axis=0)  19.1 us
    add x28, other arithmetic, scatter_add(): grads = keep.astype(F32) + got.astype(F32)  16.7 us
    dot_general x10, matrix products, dot_tn(): lax.dot_general(left, right, (((0,), (0,)), ((), ())), preferred_element_...  14.8 us
    pallas_call x1, Pallas kernels, local(): call(lambda *refs: backward_kernel(dims, *refs), (half_shape, half_shape,...  14.4 us
  transfers between devices with their start and end apart: 80, of which 29 were waited for; matrix products, arithmetic and copies ran while one was open for 34% of the time, Pallas kernels for 5%

profile of v2, /device:TPU:0, one launch (start us, length us, event | category | flops | bytes accessed | tf_op | source)
XLA Modules:
  0.0 541.5 jit_solution(3086914200687303880)
XLA Ops:
  4.7 4.1 collective-permute-start
  14.1 2.1 collective-permute-start.1
  16.3 2.8 collective-permute-done.5
  23.1 4.9 collective-permute-start.14
  30.4 7.3 %collective-permute-done.2 = bf16[128,896]{1,0:T(8,128)(2,1)S(1)} collective-permute-done((bf16[128,896]{1,0:T(8,128)(2,1)S(1)}, bf16[128,896]{1,0:T(8,128)(2,1)S(1)}, u32[]{:S(2)}, u32[]{:S(2)}) %collective-permute-start.2) | collective-permute-done | bytes 229408 | tf_op jit(solution)/shard_map/ppermute | solution.py:58
  37.8 3.4 collective-permute-start.3
  41.5 10.0 %collective-permute-done.3 = bf16[256,896]{1,0:T(8,128)(2,1)S(1)} collective-permute-done((bf16[256,896]{1,0:T(8,128)(2,1)S(1)}, bf16[256,896]{1,0:T(8,128)(2,1)S(1)}, u32[]{:S(2)}, u32[]{:S(2)}) %collective-permute-start.3) | collective-permute-done | bytes 458784 | tf_op jit(solution)/shard_map/ppermute | solution.py:58
  52.0 2.5 collective-permute-start.8
  55.6 10.1 %collective-permute-done.8 = bf16[256,896]{1,0:T(8,128)(2,1)S(1)} collective-permute-done((bf16[256,896]{1,0:T(8,128)(2,1)S(1)}, bf16[256,896]{1,0:T(8,128)(2,1)S(1)}, u32[]{:S(2)}, u32[]{:S(2)}) %collective-permute-start.8) | collective-permute-done | bytes 458784 | tf_op jit(solution)/shard_map/ppermute | solution.py:58
  71.8 7.3 %all-to-all-start.1 = ((bf16[32,32,88]{2,1,0:T(8,128)(2,1)}), bf16[32,32,88]{2,1,0:T(8,128)(2,1)S(1)}, u32[]{:S(2)}, u32[]{:S(2)}) async-start(bf16[32,32,88]{2,1,0:T(8,128)(2,1)} %bitcast.346), calls=%async_computation.1 | async-start | bytes 524288 | tf_op jit(solution)/shard_map/all_to_all | solution.py:429
  80.8 2.8 collective-permute-start.27
  88.8 2.3 broadcast_select_fusion.2
  99.9 2.5 collective-permute-start.20
  105.1 2.4 collective-permute-done.20
  107.5 3.4 collective-permute-start.10
  118.0 2.9 collective-permute-start.16
  125.9 8.2 %collective-permute-done.11 = bf16[288,512]{1,0:T(8,128)(2,1)S(1)} collective-permute-done((bf16[288,512]{1,0:T(8,128)(2,1)}, bf16[288,512]{1,0:T(8,128)(2,1)S(1)}, u32[]{:S(2)}, u32[]{:S(2)}) %collective-permute-start.11) | collective-permute-done | bytes 294944 | tf_op jit(solution)/shard_map/ppermute | solution.py:58
  138.1 6.1 %collective-permute-done.35 = bf16[88,1024]{0,1:T(8,128)(2,1)S(1)} collective-permute-done((bf16[88,1024]{0,1:T(8,128)(2,1)S(1)}, bf16[88,1024]{0,1:T(8,128)(2,1)S(1)}, u32[]{:S(2)}, u32[]{:S(2)}) %collective-permute-start.35) | collective-permute-done | bytes 180256 | tf_op jit(solution)/shard_map/ppermute | solution.py:58
  168.9 2.2 fusion.60
  200.1 11.4 %shard_map.289 = bf16[16,72,128]{2,1,0:T(8,128)(2,1)} custom-call(s32[1]{0:T(128)} %bitcast.10.refs_0_, s32[2,3]{1,0:T(2,128)S(1)} %copy-done.4, f32[448,512]{1,0:T(8,128)S(1)} %shard_map.288.refs_2_, bf16[8,2,72,192]{3,2,1,0:T(8,128)(2,1)S(1)} %bitcast.276, bf16[8,2,72,192]{3,2,1,0:T(8,128)(2,1)S(1)} %bitcast.278), custom_call_target="tpu_custom_call" | custom-call | flops 1073741824 | bytes 4194304 | tf_op jit(solution)/shard_map/pallas_call | solution.py:484
  211.6 3.9 all-to-all-start
  219.9 6.1 %all-to-all-done = bf16[16,72,128]{2,1,0:T(8,128)(2,1)S(1)} async-done(((bf16[16,72,128]{2,1,0:T(8,128)(2,1)}), bf16[16,72,128]{2,1,0:T(8,128)(2,1)S(1)}, u32[]{:S(2)}, u32[]{:S(2)}) %all-to-all-start) | async-done | bytes 294944 | tf_op jit(solution)/shard_map/all_to_all | solution.py:498
  226.9 2.7 multiply_reduce_fusion.4
  235.8 2.9 collective-permute-done.25
  245.3 6.0 %collective-permute-done.37 = bf16[352,1024]{1,0:T(8,128)(2,1)S(1)} collective-permute-done((bf16[352,1024]{1,0:T(8,128)(2,1)}, bf16[352,1024]{1,0:T(8,128)(2,1)S(1)}, u32[]{:S(2)}, u32[]{:S(2)}) %collective-permute-start.37) | collective-permute-done | bytes 720928 | tf_op jit(solution)/shard_map/ppermute | solution.py:58
  254.3 3.8 concatenate.193
  259.3 2.7 fusion.82
  262.0 2.2 fusion.81
  264.3 3.5 fusion.5
  273.1 2.3 convolution_convert_fusion.6
  277.0 2.3 convolution_convert_fusion.7
  279.9 2.4 convolution_convert_fusion.5
  286.7 7.8 %collective-permute-done.70 = bf16[352,1024]{1,0:T(8,128)(2,1)S(1)} collective-permute-done((bf16[352,1024]{1,0:T(8,128)(2,1)S(1)}, bf16[352,1024]{1,0:T(8,128)(2,1)S(1)}, u32[]{:S(2)}, u32[]{:S(2)}) %collective-permute-start.70) | collective-permute-done | bytes 720928 | tf_op jit(solution)/shard_map/ppermute | solution.py:58
  297.3 11.5 %collective-permute-done.67 = bf16[352,1024]{1,0:T(8,128)(2,1)S(1)} collective-permute-done((bf16[352,1024]{1,0:T(8,128)(2,1)S(1)}, bf16[352,1024]{1,0:T(8,128)(2,1)S(1)}, u32[]{:S(2)}, u32[]{:S(2)}) %collective-permute-start.67) | collective-permute-done | bytes 720928 | tf_op jit(solution)/shard_map/ppermute | solution.py:58
  311.4 2.3 convolution_convert_fusion.8
  315.7 3.5 all-to-all-start.2
  319.2 2.6 convert_add_fusion.5
  325.1 4.6 all-to-all-done.2.refs_5_
  331.9 14.4 %shard_map.290 = (bf16[8,2,72,192]{3,2,1,0:T(8,128)(2,1)S(1)}, bf16[8,2,72,192]{3,2,1,0:T(8,128)(2,1)S(1)}, f32[448,512]{1,0:T(8,128)S(1)}) custom-call(s32[1]{0:T(128)} %bitcast.10.refs_0_, s32[2,3]{1,0:T(2,128)S(1)} %copy-done.4, f32[448,512]{1,0:T(8,128)S(1)} %shard_map.288.refs_2_, bf16[8,2,72,192]{3,2,1,0:T(8,128)(2,1)S(1)} %bitcast.277, ...), custom_call_target="tpu_custom_call" | custom-call | flops 3221225472 | bytes 8388608 | tf_op jit(solution)/shard_map/pallas_call | solution.py:525
  353.9 2.4 fusion.20
  364.2 2.4 fusion.13
  372.6 5.5 %collective-permute-done.71 = bf16[176,1024]{1,0:T(8,128)(2,1)} collective-permute-done((bf16[176,1024]{1,0:T(8,128)(2,1)}, bf16[176,1024]{1,0:T(8,128)(2,1)}, u32[]{:S(2)}, u32[]{:S(2)}) %collective-permute-start.71) | collective-permute-done | bytes 360480 | tf_op jit(solution)/shard_map/ppermute | solution.py:58
  382.9 8.8 %collective-permute-done.75 = bf16[88,1024]{1,0:T(8,128)(2,1)S(1)} collective-permute-done((bf16[88,1024]{1,0:T(8,128)(2,1)S(1)}, bf16[88,1024]{1,0:T(8,128)(2,1)S(1)}, u32[]{:S(2)}, u32[]{:S(2)}) %collective-permute-start.75) | collective-permute-done | bytes 180256 | tf_op jit(solution)/shard_map/ppermute | solution.py:58
  392.8 4.7 all-to-all-start.3
  397.5 2.9 collective-permute-start.69
  402.6 2.1 collective-permute-start.41
  406.4 14.9 %collective-permute-done.69 = bf16[88,1024]{1,0:T(8,128)(2,1)S(1)} collective-permute-done((bf16[88,1024]{1,0:T(8,128)(2,1)}, bf16[88,1024]{1,0:T(8,128)(2,1)S(1)}, u32[]{:S(2)}, u32[]{:S(2)}) %collective-permute-start.69) | collective-permute-done | bytes 180256 | tf_op jit(solution)/shard_map/ppermute | solution.py:58
  430.8 8.5 %collective-permute-done.63 = bf16[256,1024]{1,0:T(8,128)(2,1)S(1)} collective-permute-done((bf16[256,1024]{1,0:T(8,128)(2,1)S(1)}, bf16[256,1024]{1,0:T(8,128)(2,1)S(1)}, u32[]{:S(2)}, u32[]{:S(2)}) %collective-permute-start.63) | collective-permute-done | bytes 524320 | tf_op jit(solution)/shard_map/ppermute | solution.py:58
  445.8 2.4 collective-permute-done.64
  449.8 2.1 collective-permute-start.44
  451.9 10.4 %collective-permute-done.65 = bf16[64,1024]{1,0:T(8,128)(2,1)S(1)} collective-permute-done((bf16[64,1024]{1,0:T(8,128)(2,1)S(1)}, bf16[64,1024]{1,0:T(8,128)(2,1)S(1)}, u32[]{:S(2)}, u32[]{:S(2)}) %collective-permute-start.65) | collective-permute-done | bytes 131104 | tf_op jit(solution)/shard_map/ppermute | solution.py:58
  464.3 2.5 collective-permute-start.48
  466.8 9.4 %collective-permute-done.66 = bf16[32,1024]{1,0:T(8,128)(2,1)S(1)} collective-permute-done((bf16[32,1024]{1,0:T(8,128)(2,1)S(1)}, bf16[32,1024]{1,0:T(8,128)(2,1)S(1)}, u32[]{:S(2)}, u32[]{:S(2)}) %collective-permute-start.66) | collective-permute-done | bytes 65568 | tf_op jit(solution)/shard_map/ppermute | solution.py:58
  477.1 5.6 %collective-permute-done.48 = bf16[288,512]{1,0:T(8,128)(2,1)S(1)} collective-permute-done((bf16[288,512]{1,0:T(8,128)(2,1)S(1)}, bf16[288,512]{1,0:T(8,128)(2,1)S(1)}, u32[]{:S(2)}, u32[]{:S(2)}) %collective-permute-start.48) | collective-permute-done | bytes 294944 | tf_op jit(solution)/shard_map/ppermute | solution.py:58
  485.0 3.0 collective-permute-done.49
  493.5 3.0 collective-permute-start.61
  502.2 3.7 collective-permute-start.51
  506.3 2.0 collective-permute-start.56
  508.4 8.5 %collective-permute-done.51 = bf16[256,896]{1,0:T(8,128)(2,1)S(1)} collective-permute-done((bf16[256,896]{1,0:T(8,128)(2,1)S(1)}, bf16[256,896]{1,0:T(8,128)(2,1)S(1)}, u32[]{:S(2)}, u32[]{:S(2)}) %collective-permute-start.51) | collective-permute-done | bytes 458784 | tf_op jit(solution)/shard_map/ppermute | solution.py:58
  517.2 2.3 collective-permute-start.57
  519.6 5.8 %collective-permute-done.52 = bf16[128,896]{1,0:T(8,128)(2,1)S(1)} collective-permute-done((bf16[128,896]{1,0:T(8,128)(2,1)S(1)}, bf16[128,896]{1,0:T(8,128)(2,1)S(1)}, u32[]{:S(2)}, u32[]{:S(2)}) %collective-permute-start.52) | collective-permute-done | bytes 229408 | tf_op jit(solution)/shard_map/ppermute | solution.py:58
  528.8 4.1 collective-permute-done.58
  532.9 2.4 collective-permute-start.59
  536.0 3.0 collective-permute-done.59
  (664 shorter events, 223.2 us)
Async XLA Ops:
  19.1 9.9 %collective-permute-start.6 = (bf16[64,896]{1,0:T(8,128)(2,1)S(1)}, bf16[64,896]{1,0:T(8,128)(2,1)S(1)}, u32[]{:S(2)}, u32[]{:S(2)}) collective-permute-start(bf16[64,896]{1,0:T(8,128)(2,1)S(1)} %pad_maximum_fusion.31), channel_id=1, source_target_pairs={{0,4},{1,5},{2,6},{3,7},{4,0},{5,1},{6,2},{7,3},{8,12},{9,13},{10,... | collective-permute-start | bytes 344072 | tf_op jit(solution)/shard_map/ppermute | solution.py:58
  22.4 32.9 %collective-permute-start.13 = (bf16[96,1024]{1,0:T(8,128)(2,1)S(1)}, bf16[96,1024]{1,0:T(8,128)(2,1)S(1)}, u32[]{:S(2)}, u32[]{:S(2)}) collective-permute-start(bf16[96,1024]{1,0:T(8,128)(2,1)S(1)} %maximum_add_fusion.1), channel_id=1, source_target_pairs={{0,0},{1,16},{2,1},{3,17},{4,2},{5,18},{6,3},{7,19},{8,4},{9,20},{... | collective-permute-start | bytes 589832 | tf_op jit(solution)/shard_map/ppermute | solution.py:413
  23.1 32.2 %collective-permute-start.14 = (bf16[96,1024]{1,0:T(8,128)(2,1)S(1)}, bf16[96,1024]{1,0:T(8,128)(2,1)S(1)}, u32[]{:S(2)}, u32[]{:S(2)}) collective-permute-start(bf16[96,1024]{1,0:T(8,128)(2,1)S(1)} %maximum_add_fusion.1), channel_id=1, source_target_pairs={{0,16},{1,0},{2,17},{3,1},{4,18},{5,2},{6,19},{7,3},{8,20},{9,4},{... | collective-permute-start | bytes 589832 | tf_op jit(solution)/shard_map/ppermute | solution.py:413
  28.0 9.6 %collective-permute-start.2 = (bf16[128,896]{1,0:T(8,128)(2,1)S(1)}, bf16[128,896]{1,0:T(8,128)(2,1)S(1)}, u32[]{:S(2)}, u32[]{:S(2)}) collective-permute-start(bf16[128,896]{1,0:T(8,128)(2,1)S(1)} %pad_maximum_fusion.22), channel_id=1, source_target_pairs={{0,16},{16,0},{1,17},{17,1},{2,18},{18,2},{3,19},{19,3},{4,20},{20... | collective-permute-start | bytes 688136 | tf_op jit(solution)/shard_map/ppermute | solution.py:58
  29.1 12.1 %collective-permute-start.7 = (bf16[128,896]{1,0:T(8,128)(2,1)S(1)}, bf16[128,896]{1,0:T(8,128)(2,1)S(1)}, u32[]{:S(2)}, u32[]{:S(2)}) collective-permute-start(bf16[128,896]{1,0:T(8,128)(2,1)S(1)} %pad_maximum_fusion.23), channel_id=1, source_target_pairs={{0,2},{1,3},{2,0},{3,1},{4,6},{5,7},{6,4},{7,5},{8,10},{9,11},{10,... | collective-permute-start | bytes 688136 | tf_op jit(solution)/shard_map/ppermute | solution.py:58
  37.8 13.7 %collective-permute-start.3 = (bf16[256,896]{1,0:T(8,128)(2,1)S(1)}, bf16[256,896]{1,0:T(8,128)(2,1)S(1)}, u32[]{:S(2)}, u32[]{:S(2)}) collective-permute-start(bf16[256,896]{1,0:T(8,128)(2,1)S(1)} %pad_maximum_fusion.15), channel_id=1, source_target_pairs={{0,2},{1,3},{2,0},{3,1},{4,6},{5,7},{6,4},{7,5},{8,10},{9,11},{10,... | collective-permute-start | bytes 1376264 | tf_op jit(solution)/shard_map/ppermute | solution.py:58
  51.9 15.0 %collective-permute-start.4 = (bf16[512,896]{1,0:T(8,128)(2,1)S(1)}, bf16[512,896]{1,0:T(8,128)(2,1)S(1)}, u32[]{:S(2)}, u32[]{:S(2)}) collective-permute-start(bf16[512,896]{1,0:T(8,128)(2,1)S(1)} %constant_dynamic-update-slice_fusion), channel_id=1, source_target_pairs={{0,1},{1,0},{2,3},{3,2},{4,5},{5,4},{6,7},{7,6},{8,9},{9,8},{10,11... | collective-permute-start | bytes 2752520 | tf_op jit(solution)/shard_map/ppermute | solution.py:58
  52.0 13.7 %collective-permute-start.8 = (bf16[256,896]{1,0:T(8,128)(2,1)S(1)}, bf16[256,896]{1,0:T(8,128)(2,1)S(1)}, u32[]{:S(2)}, u32[]{:S(2)}) collective-permute-start(bf16[256,896]{1,0:T(8,128)(2,1)S(1)} %constant_dynamic-update-slice_fusion.48), channel_id=1, source_target_pairs={{0,16},{16,0},{1,17},{17,1},{2,18},{18,2},{3,19},{19,3},{4,20},{20... | collective-permute-start | bytes 1376264 | tf_op jit(solution)/shard_map/ppermute | solution.py:58
  66.9 21.9 %collective-permute-start.9 = (bf16[512,896]{1,0:T(8,128)(2,1)}, bf16[512,896]{1,0:T(8,128)(2,1)}, u32[]{:S(2)}, u32[]{:S(2)}) collective-permute-start(bf16[512,896]{1,0:T(8,128)(2,1)} %pad_maximum_fusion.3), channel_id=1, source_target_pairs={{0,1},{1,0},{2,3},{3,2},{4,5},{5,4},{6,7},{7,6},{8,9},{9,8},{10,11... | collective-permute-start | bytes 2752520 | tf_op jit(solution)/shard_map/ppermute | solution.py:58
  71.8 54.1 %all-to-all-start.1 = ((bf16[32,32,88]{2,1,0:T(8,128)(2,1)}), bf16[32,32,88]{2,1,0:T(8,128)(2,1)S(1)}, u32[]{:S(2)}, u32[]{:S(2)}) async-start(bf16[32,32,88]{2,1,0:T(8,128)(2,1)} %bitcast.346), calls=%async_computation.1 | async-start | bytes 524288 | tf_op jit(solution)/shard_map/all_to_all | solution.py:429
  80.8 30.1 %collective-permute-start.27 = (bf16[88,1024]{1,0:T(8,128)(2,1)}, bf16[88,1024]{1,0:T(8,128)(2,1)}, u32[]{:S(2)}, u32[]{:S(2)}) collective-permute-start(bf16[88,1024]{1,0:T(8,128)(2,1)} %get-tuple-element.43), channel_id=1, source_target_pairs={{0,8},{1,9},{2,10},{3,11},{4,12},{5,13},{6,14},{7,15},{8,0},{9,1},... | collective-permute-start | bytes 540680 | tf_op jit(solution)/shard_map/ppermute | solution.py:58
  85.3 27.5 %collective-permute-start.30 = (bf16[88,1024]{1,0:T(8,128)(2,1)}, bf16[88,1024]{1,0:T(8,128)(2,1)}, u32[]{:S(2)}, u32[]{:S(2)}) collective-permute-start(bf16[88,1024]{1,0:T(8,128)(2,1)} %get-tuple-element.45), channel_id=1, source_target_pairs={{0,8},{1,9},{2,10},{3,11},{4,12},{5,13},{6,14},{7,15},{8,0},{9,1},... | collective-permute-start | bytes 540680 | tf_op jit(solution)/shard_map/ppermute | solution.py:58
  98.0 24.5 %collective-permute-start.33 = (bf16[144,1024]{1,0:T(8,128)(2,1)}, bf16[144,1024]{1,0:T(8,128)(2,1)}, u32[]{:S(2)}, u32[]{:S(2)}) collective-permute-start(bf16[144,1024]{1,0:T(8,128)(2,1)} %bitcast.31), channel_id=1, source_target_pairs={{0,4},{1,5},{2,6},{3,7},{4,0},{5,1},{6,2},{7,3},{8,12},{9,13},{10,... | collective-permute-start | bytes 884744 | tf_op jit(solution)/shard_map/ppermute | solution.py:58
  102.4 13.7 %collective-permute-start.15 = (bf16[144,512]{1,0:T(8,128)(2,1)S(1)}, bf16[144,512]{1,0:T(8,128)(2,1)S(1)}, u32[]{:S(2)}, u32[]{:S(2)}) collective-permute-start(bf16[144,512]{1,0:T(8,128)(2,1)S(1)} %get-tuple-element.110), channel_id=1, source_target_pairs={{0,2},{1,3},{2,0},{3,1},{4,6},{5,7},{6,4},{7,5},{8,10},{9,11},{10,... | collective-permute-start | bytes 442376 | tf_op jit(solution)/shard_map/ppermute | solution.py:58
  107.5 10.5 %collective-permute-start.10 = (bf16[144,512]{1,0:T(8,128)(2,1)S(1)}, bf16[144,512]{1,0:T(8,128)(2,1)S(1)}, u32[]{:S(2)}, u32[]{:S(2)}) collective-permute-start(bf16[144,512]{1,0:T(8,128)(2,1)S(1)} %get-tuple-element.107), channel_id=1, source_target_pairs={{0,8},{1,9},{2,10},{3,11},{4,12},{5,13},{6,14},{7,15},{8,0},{9,1},... | collective-permute-start | bytes 442376 | tf_op jit(solution)/shard_map/ppermute | solution.py:58
  110.9 10.7 %collective-permute-start.21 = (bf16[64,1024]{1,0:T(8,128)(2,1)S(1)}, bf16[64,1024]{1,0:T(8,128)(2,1)S(1)}, u32[]{:S(2)}, u32[]{:S(2)}) collective-permute-start(bf16[64,1024]{1,0:T(8,128)(2,1)S(1)} %pad_maximum_fusion.29), channel_id=1, source_target_pairs={{0,4},{1,5},{2,6},{3,7},{4,0},{5,1},{6,2},{7,3},{8,12},{9,13},{10,... | collective-permute-start | bytes 393224 | tf_op jit(solution)/shard_map/ppermute | solution.py:58
  112.8 33.8 %collective-permute-start.28 = (bf16[176,1024]{1,0:T(8,128)(2,1)}, bf16[176,1024]{1,0:T(8,128)(2,1)}, u32[]{:S(2)}, u32[]{:S(2)}) collective-permute-start(bf16[176,1024]{1,0:T(8,128)(2,1)} %pad_maximum_fusion.17), channel_id=1, source_target_pairs={{0,2},{1,3},{2,0},{3,1},{4,6},{5,7},{6,4},{7,5},{8,10},{9,11},{10,... | collective-permute-start | bytes 1081352 | tf_op jit(solution)/shard_map/ppermute | solution.py:58
  116.0 37.0 %collective-permute-start.31 = (bf16[176,1024]{1,0:T(8,128)(2,1)}, bf16[176,1024]{1,0:T(8,128)(2,1)}, u32[]{:S(2)}, u32[]{:S(2)}) collective-permute-start(bf16[176,1024]{1,0:T(8,128)(2,1)} %pad_maximum_fusion.18), channel_id=1, source_target_pairs={{0,2},{1,3},{2,0},{3,1},{4,6},{5,7},{6,4},{7,5},{8,10},{9,11},{10,... | collective-permute-start | bytes 1081352 | tf_op jit(solution)/shard_map/ppermute | solution.py:58
  118.0 16.3 %collective-permute-start.16 = (bf16[288,512]{1,0:T(8,128)(2,1)}, bf16[288,512]{1,0:T(8,128)(2,1)}, u32[]{:S(2)}, u32[]{:S(2)}) collective-permute-start(bf16[288,512]{1,0:T(8,128)(2,1)} %pad_maximum_fusion.20), channel_id=1, source_target_pairs={{0,8},{1,9},{2,10},{3,11},{4,12},{5,13},{6,14},{7,15},{8,0},{9,1},... | collective-permute-start | bytes 884744 | tf_op jit(solution)/shard_map/ppermute | solution.py:58
  121.6 12.5 %collective-permute-start.11 = (bf16[288,512]{1,0:T(8,128)(2,1)}, bf16[288,512]{1,0:T(8,128)(2,1)S(1)}, u32[]{:S(2)}, u32[]{:S(2)}) collective-permute-start(bf16[288,512]{1,0:T(8,128)(2,1)} %pad_maximum_fusion.19), channel_id=1, source_target_pairs={{0,4},{1,5},{2,6},{3,7},{4,0},{5,1},{6,2},{7,3},{8,12},{9,13},{10,... | collective-permute-start | bytes 884744 | tf_op jit(solution)/shard_map/ppermute | solution.py:58
  122.5 13.0 %collective-permute-start.22 = (bf16[128,1024]{1,0:T(8,128)(2,1)}, bf16[128,1024]{1,0:T(8,128)(2,1)}, u32[]{:S(2)}, u32[]{:S(2)}) collective-permute-start(bf16[128,1024]{1,0:T(8,128)(2,1)} %pad_maximum_fusion.21), channel_id=1, source_target_pairs={{0,2},{1,3},{2,0},{3,1},{4,6},{5,7},{6,4},{7,5},{8,10},{9,11},{10,... | collective-permute-start | bytes 786440 | tf_op jit(solution)/shard_map/ppermute | solution.py:58
  134.2 9.9 %collective-permute-start.35 = (bf16[88,1024]{0,1:T(8,128)(2,1)S(1)}, bf16[88,1024]{0,1:T(8,128)(2,1)S(1)}, u32[]{:S(2)}, u32[]{:S(2)}) collective-permute-start(bf16[88,1024]{0,1:T(8,128)(2,1)S(1)} %bitcast.305), channel_id=1, source_target_pairs={{0,8},{1,9},{2,10},{3,11},{4,12},{5,13},{6,14},{7,15},{8,0},{9,1},... | collective-permute-start | bytes 540680 | tf_op jit(solution)/shard_map/ppermute | solution.py:58
  134.3 106.2 %collective-permute-start.34 = (bf16[288,1024]{1,0:T(8,128)(2,1)}, bf16[288,1024]{1,0:T(8,128)(2,1)}, u32[]{:S(2)}, u32[]{:S(2)}) collective-permute-start(bf16[288,1024]{1,0:T(8,128)(2,1)} %pad_maximum_fusion.12), channel_id=1, source_target_pairs={{0,1},{1,0},{2,3},{3,2},{4,5},{5,4},{6,7},{7,6},{8,9},{9,8},{10,11... | collective-permute-start | bytes 1769480 | tf_op jit(solution)/shard_map/ppermute | solution.py:58
  135.5 29.5 %collective-permute-start.17 = (bf16[576,512]{1,0:T(8,128)(2,1)S(1)}, bf16[576,512]{1,0:T(8,128)(2,1)S(1)}, u32[]{:S(2)}, u32[]{:S(2)}) collective-permute-start(bf16[576,512]{1,0:T(8,128)(2,1)S(1)} %pad_maximum_fusion.10), channel_id=1, source_target_pairs={{0,4},{1,5},{2,6},{3,7},{4,0},{5,1},{6,2},{7,3},{8,12},{9,13},{10,... | collective-permute-start | bytes 1769480 | tf_op jit(solution)/shard_map/ppermute | solution.py:58
  144.1 24.1 %collective-permute-start.12 = (bf16[576,512]{1,0:T(8,128)(2,1)S(1)}, bf16[576,512]{1,0:T(8,128)(2,1)S(1)}, u32[]{:S(2)}, u32[]{:S(2)}) collective-permute-start(bf16[576,512]{1,0:T(8,128)(2,1)S(1)} %pad_maximum_fusion.9), channel_id=1, source_target_pairs={{0,2},{1,3},{2,0},{3,1},{4,6},{5,7},{6,4},{7,5},{8,10},{9,11},{10,... | collective-permute-start | bytes 1769480 | tf_op jit(solution)/shard_map/ppermute | solution.py:58
  146.6 15.7 %collective-permute-start.23 = (bf16[256,1024]{1,0:T(8,128)(2,1)S(1)}, bf16[256,1024]{1,0:T(8,128)(2,1)S(1)}, u32[]{:S(2)}, u32[]{:S(2)}) collective-permute-start(bf16[256,1024]{1,0:T(8,128)(2,1)S(1)} %constant_dynamic-update-slice_fusion.101), channel_id=1, source_target_pairs={{0,16},{16,0},{1,17},{17,1},{2,18},{18,2},{3,19},{19,3},{4,20},{20... | collective-permute-start | bytes 1572872 | tf_op jit(solution)/shard_map/ppermute | solution.py:58
  153.1 76.9 %collective-permute-start.36 = (bf16[176,1024]{0,1:T(8,128)(2,1)}, bf16[176,1024]{0,1:T(8,128)(2,1)}, u32[]{:S(2)}, u32[]{:S(2)}) collective-permute-start(bf16[176,1024]{0,1:T(8,128)(2,1)} %pad_maximum_fusion.14), channel_id=1, source_target_pairs={{0,16},{16,0},{1,17},{17,1},{2,18},{18,2},{3,19},{19,3},{4,20},{20... | collective-permute-start | bytes 1081352 | tf_op jit(solution)/shard_map/ppermute | solution.py:58
  162.3 80.1 %collective-permute-start.29 = (bf16[352,1024]{1,0:T(8,128)(2,1)}, bf16[352,1024]{1,0:T(8,128)(2,1)}, u32[]{:S(2)}, u32[]{:S(2)}) collective-permute-start(bf16[352,1024]{1,0:T(8,128)(2,1)} %pad_maximum_fusion.5), channel_id=1, source_target_pairs={{0,16},{16,0},{1,17},{17,1},{2,18},{18,2},{3,19},{19,3},{4,20},{20... | collective-permute-start | bytes 2162696 | tf_op jit(solution)/shard_map/ppermute | solution.py:58
  168.2 25.9 %collective-permute-start.19 = (bf16[1152,512]{1,0:T(8,128)(2,1)}, bf16[1152,512]{1,0:T(8,128)(2,1)}, u32[]{:S(2)}, u32[]{:S(2)}) collective-permute-start(bf16[1152,512]{1,0:T(8,128)(2,1)} %constant_dynamic-update-slice_fusion.96), channel_id=1, source_target_pairs={{0,1},{1,0},{2,3},{3,2},{4,5},{5,4},{6,7},{7,6},{8,9},{9,8},{10,11... | collective-permute-start | bytes 3538952 | tf_op jit(solution)/shard_map/ppermute | solution.py:58
  173.8 22.7 %collective-permute-start.18 = (bf16[1152,512]{1,0:T(8,128)(2,1)}, bf16[1152,512]{1,0:T(8,128)(2,1)S(1)}, u32[]{:S(2)}, u32[]{:S(2)}) collective-permute-start(bf16[1152,512]{1,0:T(8,128)(2,1)} %copy-done.18), channel_id=1, source_target_pairs={{0,1},{1,0},{2,3},{3,2},{4,5},{5,4},{6,7},{7,6},{8,9},{9,8},{10,11... | collective-permute-start | bytes 3538952 | tf_op jit(solution)/shard_map/ppermute | solution.py:58
  194.1 49.5 %collective-permute-start.32 = (bf16[352,1024]{1,0:T(8,128)(2,1)}, bf16[352,1024]{1,0:T(8,128)(2,1)}, u32[]{:S(2)}, u32[]{:S(2)}) collective-permute-start(bf16[352,1024]{1,0:T(8,128)(2,1)} %pad_maximum_fusion.6), channel_id=1, source_target_pairs={{0,16},{16,0},{1,17},{17,1},{2,18},{18,2},{3,19},{19,3},{4,20},{20... | collective-permute-start | bytes 2162696 | tf_op jit(solution)/shard_map/ppermute | solution.py:58
  211.6 14.5 %all-to-all-start = ((bf16[16,72,128]{2,1,0:T(8,128)(2,1)}), bf16[16,72,128]{2,1,0:T(8,128)(2,1)S(1)}, u32[]{:S(2)}, u32[]{:S(2)}) async-start(bf16[16,72,128]{2,1,0:T(8,128)(2,1)} %shard_map.289), calls=%async_computation | async-start | bytes 589824 | tf_op jit(solution)/shard_map/all_to_all | solution.py:498
  232.6 18.7 %collective-permute-start.37 = (bf16[352,1024]{1,0:T(8,128)(2,1)}, bf16[352,1024]{1,0:T(8,128)(2,1)S(1)}, u32[]{:S(2)}, u32[]{:S(2)}) collective-permute-start(bf16[352,1024]{1,0:T(8,128)(2,1)} %copy.98), channel_id=1, source_target_pairs={{0,2},{1,3},{2,0},{3,1},{4,6},{5,7},{6,4},{7,5},{8,10},{9,11},{10,... | collective-permute-start | bytes 2162696 | tf_op jit(solution)/shard_map/ppermute | solution.py:58
  240.5 17.6 %collective-permute-start.26 = (bf16[288,1024]{1,0:T(8,128)(2,1)}, bf16[288,1024]{1,0:T(8,128)(2,1)}, u32[]{:S(2)}, u32[]{:S(2)}) collective-permute-start(bf16[288,1024]{1,0:T(8,128)(2,1)} %pad_maximum_fusion.11), channel_id=1, source_target_pairs={{0,1},{1,0},{2,3},{3,2},{4,5},{5,4},{6,7},{7,6},{8,9},{9,8},{10,11... | collective-permute-start | bytes 1769480 | tf_op jit(solution)/shard_map/ppermute | solution.py:58
  272.3 23.6 %collective-permute-start.38 = (f32[288,1024]{1,0:T(8,128)S(1)}, f32[288,1024]{1,0:T(8,128)S(1)}, u32[]{:S(2)}, u32[]{:S(2)}) collective-permute-start(f32[288,1024]{1,0:T(8,128)S(1)} %bitcast.345), channel_id=1, source_target_pairs={{0,1},{1,0},{2,3},{3,2},{4,5},{5,4},{6,7},{7,6},{8,9},{9,8},{10,11... | collective-permute-start | bytes 3538952 | tf_op jit(solution)/shard_map/ppermute | solution.py:58
  275.4 19.1 %collective-permute-start.70 = (bf16[352,1024]{1,0:T(8,128)(2,1)S(1)}, bf16[352,1024]{1,0:T(8,128)(2,1)S(1)}, u32[]{:S(2)}, u32[]{:S(2)}) collective-permute-start(bf16[352,1024]{1,0:T(8,128)(2,1)S(1)} %slice.1220), channel_id=1, source_target_pairs={{0,16},{16,0},{1,17},{17,1},{2,18},{18,2},{3,19},{19,3},{4,20},{20... | collective-permute-start | bytes 2162696 | tf_op jit(solution)/shard_map/ppermute | solution.py:58
  279.3 29.5 %collective-permute-start.67 = (bf16[352,1024]{1,0:T(8,128)(2,1)S(1)}, bf16[352,1024]{1,0:T(8,128)(2,1)S(1)}, u32[]{:S(2)}, u32[]{:S(2)}) collective-permute-start(bf16[352,1024]{1,0:T(8,128)(2,1)S(1)} %slice.1214), channel_id=1, source_target_pairs={{0,16},{16,0},{1,17},{17,1},{2,18},{18,2},{3,19},{19,3},{4,20},{20... | collective-permute-start | bytes 2162696 | tf_op jit(solution)/shard_map/ppermute | solution.py:58
  284.8 34.4 %collective-permute-start.73 = (bf16[352,1024]{1,0:T(8,128)(2,1)}, bf16[352,1024]{1,0:T(8,128)(2,1)}, u32[]{:S(2)}, u32[]{:S(2)}) collective-permute-start(bf16[352,1024]{1,0:T(8,128)(2,1)} %bitcast.130), channel_id=1, source_target_pairs={{0,2},{1,3},{2,0},{3,1},{4,6},{5,7},{6,4},{7,5},{8,10},{9,11},{10,... | collective-permute-start | bytes 2162696 | tf_op jit(solution)/shard_map/ppermute | solution.py:58
  296.2 14.0 %collective-permute-start.39 = (bf16[144,1024]{1,0:T(8,128)(2,1)S(1)}, bf16[144,1024]{1,0:T(8,128)(2,1)S(1)}, u32[]{:S(2)}, u32[]{:S(2)}) collective-permute-start(bf16[144,1024]{1,0:T(8,128)(2,1)S(1)} %slice.1467), channel_id=1, source_target_pairs={{0,4},{1,5},{2,6},{3,7},{4,0},{5,1},{6,2},{7,3},{8,12},{9,13},{10,... | collective-permute-start | bytes 884744 | tf_op jit(solution)/shard_map/ppermute | solution.py:58
  315.7 14.1 %all-to-all-start.2 = ((bf16[16,72,128]{2,1,0:T(8,128)(2,1)}), bf16[16,72,128]{2,1,0:T(8,128)(2,1)S(1)}, u32[]{:S(2)}, u32[]{:S(2)}) async-start(bf16[16,72,128]{2,1,0:T(8,128)(2,1)} %reshape.426), calls=%async_computation.2 | async-start | bytes 589824 | tf_op jit(solution)/shard_map/all_to_all | solution.py:523
  324.9 72.6 %collective-permute-start.40 = (f32[288,1024]{1,0:T(8,128)}, f32[288,1024]{1,0:T(8,128)}, u32[]{:S(2)}, u32[]{:S(2)}) collective-permute-start(f32[288,1024]{1,0:T(8,128)} %bitcast.43), channel_id=1, source_target_pairs={{0,1},{1,0},{2,3},{3,2},{4,5},{5,4},{6,7},{7,6},{8,9},{9,8},{10,11... | collective-permute-start | bytes 3538952 | tf_op jit(solution)/shard_map/ppermute | solution.py:58
  352.4 18.8 %collective-permute-start.74 = (bf16[176,1024]{1,0:T(8,128)(2,1)}, bf16[176,1024]{1,0:T(8,128)(2,1)}, u32[]{:S(2)}, u32[]{:S(2)}) collective-permute-start(bf16[176,1024]{1,0:T(8,128)(2,1)} %fusion.18), channel_id=1, source_target_pairs={{0,16},{16,0},{1,17},{17,1},{2,18},{18,2},{3,19},{19,3},{4,20},{20... | collective-permute-start | bytes 1081352 | tf_op jit(solution)/shard_map/ppermute | solution.py:58
  356.3 23.7 %collective-permute-start.68 = (bf16[176,1024]{1,0:T(8,128)(2,1)}, bf16[176,1024]{1,0:T(8,128)(2,1)}, u32[]{:S(2)}, u32[]{:S(2)}) collective-permute-start(bf16[176,1024]{1,0:T(8,128)(2,1)} %bitcast.122), channel_id=1, source_target_pairs={{0,2},{1,3},{2,0},{3,1},{4,6},{5,7},{6,4},{7,5},{8,10},{9,11},{10,... | collective-permute-start | bytes 1081352 | tf_op jit(solution)/shard_map/ppermute | solution.py:58
  359.9 63.7 %collective-permute-start.62 = (bf16[512,1024]{1,0:T(8,128)(2,1)}, bf16[512,1024]{1,0:T(8,128)(2,1)}, u32[]{:S(2)}, u32[]{:S(2)}) collective-permute-start(bf16[512,1024]{1,0:T(8,128)(2,1)} %bitcast.105), channel_id=1, source_target_pairs={{0,1},{1,0},{2,3},{3,2},{4,5},{5,4},{6,7},{7,6},{8,9},{9,8},{10,11... | collective-permute-start | bytes 3145736 | tf_op jit(solution)/shard_map/ppermute | solution.py:58
  367.4 10.7 %collective-permute-start.71 = (bf16[176,1024]{1,0:T(8,128)(2,1)}, bf16[176,1024]{1,0:T(8,128)(2,1)}, u32[]{:S(2)}, u32[]{:S(2)}) collective-permute-start(bf16[176,1024]{1,0:T(8,128)(2,1)} %bitcast.126), channel_id=1, source_target_pairs={{0,2},{1,3},{2,0},{3,1},{4,6},{5,7},{6,4},{7,5},{8,10},{9,11},{10,... | collective-permute-start | bytes 1081352 | tf_op jit(solution)/shard_map/ppermute | solution.py:58
  371.2 54.7 %collective-permute-start.42 = (bf16[1152,512]{1,0:T(8,128)(2,1)}, bf16[1152,512]{1,0:T(8,128)(2,1)}, u32[]{:S(2)}, u32[]{:S(2)}) collective-permute-start(bf16[1152,512]{1,0:T(8,128)(2,1)} %convolution_convert_fusion.1), channel_id=1, source_target_pairs={{0,1},{1,0},{2,3},{3,2},{4,5},{5,4},{6,7},{7,6},{8,9},{9,8},{10,11... | collective-permute-start | bytes 3538952 | tf_op jit(solution)/shard_map/ppermute | solution.py:58
  378.1 50.9 %collective-permute-start.46 = (bf16[1152,512]{1,0:T(8,128)(2,1)}, bf16[1152,512]{1,0:T(8,128)(2,1)}, u32[]{:S(2)}, u32[]{:S(2)}) collective-permute-start(bf16[1152,512]{1,0:T(8,128)(2,1)} %convolution_convert_fusion), channel_id=1, source_target_pairs={{0,1},{1,0},{2,3},{3,2},{4,5},{5,4},{6,7},{7,6},{8,9},{9,8},{10,11... | collective-permute-start | bytes 3538952 | tf_op jit(solution)/shard_map/ppermute | solution.py:58
  380.0 11.7 %collective-permute-start.75 = (bf16[88,1024]{1,0:T(8,128)(2,1)S(1)}, bf16[88,1024]{1,0:T(8,128)(2,1)S(1)}, u32[]{:S(2)}, u32[]{:S(2)}) collective-permute-start(bf16[88,1024]{1,0:T(8,128)(2,1)S(1)} %slice.1469), channel_id=1, source_target_pairs={{0,8},{1,9},{2,10},{3,11},{4,12},{5,13},{6,14},{7,15},{8,0},{9,1},... | collective-permute-start | bytes 540680 | tf_op jit(solution)/shard_map/ppermute | solution.py:58
  391.7 10.9 %collective-permute-start.72 = (bf16[88,1024]{1,0:T(8,128)(2,1)}, bf16[88,1024]{1,0:T(8,128)(2,1)}, u32[]{:S(2)}, u32[]{:S(2)}) collective-permute-start(bf16[88,1024]{1,0:T(8,128)(2,1)} %slice.1470), channel_id=1, source_target_pairs={{0,8},{1,9},{2,10},{3,11},{4,12},{5,13},{6,14},{7,15},{8,0},{9,1},... | collective-permute-start | bytes 540680 | tf_op jit(solution)/shard_map/ppermute | solution.py:58
  392.8 49.5 %all-to-all-start.3 = ((f32[32,32,88]{2,1,0:T(8,128)}), f32[32,32,88]{2,1,0:T(8,128)}, u32[]{:S(2)}, u32[]{:S(2)}) async-start(f32[32,32,88]{2,1,0:T(8,128)} %bitcast.132), calls=%async_computation.3 | async-start | bytes 1048576 | tf_op jit(solution)/shard_map/all_to_all | solution.py:559
  397.5 23.8 %collective-permute-start.69 = (bf16[88,1024]{1,0:T(8,128)(2,1)}, bf16[88,1024]{1,0:T(8,128)(2,1)S(1)}, u32[]{:S(2)}, u32[]{:S(2)}) collective-permute-start(bf16[88,1024]{1,0:T(8,128)(2,1)} %slice.1471), channel_id=1, source_target_pairs={{0,8},{1,9},{2,10},{3,11},{4,12},{5,13},{6,14},{7,15},{8,0},{9,1},... | collective-permute-start | bytes 540680 | tf_op jit(solution)/shard_map/ppermute | solution.py:58
  402.6 19.5 %collective-permute-start.41 = (bf16[144,1024]{1,0:T(8,128)(2,1)S(1)}, bf16[144,1024]{1,0:T(8,128)(2,1)S(1)}, u32[]{:S(2)}, u32[]{:S(2)}) collective-permute-start(bf16[144,1024]{1,0:T(8,128)(2,1)S(1)} %fusion.23), channel_id=1, source_target_pairs={{0,4},{1,5},{2,6},{3,7},{4,0},{5,1},{6,2},{7,3},{8,12},{9,13},{10,... | collective-permute-start | bytes 884744 | tf_op jit(solution)/shard_map/ppermute | solution.py:58
  425.4 13.9 %collective-permute-start.63 = (bf16[256,1024]{1,0:T(8,128)(2,1)S(1)}, bf16[256,1024]{1,0:T(8,128)(2,1)S(1)}, u32[]{:S(2)}, u32[]{:S(2)}) collective-permute-start(bf16[256,1024]{1,0:T(8,128)(2,1)S(1)} %fusion.29), channel_id=1, source_target_pairs={{0,16},{16,0},{1,17},{17,1},{2,18},{18,2},{3,19},{19,3},{4,20},{20... | collective-permute-start | bytes 1572872 | tf_op jit(solution)/shard_map/ppermute | solution.py:58
  427.7 20.7 %collective-permute-start.43 = (bf16[576,512]{1,0:T(8,128)(2,1)S(1)}, bf16[576,512]{1,0:T(8,128)(2,1)}, u32[]{:S(2)}, u32[]{:S(2)}) collective-permute-start(bf16[576,512]{1,0:T(8,128)(2,1)S(1)} %bitcast.359), channel_id=1, source_target_pairs={{0,2},{1,3},{2,0},{3,1},{4,6},{5,7},{6,4},{7,5},{8,10},{9,11},{10,... | collective-permute-start | bytes 1769480 | tf_op jit(solution)/shard_map/ppermute | solution.py:58
  442.2 20.6 %collective-permute-start.47 = (bf16[576,512]{1,0:T(8,128)(2,1)}, bf16[576,512]{1,0:T(8,128)(2,1)}, u32[]{:S(2)}, u32[]{:S(2)}) collective-permute-start(bf16[576,512]{1,0:T(8,128)(2,1)} %bitcast.58), channel_id=1, source_target_pairs={{0,4},{1,5},{2,6},{3,7},{4,0},{5,1},{6,2},{7,3},{8,12},{9,13},{10,... | collective-permute-start | bytes 1769480 | tf_op jit(solution)/shard_map/ppermute | solution.py:58
  448.3 13.9 %collective-permute-start.65 = (bf16[64,1024]{1,0:T(8,128)(2,1)S(1)}, bf16[64,1024]{1,0:T(8,128)(2,1)S(1)}, u32[]{:S(2)}, u32[]{:S(2)}) collective-permute-start(bf16[64,1024]{1,0:T(8,128)(2,1)S(1)} %bitcast.368), channel_id=1, source_target_pairs={{0,4},{1,5},{2,6},{3,7},{4,0},{5,1},{6,2},{7,3},{8,12},{9,13},{10,... | collective-permute-start | bytes 393224 | tf_op jit(solution)/shard_map/ppermute | solution.py:58
  449.8 27.1 %collective-permute-start.44 = (bf16[288,512]{1,0:T(8,128)(2,1)S(1)}, bf16[288,512]{1,0:T(8,128)(2,1)S(1)}, u32[]{:S(2)}, u32[]{:S(2)}) collective-permute-start(bf16[288,512]{1,0:T(8,128)(2,1)S(1)} %bitcast.361), channel_id=1, source_target_pairs={{0,4},{1,5},{2,6},{3,7},{4,0},{5,1},{6,2},{7,3},{8,12},{9,13},{10,... | collective-permute-start | bytes 884744 | tf_op jit(solution)/shard_map/ppermute | solution.py:58
  462.3 13.9 %collective-permute-start.66 = (bf16[32,1024]{1,0:T(8,128)(2,1)S(1)}, bf16[32,1024]{1,0:T(8,128)(2,1)S(1)}, u32[]{:S(2)}, u32[]{:S(2)}) collective-permute-start(bf16[32,1024]{1,0:T(8,128)(2,1)S(1)} %fusion.72), channel_id=1, source_target_pairs={{0,8},{1,9},{2,10},{3,11},{4,12},{5,13},{6,14},{7,15},{8,0},{9,1},... | collective-permute-start | bytes 196616 | tf_op jit(solution)/shard_map/ppermute | solution.py:58
  464.3 18.5 %collective-permute-start.48 = (bf16[288,512]{1,0:T(8,128)(2,1)S(1)}, bf16[288,512]{1,0:T(8,128)(2,1)S(1)}, u32[]{:S(2)}, u32[]{:S(2)}) collective-permute-start(bf16[288,512]{1,0:T(8,128)(2,1)S(1)} %slice.1465), channel_id=1, source_target_pairs={{0,8},{1,9},{2,10},{3,11},{4,12},{5,13},{6,14},{7,15},{8,0},{9,1},... | collective-permute-start | bytes 884744 | tf_op jit(solution)/shard_map/ppermute | solution.py:58
  496.9 9.0 %collective-permute-start.55 = (bf16[512,896]{1,0:T(8,128)(2,1)S(1)}, bf16[512,896]{1,0:T(8,128)(2,1)S(1)}, u32[]{:S(2)}, u32[]{:S(2)}) collective-permute-start(bf16[512,896]{1,0:T(8,128)(2,1)S(1)} %bitcast.350), channel_id=1, source_target_pairs={{0,1},{1,0},{2,3},{3,2},{4,5},{5,4},{6,7},{7,6},{8,9},{9,8},{10,11... | collective-permute-start | bytes 2752520 | tf_op jit(solution)/shard_map/ppermute | solution.py:58
  502.2 14.7 %collective-permute-start.51 = (bf16[256,896]{1,0:T(8,128)(2,1)S(1)}, bf16[256,896]{1,0:T(8,128)(2,1)S(1)}, u32[]{:S(2)}, u32[]{:S(2)}) collective-permute-start(bf16[256,896]{1,0:T(8,128)(2,1)S(1)} %bitcast.360), channel_id=1, source_target_pairs={{0,2},{1,3},{2,0},{3,1},{4,6},{5,7},{6,4},{7,5},{8,10},{9,11},{10,... | collective-permute-start | bytes 1376264 | tf_op jit(solution)/shard_map/ppermute | solution.py:58
  506.3 10.8 %collective-permute-start.56 = (bf16[256,896]{1,0:T(8,128)(2,1)S(1)}, bf16[256,896]{1,0:T(8,128)(2,1)S(1)}, u32[]{:S(2)}, u32[]{:S(2)}) collective-permute-start(bf16[256,896]{1,0:T(8,128)(2,1)S(1)} %fusion.30), channel_id=1, source_target_pairs={{0,16},{16,0},{1,17},{17,1},{2,18},{18,2},{3,19},{19,3},{4,20},{20... | collective-permute-start | bytes 1376264 | tf_op jit(solution)/shard_map/ppermute | solution.py:58
  517.2 10.1 %collective-permute-start.57 = (bf16[128,896]{1,0:T(8,128)(2,1)S(1)}, bf16[128,896]{1,0:T(8,128)(2,1)S(1)}, u32[]{:S(2)}, u32[]{:S(2)}) collective-permute-start(bf16[128,896]{1,0:T(8,128)(2,1)S(1)} %bitcast.363), channel_id=1, source_target_pairs={{0,2},{1,3},{2,0},{3,1},{4,6},{5,7},{6,4},{7,5},{8,10},{9,11},{10,... | collective-permute-start | bytes 688136 | tf_op jit(solution)/shard_map/ppermute | solution.py:58
  525.4 9.9 %collective-permute-start.53 = (bf16[64,896]{1,0:T(8,128)(2,1)S(1)}, bf16[64,896]{1,0:T(8,128)(2,1)S(1)}, u32[]{:S(2)}, u32[]{:S(2)}) collective-permute-start(bf16[64,896]{1,0:T(8,128)(2,1)S(1)} %bitcast.369), channel_id=1, source_target_pairs={{0,4},{1,5},{2,6},{3,7},{4,0},{5,1},{6,2},{7,3},{8,12},{9,13},{10,... | collective-permute-start | bytes 344072 | tf_op jit(solution)/shard_map/ppermute | solution.py:58
  (100 other events, 1200.1 us)

commit v3 on v2

--- a/solution.py
+++ b/solution.py
@@ -52,6 +52,10 @@
     return gelu_tanh(gate_pre) * up_pre
 
 
+SEQ = "seq"
+BOTH = ("dp", "seq")
+
+
 def swap(array, step):
     axis, bit = step
     count = lax.axis_size(axis)
@@ -59,66 +63,59 @@
 
 
 def my_bit(step):
-    axis, bit = step
-    return (lax.axis_index(axis) >> bit) & 1
+    return (lax.axis_index(step[0]) >> step[1]) & 1
 
 
 def rank(step):
     return (1000 if step[0] == "dp" else 0) + step[1]
 
 
-def after(value, signal):
-    return value + (signal[(0,) * signal.ndim] * 0).astype(value.dtype)
-
-
-def gather(block, order, absolute, hold=None):
-    have = []
-    stages = []
+def together(*arrays):
+    return lax.optimization_barrier(arrays)
+
+
+def joined(mine, other, step, have, absolute):
+    at = sum(1 for done in have if rank(done) > rank(step))
+    if absolute:
+        bit = my_bit(step) == 1
+        mine, other = jnp.where(bit, other, mine), jnp.where(bit, mine, other)
+    shape = (2**at, 1, mine.shape[0] >> at, mine.shape[1])
+    return jnp.concatenate([mine.reshape(shape), other.reshape(shape)], axis=1).reshape(
+        -1, mine.shape[1]
+    )
+
+
+def halves(grads, step, every, absolute):
+    at = sum(1 for other in every if rank(other) > rank(step))
+    rows, width = grads.shape[0] // 2, grads.shape[1]
+    view = grads.reshape(2**at, 2, rows >> at, width)
+    if absolute:
+        bit = my_bit(step)
+        keep = lax.dynamic_slice_in_dim(view, bit, 1, 1)
+        send = lax.dynamic_slice_in_dim(view, 1 - bit, 1, 1)
+    else:
+        keep, send = view[:, 0], view[:, 1]
+    return keep.reshape(rows, width), send.reshape(rows, width)
+
+
+def gather(block, order, absolute, hooks=None):
     for number, step in enumerate(order):
-        if hold and number in hold:
-            block = after(block, hold[number])
         other = swap(block, step)
-        at = sum(1 for done in have if rank(done) > rank(step))
-        mine = block
-        if absolute:
-            bit = my_bit(step) == 1
-            mine, other = jnp.where(bit, other, mine), jnp.where(bit, mine, other)
-        outer = 2**at
-        size = block.shape[0] // outer
-        parts = []
-        for which in range(outer):
-            parts += [mine[which * size : (which + 1) * size], other[which * size : (which + 1) * size]]
-        have.append(step)
-        block = jnp.concatenate(parts, axis=0)
-        stages.append(block)
-    return stages
-
-
-def scatter_add(grads, order, every, absolute, wide=(), hold=None):
-    every = sorted(every, key=rank, reverse=True)
-    width = grads.shape[1]
-    stages = []
+        if hooks and number in hooks:
+            block = hooks[number](block)
+        block = joined(block, other, step, order[:number], absolute)
+    return block
+
+
+def scatter_add(grads, order, every, absolute, hooks=None):
     for number, step in enumerate(order):
-        at = every.index(step)
-        rows = grads.shape[0] // 2
-        if absolute:
-            view = grads.reshape(2**at, 2, rows // 2**at, width)
-            bit = my_bit(step)
-            keep = lax.dynamic_slice_in_dim(view, bit, 1, 1).reshape(rows, width)
-            send = lax.dynamic_slice_in_dim(view, 1 - bit, 1, 1).reshape(rows, width)
-        elif at == 0:
-            keep, send = grads[:rows], grads[rows:]
-        else:
-            view = grads.reshape(2**at, 2, rows // 2**at, width)
-            keep, send = view[:, 0].reshape(rows, width), view[:, 1].reshape(rows, width)
-        if hold and number in hold:
-            send = after(send, hold[number])
-        kind = F32 if step in wide else BF16
-        got = swap(send.astype(kind), step)
-        grads = keep.astype(F32) + got.astype(F32)
-        every = [other for other in every if other != step]
-        stages.append(grads)
-    return stages
+        left = [other for other in every if other not in order[:number]]
+        keep, send = halves(grads, step, left, absolute)
+        other = swap(send.astype(BF16), step)
+        if hooks and number in hooks:
+            keep = hooks[number](keep)
+        grads = keep.astype(F32) + other.astype(F32)
+    return grads
 
 
 def bias_kernel(table_ref, out_ref):
@@ -353,9 +350,9 @@
     patch_features, text_embeds, text_lengths, w_in, b_in, gain_attn, w_query, w_key, w_value,
     w_out, gain_ffn, w_gate, w_up, w_down, position_bias, d_patch, d_text,
 ):
-    seq_count, dp_count = lax.axis_size("seq"), lax.axis_size("dp")
+    seq_count, dp_count = lax.axis_size(SEQ), lax.axis_size("dp")
     dev_count = seq_count * dp_count
-    seq_index, dp_index = lax.axis_index("seq"), lax.axis_index("dp")
+    seq_index, dp_index = lax.axis_index(SEQ), lax.axis_index("dp")
     rows, patch_dev, vit = patch_features.shape
     text_dev = text_embeds.shape[1]
     tok = patch_dev + text_dev
@@ -364,11 +361,10 @@
     cols = w_in.shape[1]
     images = text_lengths.shape[1]
     slots = text_dev * seq_count
-    core, near, team_bit = ("seq", 0), ("seq", 1), ("seq", 2)
+    core, near, team_bit = ("seq", 0), ("seq", 1), ("seq", 3)
     seq_high = [("seq", bit) for bit in range(seq_count.bit_length() - 2, 1, -1)]
     dp_bits = [("dp", bit) for bit in range(dp_count.bit_length() - 1)]
     every = dp_bits + seq_high + [near, core]
-    both = ("dp", "seq")
 
     bias_count = position_bias.shape[0]
     pack = jnp.concatenate(
@@ -379,16 +375,12 @@
             gain_ffn[None],
             jnp.pad(position_bias, (0, cols - bias_count))[None],
             jnp.zeros((124, cols), BF16),
+            w_out,
         ],
         axis=0,
     ).T
     wide = vit + 128
-    half_in = wide // 256 * 128
-    in_low_stages = gather(pack[:, :half_in], seq_high + dp_bits + [near, core], True)
-    in_high_stages = gather(pack[:, half_in:], seq_high + [near] + dp_bits + [core], True)
-    in_low, in_high = in_low_stages[-1], in_high_stages[-1]
-    in_part = in_low_stages[len(seq_high) - 1]
-
+    half_in = (wide + d_model) // 256 * 128
     per_head = dev_count // HEADS
     twins = seq_count // HEADS
     head = seq_index // twins
@@ -396,7 +388,6 @@
     place_in_head = dp_index * twins + twin
     row_count = rows // twins
     three = jnp.concatenate([w_query.T, w_key.T, w_value.T], axis=0)
-    three = after(three, in_part)
 
     def to_rank(which_head, place):
         return (place // twins) * seq_count + which_head * twins + place % twins
@@ -410,33 +401,48 @@
                 pairs.append((user, owner) if back else (owner, user))
         return pairs
 
-    pieces = jnp.stack([lax.ppermute(three, both, rounds(turn, False)) for turn in range(per_head)])
-    pieces = pieces.reshape(per_head, 3, cols, d_model)
-    ordered = [
-        lax.dynamic_index_in_dim(pieces, (place_in_head - i) % per_head, 0, keepdims=False)
-        for i in range(per_head)
-    ]
-    w_head = jnp.stack(ordered, axis=1).reshape(3 * HEAD_DIM, d_model)
-
     team = [team_bit, core]
-    ff_high = [step for step in seq_high if step != team_bit]
-    ff_order = ff_high + [near] + dp_bits
-    ff_other = ff_high + dp_bits + [near]
+    ff_far = [step for step in seq_high if step != team_bit]
     units = w_gate.shape[1]
-    full_gate = gather(w_gate.T, ff_order, False, {0: in_low})[-1]
-    full_up = gather(w_up.T, ff_order, False, {0: in_low})[-1]
     down_out = jnp.transpose(w_down.reshape(dev_count, units, cols), (0, 2, 1))
-    down_in = lax.all_to_all(after(down_out, in_low), both, 0, 0, tiled=True)
-    full_down = gather(down_in.reshape(d_model, units).T, ff_other, False)[-1]
+    upstream = jnp.concatenate([d_patch, d_text], axis=1).reshape(mine, d_model)
+    late = {}
+
+    down_in = lax.all_to_all(down_out, BOTH, 0, 0, tiled=True)
+    ff_order = ff_far + [near] + dp_bits
+
+    def while_split(block):
+        block, down = together(block, down_in)
+        late["ff"] = jnp.concatenate(
+            [w_gate.T, w_up.T, down.reshape(d_model, units).T], axis=1
+        )
+        for step in ff_far[:-1]:
+            late["ff"] = jnp.concatenate([late["ff"], swap(late["ff"], step)], axis=0)
+        late["ff_got"] = swap(late["ff"], ff_far[-1])
+        return block
+
+    def while_core(block):
+        block, send = together(block, three)
+        late["pieces"] = [lax.ppermute(send, BOTH, rounds(turn, False)) for turn in range(per_head)]
+        return block
+
+    in_low = gather(
+        pack[:, :half_in],
+        seq_high + dp_bits + [near, core],
+        True,
+        {len(seq_high): while_split, len(every) - 1: while_core},
+    )
+    in_high = gather(pack[:, half_in:], seq_high + [near] + dp_bits + [core], True)
+    full_out = in_high[:, wide - half_in :]
 
     features = patch_features.reshape(rows * patch_dev, vit)
     ones = jnp.zeros((rows * patch_dev, 128), BF16).at[:, 0].set(1)
     features_more = jnp.concatenate([features, ones], axis=1)
     patch_rows = dot_nt(features_more[:, :half_in], in_low) + dot_nt(
-        features_more[:, half_in:], in_high
+        features_more[:, half_in:], in_high[:, : wide - half_in]
     )
     units_eye = jnp.eye(8, 128, dtype=BF16)
-    small = dot_nt(units_eye, in_high[:, wide - half_in - 128 :])
+    small = dot_nt(units_eye, in_high[:, wide - half_in - 128 : wide - half_in])
     gain_one, gain_two = small[1], small[2]
     table = small[3].reshape(dev_count, cols)[:, :bias_count].reshape(BUCKETS, HEADS)
     my_table = lax.dynamic_slice_in_dim(table, head, 1, 1).reshape(1, BUCKETS)
@@ -447,9 +453,24 @@
     half = d_model // 2
     order_low = seq_high + [near]
     order_high = [near] + seq_high
-    low_stages = gather(normed_one[:, :half], order_low, False)
-    high_stages = gather(normed_one[:, half:], order_high, False)
     chips = seq_count // 2
+    normed_one, *pieces = together(normed_one, *late["pieces"])
+
+    def while_last(block):
+        block, late["up"] = together(block, upstream)
+        late["up_got"] = swap(late["up"], team_bit)
+        return block
+
+    own_low = gather(normed_one[:, :half], order_low, False, {len(seq_high): while_last})
+    own_high = gather(normed_one[:, half:], order_high, False)
+    own_low, own_high, ff_got, up_got = together(
+        own_low, own_high, late["ff_got"], late["up_got"]
+    )
+    other_low, other_high = swap(own_low, core), swap(own_high, core)
+    ff_block = jnp.concatenate([late["ff"], ff_got], axis=0)
+    ff_got = swap(ff_block, near)
+    team_up = jnp.concatenate([late["up"], up_got], axis=0)
+    team_up = jnp.concatenate([team_up, swap(team_up, core)], axis=0)
 
     def my_rows(array):
         if twins == 1:
@@ -458,10 +479,15 @@
         view = lax.dynamic_slice_in_dim(view, twin * row_count, row_count, 1)
         return view.reshape(chips * row_count * tok, array.shape[1])
 
-    own_low, own_high = low_stages[-1], high_stages[-1]
+    pieces = jnp.stack(pieces).reshape(per_head, 3, cols, d_model)
+    ordered = [
+        lax.dynamic_index_in_dim(pieces, (place_in_head - i) % per_head, 0, keepdims=False)
+        for i in range(per_head)
+    ]
+    w_head = jnp.stack(ordered, axis=1).reshape(3 * HEAD_DIM, d_model)
     normed_pairs = [
         (my_rows(own_low), my_rows(own_high)),
-        (my_rows(swap(own_low, core)), my_rows(swap(own_high, core))),
+        (my_rows(other_low), my_rows(other_high)),
     ]
     qkv = [
         (dot_nt(low, w_head[:, :half]) + dot_nt(high, w_head[:, half:]))
@@ -469,9 +495,15 @@
         .reshape(chips, row_count, tok, 3 * HEAD_DIM)
         for low, high in normed_pairs
     ]
-    full_out = gather(
-        w_out.T, seq_high + [near] + dp_bits + [core], True, {0: low_stages[len(seq_high) - 1]}
-    )[-1]
+    *qkv, ff_got = together(*qkv, ff_got)
+    ff_mine = []
+    for which in range(3):
+        part = slice(which * d_model, (which + 1) * d_model)
+        block = jnp.concatenate([ff_block[:, part], ff_got[:, part]], axis=0)
+        for step in dp_bits[:-1]:
+            block = jnp.concatenate([block, swap(block, step)], axis=0)
+        ff_mine.append(block)
+    ff_theirs = [swap(block, dp_bits[-1]) for block in ff_mine]
     lengths = lax.dynamic_slice_in_dim(text_lengths, twin * row_count, row_count, 0)
     me = seq_index.reshape(1).astype(jnp.int32)
     dims = (row_count, images, patch_dev, text_dev, slots)
@@ -491,28 +523,52 @@
             pltpu.VMEM((row_count, patches, HEAD_DIM), BF16),
             pltpu.VMEM((row_count, text_rows, HEAD_DIM), F32),
         ),
-        1 << 30,
-        4 << 20,
+        1 << 24,
+        1 << 20,
         20,
     )(me, lengths, bias, *qkv)
-    mixed = lax.all_to_all(mixed, "seq", 0, 0, tiled=True)
-    mixed = mixed.reshape(HEADS, twins, tok, row_count, HEAD_DIM)
-    attn_out = jnp.transpose(mixed, (1, 3, 2, 0, 4)).reshape(mine, d_model)
+    mixed, ff_theirs[0] = together(mixed, ff_theirs[0])
+    mixed_got = lax.all_to_all(mixed, SEQ, 0, 0, tiled=True)
+    mixed_got, ff_theirs[1] = together(mixed_got, ff_theirs[1])
+    mixed_got = mixed_got.reshape(HEADS, twins, tok, row_count, HEAD_DIM)
+    attn_out = jnp.transpose(mixed_got, (1, 3, 2, 0, 4)).reshape(mine, d_model)
     resid_one = resid + dot_nt(attn_out, full_out)
     normed_two = rms_norm(resid_one, gain_two).astype(BF16)
-    upstream = jnp.concatenate([d_patch, d_text], axis=1).reshape(mine, d_model)
-    team_up = gather(upstream, team, False, {0: own_low})[-1]
-    team_normed = gather(normed_two, team, False)[-1]
-    gate_pre = dot_nt(team_normed, full_gate)
-    up_pre = dot_nt(team_normed, full_up)
-    hidden, gated_back = jax.vjp(gated_unit, gate_pre, up_pre)
-    hidden = hidden.astype(BF16)
-
-    d_hidden = dot_nt(team_up, full_down)
-    d_gate, d_up = gated_back(d_hidden)
-    d_gate, d_up = d_gate.astype(BF16), d_up.astype(BF16)
-    d_normed_part = dot_nn(d_gate, full_gate) + dot_nn(d_up, full_up)
-    d_normed_two = scatter_add(d_normed_part, [core, team_bit], team, False, (core,))[-1]
+    team_normed = normed_two
+    for step in team:
+        team_normed = jnp.concatenate([team_normed, swap(team_normed, step)], axis=0)
+    weights_at = [ff_mine, ff_theirs]
+    d_normed_part, unit_grads = 0.0, []
+    for full_gate, full_up, full_down in weights_at:
+        gate_pre = dot_nt(team_normed, full_gate)
+        up_pre = dot_nt(team_normed, full_up)
+        hidden, gated_back = jax.vjp(gated_unit, gate_pre, up_pre)
+        d_gate, d_up = gated_back(dot_nt(team_up, full_down))
+        unit_grads.append([d_gate.astype(BF16), d_up.astype(BF16), hidden.astype(BF16)])
+        for grad, full in zip(unit_grads[-1], (full_gate, full_up)):
+            d_normed_part = d_normed_part + dot_nn(grad, full)
+
+    def unit_weight_grads(d_gate, d_up, hidden):
+        return jnp.concatenate(
+            [
+                dot_tn(d_gate, team_normed).astype(BF16),
+                dot_tn(d_up, team_normed).astype(BF16),
+                dot_tn(hidden, team_up).astype(BF16),
+            ],
+            axis=1,
+        )
+
+    def ff_grads_start(keep):
+        keep, *grads = together(keep, *unit_grads[1])
+        keep, send = together(keep, unit_weight_grads(*grads))
+        late["ff_got"] = swap(send, dp_bits[-1])
+        return keep
+
+    keep, send = halves(d_normed_part, core, [core], False)
+    d_normed_two = keep + swap(send.astype(BF16), core).astype(F32)
+    keep, send = halves(d_normed_two, team_bit, [team_bit], False)
+    got = swap(send.astype(BF16), team_bit)
+    d_normed_two = ff_grads_start(keep) + got.astype(F32)
     _, norm_back_two = jax.vjp(rms_norm, resid_one, gain_two)
     d_resid_one, grad_gain_two = norm_back_two(d_normed_two)
     d_resid_one = d_resid_one + upstream.astype(F32)
@@ -520,7 +576,17 @@
     d_attn = dot_nn(d_mix, full_out).astype(BF16)
     d_attn = d_attn.reshape(twins, row_count, tok, HEADS, HEAD_DIM)
     d_attn = jnp.transpose(d_attn, (3, 0, 2, 1, 4)).reshape(packed_shape.shape)
-    d_attn = lax.all_to_all(d_attn, "seq", 0, 0, tiled=True)
+    d_attn_got = lax.all_to_all(d_attn, SEQ, 0, 0, tiled=True)
+
+    d_mix, *grads = together(d_mix, *unit_grads[0])
+    ff_keep = unit_weight_grads(*grads)
+    out_part = dot_nn(grads[2], weights_at[0][2]) + dot_nn(unit_grads[1][2], weights_at[1][2])
+    out_keep, send = halves(out_part, core, [core], False)
+    out_grad = dot_tn(d_mix, attn_out).astype(BF16)
+    d_attn_got, send, ff_keep, out_grad = together(
+        d_attn_got, send.astype(BF16), ff_keep, out_grad
+    )
+    out_got = swap(send, core)
     half_shape = jax.ShapeDtypeStruct(qkv[0].shape, BF16)
     d_own, d_other, d_bias = call(
         lambda *refs: backward_kernel(dims, *refs),
@@ -534,39 +600,11 @@
             pltpu.VMEM((row_count, patches, 3 * HEAD_DIM), BF16),
             pltpu.VMEM((row_count, text_rows, 3 * HEAD_DIM), F32),
         ),
-        3 << 30,
-        8 << 20,
+        1 << 24,
+        1 << 20,
         28,
-    )(me, lengths, bias, *qkv, d_attn)
-    d_qkv = [
-        array.reshape(chips * row_count * tok, 3 * HEAD_DIM) for array in (d_own, d_other)
-    ]
-
-    ff_hold = {1: d_own}
-    grad_gate = scatter_add(
-        dot_tn(after(d_gate, d_normed_part), team_normed).astype(BF16),
-        ff_order[::-1], ff_order, False, (), ff_hold,
-    )[-1]
-    grad_up = scatter_add(
-        dot_tn(after(d_up, d_normed_part), team_normed).astype(BF16),
-        ff_order[::-1], ff_order, False, (), ff_hold,
-    )[-1]
-    grad_down = scatter_add(
-        dot_tn(after(hidden, d_normed_part), team_up).astype(BF16),
-        ff_other[::-1], ff_order, False, (), ff_hold,
-    )[-1]
-    down_back = grad_down.T.reshape(dev_count, cols, units)
-    down_back = lax.all_to_all(down_back, both, 0, 0, tiled=True)
-    grad_down = jnp.transpose(down_back, (0, 2, 1)).reshape(dev_count * units, cols)
-    out_part = dot_nn(after(hidden, d_normed_part), full_down)
-    result = scatter_add(
-        out_part, [core, team_bit], team, False, (core,), {0: d_normed_two, 1: d_own}
-    )[-1]
-    result = (resid_one + result).astype(BF16).reshape(rows, tok, d_model)
-
-    d_table = call(
-        bucket_kernel, jax.ShapeDtypeStruct((BUCKETS, 128), F32), [VMEM], (), 1 << 25, 1 << 20, 8
-    )(d_bias)[:, 0]
+    )(me, lengths, bias, *qkv, d_attn_got)
+    d_qkv = [array.reshape(chips * row_count * tok, 3 * HEAD_DIM) for array in (d_own, d_other)]
 
     def all_rows(array):
         if twins == 1:
@@ -577,48 +615,74 @@
         return view.reshape(chips * mine, array.shape[1])
 
     chip_bits = seq_high + [near]
-
-    def d_normed(weights, order):
-        other = all_rows(dot_nn(d_qkv[1], weights).astype(BF16))
-        own = all_rows(dot_nn(d_qkv[0], weights))
-        return scatter_add(
-            own + swap(other, core).astype(F32), order, chip_bits, False
+    weights = (w_head[:, :half], w_head[:, half:])
+    sends = together(*[all_rows(dot_nn(d_qkv[1], part).astype(BF16)) for part in weights], d_own)
+    others = [swap(send, core) for send in sends[:2]]
+    d_qkv[0] = sends[2].reshape(d_qkv[0].shape)
+    owns = [
+        all_rows(dot_nn(d_qkv[0], part)) + other.astype(F32) for part, other in zip(weights, others)
+    ]
+    state = {}
+
+    def ff_take(keep, step):
+        keep, got = together(keep, state["ff_got"])
+        state["ff"] = state["ff_keep"].astype(F32) + got.astype(F32)
+        return keep
+
+    def ff_start(keep, step):
+        count = state["ff"].shape[0] // 2
+        state["ff_keep"] = state["ff"][:count]
+        keep, send = together(keep, state["ff"][count:].astype(BF16))
+        state["ff_got"] = swap(send, step)
+        return keep
+
+    ff_back = ff_order[::-1]
+    state.update(ff_keep=ff_keep, ff_got=late["ff_got"])
+
+    def while_first(keep):
+        keep = ff_take(keep, ff_back[0])
+        for step in ff_back[1 : len(dp_bits)]:
+            keep = ff_take(ff_start(keep, step), step)
+        return ff_start(keep, near)
+
+    def while_last_again(keep):
+        keep = ff_take(keep, near)
+        for step in ff_far[:0:-1]:
+            keep = ff_take(ff_start(keep, step), step)
+        return ff_start(keep, ff_far[0])
+
+    def while_middle(keep):
+        keep, grads_own, grads_other = together(keep, *d_qkv)
+        d_head = jnp.concatenate(
+            [
+                dot_tn(grads_own, normed_pairs[0][which])
+                + dot_tn(grads_other, normed_pairs[1][which])
+                for which in range(2)
+            ],
+            axis=1,
         )
-
-    low_sums = d_normed(w_head[:, :half], order_low[::-1])
-    high_sums = d_normed(w_head[:, half:], order_high[::-1])
-    d_normed_one = jnp.concatenate([low_sums[-1], high_sums[-1]], axis=1)
-    out_order = [core] + dp_bits[::-1] + [near] + seq_high[::-1]
-    grad_out = scatter_add(
-        dot_tn(after(d_mix, d_attn), attn_out).astype(BF16), out_order, every, True, (), {1: d_own}
-    )[-1]
-
-    d_head = jnp.concatenate(
-        [
-            sum(dot_tn(grads, pair[which]) for grads, pair in zip(d_qkv, normed_pairs))
-            for which in range(2)
-        ],
-        axis=1,
-    )
-    d_head = d_head.reshape(3, per_head, cols, d_model).astype(BF16)
-    d_head = after(d_head, low_sums[-1])
-    d_three = 0.0
-    for turn in range(per_head):
-        piece = lax.dynamic_index_in_dim(
-            d_head, (place_in_head - turn) % per_head, 1, keepdims=False
-        )
-        got = lax.ppermute(piece.reshape(3 * cols, d_model), both, rounds(turn, True))
-        d_three = d_three + got.astype(F32)
-
+        d_head = d_head.reshape(3, per_head, cols, d_model).astype(BF16)
+        sends = [
+            lax.dynamic_index_in_dim(
+                d_head, (place_in_head - turn) % per_head, 1, keepdims=False
+            ).reshape(3 * cols, d_model)
+            for turn in range(per_head)
+        ]
+        keep, *state["sends"] = together(keep, *sends)
+        return keep
+
+    low_sums = scatter_add(owns[0], order_low[::-1], chip_bits, False, {0: while_first, 1: while_middle, len(order_low) - 1: while_last_again})
+    high_sums = scatter_add(owns[1], order_high[::-1], chip_bits, False)
+    d_normed_one = jnp.concatenate([low_sums, high_sums], axis=1)
+    d_table = call(
+        bucket_kernel, jax.ShapeDtypeStruct((BUCKETS, 128), F32), [VMEM], (), 1 << 20, 1 << 20, 8
+    )(d_bias)[:, 0]
     _, norm_back_one = jax.vjp(rms_norm, resid, gain_one)
     d_resid, grad_gain_one = norm_back_one(d_normed_one)
     d_resid = (d_resid + d_resid_one).reshape(rows, tok, d_model)
     text_grad = d_resid[:, patch_dev:]
     d_patch_rows = d_resid[:, :patch_dev].reshape(rows * patch_dev, d_model)
     d_low = d_patch_rows.astype(BF16)
-    feature_grad = jnp.concatenate(
-        [dot_nn(d_low, in_low), dot_nn(d_low, in_high[:, : vit - half_in])], axis=1
-    ).reshape(rows, patch_dev, vit)
     pos_grads = d_table[:, None] * (jnp.arange(HEADS)[None, :] == head).astype(F32)
     pos_grads = jnp.pad(
         pos_grads.reshape(dev_count, bias_count), ((0, 0), (0, cols - bias_count))
@@ -641,25 +705,57 @@
         ],
         axis=0,
     )
-    in_grads = jnp.concatenate(
-        [
-            scatter_add(
-                dot_tn(left, right[:, :half_in]).astype(BF16),
-                [core, near] + dp_bits[::-1] + seq_high[::-1],
-                every,
-                True,
-            )[-1],
-            scatter_add(
-                dot_tn(left, right[:, half_in:]).astype(BF16),
-                [core] + dp_bits[::-1] + [near] + seq_high[::-1],
-                every,
-                True,
-            )[-1],
-        ],
-        axis=1,
-    )
-    small_out = in_grads[:, vit:]
-    d_three = d_three.reshape(3, cols, d_model)
+
+    def while_core_again(keep):
+        keep, got, *sends = together(keep, out_got, *state["sends"])
+        part = out_keep + got.astype(F32)
+        state["out_keep"], send = halves(part, team_bit, [team_bit], False)
+        keep, send, state["d_low"] = together(keep, send.astype(BF16), d_low)
+        state["three"] = [
+            lax.ppermute(send, BOTH, rounds(turn, True)) for turn, send in enumerate(sends)
+        ]
+        state["out_got"] = swap(send, team_bit)
+        return keep
+
+    def while_end(keep):
+        keep, *state["three"] = together(keep, *state["three"])
+        return keep
+
+    def while_split_again(keep):
+        keep = ff_take(keep, ff_far[0])
+        down = state["ff"][:, 2 * d_model :]
+        down_back = down.T.reshape(dev_count, cols, units)
+        keep, down_back = together(keep, down_back)
+        state["down_back"] = lax.all_to_all(down_back, BOTH, 0, 0, tiled=True)
+        return keep
+
+    out_grad = dot_tn(d_mix, attn_out).astype(BF16)
+    in_low_sums = scatter_add(
+        dot_tn(left, right[:, :half_in]).astype(BF16),
+        [core, near] + dp_bits[::-1] + seq_high[::-1],
+        every,
+        True,
+        {0: while_core_again, 2: while_split_again, len(every) - 1: while_end},
+    )
+    in_high_sums = scatter_add(
+        jnp.concatenate([dot_tn(left, right[:, half_in:]).astype(BF16), out_grad], axis=1),
+        [core] + dp_bits[::-1] + [near] + seq_high[::-1],
+        every,
+        True,
+    )
+    in_grads = jnp.concatenate([in_low_sums, in_high_sums], axis=1)
+    small_out, grad_w_out = in_grads[:, vit:wide], in_grads[:, wide:]
+    d_low = state["d_low"]
+    feature_grad = jnp.concatenate(
+        [dot_nn(d_low, in_low), dot_nn(d_low, in_high[:, : vit - half_in])], axis=1
+    ).reshape(rows, patch_dev, vit)
+    result = resid_one + state["out_keep"] + state["out_got"].astype(F32)
+    result = result.astype(BF16).reshape(rows, tok, d_model)
+    grad_gate = state["ff"][:, :d_model]
+    grad_up = state["ff"][:, d_model : 2 * d_model]
+    grad_down = jnp.transpose(state["down_back"], (0, 2, 1)).reshape(dev_count * units, cols)
+    grad_down = grad_down.astype(F32)
+    d_three = sum(got.astype(F32) for got in state["three"]).reshape(3, cols, d_model)
     return (
         result[:, :patch_dev],
         result[:, patch_dev:],
@@ -671,7 +767,7 @@
         d_three[0].T,
         d_three[1].T,
         d_three[2].T,
-        grad_out.T,
+        grad_w_out.T,
         small_out[:, 2],
         grad_gate.T,
         grad_up.T,
@@ -681,9 +777,9 @@
 
 
 def solution(mesh):
-    token = P("dp", "seq", None)
-    matrix = P(None, ("dp", "seq"))
-    vector = P(("dp", "seq"))
+    token = P("dp", SEQ, None)
+    matrix = P(None, BOTH)
+    vector = P(BOTH)
     return jax.shard_map(
         local,
         mesh=mesh,

time: 548 us -> 473 us (0.86)
  local copies, waits for them, and re-layouts: 103 us -> 61.6 us
  other arithmetic: 64.2 us -> 36.6 us
  starting transfers between devices: 112 us -> 94.2 us
  matrix products: 47 us -> 57.5 us
  waiting for transfers between devices: 178 us -> 186 us
  between operations: 9.36 us -> 3.53 us
    unnamed x311 -> x165, local copies, waits for them, and re-layouts: 46.8 us -> 11.1 us
    ppermute x72 -> x52, waiting for transfers between devices: 166 us -> 186 us  [swap(): return lax.ppermute(array, axis, [(i, i ^ 1 << bit) for i in range(count)])]
    slice x37 -> x10, local copies, waits for them, and re-layouts: 20.6 us -> 3.7 us  [the longest x2 2.3 us: local(): block = jnp.concatenate([ff_block[:, part], ff_got[:, part]], axis=0)]
    add x37 -> x22, other arithmetic: 20.3 us -> 7.18 us  [the longest x3 2.77 us: ff_take(): state['ff'] = state['ff_keep'].astype(F32) + got.astype(F32)]
    ppermute x72 -> x52, starting transfers between devices: 83.1 us -> 70.3 us  [swap(): return lax.ppermute(array, axis, [(i, i ^ 1 << bit) for i in range(count)])]
    all_to_all x4, waiting for transfers between devices: 10.7 us -> 0.01 us  [the longest x1 0.01 us: local(): mixed_got = lax.all_to_all(mixed, SEQ, 0, 0, tiled=True)]
    dot_general x10 -> x13, matrix products: 12.9 us -> 19.7 us  [dot_nn(): lax.dot_general(left, right, (((1,), (0,)), ((), ())), preferred_element_...]
    reshape x3 -> x8, local copies, waits for them, and re-layouts: 1.69 us -> 7.77 us  [the longest x2 2.33 us: local(): down_out = jnp.transpose(w_down.reshape(dev_count, units, cols), (0, 2, 1))]
  transfers between devices with their start and end apart: 80 -> 60, of which waited for: 29 -> 27; matrix products, arithmetic and copies ran while one was open for 34% -> 26% of each run, Pallas kernels for 5% -> 6%
where the time goes in v3:
time: 473 us; the launch traced here: 468 us
  waiting for transfers between devices  186 us (39%)
  starting transfers between devices  94.2 us (20%)
  local copies, waits for them, and re-layouts  61.6 us (13%)
  matrix products  57.5 us (12%)
  other arithmetic  36.6 us (8%)
  Pallas kernels  28.8 us (6%)
    ppermute x52, waiting for transfers between devices, swap(): return lax.ppermute(array, axis, [(i, i ^ 1 << bit) for i in range(count)])  186 us
    ppermute x52, starting transfers between devices, swap(): return lax.ppermute(array, axis, [(i, i ^ 1 << bit) for i in range(count)])  70.3 us
    dot_general x14, matrix products, dot_nt(): lax.dot_general(left, right, (((1,), (1,)), ((), ())), preferred_element_...  20.5 us
    dot_general x13, matrix products, dot_nn(): lax.dot_general(left, right, (((1,), (0,)), ((), ())), preferred_element_...  19.7 us
    dot_general x13, matrix products, dot_tn(): lax.dot_general(left, right, (((0,), (0,)), ((), ())), preferred_element_...  17.3 us
    pallas_call x1, Pallas kernels, local(): call(lambda *refs: backward_kernel(dims, *refs), (half_shape, half_shape,...  14.9 us
    pallas_call x1, Pallas kernels, local(): call(lambda *refs: forward_kernel(dims, *refs), packed_shape, [SMEM, SMEM...  11.5 us
    unnamed x165, local copies, waits for them, and re-layouts  11.1 us
  transfers between devices with their start and end apart: 60, of which 27 were waited for; matrix products, arithmetic and copies ran while one was open for 26% of the time, Pallas kernels for 6%

profile of v3, /device:TPU:0, one launch (start us, length us, event | category | flops | bytes accessed | tf_op | source)
XLA Modules:
  0.0 468.2 jit_solution(3723356122644056152)
XLA Ops:
  4.7 4.1 collective-permute-start
  11.1 3.8 all-to-all-start
  15.0 2.7 collective-permute-start.5
  19.3 8.9 %collective-permute-done.5 = bf16[32,1408]{1,0:T(8,128)(2,1)S(1)} collective-permute-done((bf16[32,1408]{1,0:T(8,128)(2,1)S(1)}, bf16[32,1408]{1,0:T(8,128)(2,1)S(1)}, u32[]{:S(2)}, u32[]{:S(2)}) %collective-permute-start.5) | collective-permute-done | bytes 90144 | tf_op jit(solution)/shard_map/ppermute | solution.py:62
  30.0 4.4 collective-permute-done.6
  36.0 2.4 collective-permute-done.2
  40.2 5.8 %collective-permute-done.7 = bf16[128,1408]{1,0:T(8,128)(2,1)S(1)} collective-permute-done((bf16[128,1408]{1,0:T(8,128)(2,1)S(1)}, bf16[128,1408]{1,0:T(8,128)(2,1)S(1)}, u32[]{:S(2)}, u32[]{:S(2)}) %collective-permute-start.7) | collective-permute-done | bytes 360480 | tf_op jit(solution)/shard_map/ppermute | solution.py:62
  47.6 11.4 %collective-permute-done.3 = bf16[256,1408]{1,0:T(8,128)(2,1)S(1)} collective-permute-done((bf16[256,1408]{1,0:T(8,128)(2,1)S(1)}, bf16[256,1408]{1,0:T(8,128)(2,1)S(1)}, u32[]{:S(2)}, u32[]{:S(2)}) %collective-permute-start.3) | collective-permute-done | bytes 720928 | tf_op jit(solution)/shard_map/ppermute | solution.py:62
  63.6 1.8 collective-permute-start.10
  67.4 2.7 broadcast_select_fusion.1
  74.8 9.4 %collective-permute-start.12 = (bf16[144,512]{1,0:T(8,128)(2,1)S(1)}, bf16[144,512]{1,0:T(8,128)(2,1)S(1)}, u32[]{:S(2)}, u32[]{:S(2)}) collective-permute-start(bf16[144,512]{1,0:T(8,128)(2,1)S(1)} %get-tuple-element.220), channel_id=1, source_target_pairs={{0,8},{1,9},{2,10},{3,11},{4,12},{5,13},{6,14},{7,15},{8,0},{9,1},... | collective-permute-start | bytes 442376 | tf_op jit(solution)/shard_map/ppermute | solution.py:62
  84.1 5.7 %collective-permute-start.15 = (bf16[144,512]{1,0:T(8,128)(2,1)S(1)}, bf16[144,512]{1,0:T(8,128)(2,1)S(1)}, u32[]{:S(2)}, u32[]{:S(2)}) collective-permute-start(bf16[144,512]{1,0:T(8,128)(2,1)S(1)} %get-tuple-element.219), channel_id=1, source_target_pairs={{0,2},{1,3},{2,0},{3,1},{4,6},{5,7},{6,4},{7,5},{8,10},{9,11},{10,... | collective-permute-start | bytes 442376 | tf_op jit(solution)/shard_map/ppermute | solution.py:62
  94.2 9.5 %collective-permute-done.13 = bf16[288,512]{1,0:T(8,128)(2,1)S(1)} collective-permute-done((bf16[288,512]{1,0:T(8,128)(2,1)S(1)}, bf16[288,512]{1,0:T(8,128)(2,1)S(1)}, u32[]{:S(2)}, u32[]{:S(2)}) %collective-permute-start.13) | collective-permute-done | bytes 294944 | tf_op jit(solution)/shard_map/ppermute | solution.py:62
  104.7 4.6 collective-permute-done.16
  111.6 2.0 collective-permute-start.18
  115.2 18.0 %collective-permute-done.17 = bf16[576,512]{1,0:T(8,128)(2,1)} collective-permute-done((bf16[576,512]{1,0:T(8,128)(2,1)}, bf16[576,512]{1,0:T(8,128)(2,1)}, u32[]{:S(2)}, u32[]{:S(2)}) %collective-permute-start.17) | collective-permute-done | bytes 589856 | tf_op jit(solution)/shard_map/ppermute | solution.py:62
  134.3 2.9 pad_maximum_fusion.8
  137.2 5.6 %collective-permute-done.18 = bf16[88,3072]{1,0:T(8,128)(2,1)S(1)} collective-permute-done((bf16[88,3072]{1,0:T(8,128)(2,1)}, bf16[88,3072]{1,0:T(8,128)(2,1)S(1)}, u32[]{:S(2)}, u32[]{:S(2)}) %collective-permute-start.18) | collective-permute-done | bytes 540704 | tf_op jit(solution)/shard_map/ppermute | solution.py:62
  145.3 2.0 pad_maximum_fusion.5
  149.4 2.6 fusion
  154.4 1.8 fusion.66
  156.3 1.8 fusion.1
  158.4 16.6 %collective-permute-done.22 = bf16[176,3072]{1,0:T(8,128)(2,1)} collective-permute-done((bf16[176,3072]{1,0:T(8,128)(2,1)}, bf16[176,3072]{1,0:T(8,128)(2,1)}, u32[]{:S(2)}, u32[]{:S(2)}) %collective-permute-start.22) | collective-permute-done | bytes 1081376 | tf_op jit(solution)/shard_map/ppermute | solution.py:62
  185.1 11.5 %shard_map.289 = bf16[16,72,128]{2,1,0:T(8,128)(2,1)} custom-call(s32[1]{0:T(128)} %bitcast.46.refs_0_, s32[2,3]{1,0:T(2,128)S(1)} %copy-done.4, f32[448,512]{1,0:T(8,128)S(1)} %shard_map.288.refs_2_, bf16[8,2,72,192]{3,2,1,0:T(8,128)(2,1)S(1)} %bitcast.334, bf16[8,2,72,192]{3,2,1,0:T(8,128)(2,1)S(1)} %bitcast.336), custom_call_target="tpu_custom_call" | custom-call | flops 16777216 | bytes 1048576 | tf_op jit(solution)/shard_map/pallas_call | solution.py:516
  196.6 2.0 collective-permute-done.23
  198.6 4.4 all-to-all-start.1
  207.7 6.4 %collective-permute-done.24 = bf16[352,1024]{1,0:T(8,128)(2,1)} collective-permute-done((bf16[352,1024]{1,0:T(8,128)(2,1)}, bf16[352,1024]{1,0:T(8,128)(2,1)}, u32[]{:S(2)}, u32[]{:S(2)}) %collective-permute-start.24) | collective-permute-done | bytes 720928 | tf_op jit(solution)/shard_map/ppermute | solution.py:62
  214.0 2.1 reshape.539
  216.1 2.0 copy.105
  218.1 2.2 reshape.540
  220.3 2.7 multiply_reduce_fusion.4
  225.3 13.3 %collective-permute-done.25 = bf16[144,1024]{1,0:T(8,128)(2,1)S(1)} collective-permute-done((bf16[144,1024]{1,0:T(8,128)(2,1)S(1)}, bf16[144,1024]{1,0:T(8,128)(2,1)S(1)}, u32[]{:S(2)}, u32[]{:S(2)}) %collective-permute-start.25) | collective-permute-done | bytes 294944 | tf_op jit(solution)/shard_map/ppermute | solution.py:62
  239.5 2.0 fusion.101
  246.2 1.9 fusion.90
  248.1 2.6 multiply_convert_fusion.1
  250.7 2.0 fusion.102
  252.7 2.0 add_add_fusion
  262.5 10.3 %collective-permute-done.30 = bf16[144,1024]{1,0:T(8,128)(2,1)S(1)} collective-permute-done((bf16[144,1024]{1,0:T(8,128)(2,1)S(1)}, bf16[144,1024]{1,0:T(8,128)(2,1)S(1)}, u32[]{:S(2)}, u32[]{:S(2)}) %collective-permute-start.30) | collective-permute-done | bytes 294944 | tf_op jit(solution)/shard_map/ppermute | solution.py:62
  276.9 2.3 fusion.103
  281.2 3.9 all-to-all-start.2
  285.1 2.9 convolution_add_fusion.2
  290.3 2.1 convolution_convert_fusion.3
  297.8 14.9 %shard_map.290 = (bf16[8,2,72,192]{3,2,1,0:T(8,128)(2,1)S(1)}, bf16[8,2,72,192]{3,2,1,0:T(8,128)(2,1)S(1)}, f32[448,512]{1,0:T(8,128)S(1)}) custom-call(s32[1]{0:T(128)} %bitcast.46.refs_0_, s32[2,3]{1,0:T(2,128)S(1)} %copy-done.4, f32[448,512]{1,0:T(8,128)S(1)} %shard_map.288.refs_2_, bf16[8,2,72,192]{3,2,1,0:T(8,128)(2,1)S(1)} %bitcast.335, ...), custom_call_target="tpu_custom_call" | custom-call | flops 16777216 | bytes 1048576 | tf_op jit(solution)/shard_map/pallas_call | solution.py:591
  326.2 2.4 convert_add_fusion
  329.4 10.7 %collective-permute-done.38 = bf16[576,512]{1,0:T(8,128)(2,1)S(1)} collective-permute-done((bf16[576,512]{1,0:T(8,128)(2,1)S(1)}, bf16[576,512]{1,0:T(8,128)(2,1)S(1)}, u32[]{:S(2)}, u32[]{:S(2)}) %collective-permute-start.38) | collective-permute-done | bytes 589856 | tf_op jit(solution)/shard_map/ppermute | solution.py:62
  340.3 2.4 collective-permute-start.39
  351.0 4.8 %collective-permute-done.39 = bf16[288,512]{1,0:T(8,128)(2,1)S(1)} collective-permute-done((bf16[288,512]{1,0:T(8,128)(2,1)S(1)}, bf16[288,512]{1,0:T(8,128)(2,1)S(1)}, u32[]{:S(2)}, u32[]{:S(2)}) %collective-permute-start.39) | collective-permute-done | bytes 294944 | tf_op jit(solution)/shard_map/ppermute | solution.py:62
  356.4 5.7 %collective-permute-done.34 = bf16[288,512]{1,0:T(8,128)(2,1)S(1)} collective-permute-done((bf16[288,512]{1,0:T(8,128)(2,1)S(1)}, bf16[288,512]{1,0:T(8,128)(2,1)S(1)}, u32[]{:S(2)}, u32[]{:S(2)}) %collective-permute-start.34) | collective-permute-done | bytes 294944 | tf_op jit(solution)/shard_map/ppermute | solution.py:62
  366.2 5.8 %collective-permute-done.36 = bf16[144,512]{1,0:T(8,128)(2,1)S(1)} collective-permute-done((bf16[144,512]{1,0:T(8,128)(2,1)S(1)}, bf16[144,512]{1,0:T(8,128)(2,1)S(1)}, u32[]{:S(2)}, u32[]{:S(2)}) %collective-permute-start.36) | collective-permute-done | bytes 147488 | tf_op jit(solution)/shard_map/ppermute | solution.py:62
  375.3 1.9 pad_maximum_fusion.2
  377.3 2.6 convolution_convert_fusion
  379.9 2.9 copy.110
  382.8 3.3 constant_dynamic-slice_fusion.3
  390.9 2.2 collective-permute-start.45
  393.1 3.0 collective-permute-start.48
  396.9 6.8 %collective-permute-done.42 = bf16[144,1024]{1,0:T(8,128)(2,1)S(1)} collective-permute-done((bf16[144,1024]{1,0:T(8,128)(2,1)S(1)}, bf16[144,1024]{1,0:T(8,128)(2,1)S(1)}, u32[]{:S(2)}, u32[]{:S(2)}) %collective-permute-start.42) | collective-permute-done | bytes 294944 | tf_op jit(solution)/shard_map/ppermute | solution.py:62
  405.9 2.1 collective-permute-start.52
  408.5 16.9 %collective-permute-done.52 = bf16[256,1408]{1,0:T(8,128)(2,1)S(1)} collective-permute-done((bf16[256,1408]{1,0:T(8,128)(2,1)S(1)}, bf16[256,1408]{1,0:T(8,128)(2,1)S(1)}, u32[]{:S(2)}, u32[]{:S(2)}) %collective-permute-start.52) | collective-permute-done | bytes 720928 | tf_op jit(solution)/shard_map/ppermute | solution.py:62
  433.5 5.3 %all-to-all-start.3 = ((f32[32,32,88]{2,1,0:T(8,128)}), f32[32,32,88]{2,1,0:T(8,128)S(1)}, u32[]{:S(2)}, u32[]{:S(2)}) async-start(f32[32,32,88]{2,1,0:T(8,128)} %bitcast.134), calls=%async_computation.3 | async-start | bytes 1048576 | tf_op jit(solution)/shard_map/all_to_all | solution.py:729
  438.9 1.8 collective-permute-start.54
  440.9 5.1 %collective-permute-start.47 = (bf16[64,1408]{1,0:T(8,128)(2,1)S(1)}, bf16[64,1408]{1,0:T(8,128)(2,1)S(1)}, u32[]{:S(2)}, u32[]{:S(2)}) collective-permute-start(bf16[64,1408]{1,0:T(8,128)(2,1)S(1)} %bitcast.466), channel_id=1, source_target_pairs={{0,4},{1,5},{2,6},{3,7},{4,0},{5,1},{6,2},{7,3},{8,12},{9,13},{10,... | collective-permute-start | bytes 540680 | tf_op jit(solution)/shard_map/ppermute | solution.py:62
  446.0 8.3 %collective-permute-done.54 = bf16[64,1408]{1,0:T(8,128)(2,1)S(1)} collective-permute-done((bf16[64,1408]{1,0:T(8,128)(2,1)S(1)}, bf16[64,1408]{1,0:T(8,128)(2,1)S(1)}, u32[]{:S(2)}, u32[]{:S(2)}) %collective-permute-start.54) | collective-permute-done | bytes 180256 | tf_op jit(solution)/shard_map/ppermute | solution.py:62
  454.4 2.5 collective-permute-start.55
  458.8 2.0 collective-permute-start.50
  (443 shorter events, 142.4 us)
Async XLA Ops:
  4.7 10.3 %collective-permute-start = (bf16[32,1408]{1,0:T(8,128)(2,1)S(1)}, bf16[32,1408]{1,0:T(8,128)(2,1)S(1)}, u32[]{:S(2)}, u32[]{:S(2)}) collective-permute-start(bf16[32,1408]{1,0:T(8,128)(2,1)S(1)} %slice.298), channel_id=1, source_target_pairs={{0,8},{1,9},{2,10},{3,11},{4,12},{5,13},{6,14},{7,15},{8,0},{9,1},... | collective-permute-start | bytes 270344 | tf_op jit(solution)/shard_map/ppermute | solution.py:62
  11.1 18.9 %all-to-all-start = ((bf16[32,32,88]{2,1,0:T(8,128)(2,1)}), bf16[32,32,88]{2,1,0:T(8,128)(2,1)S(1)}, u32[]{:S(2)}, u32[]{:S(2)}) async-start(bf16[32,32,88]{2,1,0:T(8,128)(2,1)} %bitcast.324), calls=%async_computation | async-start | bytes 524288 | tf_op jit(solution)/shard_map/all_to_all | solution.py:411
  15.0 13.2 %collective-permute-start.5 = (bf16[32,1408]{1,0:T(8,128)(2,1)S(1)}, bf16[32,1408]{1,0:T(8,128)(2,1)S(1)}, u32[]{:S(2)}, u32[]{:S(2)}) collective-permute-start(bf16[32,1408]{1,0:T(8,128)(2,1)S(1)} %get-tuple-element.227), channel_id=1, source_target_pairs={{0,8},{1,9},{2,10},{3,11},{4,12},{5,13},{6,14},{7,15},{8,0},{9,1},... | collective-permute-start | bytes 270344 | tf_op jit(solution)/shard_map/ppermute | solution.py:62
  17.8 10.6 %collective-permute-start.1 = (bf16[64,1408]{1,0:T(8,128)(2,1)S(1)}, bf16[64,1408]{1,0:T(8,128)(2,1)S(1)}, u32[]{:S(2)}, u32[]{:S(2)}) collective-permute-start(bf16[64,1408]{1,0:T(8,128)(2,1)S(1)} %bitcast.451), channel_id=1, source_target_pairs={{0,4},{1,5},{2,6},{3,7},{4,0},{5,1},{6,2},{7,3},{8,12},{9,13},{10,... | collective-permute-start | bytes 540680 | tf_op jit(solution)/shard_map/ppermute | solution.py:62
  28.2 6.2 %collective-permute-start.6 = (bf16[64,1408]{1,0:T(8,128)(2,1)S(1)}, bf16[64,1408]{1,0:T(8,128)(2,1)S(1)}, u32[]{:S(2)}, u32[]{:S(2)}) collective-permute-start(bf16[64,1408]{1,0:T(8,128)(2,1)S(1)} %bitcast.450), channel_id=1, source_target_pairs={{0,4},{1,5},{2,6},{3,7},{4,0},{5,1},{6,2},{7,3},{8,12},{9,13},{10,... | collective-permute-start | bytes 540680 | tf_op jit(solution)/shard_map/ppermute | solution.py:62
  28.4 10.0 %collective-permute-start.2 = (bf16[128,1408]{1,0:T(8,128)(2,1)S(1)}, bf16[128,1408]{1,0:T(8,128)(2,1)S(1)}, u32[]{:S(2)}, u32[]{:S(2)}) collective-permute-start(bf16[128,1408]{1,0:T(8,128)(2,1)S(1)} %bitcast.437), channel_id=1, source_target_pairs={{0,16},{16,0},{1,17},{17,1},{2,18},{18,2},{3,19},{19,3},{4,20},{20... | collective-permute-start | bytes 1081352 | tf_op jit(solution)/shard_map/ppermute | solution.py:62
  30.0 80.2 %copy-start.40 = (bf16[32,32,88]{2,1,0:T(8,128)(2,1)}, bf16[32,32,88]{2,1,0:T(8,128)(2,1)S(1)}, u32[]{:S(2)}) copy-start(bf16[32,32,88]{2,1,0:T(8,128)(2,1)S(1)} %all-to-all-done) | copy-start | bytes 540676
  34.5 11.4 %collective-permute-start.7 = (bf16[128,1408]{1,0:T(8,128)(2,1)S(1)}, bf16[128,1408]{1,0:T(8,128)(2,1)S(1)}, u32[]{:S(2)}, u32[]{:S(2)}) collective-permute-start(bf16[128,1408]{1,0:T(8,128)(2,1)S(1)} %bitcast.439), channel_id=1, source_target_pairs={{0,2},{1,3},{2,0},{3,1},{4,6},{5,7},{6,4},{7,5},{8,10},{9,11},{10,... | collective-permute-start | bytes 1081352 | tf_op jit(solution)/shard_map/ppermute | solution.py:62
  38.6 20.5 %collective-permute-start.3 = (bf16[256,1408]{1,0:T(8,128)(2,1)S(1)}, bf16[256,1408]{1,0:T(8,128)(2,1)S(1)}, u32[]{:S(2)}, u32[]{:S(2)}) collective-permute-start(bf16[256,1408]{1,0:T(8,128)(2,1)S(1)} %bitcast.405), channel_id=1, source_target_pairs={{0,2},{1,3},{2,0},{3,1},{4,6},{5,7},{6,4},{7,5},{8,10},{9,11},{10,... | collective-permute-start | bytes 2162696 | tf_op jit(solution)/shard_map/ppermute | solution.py:62
  46.1 13.6 %collective-permute-start.8 = (bf16[256,1408]{1,0:T(8,128)(2,1)S(1)}, bf16[256,1408]{1,0:T(8,128)(2,1)S(1)}, u32[]{:S(2)}, u32[]{:S(2)}) collective-permute-start(bf16[256,1408]{1,0:T(8,128)(2,1)S(1)} %bitcast.404), channel_id=1, source_target_pairs={{0,16},{16,0},{1,17},{17,1},{2,18},{18,2},{3,19},{19,3},{4,20},{20... | collective-permute-start | bytes 2162696 | tf_op jit(solution)/shard_map/ppermute | solution.py:62
  59.6 5.8 %collective-permute-start.4 = (bf16[512,1408]{1,0:T(8,128)(2,1)S(1)}, bf16[512,1408]{1,0:T(8,128)(2,1)}, u32[]{:S(2)}, u32[]{:S(2)}) collective-permute-start(bf16[512,1408]{1,0:T(8,128)(2,1)S(1)} %bitcast.372), channel_id=1, source_target_pairs={{0,1},{1,0},{2,3},{3,2},{4,5},{5,4},{6,7},{7,6},{8,9},{9,8},{10,11... | collective-permute-start | bytes 4325384 | tf_op jit(solution)/shard_map/ppermute | solution.py:62
  60.1 7.2 %collective-permute-start.9 = (bf16[512,1408]{1,0:T(8,128)(2,1)S(1)}, bf16[512,1408]{1,0:T(8,128)(2,1)}, u32[]{:S(2)}, u32[]{:S(2)}) collective-permute-start(bf16[512,1408]{1,0:T(8,128)(2,1)S(1)} %bitcast.374), channel_id=1, source_target_pairs={{0,1},{1,0},{2,3},{3,2},{4,5},{5,4},{6,7},{7,6},{8,9},{9,8},{10,11... | collective-permute-start | bytes 4325384 | tf_op jit(solution)/shard_map/ppermute | solution.py:62
  62.0 12.7 %collective-permute-start.11 = (bf16[96,1024]{1,0:T(8,128)(2,1)S(1)}, bf16[96,1024]{1,0:T(8,128)(2,1)S(1)}, u32[]{:S(2)}, u32[]{:S(2)}) collective-permute-start(bf16[96,1024]{1,0:T(8,128)(2,1)S(1)} %pad_maximum_fusion.32), channel_id=1, source_target_pairs={{0,16},{1,0},{2,17},{3,1},{4,18},{5,2},{6,19},{7,3},{8,20},{9,4},{... | collective-permute-start | bytes 589832 | tf_op jit(solution)/shard_map/ppermute | solution.py:426
  63.6 11.2 %collective-permute-start.10 = (bf16[96,1024]{1,0:T(8,128)(2,1)S(1)}, bf16[96,1024]{1,0:T(8,128)(2,1)}, u32[]{:S(2)}, u32[]{:S(2)}) collective-permute-start(bf16[96,1024]{1,0:T(8,128)(2,1)S(1)} %pad_maximum_fusion.32), channel_id=1, source_target_pairs={{0,0},{1,16},{2,1},{3,17},{4,2},{5,18},{6,3},{7,19},{8,4},{9,20},{... | collective-permute-start | bytes 589832 | tf_op jit(solution)/shard_map/ppermute | solution.py:426
  74.8 15.1 %collective-permute-start.12 = (bf16[144,512]{1,0:T(8,128)(2,1)S(1)}, bf16[144,512]{1,0:T(8,128)(2,1)S(1)}, u32[]{:S(2)}, u32[]{:S(2)}) collective-permute-start(bf16[144,512]{1,0:T(8,128)(2,1)S(1)} %get-tuple-element.220), channel_id=1, source_target_pairs={{0,8},{1,9},{2,10},{3,11},{4,12},{5,13},{6,14},{7,15},{8,0},{9,1},... | collective-permute-start | bytes 442376 | tf_op jit(solution)/shard_map/ppermute | solution.py:62
  84.1 8.8 %collective-permute-start.15 = (bf16[144,512]{1,0:T(8,128)(2,1)S(1)}, bf16[144,512]{1,0:T(8,128)(2,1)S(1)}, u32[]{:S(2)}, u32[]{:S(2)}) collective-permute-start(bf16[144,512]{1,0:T(8,128)(2,1)S(1)} %get-tuple-element.219), channel_id=1, source_target_pairs={{0,2},{1,3},{2,0},{3,1},{4,6},{5,7},{6,4},{7,5},{8,10},{9,11},{10,... | collective-permute-start | bytes 442376 | tf_op jit(solution)/shard_map/ppermute | solution.py:62
  89.9 13.8 %collective-permute-start.13 = (bf16[288,512]{1,0:T(8,128)(2,1)S(1)}, bf16[288,512]{1,0:T(8,128)(2,1)S(1)}, u32[]{:S(2)}, u32[]{:S(2)}) collective-permute-start(bf16[288,512]{1,0:T(8,128)(2,1)S(1)} %bitcast.460), channel_id=1, source_target_pairs={{0,4},{1,5},{2,6},{3,7},{4,0},{5,1},{6,2},{7,3},{8,12},{9,13},{10,... | collective-permute-start | bytes 884744 | tf_op jit(solution)/shard_map/ppermute | solution.py:62
  93.0 16.3 %collective-permute-start.16 = (bf16[288,512]{1,0:T(8,128)(2,1)S(1)}, bf16[288,512]{1,0:T(8,128)(2,1)S(1)}, u32[]{:S(2)}, u32[]{:S(2)}) collective-permute-start(bf16[288,512]{1,0:T(8,128)(2,1)S(1)} %bitcast.442), channel_id=1, source_target_pairs={{0,8},{1,9},{2,10},{3,11},{4,12},{5,13},{6,14},{7,15},{8,0},{9,1},... | collective-permute-start | bytes 884744 | tf_op jit(solution)/shard_map/ppermute | solution.py:62
  110.2 22.9 %collective-permute-start.17 = (bf16[576,512]{1,0:T(8,128)(2,1)}, bf16[576,512]{1,0:T(8,128)(2,1)}, u32[]{:S(2)}, u32[]{:S(2)}) collective-permute-start(bf16[576,512]{1,0:T(8,128)(2,1)} %bitcast.67), channel_id=1, source_target_pairs={{0,4},{1,5},{2,6},{3,7},{4,0},{5,1},{6,2},{7,3},{8,12},{9,13},{10,... | collective-permute-start | bytes 1769480 | tf_op jit(solution)/shard_map/ppermute | solution.py:62
  110.2 24.1 %collective-permute-start.14 = (bf16[576,512]{1,0:T(8,128)(2,1)}, bf16[576,512]{1,0:T(8,128)(2,1)}, u32[]{:S(2)}, u32[]{:S(2)}) collective-permute-start(bf16[576,512]{1,0:T(8,128)(2,1)} %bitcast.54), channel_id=1, source_target_pairs={{0,2},{1,3},{2,0},{3,1},{4,6},{5,7},{6,4},{7,5},{8,10},{9,11},{10,... | collective-permute-start | bytes 1769480 | tf_op jit(solution)/shard_map/ppermute | solution.py:62
  111.6 31.2 %collective-permute-start.18 = (bf16[88,3072]{1,0:T(8,128)(2,1)}, bf16[88,3072]{1,0:T(8,128)(2,1)S(1)}, u32[]{:S(2)}, u32[]{:S(2)}) collective-permute-start(bf16[88,3072]{1,0:T(8,128)(2,1)} %copy.96), channel_id=1, source_target_pairs={{0,4},{1,5},{2,6},{3,7},{4,0},{5,1},{6,2},{7,3},{8,12},{9,13},{10,... | collective-permute-start | bytes 1622024 | tf_op jit(solution)/shard_map/ppermute | solution.py:62
  114.8 28.0 %collective-permute-start.19 = (bf16[144,1024]{1,0:T(8,128)(2,1)S(1)}, bf16[144,1024]{1,0:T(8,128)(2,1)S(1)}, u32[]{:S(2)}, u32[]{:S(2)}) collective-permute-start(bf16[144,1024]{1,0:T(8,128)(2,1)S(1)} %bitcast.382), channel_id=1, source_target_pairs={{0,8},{1,9},{2,10},{3,11},{4,12},{5,13},{6,14},{7,15},{8,0},{9,1},... | collective-permute-start | bytes 884744 | tf_op jit(solution)/shard_map/ppermute | solution.py:62
  115.2 34.3 %copy-start.9 = (bf16[3,2,32,1024]{3,2,1,0:T(8,128)(2,1)}, bf16[3,2,32,1024]{3,2,1,0:T(8,128)(2,1)S(1)}, u32[]{:S(2)}) copy-start(bf16[3,2,32,1024]{3,2,1,0:T(8,128)(2,1)S(1)} %pad_maximum_fusion.24) | copy-start | bytes 1179652
  144.8 11.5 %collective-permute-start.20 = (bf16[1152,512]{1,0:T(8,128)(2,1)}, bf16[1152,512]{1,0:T(8,128)(2,1)}, u32[]{:S(2)}, u32[]{:S(2)}) collective-permute-start(bf16[1152,512]{1,0:T(8,128)(2,1)} %bitcast.60), channel_id=1, source_target_pairs={{0,1},{1,0},{2,3},{3,2},{4,5},{5,4},{6,7},{7,6},{8,9},{9,8},{10,11... | collective-permute-start | bytes 3538952 | tf_op jit(solution)/shard_map/ppermute | solution.py:62
  144.8 9.7 %collective-permute-start.21 = (bf16[1152,512]{1,0:T(8,128)(2,1)S(1)}, bf16[1152,512]{1,0:T(8,128)(2,1)}, u32[]{:S(2)}, u32[]{:S(2)}) collective-permute-start(bf16[1152,512]{1,0:T(8,128)(2,1)S(1)} %bitcast.343), channel_id=1, source_target_pairs={{0,1},{1,0},{2,3},{3,2},{4,5},{5,4},{6,7},{7,6},{8,9},{9,8},{10,11... | collective-permute-start | bytes 3538952 | tf_op jit(solution)/shard_map/ppermute | solution.py:62
  148.9 26.1 %collective-permute-start.22 = (bf16[176,3072]{1,0:T(8,128)(2,1)}, bf16[176,3072]{1,0:T(8,128)(2,1)}, u32[]{:S(2)}, u32[]{:S(2)}) collective-permute-start(bf16[176,3072]{1,0:T(8,128)(2,1)} %copy.100), channel_id=1, source_target_pairs={{0,2},{1,3},{2,0},{3,1},{4,6},{5,7},{6,4},{7,5},{8,10},{9,11},{10,... | collective-permute-start | bytes 3244040 | tf_op jit(solution)/shard_map/ppermute | solution.py:62
  179.2 19.4 %collective-permute-start.23 = (bf16[352,1024]{1,0:T(8,128)(2,1)}, bf16[352,1024]{1,0:T(8,128)(2,1)}, u32[]{:S(2)}, u32[]{:S(2)}) collective-permute-start(bf16[352,1024]{1,0:T(8,128)(2,1)} %copy.102), channel_id=1, source_target_pairs={{0,16},{16,0},{1,17},{17,1},{2,18},{18,2},{3,19},{19,3},{4,20},{20... | collective-permute-start | bytes 2162696 | tf_op jit(solution)/shard_map/ppermute | solution.py:62
  182.8 31.3 %collective-permute-start.24 = (bf16[352,1024]{1,0:T(8,128)(2,1)}, bf16[352,1024]{1,0:T(8,128)(2,1)}, u32[]{:S(2)}, u32[]{:S(2)}) collective-permute-start(bf16[352,1024]{1,0:T(8,128)(2,1)} %copy.104), channel_id=1, source_target_pairs={{0,16},{16,0},{1,17},{17,1},{2,18},{18,2},{3,19},{19,3},{4,20},{20... | collective-permute-start | bytes 2162696 | tf_op jit(solution)/shard_map/ppermute | solution.py:62
  198.6 15.5 %all-to-all-start.1 = ((bf16[16,72,128]{2,1,0:T(8,128)(2,1)}), bf16[16,72,128]{2,1,0:T(8,128)(2,1)}, u32[]{:S(2)}, u32[]{:S(2)}) async-start(bf16[16,72,128]{2,1,0:T(8,128)(2,1)} %shard_map.289), calls=%async_computation.1 | async-start | bytes 589824 | tf_op jit(solution)/shard_map/all_to_all | solution.py:531
  203.8 20.4 %collective-permute-start.27 = (bf16[288,1024]{1,0:T(8,128)(2,1)}, bf16[288,1024]{1,0:T(8,128)(2,1)}, u32[]{:S(2)}, u32[]{:S(2)}) collective-permute-start(bf16[288,1024]{1,0:T(8,128)(2,1)} %pad_maximum_fusion.22), channel_id=1, source_target_pairs={{0,1},{1,0},{2,3},{3,2},{4,5},{5,4},{6,7},{7,6},{8,9},{9,8},{10,11... | collective-permute-start | bytes 1769480 | tf_op jit(solution)/shard_map/ppermute | solution.py:62
  206.6 32.9 %collective-permute-start.28 = (bf16[352,1024]{1,0:T(8,128)(2,1)}, bf16[352,1024]{1,0:T(8,128)(2,1)}, u32[]{:S(2)}, u32[]{:S(2)}) collective-permute-start(bf16[352,1024]{1,0:T(8,128)(2,1)} %copy.107), channel_id=1, source_target_pairs={{0,16},{16,0},{1,17},{17,1},{2,18},{18,2},{3,19},{19,3},{4,20},{20... | collective-permute-start | bytes 2162696 | tf_op jit(solution)/shard_map/ppermute | solution.py:62
  223.0 49.9 %copy-start.13 = (f32[144,1024]{1,0:T(8,128)}, f32[144,1024]{1,0:T(8,128)S(1)}, u32[]{:S(2)}) copy-start(f32[144,1024]{1,0:T(8,128)S(1)} %get-tuple-element.234) | copy-start | bytes 1769476
  223.2 35.7 %copy-start.56 = (bf16[144,1024]{1,0:T(8,128)(2,1)}, bf16[144,1024]{1,0:T(8,128)(2,1)S(1)}, u32[]{:S(2)}) copy-start(bf16[144,1024]{1,0:T(8,128)(2,1)S(1)} %multiply_convert_fusion.4) | copy-start | bytes 884740
  223.2 15.4 %collective-permute-start.25 = (bf16[144,1024]{1,0:T(8,128)(2,1)S(1)}, bf16[144,1024]{1,0:T(8,128)(2,1)S(1)}, u32[]{:S(2)}, u32[]{:S(2)}) collective-permute-start(bf16[144,1024]{1,0:T(8,128)(2,1)S(1)} %multiply_convert_fusion.4), channel_id=1, source_target_pairs={{0,8},{1,9},{2,10},{3,11},{4,12},{5,13},{6,14},{7,15},{8,0},{9,1},... | collective-permute-start | bytes 884744 | tf_op jit(solution)/shard_map/ppermute | solution.py:62
  238.7 2.9 collective-permute-start.26
  254.8 2.2 collective-permute-start.29
  257.3 15.5 %collective-permute-start.30 = (bf16[144,1024]{1,0:T(8,128)(2,1)S(1)}, bf16[144,1024]{1,0:T(8,128)(2,1)S(1)}, u32[]{:S(2)}, u32[]{:S(2)}) collective-permute-start(bf16[144,1024]{1,0:T(8,128)(2,1)S(1)} %fusion.49), channel_id=1, source_target_pairs={{0,8},{1,9},{2,10},{3,11},{4,12},{5,13},{6,14},{7,15},{8,0},{9,1},... | collective-permute-start | bytes 884744 | tf_op jit(solution)/shard_map/ppermute | solution.py:62
  261.4 64.8 %collective-permute-start.32 = (bf16[352,3072]{1,0:T(8,128)(2,1)}, bf16[352,3072]{1,0:T(8,128)(2,1)}, u32[]{:S(2)}, u32[]{:S(2)}) collective-permute-start(bf16[352,3072]{1,0:T(8,128)(2,1)} %pad_maximum_fusion.3), channel_id=1, source_target_pairs={{0,16},{16,0},{1,17},{17,1},{2,18},{18,2},{3,19},{19,3},{4,20},{20... | collective-permute-start | bytes 6488072 | tf_op jit(solution)/shard_map/ppermute | solution.py:62
  281.2 14.9 %all-to-all-start.2 = ((bf16[16,72,128]{2,1,0:T(8,128)(2,1)}), bf16[16,72,128]{2,1,0:T(8,128)(2,1)S(1)}, u32[]{:S(2)}, u32[]{:S(2)}) async-start(bf16[16,72,128]{2,1,0:T(8,128)(2,1)} %reshape.545), calls=%async_computation.2 | async-start | bytes 589824 | tf_op jit(solution)/shard_map/all_to_all | solution.py:579
  315.7 3.4 collective-permute-start.31
  316.1 5.0 %collective-permute-start.37 = (bf16[1152,512]{1,0:T(8,128)(2,1)}, bf16[1152,512]{1,0:T(8,128)(2,1)}, u32[]{:S(2)}, u32[]{:S(2)}) collective-permute-start(bf16[1152,512]{1,0:T(8,128)(2,1)} %convolution_convert_fusion.1), channel_id=1, source_target_pairs={{0,1},{1,0},{2,3},{3,2},{4,5},{5,4},{6,7},{7,6},{8,9},{9,8},{10,11... | collective-permute-start | bytes 3538952 | tf_op jit(solution)/shard_map/ppermute | solution.py:62
  318.7 67.3 %collective-permute-start.41 = (bf16[288,1024]{1,0:T(8,128)(2,1)}, bf16[288,1024]{1,0:T(8,128)(2,1)}, u32[]{:S(2)}, u32[]{:S(2)}) collective-permute-start(bf16[288,1024]{1,0:T(8,128)(2,1)} %fusion.36), channel_id=1, source_target_pairs={{0,1},{1,0},{2,3},{3,2},{4,5},{5,4},{6,7},{7,6},{8,9},{9,8},{10,11... | collective-permute-start | bytes 1769480 | tf_op jit(solution)/shard_map/ppermute | solution.py:62
  323.0 19.7 %collective-permute-start.33 = (bf16[576,512]{1,0:T(8,128)(2,1)S(1)}, bf16[576,512]{1,0:T(8,128)(2,1)S(1)}, u32[]{:S(2)}, u32[]{:S(2)}) collective-permute-start(bf16[576,512]{1,0:T(8,128)(2,1)S(1)} %bitcast.458), channel_id=1, source_target_pairs={{0,2},{1,3},{2,0},{3,1},{4,6},{5,7},{6,4},{7,5},{8,10},{9,11},{10,... | collective-permute-start | bytes 1769480 | tf_op jit(solution)/shard_map/ppermute | solution.py:62
  324.8 15.3 %collective-permute-start.38 = (bf16[576,512]{1,0:T(8,128)(2,1)S(1)}, bf16[576,512]{1,0:T(8,128)(2,1)S(1)}, u32[]{:S(2)}, u32[]{:S(2)}) collective-permute-start(bf16[576,512]{1,0:T(8,128)(2,1)S(1)} %bitcast.459), channel_id=1, source_target_pairs={{0,4},{1,5},{2,6},{3,7},{4,0},{5,1},{6,2},{7,3},{8,12},{9,13},{10,... | collective-permute-start | bytes 1769480 | tf_op jit(solution)/shard_map/ppermute | solution.py:62
  328.8 36.2 %collective-permute-start.35 = (bf16[176,3072]{1,0:T(8,128)(2,1)S(1)}, bf16[176,3072]{1,0:T(8,128)(2,1)S(1)}, u32[]{:S(2)}, u32[]{:S(2)}) collective-permute-start(bf16[176,3072]{1,0:T(8,128)(2,1)S(1)} %slice.470), channel_id=1, source_target_pairs={{0,2},{1,3},{2,0},{3,1},{4,6},{5,7},{6,4},{7,5},{8,10},{9,11},{10,... | collective-permute-start | bytes 3244040 | tf_op jit(solution)/shard_map/ppermute | solution.py:62
  340.3 15.5 %collective-permute-start.39 = (bf16[288,512]{1,0:T(8,128)(2,1)S(1)}, bf16[288,512]{1,0:T(8,128)(2,1)S(1)}, u32[]{:S(2)}, u32[]{:S(2)}) collective-permute-start(bf16[288,512]{1,0:T(8,128)(2,1)S(1)} %fusion.50), channel_id=1, source_target_pairs={{0,8},{1,9},{2,10},{3,11},{4,12},{5,13},{6,14},{7,15},{8,0},{9,1},... | collective-permute-start | bytes 884744 | tf_op jit(solution)/shard_map/ppermute | solution.py:62
  349.6 12.5 %collective-permute-start.34 = (bf16[288,512]{1,0:T(8,128)(2,1)S(1)}, bf16[288,512]{1,0:T(8,128)(2,1)S(1)}, u32[]{:S(2)}, u32[]{:S(2)}) collective-permute-start(bf16[288,512]{1,0:T(8,128)(2,1)S(1)} %bitcast.462), channel_id=1, source_target_pairs={{0,4},{1,5},{2,6},{3,7},{4,0},{5,1},{6,2},{7,3},{8,12},{9,13},{10,... | collective-permute-start | bytes 884744 | tf_op jit(solution)/shard_map/ppermute | solution.py:62
  355.9 9.0 %collective-permute-start.40 = (bf16[144,512]{1,0:T(8,128)(2,1)S(1)}, bf16[144,512]{1,0:T(8,128)(2,1)S(1)}, u32[]{:S(2)}, u32[]{:S(2)}) collective-permute-start(bf16[144,512]{1,0:T(8,128)(2,1)S(1)} %fusion.62), channel_id=1, source_target_pairs={{0,2},{1,3},{2,0},{3,1},{4,6},{5,7},{6,4},{7,5},{8,10},{9,11},{10,... | collective-permute-start | bytes 442376 | tf_op jit(solution)/shard_map/ppermute | solution.py:62
  362.1 9.9 %collective-permute-start.36 = (bf16[144,512]{1,0:T(8,128)(2,1)S(1)}, bf16[144,512]{1,0:T(8,128)(2,1)S(1)}, u32[]{:S(2)}, u32[]{:S(2)}) collective-permute-start(bf16[144,512]{1,0:T(8,128)(2,1)S(1)} %fusion.61), channel_id=1, source_target_pairs={{0,8},{1,9},{2,10},{3,11},{4,12},{5,13},{6,14},{7,15},{8,0},{9,1},... | collective-permute-start | bytes 442376 | tf_op jit(solution)/shard_map/ppermute | solution.py:62
  386.1 19.3 %collective-permute-start.51 = (bf16[512,1408]{1,0:T(8,128)(2,1)S(1)}, bf16[512,1408]{1,0:T(8,128)(2,1)S(1)}, u32[]{:S(2)}, u32[]{:S(2)}) collective-permute-start(bf16[512,1408]{1,0:T(8,128)(2,1)S(1)} %bitcast.436), channel_id=1, source_target_pairs={{0,1},{1,0},{2,3},{3,2},{4,5},{5,4},{6,7},{7,6},{8,9},{9,8},{10,11... | collective-permute-start | bytes 4325384 | tf_op jit(solution)/shard_map/ppermute | solution.py:62
  387.6 16.1 %collective-permute-start.42 = (bf16[144,1024]{1,0:T(8,128)(2,1)S(1)}, bf16[144,1024]{1,0:T(8,128)(2,1)S(1)}, u32[]{:S(2)}, u32[]{:S(2)}) collective-permute-start(bf16[144,1024]{1,0:T(8,128)(2,1)S(1)} %fusion.51), channel_id=1, source_target_pairs={{0,8},{1,9},{2,10},{3,11},{4,12},{5,13},{6,14},{7,15},{8,0},{9,1},... | collective-permute-start | bytes 884744 | tf_op jit(solution)/shard_map/ppermute | solution.py:62
  387.7 20.2 %collective-permute-start.43 = (bf16[512,1408]{1,0:T(8,128)(2,1)S(1)}, bf16[512,1408]{1,0:T(8,128)(2,1)S(1)}, u32[]{:S(2)}, u32[]{:S(2)}) collective-permute-start(bf16[512,1408]{1,0:T(8,128)(2,1)S(1)} %bitcast.435), channel_id=1, source_target_pairs={{0,1},{1,0},{2,3},{3,2},{4,5},{5,4},{6,7},{7,6},{8,9},{9,8},{10,11... | collective-permute-start | bytes 4325384 | tf_op jit(solution)/shard_map/ppermute | solution.py:62
  390.9 36.6 %collective-permute-start.45 = (bf16[88,3072]{1,0:T(8,128)(2,1)S(1)}, bf16[88,3072]{1,0:T(8,128)(2,1)S(1)}, u32[]{:S(2)}, u32[]{:S(2)}) collective-permute-start(bf16[88,3072]{1,0:T(8,128)(2,1)S(1)} %copy-done.59), channel_id=1, source_target_pairs={{0,4},{1,5},{2,6},{3,7},{4,0},{5,1},{6,2},{7,3},{8,12},{9,13},{10,... | collective-permute-start | bytes 1622024 | tf_op jit(solution)/shard_map/ppermute | solution.py:62
  393.1 65.7 %collective-permute-start.48 = (bf16[96,1024]{1,0:T(8,128)(2,1)}, bf16[96,1024]{1,0:T(8,128)(2,1)}, u32[]{:S(2)}, u32[]{:S(2)}) collective-permute-start(bf16[96,1024]{1,0:T(8,128)(2,1)} %bitcast.101), channel_id=1, source_target_pairs={{0,0},{16,1},{1,2},{17,3},{2,4},{18,5},{3,6},{19,7},{4,8},{20,9},{... | collective-permute-start | bytes 589832 | tf_op jit(solution)/shard_map/ppermute | solution.py:715
  403.8 55.0 %collective-permute-start.49 = (bf16[96,1024]{1,0:T(8,128)(2,1)}, bf16[96,1024]{1,0:T(8,128)(2,1)}, u32[]{:S(2)}, u32[]{:S(2)}) collective-permute-start(bf16[96,1024]{1,0:T(8,128)(2,1)} %bitcast.102), channel_id=1, source_target_pairs={{16,0},{0,1},{17,2},{1,3},{18,4},{2,5},{19,6},{3,7},{20,8},{4,9},{... | collective-permute-start | bytes 589832 | tf_op jit(solution)/shard_map/ppermute | solution.py:715
  405.9 19.5 %collective-permute-start.52 = (bf16[256,1408]{1,0:T(8,128)(2,1)S(1)}, bf16[256,1408]{1,0:T(8,128)(2,1)S(1)}, u32[]{:S(2)}, u32[]{:S(2)}) collective-permute-start(bf16[256,1408]{1,0:T(8,128)(2,1)S(1)} %fusion.32), channel_id=1, source_target_pairs={{0,16},{16,0},{1,17},{17,1},{2,18},{18,2},{3,19},{19,3},{4,20},{20... | collective-permute-start | bytes 2162696 | tf_op jit(solution)/shard_map/ppermute | solution.py:62
  408.4 19.0 %collective-permute-start.44 = (bf16[256,1408]{1,0:T(8,128)(2,1)S(1)}, bf16[256,1408]{1,0:T(8,128)(2,1)S(1)}, u32[]{:S(2)}, u32[]{:S(2)}) collective-permute-start(bf16[256,1408]{1,0:T(8,128)(2,1)S(1)} %bitcast.452), channel_id=1, source_target_pairs={{0,2},{1,3},{2,0},{3,1},{4,6},{5,7},{6,4},{7,5},{8,10},{9,11},{10,... | collective-permute-start | bytes 2162696 | tf_op jit(solution)/shard_map/ppermute | solution.py:62
  426.4 12.4 %collective-permute-start.53 = (bf16[128,1408]{1,0:T(8,128)(2,1)}, bf16[128,1408]{1,0:T(8,128)(2,1)S(1)}, u32[]{:S(2)}, u32[]{:S(2)}) collective-permute-start(bf16[128,1408]{1,0:T(8,128)(2,1)} %bitcast.150), channel_id=1, source_target_pairs={{0,2},{1,3},{2,0},{3,1},{4,6},{5,7},{6,4},{7,5},{8,10},{9,11},{10,... | collective-permute-start | bytes 1081352 | tf_op jit(solution)/shard_map/ppermute | solution.py:62
  430.8 10.0 %collective-permute-start.46 = (bf16[128,1408]{1,0:T(8,128)(2,1)}, bf16[128,1408]{1,0:T(8,128)(2,1)S(1)}, u32[]{:S(2)}, u32[]{:S(2)}) collective-permute-start(bf16[128,1408]{1,0:T(8,128)(2,1)} %fusion.47), channel_id=1, source_target_pairs={{0,16},{16,0},{1,17},{17,1},{2,18},{18,2},{3,19},{19,3},{4,20},{20... | collective-permute-start | bytes 1081352 | tf_op jit(solution)/shard_map/ppermute | solution.py:62
  433.5 33.2 %all-to-all-start.3 = ((f32[32,32,88]{2,1,0:T(8,128)}), f32[32,32,88]{2,1,0:T(8,128)S(1)}, u32[]{:S(2)}, u32[]{:S(2)}) async-start(f32[32,32,88]{2,1,0:T(8,128)} %bitcast.134), calls=%async_computation.3 | async-start | bytes 1048576 | tf_op jit(solution)/shard_map/all_to_all | solution.py:729
  438.9 15.4 %collective-permute-start.54 = (bf16[64,1408]{1,0:T(8,128)(2,1)S(1)}, bf16[64,1408]{1,0:T(8,128)(2,1)S(1)}, u32[]{:S(2)}, u32[]{:S(2)}) collective-permute-start(bf16[64,1408]{1,0:T(8,128)(2,1)S(1)} %bitcast.465), channel_id=1, source_target_pairs={{0,4},{1,5},{2,6},{3,7},{4,0},{5,1},{6,2},{7,3},{8,12},{9,13},{10,... | collective-permute-start | bytes 540680 | tf_op jit(solution)/shard_map/ppermute | solution.py:62
  440.9 17.8 %collective-permute-start.47 = (bf16[64,1408]{1,0:T(8,128)(2,1)S(1)}, bf16[64,1408]{1,0:T(8,128)(2,1)S(1)}, u32[]{:S(2)}, u32[]{:S(2)}) collective-permute-start(bf16[64,1408]{1,0:T(8,128)(2,1)S(1)} %bitcast.466), channel_id=1, source_target_pairs={{0,4},{1,5},{2,6},{3,7},{4,0},{5,1},{6,2},{7,3},{8,12},{9,13},{10,... | collective-permute-start | bytes 540680 | tf_op jit(solution)/shard_map/ppermute | solution.py:62
  454.4 9.4 %collective-permute-start.55 = (bf16[32,1408]{1,0:T(8,128)(2,1)S(1)}, bf16[32,1408]{1,0:T(8,128)(2,1)S(1)}, u32[]{:S(2)}, u32[]{:S(2)}) collective-permute-start(bf16[32,1408]{1,0:T(8,128)(2,1)S(1)} %fusion.80), channel_id=1, source_target_pairs={{0,8},{1,9},{2,10},{3,11},{4,12},{5,13},{6,14},{7,15},{8,0},{9,1},... | collective-permute-start | bytes 270344 | tf_op jit(solution)/shard_map/ppermute | solution.py:62
  458.8 7.1 %collective-permute-start.50 = (bf16[32,1408]{1,0:T(8,128)(2,1)S(1)}, bf16[32,1408]{1,0:T(8,128)(2,1)S(1)}, u32[]{:S(2)}, u32[]{:S(2)}) collective-permute-start(bf16[32,1408]{1,0:T(8,128)(2,1)S(1)} %fusion.79), channel_id=1, source_target_pairs={{0,8},{1,9},{2,10},{3,11},{4,12},{5,13},{6,14},{7,15},{8,0},{9,1},... | collective-permute-start | bytes 270344 | tf_op jit(solution)/shard_map/ppermute | solution.py:62
  (76 other events, 422.9 us)

commit v4 on v3

--- a/solution.py
+++ b/solution.py
@@ -68,6 +68,10 @@
 
 def rank(step):
     return (1000 if step[0] == "dp" else 0) + step[1]
+
+
+def after(value, signal):
+    return value + (signal[(0,) * signal.ndim] * 0).astype(value.dtype)
 
 
 def together(*arrays):
@@ -98,12 +102,12 @@
     return keep.reshape(rows, width), send.reshape(rows, width)
 
 
-def gather(block, order, absolute, hooks=None):
+def gather(block, order, absolute, hooks=None, have=()):
     for number, step in enumerate(order):
         other = swap(block, step)
         if hooks and number in hooks:
             block = hooks[number](block)
-        block = joined(block, other, step, order[:number], absolute)
+        block = joined(block, other, step, list(have) + order[:number], absolute)
     return block
 
 
@@ -361,7 +365,7 @@
     cols = w_in.shape[1]
     images = text_lengths.shape[1]
     slots = text_dev * seq_count
-    core, near, team_bit = ("seq", 0), ("seq", 1), ("seq", 3)
+    core, near = ("seq", 0), ("seq", 1)
     seq_high = [("seq", bit) for bit in range(seq_count.bit_length() - 2, 1, -1)]
     dp_bits = [("dp", bit) for bit in range(dp_count.bit_length() - 1)]
     every = dp_bits + seq_high + [near, core]
@@ -383,14 +387,17 @@
     half_in = (wide + d_model) // 256 * 128
     per_head = dev_count // HEADS
     twins = seq_count // HEADS
-    head = seq_index // twins
-    twin = seq_index % twins
+    chips = seq_count // 2
+    head_slot = (seq_index % 2) * chips + seq_index // 2
+    head = head_slot // twins
+    twin = head_slot % twins
     place_in_head = dp_index * twins + twin
     row_count = rows // twins
     three = jnp.concatenate([w_query.T, w_key.T, w_value.T], axis=0)
 
     def to_rank(which_head, place):
-        return (place // twins) * seq_count + which_head * twins + place % twins
+        slot = which_head * twins + place % twins
+        return (place // twins) * seq_count + 2 * (slot % chips) + slot // chips
 
     def rounds(turn, back):
         pairs = []
@@ -401,38 +408,42 @@
                 pairs.append((user, owner) if back else (owner, user))
         return pairs
 
-    team = [team_bit, core]
-    ff_far = [step for step in seq_high if step != team_bit]
+    team = [("seq", 2), near, core]
+    ff_far = [step for step in seq_high if step not in team]
+    ff_order = ff_far + dp_bits
     units = w_gate.shape[1]
     down_out = jnp.transpose(w_down.reshape(dev_count, units, cols), (0, 2, 1))
+    down_in = lax.all_to_all(down_out, BOTH, 0, 0, tiled=True)
     upstream = jnp.concatenate([d_patch, d_text], axis=1).reshape(mine, d_model)
+    up_got = swap(upstream, team[0])
     late = {}
 
-    down_in = lax.all_to_all(down_out, BOTH, 0, 0, tiled=True)
-    ff_order = ff_far + [near] + dp_bits
-
     def while_split(block):
-        block, down = together(block, down_in)
+        block, late["down"] = together(block, down_in)
+        return block
+
+    def while_core(block):
+        block, send, gate, up, got = together(block, three, w_gate, w_up, up_got)
         late["ff"] = jnp.concatenate(
-            [w_gate.T, w_up.T, down.reshape(d_model, units).T], axis=1
+            [gate.T, up.T, late["down"].reshape(d_model, units).T], axis=1
         )
         for step in ff_far[:-1]:
             late["ff"] = jnp.concatenate([late["ff"], swap(late["ff"], step)], axis=0)
         late["ff_got"] = swap(late["ff"], ff_far[-1])
-        return block
-
-    def while_core(block):
-        block, send = together(block, three)
+        late["up"] = jnp.concatenate([upstream, got], axis=0)
+        late["up_got"] = swap(late["up"], team[1])
         late["pieces"] = [lax.ppermute(send, BOTH, rounds(turn, False)) for turn in range(per_head)]
         return block
 
+    pack = gather(pack, seq_high, True)
     in_low = gather(
         pack[:, :half_in],
-        seq_high + dp_bits + [near, core],
+        dp_bits + [near, core],
         True,
-        {len(seq_high): while_split, len(every) - 1: while_core},
-    )
-    in_high = gather(pack[:, half_in:], seq_high + [near] + dp_bits + [core], True)
+        {0: while_split, len(dp_bits) + 1: while_core},
+        seq_high,
+    )
+    in_high = gather(pack[:, half_in:], [near] + dp_bits + [core], True, None, seq_high)
     full_out = in_high[:, wide - half_in :]
 
     features = patch_features.reshape(rows * patch_dev, vit)
@@ -453,24 +464,27 @@
     half = d_model // 2
     order_low = seq_high + [near]
     order_high = [near] + seq_high
-    chips = seq_count // 2
-    normed_one, *pieces = together(normed_one, *late["pieces"])
-
-    def while_last(block):
-        block, late["up"] = together(block, upstream)
-        late["up_got"] = swap(late["up"], team_bit)
+    for piece in late["pieces"]:
+        normed_one = after(normed_one, piece)
+
+    def while_start(block):
+        block, late["ff_got"], late["up_got"] = together(block, late["ff_got"], late["up_got"])
         return block
 
-    own_low = gather(normed_one[:, :half], order_low, False, {len(seq_high): while_last})
+    own_low = gather(normed_one[:, :half], order_low, False, {0: while_start})
+    ff_block = jnp.concatenate([late["ff"], late["ff_got"]], axis=0)
+    for step in dp_bits[:-1]:
+        ff_block = jnp.concatenate([ff_block, swap(ff_block, step)], axis=0)
+    ff_got = swap(ff_block, dp_bits[-1])
+    team_up = jnp.concatenate([late["up"], late["up_got"]], axis=0)
+    team_up = jnp.concatenate([team_up, swap(team_up, core)], axis=0)
     own_high = gather(normed_one[:, half:], order_high, False)
-    own_low, own_high, ff_got, up_got = together(
-        own_low, own_high, late["ff_got"], late["up_got"]
-    )
+    own_low, own_high, ff_got = together(own_low, own_high, ff_got)
+    full_gate, full_up, full_down = [
+        jnp.concatenate([array[:, which * d_model : (which + 1) * d_model] for array in (ff_block, ff_got)], axis=0)
+        for which in range(3)
+    ]
     other_low, other_high = swap(own_low, core), swap(own_high, core)
-    ff_block = jnp.concatenate([late["ff"], ff_got], axis=0)
-    ff_got = swap(ff_block, near)
-    team_up = jnp.concatenate([late["up"], up_got], axis=0)
-    team_up = jnp.concatenate([team_up, swap(team_up, core)], axis=0)
 
     def my_rows(array):
         if twins == 1:
@@ -479,7 +493,7 @@
         view = lax.dynamic_slice_in_dim(view, twin * row_count, row_count, 1)
         return view.reshape(chips * row_count * tok, array.shape[1])
 
-    pieces = jnp.stack(pieces).reshape(per_head, 3, cols, d_model)
+    pieces = jnp.stack(late["pieces"]).reshape(per_head, 3, cols, d_model)
     ordered = [
         lax.dynamic_index_in_dim(pieces, (place_in_head - i) % per_head, 0, keepdims=False)
         for i in range(per_head)
@@ -495,15 +509,6 @@
         .reshape(chips, row_count, tok, 3 * HEAD_DIM)
         for low, high in normed_pairs
     ]
-    *qkv, ff_got = together(*qkv, ff_got)
-    ff_mine = []
-    for which in range(3):
-        part = slice(which * d_model, (which + 1) * d_model)
-        block = jnp.concatenate([ff_block[:, part], ff_got[:, part]], axis=0)
-        for step in dp_bits[:-1]:
-            block = jnp.concatenate([block, swap(block, step)], axis=0)
-        ff_mine.append(block)
-    ff_theirs = [swap(block, dp_bits[-1]) for block in ff_mine]
     lengths = lax.dynamic_slice_in_dim(text_lengths, twin * row_count, row_count, 0)
     me = seq_index.reshape(1).astype(jnp.int32)
     dims = (row_count, images, patch_dev, text_dev, slots)
@@ -527,9 +532,8 @@
         1 << 20,
         20,
     )(me, lengths, bias, *qkv)
-    mixed, ff_theirs[0] = together(mixed, ff_theirs[0])
     mixed_got = lax.all_to_all(mixed, SEQ, 0, 0, tiled=True)
-    mixed_got, ff_theirs[1] = together(mixed_got, ff_theirs[1])
+    mixed_got = mixed_got.reshape(chips, 2, tok, row_count, HEAD_DIM).swapaxes(0, 1)
     mixed_got = mixed_got.reshape(HEADS, twins, tok, row_count, HEAD_DIM)
     attn_out = jnp.transpose(mixed_got, (1, 3, 2, 0, 4)).reshape(mine, d_model)
     resid_one = resid + dot_nt(attn_out, full_out)
@@ -537,56 +541,62 @@
     team_normed = normed_two
     for step in team:
         team_normed = jnp.concatenate([team_normed, swap(team_normed, step)], axis=0)
-    weights_at = [ff_mine, ff_theirs]
-    d_normed_part, unit_grads = 0.0, []
-    for full_gate, full_up, full_down in weights_at:
-        gate_pre = dot_nt(team_normed, full_gate)
-        up_pre = dot_nt(team_normed, full_up)
-        hidden, gated_back = jax.vjp(gated_unit, gate_pre, up_pre)
-        d_gate, d_up = gated_back(dot_nt(team_up, full_down))
-        unit_grads.append([d_gate.astype(BF16), d_up.astype(BF16), hidden.astype(BF16)])
-        for grad, full in zip(unit_grads[-1], (full_gate, full_up)):
-            d_normed_part = d_normed_part + dot_nn(grad, full)
-
-    def unit_weight_grads(d_gate, d_up, hidden):
-        return jnp.concatenate(
+    gate_pre = dot_nt(team_normed, full_gate)
+    up_pre = dot_nt(team_normed, full_up)
+    hidden, gated_back = jax.vjp(gated_unit, gate_pre, up_pre)
+    hidden = hidden.astype(BF16)
+
+    d_gate, d_up = gated_back(dot_nt(team_up, full_down))
+    d_gate, d_up = d_gate.astype(BF16), d_up.astype(BF16)
+    d_normed_two = dot_nn(d_gate, full_gate) + dot_nn(d_up, full_up)
+    state = {}
+
+    def ff_take(keep):
+        keep, got = together(keep, state["ff_got"])
+        state["ff"] = state["ff_keep"].astype(F32) + got.astype(F32)
+        return keep
+
+    def ff_start(keep, step):
+        count = state["ff"].shape[0] // 2
+        state["ff_keep"] = state["ff"][:count]
+        keep, send = together(keep, state["ff"][count:].astype(BF16))
+        state["ff_got"] = swap(send, step)
+        return keep
+
+    def while_team(keep):
+        keep, *grads = together(keep, d_gate, d_up, hidden)
+        state["ff"] = jnp.concatenate(
             [
-                dot_tn(d_gate, team_normed).astype(BF16),
-                dot_tn(d_up, team_normed).astype(BF16),
-                dot_tn(hidden, team_up).astype(BF16),
+                dot_tn(grad, of).astype(BF16)
+                for grad, of in zip(grads, (team_normed, team_normed, team_up))
             ],
             axis=1,
         )
-
-    def ff_grads_start(keep):
-        keep, *grads = together(keep, *unit_grads[1])
-        keep, send = together(keep, unit_weight_grads(*grads))
-        late["ff_got"] = swap(send, dp_bits[-1])
-        return keep
-
-    keep, send = halves(d_normed_part, core, [core], False)
-    d_normed_two = keep + swap(send.astype(BF16), core).astype(F32)
-    keep, send = halves(d_normed_two, team_bit, [team_bit], False)
-    got = swap(send.astype(BF16), team_bit)
-    d_normed_two = ff_grads_start(keep) + got.astype(F32)
+        return ff_start(keep, dp_bits[-1])
+
+    def team_sum(part, step, hook=None):
+        keep, send = halves(part, step, [step], False)
+        got = swap(send.astype(BF16), step)
+        return (hook(keep) if hook else keep) + got.astype(F32)
+
+    d_normed_two = team_sum(d_normed_two, team[2])
+    d_normed_two = team_sum(d_normed_two, team[1], while_team)
+    d_normed_two = team_sum(d_normed_two, team[0])
     _, norm_back_two = jax.vjp(rms_norm, resid_one, gain_two)
     d_resid_one, grad_gain_two = norm_back_two(d_normed_two)
     d_resid_one = d_resid_one + upstream.astype(F32)
     d_mix = d_resid_one.astype(BF16)
     d_attn = dot_nn(d_mix, full_out).astype(BF16)
     d_attn = d_attn.reshape(twins, row_count, tok, HEADS, HEAD_DIM)
-    d_attn = jnp.transpose(d_attn, (3, 0, 2, 1, 4)).reshape(packed_shape.shape)
+    d_attn = jnp.transpose(d_attn, (3, 0, 2, 1, 4)).reshape(2, chips, tok, row_count * HEAD_DIM)
+    d_attn = d_attn.swapaxes(0, 1).reshape(packed_shape.shape)
     d_attn_got = lax.all_to_all(d_attn, SEQ, 0, 0, tiled=True)
 
-    d_mix, *grads = together(d_mix, *unit_grads[0])
-    ff_keep = unit_weight_grads(*grads)
-    out_part = dot_nn(grads[2], weights_at[0][2]) + dot_nn(unit_grads[1][2], weights_at[1][2])
-    out_keep, send = halves(out_part, core, [core], False)
     out_grad = dot_tn(d_mix, attn_out).astype(BF16)
-    d_attn_got, send, ff_keep, out_grad = together(
-        d_attn_got, send.astype(BF16), ff_keep, out_grad
-    )
-    out_got = swap(send, core)
+    out_part = team_sum(dot_nn(hidden, full_down), core)
+    out_keep, send = halves(out_part, team[1], [team[1]], False)
+    d_attn_got, out_grad, send = together(d_attn_got, out_grad, send.astype(BF16))
+    out_got = swap(send, team[1])
     half_shape = jax.ShapeDtypeStruct(qkv[0].shape, BF16)
     d_own, d_other, d_bias = call(
         lambda *refs: backward_kernel(dims, *refs),
@@ -604,6 +614,8 @@
         1 << 20,
         28,
     )(me, lengths, bias, *qkv, d_attn_got)
+    d_other, out_got = together(d_other, out_got)
+    out_part = out_keep + out_got.astype(F32)
     d_qkv = [array.reshape(chips * row_count * tok, 3 * HEAD_DIM) for array in (d_own, d_other)]
 
     def all_rows(array):
@@ -622,34 +634,13 @@
     owns = [
         all_rows(dot_nn(d_qkv[0], part)) + other.astype(F32) for part, other in zip(weights, others)
     ]
-    state = {}
-
-    def ff_take(keep, step):
-        keep, got = together(keep, state["ff_got"])
-        state["ff"] = state["ff_keep"].astype(F32) + got.astype(F32)
+    def while_first(keep):
+        keep = ff_take(keep)
+        for step in dp_bits[-2::-1]:
+            keep = ff_take(ff_start(keep, step))
+        for step in ff_far[:0:-1]:
+            keep = ff_take(ff_start(keep, step))
         return keep
-
-    def ff_start(keep, step):
-        count = state["ff"].shape[0] // 2
-        state["ff_keep"] = state["ff"][:count]
-        keep, send = together(keep, state["ff"][count:].astype(BF16))
-        state["ff_got"] = swap(send, step)
-        return keep
-
-    ff_back = ff_order[::-1]
-    state.update(ff_keep=ff_keep, ff_got=late["ff_got"])
-
-    def while_first(keep):
-        keep = ff_take(keep, ff_back[0])
-        for step in ff_back[1 : len(dp_bits)]:
-            keep = ff_take(ff_start(keep, step), step)
-        return ff_start(keep, near)
-
-    def while_last_again(keep):
-        keep = ff_take(keep, near)
-        for step in ff_far[:0:-1]:
-            keep = ff_take(ff_start(keep, step), step)
-        return ff_start(keep, ff_far[0])
 
     def while_middle(keep):
         keep, grads_own, grads_other = together(keep, *d_qkv)
@@ -668,10 +659,17 @@
             ).reshape(3 * cols, d_model)
             for turn in range(per_head)
         ]
-        keep, *state["sends"] = together(keep, *sends)
+        keep, *sends = together(keep, *sends)
+        state["three"] = [
+            lax.ppermute(send, BOTH, rounds(turn, True)) for turn, send in enumerate(sends)
+        ]
         return keep
 
-    low_sums = scatter_add(owns[0], order_low[::-1], chip_bits, False, {0: while_first, 1: while_middle, len(order_low) - 1: while_last_again})
+    def while_late(keep):
+        keep, *state["three"] = together(keep, *state["three"])
+        return keep
+
+    low_sums = scatter_add(owns[0], order_low[::-1], chip_bits, False, {0: while_middle, 1: while_first, len(order_low) - 1: while_late})
     high_sums = scatter_add(owns[1], order_high[::-1], chip_bits, False)
     d_normed_one = jnp.concatenate([low_sums, high_sums], axis=1)
     d_table = call(
@@ -707,43 +705,45 @@
     )
 
     def while_core_again(keep):
-        keep, got, *sends = together(keep, out_got, *state["sends"])
-        part = out_keep + got.astype(F32)
-        state["out_keep"], send = halves(part, team_bit, [team_bit], False)
-        keep, send, state["d_low"] = together(keep, send.astype(BF16), d_low)
-        state["three"] = [
-            lax.ppermute(send, BOTH, rounds(turn, True)) for turn, send in enumerate(sends)
-        ]
-        state["out_got"] = swap(send, team_bit)
+        keep = ff_start(keep, ff_far[0])
+        keep, part = together(keep, out_part)
+        state["out_keep"], send = halves(part, team[0], [team[0]], False)
+        state["out_got"] = swap(send.astype(BF16), team[0])
+        keep, state["d_low"] = together(keep, d_low)
         return keep
 
-    def while_end(keep):
-        keep, *state["three"] = together(keep, *state["three"])
-        return keep
-
-    def while_split_again(keep):
-        keep = ff_take(keep, ff_far[0])
+    def while_half_again(keep):
+        keep = ff_take(keep)
         down = state["ff"][:, 2 * d_model :]
         down_back = down.T.reshape(dev_count, cols, units)
-        keep, down_back = together(keep, down_back)
+        keep, down_back, state["out_got"] = together(keep, down_back, state["out_got"])
         state["down_back"] = lax.all_to_all(down_back, BOTH, 0, 0, tiled=True)
         return keep
 
-    out_grad = dot_tn(d_mix, attn_out).astype(BF16)
+    def while_end(keep):
+        keep, state["down_back"] = together(keep, state["down_back"])
+        return keep
+
     in_low_sums = scatter_add(
         dot_tn(left, right[:, :half_in]).astype(BF16),
-        [core, near] + dp_bits[::-1] + seq_high[::-1],
+        [core, near] + dp_bits[::-1],
         every,
         True,
-        {0: while_core_again, 2: while_split_again, len(every) - 1: while_end},
+        {0: while_core_again, 2: while_half_again},
     )
     in_high_sums = scatter_add(
         jnp.concatenate([dot_tn(left, right[:, half_in:]).astype(BF16), out_grad], axis=1),
-        [core] + dp_bits[::-1] + [near] + seq_high[::-1],
+        [core] + dp_bits[::-1] + [near],
         every,
         True,
     )
-    in_grads = jnp.concatenate([in_low_sums, in_high_sums], axis=1)
+    in_grads = scatter_add(
+        jnp.concatenate([in_low_sums, in_high_sums], axis=1),
+        seq_high[::-1],
+        seq_high,
+        True,
+        {len(seq_high) - 1: while_end},
+    )
     small_out, grad_w_out = in_grads[:, vit:wide], in_grads[:, wide:]
     d_low = state["d_low"]
     feature_grad = jnp.concatenate(

time: 473 us -> 448 us (0.947)
  starting transfers between devices: 94.2 us -> 63.4 us
  blocking collectives: 0 us -> 16.1 us
  waiting for transfers between devices: 186 us -> 174 us
    ppermute x52 -> x48, waiting for transfers between devices: 186 us -> 148 us  [swap(): return lax.ppermute(array, axis, [(i, i ^ 1 << bit) for i in range(count)])]
    ppermute x52 -> x48, starting transfers between devices: 70.3 us -> 42.8 us  [swap(): return lax.ppermute(array, axis, [(i, i ^ 1 << bit) for i in range(count)])]
    all_to_all x0 -> x1, blocking collectives: none -> 16.1 us  [local(): mixed_got = lax.all_to_all(mixed, SEQ, 0, 0, tiled=True)]
    all_to_all x2 -> x1, waiting for transfers between devices: 0.01 us -> 15.2 us  [while_half_again(): state['down_back'] = lax.all_to_all(down_back, BOTH, 0, 0, tiled=True)]
    concatenate x7 -> x2, local copies, waits for them, and re-layouts: 10.2 us -> 3.67 us  [the longest x1 2.19 us: while_core(): jnp.concatenate([gate.T, up.T, late['down'].reshape(d_model, units).T], a...]
    all_to_all x1, waiting for transfers between devices: 0.01 us -> 6.23 us  [local(): d_attn_got = lax.all_to_all(d_attn, SEQ, 0, 0, tiled=True)]
    all_to_all x2 -> x1, starting transfers between devices: 9.65 us -> 4.05 us  [while_half_again(): state['down_back'] = lax.all_to_all(down_back, BOTH, 0, 0, tiled=True)]
    dot_general x13 -> x10, matrix products: 19.7 us -> 14.2 us  [dot_nn(): lax.dot_general(left, right, (((1,), (0,)), ((), ())), preferred_element_...]
  transfers between devices with their start and end apart: 60 -> 55, of which waited for: 27 -> 30; matrix products, arithmetic and copies ran while one was open for 26% -> 24% of each run, Pallas kernels for 6% -> 4%
where the time goes in v4:
time: 448 us; the launch traced here: 443 us
  waiting for transfers between devices  174 us (39%)
  starting transfers between devices  63.4 us (14%)
  local copies, waits for them, and re-layouts  60.9 us (14%)
  matrix products  55 us (12%)
  other arithmetic  41.2 us (9%)
  Pallas kernels  27.6 us (6%)
  blocking collectives  16.1 us (4%)
  between operations  4.54 us (1%)
    ppermute x48, waiting for transfers between devices, swap(): return lax.ppermute(array, axis, [(i, i ^ 1 << bit) for i in range(count)])  148 us
    ppermute x48, starting transfers between devices, swap(): return lax.ppermute(array, axis, [(i, i ^ 1 << bit) for i in range(count)])  42.8 us
    dot_general x11, matrix products, dot_nt(): lax.dot_general(left, right, (((1,), (1,)), ((), ())), preferred_element_...  21 us
    dot_general x10, matrix products, dot_tn(): lax.dot_general(left, right, (((0,), (0,)), ((), ())), preferred_element_...  19.8 us
    all_to_all x1, blocking collectives, local(): mixed_got = lax.all_to_all(mixed, SEQ, 0, 0, tiled=True)  16.1 us
    all_to_all x1, waiting for transfers between devices, while_half_again(): state['down_back'] = lax.all_to_all(down_back, BOTH, 0, 0, tiled=True)  15.2 us
    pallas_call x1, Pallas kernels, local(): call(lambda *refs: backward_kernel(dims, *refs), (half_shape, half_shape,...  14.4 us
    dot_general x10, matrix products, dot_nn(): lax.dot_general(left, right, (((1,), (0,)), ((), ())), preferred_element_...  14.2 us
  transfers between devices with their start and end apart: 55, of which 30 were waited for; matrix products, arithmetic and copies ran while one was open for 24% of the time, Pallas kernels for 4%

profile of v4, /device:TPU:0, one launch (start us, length us, event | category | flops | bytes accessed | tf_op | source)
XLA Modules:
  0.0 442.6 jit_solution(16527897973154242315)
XLA Ops:
  4.7 4.1 collective-permute-start
  8.8 8.4 %collective-permute-done = bf16[32,2816]{1,0:T(8,128)(2,1)S(1)} collective-permute-done((bf16[32,2816]{1,0:T(8,128)(2,1)S(1)}, bf16[32,2816]{1,0:T(8,128)(2,1)S(1)}, u32[]{:S(2)}, u32[]{:S(2)}) %collective-permute-start) | collective-permute-done | bytes 180256 | tf_op jit(solution)/shard_map/ppermute | solution.py:62
  18.0 8.9 %collective-permute-done.1 = bf16[64,2816]{1,0:T(8,128)(2,1)S(1)} collective-permute-done((bf16[64,2816]{1,0:T(8,128)(2,1)S(1)}, bf16[64,2816]{1,0:T(8,128)(2,1)S(1)}, u32[]{:S(2)}, u32[]{:S(2)}) %collective-permute-start.1) | collective-permute-done | bytes 360480 | tf_op jit(solution)/shard_map/ppermute | solution.py:62
  29.8 5.8 %all-to-all-start = ((bf16[32,32,88]{2,1,0:T(8,128)(2,1)}), bf16[32,32,88]{2,1,0:T(8,128)(2,1)S(1)}, u32[]{:S(2)}, u32[]{:S(2)}) async-start(bf16[32,32,88]{2,1,0:T(8,128)(2,1)} %bitcast.308), calls=%async_computation | async-start | bytes 524288 | tf_op jit(solution)/shard_map/all_to_all | solution.py:416
  37.7 2.2 collective-permute-start.5
  41.8 4.1 all-to-all-done
  46.0 3.8 collective-permute-done.2
  52.2 12.3 %collective-permute-done.7 = bf16[256,1408]{1,0:T(8,128)(2,1)S(1)} collective-permute-done((bf16[256,1408]{1,0:T(8,128)(2,1)S(1)}, bf16[256,1408]{1,0:T(8,128)(2,1)S(1)}, u32[]{:S(2)}, u32[]{:S(2)}) %collective-permute-start.7) | collective-permute-done | bytes 720928 | tf_op jit(solution)/shard_map/ppermute | solution.py:62
  71.2 3.1 collective-permute-start.9
  75.4 1.8 copy.94
  77.2 2.1 pad_maximum_fusion.14
  79.3 2.2 copy.96
  83.0 1.8 pad_maximum_fusion.23
  100.9 11.0 %collective-permute-done.11 = bf16[88,3072]{1,0:T(8,128)(2,1)} collective-permute-done((bf16[88,3072]{1,0:T(8,128)(2,1)}, bf16[88,3072]{1,0:T(8,128)(2,1)}, u32[]{:S(2)}, u32[]{:S(2)}) %collective-permute-start.11) | collective-permute-done | bytes 540704 | tf_op jit(solution)/shard_map/ppermute | solution.py:62
  116.0 2.9 collective-permute-start.17
  123.7 5.8 %collective-permute-done.14 = bf16[288,512]{1,0:T(8,128)(2,1)} collective-permute-done((bf16[288,512]{1,0:T(8,128)(2,1)}, bf16[288,512]{1,0:T(8,128)(2,1)}, u32[]{:S(2)}, u32[]{:S(2)}) %collective-permute-start.14) | collective-permute-done | bytes 294944 | tf_op jit(solution)/shard_map/ppermute | solution.py:62
  133.6 10.9 %collective-permute-done.15 = bf16[576,512]{1,0:T(8,128)(2,1)S(1)} collective-permute-done((bf16[576,512]{1,0:T(8,128)(2,1)S(1)}, bf16[576,512]{1,0:T(8,128)(2,1)S(1)}, u32[]{:S(2)}, u32[]{:S(2)}) %collective-permute-start.15) | collective-permute-done | bytes 589856 | tf_op jit(solution)/shard_map/ppermute | solution.py:62
  151.0 1.8 fusion.75
  152.8 1.8 fusion
  154.9 1.8 fusion.73
  156.8 1.8 fusion.1
  158.9 10.7 %shard_map.289 = bf16[16,72,128]{2,1,0:T(8,128)(2,1)S(1)} custom-call(s32[1]{0:T(128)} %bitcast.41.refs_0_, s32[2,3]{1,0:T(2,128)S(1)} %copy-done.2, f32[448,512]{1,0:T(8,128)S(1)} %shard_map.288.refs_2_, bf16[8,2,72,192]{3,2,1,0:T(8,128)(2,1)S(1)} %bitcast.318, bf16[8,2,72,192]{3,2,1,0:T(8,128)(2,1)S(1)} %bitcast.320), custom_call_target="tpu_custom_call" | custom-call | flops 16777216 | bytes 1048576 | tf_op jit(solution)/shard_map/pallas_call | solution.py:521
  169.6 16.1 %all_to_all.20 = bf16[16,72,128]{2,1,0:T(8,128)(2,1)} all-to-all(bf16[16,72,128]{2,1,0:T(8,128)(2,1)S(1)} %shard_map.289), channel_id=1, replica_groups=mesh['dp'=2,'seq'=16] {'seq'}, dimensions={0} | all-to-all | bytes 589824 | tf_op jit(solution)/shard_map/all_to_all | solution.py:535
  188.0 2.2 reshape.515
  190.2 2.6 multiply_reduce_fusion.4
  193.3 8.6 %collective-permute-done.22 = bf16[144,1024]{1,0:T(8,128)(2,1)S(1)} collective-permute-done((bf16[144,1024]{1,0:T(8,128)(2,1)S(1)}, bf16[144,1024]{1,0:T(8,128)(2,1)S(1)}, u32[]{:S(2)}, u32[]{:S(2)}) %collective-permute-start.22) | collective-permute-done | bytes 294944 | tf_op jit(solution)/shard_map/ppermute | solution.py:62
  202.7 2.3 pad_maximum_fusion.13
  205.0 11.3 %collective-permute-done.23 = bf16[288,1024]{1,0:T(8,128)(2,1)S(1)} collective-permute-done((bf16[288,1024]{1,0:T(8,128)(2,1)S(1)}, bf16[288,1024]{1,0:T(8,128)(2,1)S(1)}, u32[]{:S(2)}, u32[]{:S(2)}) %collective-permute-start.23) | collective-permute-done | bytes 589856 | tf_op jit(solution)/shard_map/ppermute | solution.py:62
  218.7 2.9 copy.106
  223.3 2.8 fusion.44
  226.2 2.7 fusion.49
  228.9 4.0 multiply_convert_fusion
  239.9 1.8 collective-permute-start.27
  241.7 2.5 convolution_convert_fusion.5
  244.2 2.5 convolution_convert_fusion.6
  246.8 2.4 convolution_convert_fusion.7
  250.5 5.1 %collective-permute-done.27 = bf16[288,1024]{1,0:T(8,128)(2,1)S(1)} collective-permute-done((bf16[288,1024]{1,0:T(8,128)(2,1)S(1)}, bf16[288,1024]{1,0:T(8,128)(2,1)S(1)}, u32[]{:S(2)}, u32[]{:S(2)}) %collective-permute-start.27) | collective-permute-done | bytes 589856 | tf_op jit(solution)/shard_map/ppermute | solution.py:62
  255.8 1.8 collective-permute-start.28
  257.6 1.8 fusion.2
  259.4 4.9 %collective-permute-done.28 = bf16[144,1024]{1,0:T(8,128)(2,1)S(1)} collective-permute-done((bf16[144,1024]{1,0:T(8,128)(2,1)S(1)}, bf16[144,1024]{1,0:T(8,128)(2,1)S(1)}, u32[]{:S(2)}, u32[]{:S(2)}) %collective-permute-start.28) | collective-permute-done | bytes 294944 | tf_op jit(solution)/shard_map/ppermute | solution.py:62
  271.0 3.8 all-to-all-start.2
  274.8 2.2 fusion.33
  277.0 2.2 convolution_convert_fusion.3
  279.1 6.2 %all-to-all-done.2.refs_5_ = bf16[16,72,128]{2,1,0:T(8,128)(2,1)S(1)} async-done(((bf16[16,72,128]{2,1,0:T(8,128)(2,1)}), bf16[16,72,128]{2,1,0:T(8,128)(2,1)S(1)}, u32[]{:S(2)}, u32[]{:S(2)}) %all-to-all-start.2) | async-done | bytes 294944 | tf_op jit(solution)/shard_map/all_to_all | solution.py:593
  287.1 14.4 %shard_map.290 = (bf16[8,2,72,192]{3,2,1,0:T(8,128)(2,1)S(1)}, bf16[8,2,72,192]{3,2,1,0:T(8,128)(2,1)S(1)}, f32[448,512]{1,0:T(8,128)S(1)}) custom-call(s32[1]{0:T(128)} %bitcast.41.refs_0_, s32[2,3]{1,0:T(2,128)S(1)} %copy-done.2, f32[448,512]{1,0:T(8,128)S(1)} %shard_map.288.refs_2_, bf16[8,2,72,192]{3,2,1,0:T(8,128)(2,1)S(1)} %bitcast.319, ...), custom_call_target="tpu_custom_call" | custom-call | flops 16777216 | bytes 1048576 | tf_op jit(solution)/shard_map/pallas_call | solution.py:601
  305.9 2.0 collective-permute-start.33
  309.5 2.7 fusion.23
  312.2 1.7 convert_add_fusion.3
  314.2 1.7 convert_add_fusion.2
  319.9 1.7 fusion.25
  321.7 1.7 fusion.104
  323.4 1.7 fusion.24
  327.6 4.4 collective-permute-done.32
  337.3 10.2 %collective-permute-done.40 = bf16[288,512]{1,0:T(8,128)(2,1)S(1)} collective-permute-done((bf16[288,512]{1,0:T(8,128)(2,1)S(1)}, bf16[288,512]{1,0:T(8,128)(2,1)S(1)}, u32[]{:S(2)}, u32[]{:S(2)}) %collective-permute-start.40) | collective-permute-done | bytes 294944 | tf_op jit(solution)/shard_map/ppermute | solution.py:62
  347.6 1.8 collective-permute-start.41
  349.7 3.2 collective-permute-done.41
  353.0 5.2 %collective-permute-done.37 = bf16[144,512]{1,0:T(8,128)(2,1)S(1)} collective-permute-done((bf16[144,512]{1,0:T(8,128)(2,1)S(1)}, bf16[144,512]{1,0:T(8,128)(2,1)S(1)}, u32[]{:S(2)}, u32[]{:S(2)}) %collective-permute-start.37) | collective-permute-done | bytes 147488 | tf_op jit(solution)/shard_map/ppermute | solution.py:62
  362.8 2.1 convolution_convert_fusion
  369.4 2.3 collective-permute-start.45
  376.4 17.1 %collective-permute-done.43 = bf16[256,1408]{1,0:T(8,128)(2,1)S(1)} collective-permute-done((bf16[256,1408]{1,0:T(8,128)(2,1)S(1)}, bf16[256,1408]{1,0:T(8,128)(2,1)S(1)}, u32[]{:S(2)}, u32[]{:S(2)}) %collective-permute-start.43) | collective-permute-done | bytes 720928 | tf_op jit(solution)/shard_map/ppermute | solution.py:62
  399.4 8.0 %collective-permute-done.49 = bf16[128,1408]{1,0:T(8,128)(2,1)} collective-permute-done((bf16[128,1408]{1,0:T(8,128)(2,1)}, bf16[128,1408]{1,0:T(8,128)(2,1)}, u32[]{:S(2)}, u32[]{:S(2)}) %collective-permute-start.49) | collective-permute-done | bytes 360480 | tf_op jit(solution)/shard_map/ppermute | solution.py:62
  412.7 4.0 all-to-all-start.3
  416.9 2.8 collective-permute-done.50
  421.8 15.2 %all-to-all-done.3 = f32[32,32,88]{2,1,0:T(8,128)S(1)} async-done(((f32[32,32,88]{2,1,0:T(8,128)}), f32[32,32,88]{2,1,0:T(8,128)S(1)}, u32[]{:S(2)}, u32[]{:S(2)}) %all-to-all-start.3) | async-done | bytes 360480 | tf_op jit(solution)/shard_map/all_to_all | solution.py:720
  (389 shorter events, 131.8 us)
Async XLA Ops:
  4.7 12.5 %collective-permute-start = (bf16[32,2816]{1,0:T(8,128)(2,1)S(1)}, bf16[32,2816]{1,0:T(8,128)(2,1)S(1)}, u32[]{:S(2)}, u32[]{:S(2)}) collective-permute-start(bf16[32,2816]{1,0:T(8,128)(2,1)S(1)} %bitcast.436), channel_id=1, source_target_pairs={{0,8},{1,9},{2,10},{3,11},{4,12},{5,13},{6,14},{7,15},{8,0},{9,1},... | collective-permute-start | bytes 540680 | tf_op jit(solution)/shard_map/ppermute | solution.py:62
  17.2 9.7 %collective-permute-start.1 = (bf16[64,2816]{1,0:T(8,128)(2,1)S(1)}, bf16[64,2816]{1,0:T(8,128)(2,1)S(1)}, u32[]{:S(2)}, u32[]{:S(2)}) collective-permute-start(bf16[64,2816]{1,0:T(8,128)(2,1)S(1)} %bitcast.429), channel_id=1, source_target_pairs={{0,4},{1,5},{2,6},{3,7},{4,0},{5,1},{6,2},{7,3},{8,12},{9,13},{10,... | collective-permute-start | bytes 1081352 | tf_op jit(solution)/shard_map/ppermute | solution.py:62
  27.1 8.7 %collective-permute-start.6 = (bf16[128,1408]{1,0:T(8,128)(2,1)S(1)}, bf16[128,1408]{1,0:T(8,128)(2,1)S(1)}, u32[]{:S(2)}, u32[]{:S(2)}) collective-permute-start(bf16[128,1408]{1,0:T(8,128)(2,1)S(1)} %slice.326), channel_id=1, source_target_pairs={{0,2},{1,3},{2,0},{3,1},{4,6},{5,7},{6,4},{7,5},{8,10},{9,11},{10,... | collective-permute-start | bytes 1081352 | tf_op jit(solution)/shard_map/ppermute | solution.py:62
  29.8 16.1 %all-to-all-start = ((bf16[32,32,88]{2,1,0:T(8,128)(2,1)}), bf16[32,32,88]{2,1,0:T(8,128)(2,1)S(1)}, u32[]{:S(2)}, u32[]{:S(2)}) async-start(bf16[32,32,88]{2,1,0:T(8,128)(2,1)} %bitcast.308), calls=%async_computation | async-start | bytes 524288 | tf_op jit(solution)/shard_map/all_to_all | solution.py:416
  35.9 13.9 %collective-permute-start.2 = (bf16[128,1408]{1,0:T(8,128)(2,1)S(1)}, bf16[128,1408]{1,0:T(8,128)(2,1)}, u32[]{:S(2)}, u32[]{:S(2)}) collective-permute-start(bf16[128,1408]{1,0:T(8,128)(2,1)S(1)} %get-tuple-element.82), channel_id=1, source_target_pairs={{0,16},{16,0},{1,17},{17,1},{2,18},{18,2},{3,19},{19,3},{4,20},{20... | collective-permute-start | bytes 1081352 | tf_op jit(solution)/shard_map/ppermute | solution.py:62
  37.7 45.4 %copy-start.23 = (bf16[2,72,1024]{2,1,0:T(8,128)(2,1)}, bf16[2,72,1024]{2,1,0:T(8,128)(2,1)S(1)}, u32[]{:S(2)}) copy-start(bf16[2,72,1024]{2,1,0:T(8,128)(2,1)S(1)} %pad_maximum_fusion.39) | copy-start | bytes 884740
  37.7 32.0 %collective-permute-start.5 = (bf16[144,1024]{1,0:T(8,128)(2,1)S(1)}, bf16[144,1024]{1,0:T(8,128)(2,1)S(1)}, u32[]{:S(2)}, u32[]{:S(2)}) collective-permute-start(bf16[144,1024]{1,0:T(8,128)(2,1)S(1)} %bitcast.370), channel_id=1, source_target_pairs={{0,4},{1,5},{2,6},{3,7},{4,0},{5,1},{6,2},{7,3},{8,12},{9,13},{10,... | collective-permute-start | bytes 884744 | tf_op jit(solution)/shard_map/ppermute | solution.py:62
  41.3 23.3 %collective-permute-start.7 = (bf16[256,1408]{1,0:T(8,128)(2,1)S(1)}, bf16[256,1408]{1,0:T(8,128)(2,1)S(1)}, u32[]{:S(2)}, u32[]{:S(2)}) collective-permute-start(bf16[256,1408]{1,0:T(8,128)(2,1)S(1)} %bitcast.397), channel_id=1, source_target_pairs={{0,16},{16,0},{1,17},{17,1},{2,18},{18,2},{3,19},{19,3},{4,20},{20... | collective-permute-start | bytes 2162696 | tf_op jit(solution)/shard_map/ppermute | solution.py:62
  46.0 18.8 %copy-start.34 = (bf16[32,32,88]{2,1,0:T(8,128)(2,1)}, bf16[32,32,88]{2,1,0:T(8,128)(2,1)S(1)}, u32[]{:S(2)}) copy-start(bf16[32,32,88]{2,1,0:T(8,128)(2,1)S(1)} %all-to-all-done) | copy-start | bytes 540676
  51.0 17.1 %collective-permute-start.3 = (bf16[256,1408]{1,0:T(8,128)(2,1)S(1)}, bf16[256,1408]{1,0:T(8,128)(2,1)}, u32[]{:S(2)}, u32[]{:S(2)}) collective-permute-start(bf16[256,1408]{1,0:T(8,128)(2,1)S(1)} %bitcast.396), channel_id=1, source_target_pairs={{0,2},{1,3},{2,0},{3,1},{4,6},{5,7},{6,4},{7,5},{8,10},{9,11},{10,... | collective-permute-start | bytes 2162696 | tf_op jit(solution)/shard_map/ppermute | solution.py:62
  65.0 24.7 %collective-permute-start.8 = (bf16[512,1408]{1,0:T(8,128)(2,1)S(1)}, bf16[512,1408]{1,0:T(8,128)(2,1)}, u32[]{:S(2)}, u32[]{:S(2)}) collective-permute-start(bf16[512,1408]{1,0:T(8,128)(2,1)S(1)} %bitcast.360), channel_id=1, source_target_pairs={{0,1},{1,0},{2,3},{3,2},{4,5},{5,4},{6,7},{7,6},{8,9},{9,8},{10,11... | collective-permute-start | bytes 4325384 | tf_op jit(solution)/shard_map/ppermute | solution.py:62
  69.6 23.0 %collective-permute-start.4 = (bf16[512,1408]{1,0:T(8,128)(2,1)S(1)}, bf16[512,1408]{1,0:T(8,128)(2,1)}, u32[]{:S(2)}, u32[]{:S(2)}) collective-permute-start(bf16[512,1408]{1,0:T(8,128)(2,1)S(1)} %bitcast.361), channel_id=1, source_target_pairs={{0,1},{1,0},{2,3},{3,2},{4,5},{5,4},{6,7},{7,6},{8,9},{9,8},{10,11... | collective-permute-start | bytes 4325384 | tf_op jit(solution)/shard_map/ppermute | solution.py:62
  69.7 15.1 %collective-permute-start.10 = (bf16[96,1024]{1,0:T(8,128)(2,1)}, bf16[96,1024]{1,0:T(8,128)(2,1)}, u32[]{:S(2)}, u32[]{:S(2)}) collective-permute-start(bf16[96,1024]{1,0:T(8,128)(2,1)} %pad_maximum_fusion.42), channel_id=1, source_target_pairs={{0,16},{1,0},{2,18},{3,2},{4,20},{5,4},{6,22},{7,6},{8,24},{9,8},{... | collective-permute-start | bytes 589832 | tf_op jit(solution)/shard_map/ppermute | solution.py:435
  71.2 16.7 %collective-permute-start.9 = (bf16[96,1024]{1,0:T(8,128)(2,1)}, bf16[96,1024]{1,0:T(8,128)(2,1)}, u32[]{:S(2)}, u32[]{:S(2)}) collective-permute-start(bf16[96,1024]{1,0:T(8,128)(2,1)} %pad_maximum_fusion.42), channel_id=1, source_target_pairs={{0,0},{1,16},{2,2},{3,18},{4,4},{5,20},{6,6},{7,22},{8,8},{9,24},{... | collective-permute-start | bytes 589832 | tf_op jit(solution)/shard_map/ppermute | solution.py:435
  81.5 30.4 %collective-permute-start.11 = (bf16[88,3072]{1,0:T(8,128)(2,1)}, bf16[88,3072]{1,0:T(8,128)(2,1)}, u32[]{:S(2)}, u32[]{:S(2)}) collective-permute-start(bf16[88,3072]{1,0:T(8,128)(2,1)} %copy.96), channel_id=1, source_target_pairs={{0,8},{1,9},{2,10},{3,11},{4,12},{5,13},{6,14},{7,15},{8,0},{9,1},... | collective-permute-start | bytes 1622024 | tf_op jit(solution)/shard_map/ppermute | solution.py:62
  84.9 27.0 %collective-permute-start.12 = (bf16[288,1024]{1,0:T(8,128)(2,1)}, bf16[288,1024]{1,0:T(8,128)(2,1)}, u32[]{:S(2)}, u32[]{:S(2)}) collective-permute-start(bf16[288,1024]{1,0:T(8,128)(2,1)} %pad_maximum_fusion.23), channel_id=1, source_target_pairs={{0,2},{1,3},{2,0},{3,1},{4,6},{5,7},{6,4},{7,5},{8,10},{9,11},{10,... | collective-permute-start | bytes 1769480 | tf_op jit(solution)/shard_map/ppermute | solution.py:62
  97.1 93.1 %copy-start.19 = (f32[2,72,1024]{2,1,0:T(8,128)}, f32[2,72,1024]{2,1,0:T(8,128)S(1)}, u32[]{:S(2)}) copy-start(f32[2,72,1024]{2,1,0:T(8,128)S(1)} %get-tuple-element.177) | copy-start | bytes 1769476
  97.8 14.1 %copy-start.61 = (f32[144]{0:T(256)}, f32[144]{0:T(256)S(1)}, u32[]{:S(2)}) copy-start(f32[144]{0:T(256)S(1)} %rsqrt.25) | copy-start | bytes 1732
  98.6 20.4 %copy-start.33 = (bf16[1024,88]{1,0:T(8,128)(2,1)S(1)}, bf16[1024,88]{1,0:T(8,128)(2,1)}, u32[]{:S(2)}) copy-start(bf16[1024,88]{1,0:T(8,128)(2,1)} %copy.94) | copy-start | bytes 540676
  98.6 15.8 %collective-permute-start.13 = (bf16[144,512]{1,0:T(8,128)(2,1)S(1)}, bf16[144,512]{1,0:T(8,128)(2,1)S(1)}, u32[]{:S(2)}, u32[]{:S(2)}) collective-permute-start(bf16[144,512]{1,0:T(8,128)(2,1)S(1)} %get-tuple-element.89), channel_id=1, source_target_pairs={{0,8},{1,9},{2,10},{3,11},{4,12},{5,13},{6,14},{7,15},{8,0},{9,1},... | collective-permute-start | bytes 442376 | tf_op jit(solution)/shard_map/ppermute | solution.py:62
  99.9 15.4 %collective-permute-start.16 = (bf16[144,512]{1,0:T(8,128)(2,1)S(1)}, bf16[144,512]{1,0:T(8,128)(2,1)S(1)}, u32[]{:S(2)}, u32[]{:S(2)}) collective-permute-start(bf16[144,512]{1,0:T(8,128)(2,1)S(1)} %get-tuple-element.188), channel_id=1, source_target_pairs={{0,2},{1,3},{2,0},{3,1},{4,6},{5,7},{6,4},{7,5},{8,10},{9,11},{10,... | collective-permute-start | bytes 442376 | tf_op jit(solution)/shard_map/ppermute | solution.py:62
  115.3 14.2 %collective-permute-start.14 = (bf16[288,512]{1,0:T(8,128)(2,1)}, bf16[288,512]{1,0:T(8,128)(2,1)}, u32[]{:S(2)}, u32[]{:S(2)}) collective-permute-start(bf16[288,512]{1,0:T(8,128)(2,1)} %bitcast.53), channel_id=1, source_target_pairs={{0,4},{1,5},{2,6},{3,7},{4,0},{5,1},{6,2},{7,3},{8,12},{9,13},{10,... | collective-permute-start | bytes 884744 | tf_op jit(solution)/shard_map/ppermute | solution.py:62
  116.0 16.3 %collective-permute-start.17 = (bf16[288,512]{1,0:T(8,128)(2,1)}, bf16[288,512]{1,0:T(8,128)(2,1)}, u32[]{:S(2)}, u32[]{:S(2)}) collective-permute-start(bf16[288,512]{1,0:T(8,128)(2,1)} %bitcast.62), channel_id=1, source_target_pairs={{0,8},{1,9},{2,10},{3,11},{4,12},{5,13},{6,14},{7,15},{8,0},{9,1},... | collective-permute-start | bytes 884744 | tf_op jit(solution)/shard_map/ppermute | solution.py:62
  122.1 25.9 %collective-permute-start.19 = (bf16[176,3072]{1,0:T(8,128)(2,1)}, bf16[176,3072]{1,0:T(8,128)(2,1)}, u32[]{:S(2)}, u32[]{:S(2)}) collective-permute-start(bf16[176,3072]{1,0:T(8,128)(2,1)} %copy.101), channel_id=1, source_target_pairs={{0,16},{16,0},{1,17},{17,1},{2,18},{18,2},{3,19},{19,3},{4,20},{20... | collective-permute-start | bytes 3244040 | tf_op jit(solution)/shard_map/ppermute | solution.py:62
  130.5 14.0 %collective-permute-start.15 = (bf16[576,512]{1,0:T(8,128)(2,1)S(1)}, bf16[576,512]{1,0:T(8,128)(2,1)S(1)}, u32[]{:S(2)}, u32[]{:S(2)}) collective-permute-start(bf16[576,512]{1,0:T(8,128)(2,1)S(1)} %bitcast.415), channel_id=1, source_target_pairs={{0,2},{1,3},{2,0},{3,1},{4,6},{5,7},{6,4},{7,5},{8,10},{9,11},{10,... | collective-permute-start | bytes 1769480 | tf_op jit(solution)/shard_map/ppermute | solution.py:62
  133.5 13.3 %collective-permute-start.18 = (bf16[576,512]{1,0:T(8,128)(2,1)S(1)}, bf16[576,512]{1,0:T(8,128)(2,1)S(1)}, u32[]{:S(2)}, u32[]{:S(2)}) collective-permute-start(bf16[576,512]{1,0:T(8,128)(2,1)S(1)} %bitcast.439), channel_id=1, source_target_pairs={{0,4},{1,5},{2,6},{3,7},{4,0},{5,1},{6,2},{7,3},{8,12},{9,13},{10,... | collective-permute-start | bytes 1769480 | tf_op jit(solution)/shard_map/ppermute | solution.py:62
  148.0 6.9 %collective-permute-start.21 = (bf16[1152,512]{1,0:T(8,128)(2,1)}, bf16[1152,512]{1,0:T(8,128)(2,1)}, u32[]{:S(2)}, u32[]{:S(2)}) collective-permute-start(bf16[1152,512]{1,0:T(8,128)(2,1)} %bitcast.67), channel_id=1, source_target_pairs={{0,1},{1,0},{2,3},{3,2},{4,5},{5,4},{6,7},{7,6},{8,9},{9,8},{10,11... | collective-permute-start | bytes 3538952 | tf_op jit(solution)/shard_map/ppermute | solution.py:62
  148.0 8.8 %collective-permute-start.20 = (bf16[1152,512]{1,0:T(8,128)(2,1)}, bf16[1152,512]{1,0:T(8,128)(2,1)}, u32[]{:S(2)}, u32[]{:S(2)}) collective-permute-start(bf16[1152,512]{1,0:T(8,128)(2,1)} %bitcast.58), channel_id=1, source_target_pairs={{0,1},{1,0},{2,3},{3,2},{4,5},{5,4},{6,7},{7,6},{8,9},{9,8},{10,11... | collective-permute-start | bytes 3538952 | tf_op jit(solution)/shard_map/ppermute | solution.py:62
  192.9 71.7 %copy-start.10 = (f32[144,1024]{1,0:T(8,128)}, f32[144,1024]{1,0:T(8,128)S(1)}, u32[]{:S(2)}) copy-start(f32[144,1024]{1,0:T(8,128)S(1)} %get-tuple-element.198) | copy-start | bytes 1769476
  193.1 8.9 %collective-permute-start.22 = (bf16[144,1024]{1,0:T(8,128)(2,1)S(1)}, bf16[144,1024]{1,0:T(8,128)(2,1)S(1)}, u32[]{:S(2)}, u32[]{:S(2)}) collective-permute-start(bf16[144,1024]{1,0:T(8,128)(2,1)S(1)} %multiply_convert_fusion.2), channel_id=1, source_target_pairs={{0,4},{1,5},{2,6},{3,7},{4,0},{5,1},{6,2},{7,3},{8,12},{9,13},{10,... | collective-permute-start | bytes 884744 | tf_op jit(solution)/shard_map/ppermute | solution.py:62
  201.9 14.4 %copy-start.44 = (bf16[144,1024]{1,0:T(8,128)(2,1)}, bf16[144,1024]{1,0:T(8,128)(2,1)S(1)}, u32[]{:S(2)}) copy-start(bf16[144,1024]{1,0:T(8,128)(2,1)S(1)} %collective-permute-done.22) | copy-start | bytes 884740
  202.0 14.4 %collective-permute-start.23 = (bf16[288,1024]{1,0:T(8,128)(2,1)S(1)}, bf16[288,1024]{1,0:T(8,128)(2,1)S(1)}, u32[]{:S(2)}, u32[]{:S(2)}) collective-permute-start(bf16[288,1024]{1,0:T(8,128)(2,1)S(1)} %pad_maximum_fusion.26), channel_id=1, source_target_pairs={{0,2},{1,3},{2,0},{3,1},{4,6},{5,7},{6,4},{7,5},{8,10},{9,11},{10,... | collective-permute-start | bytes 1769480 | tf_op jit(solution)/shard_map/ppermute | solution.py:62
  205.0 12.6 %copy-start.6 = (bf16[176,3072]{0,1:T(8,128)(2,1)S(1)}, bf16[176,3072]{0,1:T(8,128)(2,1)}, u32[]{:S(2)}) copy-start(bf16[176,3072]{0,1:T(8,128)(2,1)} %copy-done.5) | copy-start | bytes 3244036
  205.0 18.3 %collective-permute-start.25 = (bf16[576,1024]{1,0:T(8,128)(2,1)}, bf16[576,1024]{1,0:T(8,128)(2,1)}, u32[]{:S(2)}, u32[]{:S(2)}) collective-permute-start(bf16[576,1024]{1,0:T(8,128)(2,1)} %pad_maximum_fusion.13), channel_id=1, source_target_pairs={{0,1},{1,0},{2,3},{3,2},{4,5},{5,4},{6,7},{7,6},{8,9},{9,8},{10,11... | collective-permute-start | bytes 3538952 | tf_op jit(solution)/shard_map/ppermute | solution.py:62
  217.5 8.6 %collective-permute-start.24 = (bf16[576,1024]{1,0:T(8,128)(2,1)}, bf16[576,1024]{1,0:T(8,128)(2,1)}, u32[]{:S(2)}, u32[]{:S(2)}) collective-permute-start(bf16[576,1024]{1,0:T(8,128)(2,1)} %pad_maximum_fusion.12), channel_id=1, source_target_pairs={{0,1},{1,0},{2,3},{3,2},{4,5},{5,4},{6,7},{7,6},{8,9},{9,8},{10,11... | collective-permute-start | bytes 3538952 | tf_op jit(solution)/shard_map/ppermute | solution.py:62
  236.3 3.0 collective-permute-start.26
  238.6 19.0 %collective-permute-start.29 = (bf16[576,1024]{1,0:T(8,128)(2,1)S(1)}, bf16[576,1024]{1,0:T(8,128)(2,1)S(1)}, u32[]{:S(2)}, u32[]{:S(2)}) collective-permute-start(bf16[576,1024]{1,0:T(8,128)(2,1)S(1)} %fusion.22), channel_id=1, source_target_pairs={{0,1},{1,0},{2,3},{3,2},{4,5},{5,4},{6,7},{7,6},{8,9},{9,8},{10,11... | collective-permute-start | bytes 3538952 | tf_op jit(solution)/shard_map/ppermute | solution.py:62
  239.9 15.7 %collective-permute-start.27 = (bf16[288,1024]{1,0:T(8,128)(2,1)S(1)}, bf16[288,1024]{1,0:T(8,128)(2,1)S(1)}, u32[]{:S(2)}, u32[]{:S(2)}) collective-permute-start(bf16[288,1024]{1,0:T(8,128)(2,1)S(1)} %fusion.32), channel_id=1, source_target_pairs={{0,2},{1,3},{2,0},{3,1},{4,6},{5,7},{6,4},{7,5},{8,10},{9,11},{10,... | collective-permute-start | bytes 1769480 | tf_op jit(solution)/shard_map/ppermute | solution.py:62
  255.8 8.6 %collective-permute-start.28 = (bf16[144,1024]{1,0:T(8,128)(2,1)S(1)}, bf16[144,1024]{1,0:T(8,128)(2,1)S(1)}, u32[]{:S(2)}, u32[]{:S(2)}) collective-permute-start(bf16[144,1024]{1,0:T(8,128)(2,1)S(1)} %fusion.54), channel_id=1, source_target_pairs={{0,4},{1,5},{2,6},{3,7},{4,0},{5,1},{6,2},{7,3},{8,12},{9,13},{10,... | collective-permute-start | bytes 884744 | tf_op jit(solution)/shard_map/ppermute | solution.py:62
  271.0 14.4 %all-to-all-start.2 = ((bf16[16,72,128]{2,1,0:T(8,128)(2,1)}), bf16[16,72,128]{2,1,0:T(8,128)(2,1)S(1)}, u32[]{:S(2)}, u32[]{:S(2)}) async-start(bf16[16,72,128]{2,1,0:T(8,128)(2,1)} %bitcast.435), calls=%async_computation.2 | async-start | bytes 589824 | tf_op jit(solution)/shard_map/all_to_all | solution.py:593
  286.1 15.4 %collective-permute-start.30 = (bf16[288,1024]{1,0:T(8,128)(2,1)}, bf16[288,1024]{1,0:T(8,128)(2,1)}, u32[]{:S(2)}, u32[]{:S(2)}) collective-permute-start(bf16[288,1024]{1,0:T(8,128)(2,1)} %fusion.33), channel_id=1, source_target_pairs={{0,2},{1,3},{2,0},{3,1},{4,6},{5,7},{6,4},{7,5},{8,10},{9,11},{10,... | collective-permute-start | bytes 1769480 | tf_op jit(solution)/shard_map/ppermute | solution.py:62
  287.1 15.9 %copy-start.8 = (bf16[3,2,32,1024]{3,2,1,0:T(8,128)(2,1)S(1)}, bf16[3,2,32,1024]{3,2,1,0:T(8,128)(2,1)}, u32[]{:S(2)}) copy-start(bf16[3,2,32,1024]{3,2,1,0:T(8,128)(2,1)} %copy-done.7) | copy-start | bytes 1179652
  304.5 7.7 %collective-permute-start.31 = (bf16[1152,512]{1,0:T(8,128)(2,1)S(1)}, bf16[1152,512]{1,0:T(8,128)(2,1)}, u32[]{:S(2)}, u32[]{:S(2)}) collective-permute-start(bf16[1152,512]{1,0:T(8,128)(2,1)S(1)} %convolution_convert_fusion.2), channel_id=1, source_target_pairs={{0,1},{1,0},{2,3},{3,2},{4,5},{5,4},{6,7},{7,6},{8,9},{9,8},{10,11... | collective-permute-start | bytes 3538952 | tf_op jit(solution)/shard_map/ppermute | solution.py:62
  304.9 9.3 %collective-permute-start.38 = (bf16[1152,512]{1,0:T(8,128)(2,1)}, bf16[1152,512]{1,0:T(8,128)(2,1)}, u32[]{:S(2)}, u32[]{:S(2)}) collective-permute-start(bf16[1152,512]{1,0:T(8,128)(2,1)} %convolution_convert_fusion.1), channel_id=1, source_target_pairs={{0,1},{1,0},{2,3},{3,2},{4,5},{5,4},{6,7},{7,6},{8,9},{9,8},{10,11... | collective-permute-start | bytes 3538952 | tf_op jit(solution)/shard_map/ppermute | solution.py:62
  305.9 28.4 %collective-permute-start.33 = (bf16[176,3072]{1,0:T(8,128)(2,1)}, bf16[176,3072]{1,0:T(8,128)(2,1)}, u32[]{:S(2)}, u32[]{:S(2)}) collective-permute-start(bf16[176,3072]{1,0:T(8,128)(2,1)} %slice.349), channel_id=1, source_target_pairs={{0,16},{16,0},{1,17},{17,1},{2,18},{18,2},{3,19},{19,3},{4,20},{20... | collective-permute-start | bytes 3244040 | tf_op jit(solution)/shard_map/ppermute | solution.py:62
  316.0 16.4 %collective-permute-start.39 = (bf16[576,512]{1,0:T(8,128)(2,1)S(1)}, bf16[576,512]{1,0:T(8,128)(2,1)S(1)}, u32[]{:S(2)}, u32[]{:S(2)}) collective-permute-start(bf16[576,512]{1,0:T(8,128)(2,1)S(1)} %bitcast.440), channel_id=1, source_target_pairs={{0,4},{1,5},{2,6},{3,7},{4,0},{5,1},{6,2},{7,3},{8,12},{9,13},{10,... | collective-permute-start | bytes 1769480 | tf_op jit(solution)/shard_map/ppermute | solution.py:62
  317.4 14.7 %collective-permute-start.32 = (bf16[576,512]{1,0:T(8,128)(2,1)S(1)}, bf16[576,512]{1,0:T(8,128)(2,1)S(1)}, u32[]{:S(2)}, u32[]{:S(2)}) collective-permute-start(bf16[576,512]{1,0:T(8,128)(2,1)S(1)} %bitcast.441), channel_id=1, source_target_pairs={{0,2},{1,3},{2,0},{3,1},{4,6},{5,7},{6,4},{7,5},{8,10},{9,11},{10,... | collective-permute-start | bytes 1769480 | tf_op jit(solution)/shard_map/ppermute | solution.py:62
  325.3 24.3 %collective-permute-start.35 = (bf16[96,1024]{1,0:T(8,128)(2,1)S(1)}, bf16[96,1024]{1,0:T(8,128)(2,1)S(1)}, u32[]{:S(2)}, u32[]{:S(2)}) collective-permute-start(bf16[96,1024]{1,0:T(8,128)(2,1)S(1)} %bitcast.447), channel_id=1, source_target_pairs={{0,0},{16,1},{2,2},{18,3},{4,4},{20,5},{6,6},{22,7},{8,8},{24,9},{... | collective-permute-start | bytes 589832 | tf_op jit(solution)/shard_map/ppermute | solution.py:664
  326.2 23.4 %collective-permute-start.36 = (bf16[96,1024]{1,0:T(8,128)(2,1)S(1)}, bf16[96,1024]{1,0:T(8,128)(2,1)S(1)}, u32[]{:S(2)}, u32[]{:S(2)}) collective-permute-start(bf16[96,1024]{1,0:T(8,128)(2,1)S(1)} %bitcast.446), channel_id=1, source_target_pairs={{16,0},{0,1},{18,2},{2,3},{20,4},{4,5},{22,6},{6,7},{24,8},{8,9},{... | collective-permute-start | bytes 589832 | tf_op jit(solution)/shard_map/ppermute | solution.py:664
  332.6 14.8 %collective-permute-start.40 = (bf16[288,512]{1,0:T(8,128)(2,1)S(1)}, bf16[288,512]{1,0:T(8,128)(2,1)S(1)}, u32[]{:S(2)}, u32[]{:S(2)}) collective-permute-start(bf16[288,512]{1,0:T(8,128)(2,1)S(1)} %fusion.55), channel_id=1, source_target_pairs={{0,8},{1,9},{2,10},{3,11},{4,12},{5,13},{6,14},{7,15},{8,0},{9,1},... | collective-permute-start | bytes 884744 | tf_op jit(solution)/shard_map/ppermute | solution.py:62
  334.2 15.2 %collective-permute-start.34 = (bf16[288,512]{1,0:T(8,128)(2,1)S(1)}, bf16[288,512]{1,0:T(8,128)(2,1)S(1)}, u32[]{:S(2)}, u32[]{:S(2)}) collective-permute-start(bf16[288,512]{1,0:T(8,128)(2,1)S(1)} %bitcast.445), channel_id=1, source_target_pairs={{0,4},{1,5},{2,6},{3,7},{4,0},{5,1},{6,2},{7,3},{8,12},{9,13},{10,... | collective-permute-start | bytes 884744 | tf_op jit(solution)/shard_map/ppermute | solution.py:62
  347.6 5.3 %collective-permute-start.41 = (bf16[144,512]{1,0:T(8,128)(2,1)S(1)}, bf16[144,512]{1,0:T(8,128)(2,1)S(1)}, u32[]{:S(2)}, u32[]{:S(2)}) collective-permute-start(bf16[144,512]{1,0:T(8,128)(2,1)S(1)} %fusion.67), channel_id=1, source_target_pairs={{0,2},{1,3},{2,0},{3,1},{4,6},{5,7},{6,4},{7,5},{8,10},{9,11},{10,... | collective-permute-start | bytes 442376 | tf_op jit(solution)/shard_map/ppermute | solution.py:62
  349.6 8.6 %collective-permute-start.37 = (bf16[144,512]{1,0:T(8,128)(2,1)S(1)}, bf16[144,512]{1,0:T(8,128)(2,1)S(1)}, u32[]{:S(2)}, u32[]{:S(2)}) collective-permute-start(bf16[144,512]{1,0:T(8,128)(2,1)S(1)} %fusion.66), channel_id=1, source_target_pairs={{0,8},{1,9},{2,10},{3,11},{4,12},{5,13},{6,14},{7,15},{8,0},{9,1},... | collective-permute-start | bytes 442376 | tf_op jit(solution)/shard_map/ppermute | solution.py:62
  366.0 8.5 %collective-permute-start.42 = (bf16[512,1408]{1,0:T(8,128)(2,1)S(1)}, bf16[512,1408]{1,0:T(8,128)(2,1)S(1)}, u32[]{:S(2)}, u32[]{:S(2)}) collective-permute-start(bf16[512,1408]{1,0:T(8,128)(2,1)S(1)} %bitcast.426), channel_id=1, source_target_pairs={{0,1},{1,0},{2,3},{3,2},{4,5},{5,4},{6,7},{7,6},{8,9},{9,8},{10,11... | collective-permute-start | bytes 4325384 | tf_op jit(solution)/shard_map/ppermute | solution.py:62
  368.7 26.1 %collective-permute-start.44 = (bf16[88,3072]{1,0:T(8,128)(2,1)S(1)}, bf16[88,3072]{1,0:T(8,128)(2,1)S(1)}, u32[]{:S(2)}, u32[]{:S(2)}) collective-permute-start(bf16[88,3072]{1,0:T(8,128)(2,1)S(1)} %copy-done.49), channel_id=1, source_target_pairs={{0,8},{1,9},{2,10},{3,11},{4,12},{5,13},{6,14},{7,15},{8,0},{9,1},... | collective-permute-start | bytes 1622024 | tf_op jit(solution)/shard_map/ppermute | solution.py:62
  369.4 29.4 %collective-permute-start.45 = (bf16[144,1024]{1,0:T(8,128)(2,1)}, bf16[144,1024]{1,0:T(8,128)(2,1)}, u32[]{:S(2)}, u32[]{:S(2)}) collective-permute-start(bf16[144,1024]{1,0:T(8,128)(2,1)} %fusion.56), channel_id=1, source_target_pairs={{0,4},{1,5},{2,6},{3,7},{4,0},{5,1},{6,2},{7,3},{8,12},{9,13},{10,... | collective-permute-start | bytes 884744 | tf_op jit(solution)/shard_map/ppermute | solution.py:62
  371.7 3.5 collective-permute-start.47
  374.9 18.6 %collective-permute-start.43 = (bf16[256,1408]{1,0:T(8,128)(2,1)S(1)}, bf16[256,1408]{1,0:T(8,128)(2,1)S(1)}, u32[]{:S(2)}, u32[]{:S(2)}) collective-permute-start(bf16[256,1408]{1,0:T(8,128)(2,1)S(1)} %bitcast.437), channel_id=1, source_target_pairs={{0,2},{1,3},{2,0},{3,1},{4,6},{5,7},{6,4},{7,5},{8,10},{9,11},{10,... | collective-permute-start | bytes 2162696 | tf_op jit(solution)/shard_map/ppermute | solution.py:62
  375.7 20.1 %collective-permute-start.48 = (bf16[256,1408]{1,0:T(8,128)(2,1)S(1)}, bf16[256,1408]{1,0:T(8,128)(2,1)S(1)}, u32[]{:S(2)}, u32[]{:S(2)}) collective-permute-start(bf16[256,1408]{1,0:T(8,128)(2,1)S(1)} %fusion.29), channel_id=1, source_target_pairs={{0,16},{16,0},{1,17},{17,1},{2,18},{18,2},{3,19},{19,3},{4,20},{20... | collective-permute-start | bytes 2162696 | tf_op jit(solution)/shard_map/ppermute | solution.py:62
  396.8 10.7 %collective-permute-start.49 = (bf16[128,1408]{1,0:T(8,128)(2,1)}, bf16[128,1408]{1,0:T(8,128)(2,1)}, u32[]{:S(2)}, u32[]{:S(2)}) collective-permute-start(bf16[128,1408]{1,0:T(8,128)(2,1)} %bitcast.149), channel_id=1, source_target_pairs={{0,2},{1,3},{2,0},{3,1},{4,6},{5,7},{6,4},{7,5},{8,10},{9,11},{10,... | collective-permute-start | bytes 1081352 | tf_op jit(solution)/shard_map/ppermute | solution.py:62
  398.9 10.3 %collective-permute-start.46 = (bf16[128,1408]{1,0:T(8,128)(2,1)}, bf16[128,1408]{1,0:T(8,128)(2,1)S(1)}, u32[]{:S(2)}, u32[]{:S(2)}) collective-permute-start(bf16[128,1408]{1,0:T(8,128)(2,1)} %fusion.50), channel_id=1, source_target_pairs={{0,16},{16,0},{1,17},{17,1},{2,18},{18,2},{3,19},{19,3},{4,20},{20... | collective-permute-start | bytes 1081352 | tf_op jit(solution)/shard_map/ppermute | solution.py:62
  410.1 9.5 %collective-permute-start.50 = (bf16[64,2816]{1,0:T(8,128)(2,1)}, bf16[64,2816]{1,0:T(8,128)(2,1)}, u32[]{:S(2)}, u32[]{:S(2)}) collective-permute-start(bf16[64,2816]{1,0:T(8,128)(2,1)} %bitcast.152), channel_id=1, source_target_pairs={{0,4},{1,5},{2,6},{3,7},{4,0},{5,1},{6,2},{7,3},{8,12},{9,13},{10,... | collective-permute-start | bytes 1081352 | tf_op jit(solution)/shard_map/ppermute | solution.py:62
  412.7 24.3 %all-to-all-start.3 = ((f32[32,32,88]{2,1,0:T(8,128)}), f32[32,32,88]{2,1,0:T(8,128)S(1)}, u32[]{:S(2)}, u32[]{:S(2)}) async-start(f32[32,32,88]{2,1,0:T(8,128)} %bitcast.136), calls=%async_computation.3 | async-start | bytes 1048576 | tf_op jit(solution)/shard_map/all_to_all | solution.py:720
  420.8 18.7 %collective-permute-start.51 = (bf16[32,2816]{1,0:T(8,128)(2,1)S(1)}, bf16[32,2816]{1,0:T(8,128)(2,1)S(1)}, u32[]{:S(2)}, u32[]{:S(2)}) collective-permute-start(bf16[32,2816]{1,0:T(8,128)(2,1)S(1)} %fusion.65), channel_id=1, source_target_pairs={{0,8},{1,9},{2,10},{3,11},{4,12},{5,13},{6,14},{7,15},{8,0},{9,1},... | collective-permute-start | bytes 540680 | tf_op jit(solution)/shard_map/ppermute | solution.py:62
  (58 other events, 283.8 us)

commit v5 on v4

--- a/solution.py
+++ b/solution.py
@@ -330,6 +330,20 @@
             pl.when(odd == 1)(lambda: put(dother_ref))
 
 
+def mix_kernel(chips, twins, got_ref, weight_ref, resid_ref, gain_ref, mixed_ref, sum_ref, norm_ref):
+    tok, packed = got_ref.shape[1:]
+    for twin in range(twins):
+        for row in range(packed // HEAD_DIM):
+            lanes = slice(row * HEAD_DIM, (row + 1) * HEAD_DIM)
+            slots = [which * twins + twin for which in range(HEADS)]
+            heads = [got_ref[2 * (slot % chips) + slot // chips, :, lanes] for slot in slots]
+            low = (twin * (packed // HEAD_DIM) + row) * tok
+            mixed_ref[low : low + tok, :] = jnp.concatenate(heads, axis=1)
+    total = resid_ref[...] + dot_nt(mixed_ref[...], weight_ref[...])
+    sum_ref[...] = total
+    norm_ref[...] = rms_norm(total, gain_ref[...]).astype(BF16)
+
+
 SMEM = pl.BlockSpec(memory_space=pltpu.SMEM)
 VMEM = pl.BlockSpec(memory_space=pltpu.VMEM)
 
@@ -385,6 +399,7 @@
     ).T
     wide = vit + 128
     half_in = (wide + d_model) // 256 * 128
+    half_back = wide // 256 * 128
     per_head = dev_count // HEADS
     twins = seq_count // HEADS
     chips = seq_count // 2
@@ -418,21 +433,22 @@
     up_got = swap(upstream, team[0])
     late = {}
 
-    def while_split(block):
-        block, late["down"] = together(block, down_in)
+    def far_gather(block):
+        for step in ff_far[:-1]:
+            block = jnp.concatenate([block, swap(block, step)], axis=0)
+        return block, swap(block, ff_far[-1])
+
+    gate_up, gate_up_got = far_gather(jnp.concatenate([w_gate.T, w_up.T], axis=1))
+
+    def while_near(block):
+        block, got = together(block, up_got)
+        late["up"] = jnp.concatenate([upstream, got], axis=0)
         return block
 
     def while_core(block):
-        block, send, gate, up, got = together(block, three, w_gate, w_up, up_got)
-        late["ff"] = jnp.concatenate(
-            [gate.T, up.T, late["down"].reshape(d_model, units).T], axis=1
-        )
-        for step in ff_far[:-1]:
-            late["ff"] = jnp.concatenate([late["ff"], swap(late["ff"], step)], axis=0)
-        late["ff_got"] = swap(late["ff"], ff_far[-1])
-        late["up"] = jnp.concatenate([upstream, got], axis=0)
+        block, late["gate_up"] = together(block, gate_up_got)
         late["up_got"] = swap(late["up"], team[1])
-        late["pieces"] = [lax.ppermute(send, BOTH, rounds(turn, False)) for turn in range(per_head)]
+        late["pieces"] = [lax.ppermute(three, BOTH, rounds(turn, False)) for turn in range(per_head)]
         return block
 
     pack = gather(pack, seq_high, True)
@@ -440,7 +456,7 @@
         pack[:, :half_in],
         dp_bits + [near, core],
         True,
-        {0: while_split, len(dp_bits) + 1: while_core},
+        {len(dp_bits): while_near, len(dp_bits) + 1: while_core},
         seq_high,
     )
     in_high = gather(pack[:, half_in:], [near] + dp_bits + [core], True, None, seq_high)
@@ -464,26 +480,21 @@
     half = d_model // 2
     order_low = seq_high + [near]
     order_high = [near] + seq_high
-    for piece in late["pieces"]:
-        normed_one = after(normed_one, piece)
+    normed_one, *late["pieces"] = together(normed_one, *late["pieces"])
 
     def while_start(block):
-        block, late["ff_got"], late["up_got"] = together(block, late["ff_got"], late["up_got"])
+        block, late["up_got"] = together(block, late["up_got"])
         return block
 
     own_low = gather(normed_one[:, :half], order_low, False, {0: while_start})
-    ff_block = jnp.concatenate([late["ff"], late["ff_got"]], axis=0)
+    gate_up = jnp.concatenate([gate_up, late["gate_up"]], axis=0)
     for step in dp_bits[:-1]:
-        ff_block = jnp.concatenate([ff_block, swap(ff_block, step)], axis=0)
-    ff_got = swap(ff_block, dp_bits[-1])
+        gate_up = jnp.concatenate([gate_up, swap(gate_up, step)], axis=0)
+    gate_up_got = swap(gate_up, dp_bits[-1])
     team_up = jnp.concatenate([late["up"], late["up_got"]], axis=0)
     team_up = jnp.concatenate([team_up, swap(team_up, core)], axis=0)
     own_high = gather(normed_one[:, half:], order_high, False)
-    own_low, own_high, ff_got = together(own_low, own_high, ff_got)
-    full_gate, full_up, full_down = [
-        jnp.concatenate([array[:, which * d_model : (which + 1) * d_model] for array in (ff_block, ff_got)], axis=0)
-        for which in range(3)
-    ]
+    own_low, own_high = together(own_low, own_high)
     other_low, other_high = swap(own_low, core), swap(own_high, core)
 
     def my_rows(array):
@@ -509,6 +520,8 @@
         .reshape(chips, row_count, tok, 3 * HEAD_DIM)
         for low, high in normed_pairs
     ]
+    *qkv, down = together(*qkv, down_in)
+    full_down, down_got = far_gather(down.reshape(d_model, units).T)
     lengths = lax.dynamic_slice_in_dim(text_lengths, twin * row_count, row_count, 0)
     me = seq_index.reshape(1).astype(jnp.int32)
     dims = (row_count, images, patch_dev, text_dev, slots)
@@ -532,24 +545,60 @@
         1 << 20,
         20,
     )(me, lengths, bias, *qkv)
+    mixed, gate_up_got, down_got = together(mixed, gate_up_got, down_got)
+    full_gate, full_up = [
+        jnp.concatenate([array[:, part] for array in (gate_up, gate_up_got)], axis=0)
+        for part in (slice(0, d_model), slice(d_model, 2 * d_model))
+    ]
     mixed_got = lax.all_to_all(mixed, SEQ, 0, 0, tiled=True)
-    mixed_got = mixed_got.reshape(chips, 2, tok, row_count, HEAD_DIM).swapaxes(0, 1)
-    mixed_got = mixed_got.reshape(HEADS, twins, tok, row_count, HEAD_DIM)
-    attn_out = jnp.transpose(mixed_got, (1, 3, 2, 0, 4)).reshape(mine, d_model)
-    resid_one = resid + dot_nt(attn_out, full_out)
-    normed_two = rms_norm(resid_one, gain_two).astype(BF16)
+    full_down = jnp.concatenate([full_down, down_got], axis=0)
+    for step in dp_bits[:-1]:
+        full_down = jnp.concatenate([full_down, swap(full_down, step)], axis=0)
+    full_down = jnp.concatenate([full_down, swap(full_down, dp_bits[-1])], axis=0)
+    attn_out, resid_one, normed_two = call(
+        lambda *refs: mix_kernel(chips, twins, *refs),
+        (
+            jax.ShapeDtypeStruct((mine, d_model), BF16),
+            jax.ShapeDtypeStruct((mine, d_model), F32),
+            jax.ShapeDtypeStruct((mine, d_model), BF16),
+        ),
+        [VMEM, VMEM, VMEM, VMEM],
+        (),
+        1 << 24,
+        1 << 20,
+        12,
+    )(mixed_got, full_out, resid, gain_two[None])
     team_normed = normed_two
     for step in team:
-        team_normed = jnp.concatenate([team_normed, swap(team_normed, step)], axis=0)
+        got = swap(team_normed, step)
+        if step == near:
+            team_normed, full_gate, full_up, full_down = together(
+                team_normed, full_gate, full_up, full_down
+            )
+        team_normed = jnp.concatenate([team_normed, got], axis=0)
     gate_pre = dot_nt(team_normed, full_gate)
     up_pre = dot_nt(team_normed, full_up)
     hidden, gated_back = jax.vjp(gated_unit, gate_pre, up_pre)
     hidden = hidden.astype(BF16)
 
+    state = {}
+    grad_down = dot_tn(hidden, team_up).astype(BF16)
+
+    def down_start(step):
+        count = grad_down_of["sum"].shape[0] // 2
+        grad_down_of["keep"] = grad_down_of["sum"][:count]
+        grad_down_of["got"] = swap(grad_down_of["sum"][count:].astype(BF16), step)
+
+    def down_take(keep):
+        keep, got = together(keep, grad_down_of["got"])
+        grad_down_of["sum"] = grad_down_of["keep"].astype(F32) + got.astype(F32)
+        return keep
+
+    grad_down_of = {"sum": grad_down}
+    down_start(dp_bits[-1])
     d_gate, d_up = gated_back(dot_nt(team_up, full_down))
     d_gate, d_up = d_gate.astype(BF16), d_up.astype(BF16)
     d_normed_two = dot_nn(d_gate, full_gate) + dot_nn(d_up, full_up)
-    state = {}
 
     def ff_take(keep):
         keep, got = together(keep, state["ff_got"])
@@ -564,13 +613,14 @@
         return keep
 
     def while_team(keep):
-        keep, *grads = together(keep, d_gate, d_up, hidden)
+        keep = down_take(keep)
+        for step in dp_bits[-2::-1] + ff_far[:0:-1]:
+            down_start(step)
+            keep = down_take(keep)
+        down_start(ff_far[0])
+        keep, *grads = together(keep, d_gate, d_up)
         state["ff"] = jnp.concatenate(
-            [
-                dot_tn(grad, of).astype(BF16)
-                for grad, of in zip(grads, (team_normed, team_normed, team_up))
-            ],
-            axis=1,
+            [dot_tn(grad, team_normed).astype(BF16) for grad in grads], axis=1
         )
         return ff_start(keep, dp_bits[-1])
 
@@ -592,10 +642,23 @@
     d_attn = d_attn.swapaxes(0, 1).reshape(packed_shape.shape)
     d_attn_got = lax.all_to_all(d_attn, SEQ, 0, 0, tiled=True)
 
-    out_grad = dot_tn(d_mix, attn_out).astype(BF16)
+    out_grad = {"sum": dot_tn(d_mix, attn_out).astype(BF16), "left": list(every)}
+
+    def out_grad_start(keep, step):
+        out_grad["keep"], send = halves(out_grad["sum"], step, out_grad["left"], True)
+        keep, send = together(keep, send.astype(BF16))
+        out_grad["got"] = swap(send, step)
+        return keep
+
+    def out_grad_take(keep, step):
+        keep, got = together(keep, out_grad["got"])
+        out_grad["sum"] = out_grad["keep"].astype(F32) + got.astype(F32)
+        out_grad["left"].remove(step)
+        return keep
+
     out_part = team_sum(dot_nn(hidden, full_down), core)
     out_keep, send = halves(out_part, team[1], [team[1]], False)
-    d_attn_got, out_grad, send = together(d_attn_got, out_grad, send.astype(BF16))
+    d_attn_got, send = together(out_grad_start(d_attn_got, core), send.astype(BF16))
     out_got = swap(send, team[1])
     half_shape = jax.ShapeDtypeStruct(qkv[0].shape, BF16)
     d_own, d_other, d_bias = call(
@@ -614,8 +677,10 @@
         1 << 20,
         28,
     )(me, lengths, bias, *qkv, d_attn_got)
-    d_other, out_got = together(d_other, out_got)
+    d_other, out_got = together(down_take(d_other), out_got)
     out_part = out_keep + out_got.astype(F32)
+    down_back = grad_down_of["sum"].T.reshape(dev_count, cols, units)
+    state["down_back"] = lax.all_to_all(down_back, BOTH, 0, 0, tiled=True)
     d_qkv = [array.reshape(chips * row_count * tok, 3 * HEAD_DIM) for array in (d_own, d_other)]
 
     def all_rows(array):
@@ -640,9 +705,13 @@
             keep = ff_take(ff_start(keep, step))
         for step in ff_far[:0:-1]:
             keep = ff_take(ff_start(keep, step))
-        return keep
+        keep = out_grad_take(keep, dp_bits[-1])
+        for step in dp_bits[-2::-1]:
+            keep = out_grad_take(out_grad_start(keep, step), step)
+        return out_grad_start(keep, near)
 
     def while_middle(keep):
+        keep = out_grad_start(out_grad_take(keep, core), dp_bits[-1])
         keep, grads_own, grads_other = together(keep, *d_qkv)
         d_head = jnp.concatenate(
             [
@@ -667,7 +736,7 @@
 
     def while_late(keep):
         keep, *state["three"] = together(keep, *state["three"])
-        return keep
+        return out_grad_take(keep, near)
 
     low_sums = scatter_add(owns[0], order_low[::-1], chip_bits, False, {0: while_middle, 1: while_first, len(order_low) - 1: while_late})
     high_sums = scatter_add(owns[1], order_high[::-1], chip_bits, False)
@@ -713,11 +782,7 @@
         return keep
 
     def while_half_again(keep):
-        keep = ff_take(keep)
-        down = state["ff"][:, 2 * d_model :]
-        down_back = down.T.reshape(dev_count, cols, units)
-        keep, down_back, state["out_got"] = together(keep, down_back, state["out_got"])
-        state["down_back"] = lax.all_to_all(down_back, BOTH, 0, 0, tiled=True)
+        keep, state["out_got"] = together(ff_take(keep), state["out_got"])
         return keep
 
     def while_end(keep):
@@ -725,24 +790,24 @@
         return keep
 
     in_low_sums = scatter_add(
-        dot_tn(left, right[:, :half_in]).astype(BF16),
+        dot_tn(left, right[:, :half_back]).astype(BF16),
         [core, near] + dp_bits[::-1],
         every,
         True,
         {0: while_core_again, 2: while_half_again},
     )
     in_high_sums = scatter_add(
-        jnp.concatenate([dot_tn(left, right[:, half_in:]).astype(BF16), out_grad], axis=1),
+        dot_tn(left, right[:, half_back:]).astype(BF16),
         [core] + dp_bits[::-1] + [near],
         every,
         True,
     )
     in_grads = scatter_add(
-        jnp.concatenate([in_low_sums, in_high_sums], axis=1),
+        jnp.concatenate([in_low_sums, in_high_sums, out_grad["sum"]], axis=1),
         seq_high[::-1],
         seq_high,
         True,
-        {len(seq_high) - 1: while_end},
+        {0: while_end},
     )
     small_out, grad_w_out = in_grads[:, vit:wide], in_grads[:, wide:]
     d_low = state["d_low"]
@@ -751,8 +816,7 @@
     ).reshape(rows, patch_dev, vit)
     result = resid_one + state["out_keep"] + state["out_got"].astype(F32)
     result = result.astype(BF16).reshape(rows, tok, d_model)
-    grad_gate = state["ff"][:, :d_model]
-    grad_up = state["ff"][:, d_model : 2 * d_model]
+    grad_gate, grad_up = state["ff"][:, :d_model], state["ff"][:, d_model:]
     grad_down = jnp.transpose(state["down_back"], (0, 2, 1)).reshape(dev_count * units, cols)
     grad_down = grad_down.astype(F32)
     d_three = sum(got.astype(F32) for got in state["three"]).reshape(3, cols, d_model)

time: 448 us -> 421 us (0.940)
  matrix products: 55 us -> 37.8 us
  blocking collectives: 16.1 us -> 0 us
  local copies, waits for them, and re-layouts: 60.9 us -> 48.4 us
  starting transfers between devices: 63.4 us -> 74.6 us
  waiting for transfers between devices: 174 us -> 180 us
    ppermute x48 -> x55, waiting for transfers between devices: 148 us -> 168 us  [swap(): return lax.ppermute(array, axis, [(i, i ^ 1 << bit) for i in range(count)])]
    all_to_all x1 -> x0, blocking collectives: 16.1 us -> none  [local(): mixed_got = lax.all_to_all(mixed, SEQ, 0, 0, tiled=True)]
    ppermute x48 -> x55, starting transfers between devices: 42.8 us -> 54 us  [swap(): return lax.ppermute(array, axis, [(i, i ^ 1 << bit) for i in range(count)])]
    all_to_all x1 -> x2, waiting for transfers between devices: 15.2 us -> 6.56 us  [the longest x1 6.56 us: local(): mixed_got = lax.all_to_all(mixed, SEQ, 0, 0, tiled=True)]
    dot_general x10, matrix products: 19.8 us -> 11.2 us  [dot_tn(): lax.dot_general(left, right, (((0,), (0,)), ((), ())), preferred_element_...]
    unnamed x135 -> x148, local copies, waits for them, and re-layouts: 6.5 us -> 14.3 us
    dot_general x11 -> x10, matrix products: 21 us -> 13.4 us  [dot_nt(): lax.dot_general(left, right, (((1,), (1,)), ((), ())), preferred_element_...]
    optimization_barrier x4 -> x0, local copies, waits for them, and re-layouts: 7.26 us -> none  [together(): return lax.optimization_barrier(arrays)]
  transfers between devices with their start and end apart: 55 -> 63, of which waited for: 30 -> 34; matrix products, arithmetic and copies ran while one was open for 24% -> 22% of each run, Pallas kernels for 4% -> 7%
where the time goes in v5:
time: 421 us; the launch traced here: 413 us
  waiting for transfers between devices  180 us (43%)
  starting transfers between devices  74.6 us (18%)
  local copies, waits for them, and re-layouts  48.4 us (11%)
  other arithmetic  39.4 us (9%)
  matrix products  37.8 us (9%)
  Pallas kernels  29.5 us (7%)
    ppermute x55, waiting for transfers between devices, swap(): return lax.ppermute(array, axis, [(i, i ^ 1 << bit) for i in range(count)])  168 us
    ppermute x55, starting transfers between devices, swap(): return lax.ppermute(array, axis, [(i, i ^ 1 << bit) for i in range(count)])  54 us
    pallas_call x1, Pallas kernels, local(): call(lambda *refs: backward_kernel(dims, *refs), (half_shape, half_shape,...  14.6 us
    unnamed x148, local copies, waits for them, and re-layouts  14.3 us
    dot_general x10, matrix products, dot_nt(): lax.dot_general(left, right, (((1,), (1,)), ((), ())), preferred_element_...  13.4 us
    dot_general x10, matrix products, dot_nn(): lax.dot_general(left, right, (((1,), (0,)), ((), ())), preferred_element_...  13.1 us
    pallas_call x1, Pallas kernels, local(): call(lambda *refs: forward_kernel(dims, *refs), packed_shape, [SMEM, SMEM...  11.5 us
    dot_general x10, matrix products, dot_tn(): lax.dot_general(left, right, (((0,), (0,)), ((), ())), preferred_element_...  11.2 us
  transfers between devices with their start and end apart: 63, of which 34 were waited for; matrix products, arithmetic and copies ran while one was open for 22% of the time, Pallas kernels for 7%

profile of v5, /device:TPU:0, one launch (start us, length us, event | category | flops | bytes accessed | tf_op | source)
XLA Modules:
  0.0 413.5 jit_solution(18324081596897110977)
XLA Ops:
  4.7 4.1 collective-permute-start
  8.8 8.4 %collective-permute-done = bf16[32,2816]{1,0:T(8,128)(2,1)S(1)} collective-permute-done((bf16[32,2816]{1,0:T(8,128)(2,1)S(1)}, bf16[32,2816]{1,0:T(8,128)(2,1)S(1)}, u32[]{:S(2)}, u32[]{:S(2)}) %collective-permute-start) | collective-permute-done | bytes 180256 | tf_op jit(solution)/shard_map/ppermute | solution.py:62
  18.0 8.9 %collective-permute-done.1 = bf16[64,2816]{1,0:T(8,128)(2,1)S(1)} collective-permute-done((bf16[64,2816]{1,0:T(8,128)(2,1)S(1)}, bf16[64,2816]{1,0:T(8,128)(2,1)S(1)}, u32[]{:S(2)}, u32[]{:S(2)}) %collective-permute-start.1) | collective-permute-done | bytes 360480 | tf_op jit(solution)/shard_map/ppermute | solution.py:62
  30.0 5.9 %collective-permute-done.5 = bf16[128,1408]{1,0:T(8,128)(2,1)S(1)} collective-permute-done((bf16[128,1408]{1,0:T(8,128)(2,1)S(1)}, bf16[128,1408]{1,0:T(8,128)(2,1)S(1)}, u32[]{:S(2)}, u32[]{:S(2)}) %collective-permute-start.5) | collective-permute-done | bytes 360480 | tf_op jit(solution)/shard_map/ppermute | solution.py:62
  38.7 2.5 collective-permute-start.7
  41.3 4.9 %collective-permute-done.7 = bf16[144,1024]{1,0:T(8,128)(2,1)S(1)} collective-permute-done((bf16[144,1024]{1,0:T(8,128)(2,1)S(1)}, bf16[144,1024]{1,0:T(8,128)(2,1)S(1)}, u32[]{:S(2)}, u32[]{:S(2)}) %collective-permute-start.7) | collective-permute-done | bytes 294944 | tf_op jit(solution)/shard_map/ppermute | solution.py:62
  46.8 5.6 %collective-permute-done.6 = bf16[256,1408]{1,0:T(8,128)(2,1)S(1)} collective-permute-done((bf16[256,1408]{1,0:T(8,128)(2,1)S(1)}, bf16[256,1408]{1,0:T(8,128)(2,1)S(1)}, u32[]{:S(2)}, u32[]{:S(2)}) %collective-permute-start.6) | collective-permute-done | bytes 720928 | tf_op jit(solution)/shard_map/ppermute | solution.py:62
  52.9 8.4 %collective-permute-done.3 = bf16[256,1408]{1,0:T(8,128)(2,1)S(1)} collective-permute-done((bf16[256,1408]{1,0:T(8,128)(2,1)S(1)}, bf16[256,1408]{1,0:T(8,128)(2,1)S(1)}, u32[]{:S(2)}, u32[]{:S(2)}) %collective-permute-start.3) | collective-permute-done | bytes 720928 | tf_op jit(solution)/shard_map/ppermute | solution.py:62
  63.3 4.1 collective-permute-start.9
  68.1 3.0 collective-permute-start.10
  71.2 1.6 convert_element_type.298
  74.9 8.9 %collective-permute-done.9 = bf16[88,2048]{1,0:T(8,128)(2,1)} collective-permute-done((bf16[88,2048]{1,0:T(8,128)(2,1)}, bf16[88,2048]{1,0:T(8,128)(2,1)}, u32[]{:S(2)}, u32[]{:S(2)}) %collective-permute-start.9) | collective-permute-done | bytes 360480 | tf_op jit(solution)/shard_map/ppermute | solution.py:62
  84.3 2.3 broadcast_select_fusion.1
  93.8 6.5 %collective-permute-done.12 = bf16[288,1024]{1,0:T(8,128)(2,1)} collective-permute-done((bf16[288,1024]{1,0:T(8,128)(2,1)}, bf16[288,1024]{1,0:T(8,128)(2,1)}, u32[]{:S(2)}, u32[]{:S(2)}) %collective-permute-start.12) | collective-permute-done | bytes 589856 | tf_op jit(solution)/shard_map/ppermute | solution.py:62
  102.1 2.2 collective-permute-start.17
  104.2 10.8 %collective-permute-done.14 = bf16[288,512]{1,0:T(8,128)(2,1)S(1)} collective-permute-done((bf16[288,512]{1,0:T(8,128)(2,1)S(1)}, bf16[288,512]{1,0:T(8,128)(2,1)S(1)}, u32[]{:S(2)}, u32[]{:S(2)}) %collective-permute-start.14) | collective-permute-done | bytes 294944 | tf_op jit(solution)/shard_map/ppermute | solution.py:62
  117.6 11.7 %collective-permute-done.15 = bf16[576,512]{1,0:T(8,128)(2,1)S(1)} collective-permute-done((bf16[576,512]{1,0:T(8,128)(2,1)S(1)}, bf16[576,512]{1,0:T(8,128)(2,1)S(1)}, u32[]{:S(2)}, u32[]{:S(2)}) %collective-permute-start.15) | collective-permute-done | bytes 589856 | tf_op jit(solution)/shard_map/ppermute | solution.py:62
  130.9 1.8 reshape.523
  133.5 3.7 all-to-all-start
  137.7 1.9 pad_maximum_fusion.15
  139.6 1.7 collective-permute-start.21
  145.9 2.1 fusion.59
  148.0 1.8 fusion.1
  150.1 2.4 collective-permute-start.22
  153.8 11.5 %shard_map.289 = bf16[16,72,128]{2,1,0:T(8,128)(2,1)} custom-call(s32[1]{0:T(128)} %bitcast.refs_0_, s32[2,3]{1,0:T(2,128)S(1)} %copy-done.12, f32[448,512]{1,0:T(8,128)S(1)} %shard_map.288.refs_2_, bf16[8,2,72,192]{3,2,1,0:T(8,128)(2,1)S(1)} %bitcast.319, bf16[8,2,72,192]{3,2,1,0:T(8,128)(2,1)S(1)} %bitcast.321), custom_call_target="tpu_custom_call" | custom-call | flops 16777216 | bytes 1048576 | tf_op jit(solution)/shard_map/pallas_call | solution.py:534
  166.2 4.8 %all-to-all-start.1 = ((bf16[16,72,128]{2,1,0:T(8,128)(2,1)}), bf16[16,72,128]{2,1,0:T(8,128)(2,1)S(1)}, u32[]{:S(2)}, u32[]{:S(2)}) async-start(bf16[16,72,128]{2,1,0:T(8,128)(2,1)} %shard_map.289), calls=%async_computation.1 | async-start | bytes 589824 | tf_op jit(solution)/shard_map/all_to_all | solution.py:553
  171.0 2.0 fusion.82
  173.0 1.8 slice.331.refs_1_
  174.8 6.6 %all-to-all-done.1.refs_0_ = bf16[16,72,128]{2,1,0:T(8,128)(2,1)S(1)} async-done(((bf16[16,72,128]{2,1,0:T(8,128)(2,1)}), bf16[16,72,128]{2,1,0:T(8,128)(2,1)S(1)}, u32[]{:S(2)}, u32[]{:S(2)}) %all-to-all-start.1) | async-done | bytes 294944 | tf_op jit(solution)/shard_map/all_to_all | solution.py:553
  184.9 2.3 pad_maximum_fusion.9
  189.4 4.1 collective-permute-done.23
  197.3 5.5 %collective-permute-done.24 = bf16[176,1024]{0,1:T(8,128)(2,1)S(1)} collective-permute-done((bf16[176,1024]{0,1:T(8,128)(2,1)S(1)}, bf16[176,1024]{0,1:T(8,128)(2,1)S(1)}, u32[]{:S(2)}, u32[]{:S(2)}) %collective-permute-start.24) | collective-permute-done | bytes 360480 | tf_op jit(solution)/shard_map/ppermute | solution.py:62
  204.2 3.7 collective-permute-done.25
  210.0 2.6 fusion.34
  215.2 2.4 multiply_convert_fusion
  221.3 2.5 convolution_convert_fusion.7
  227.5 6.9 %collective-permute-done.29 = bf16[176,1024]{1,0:T(8,128)(2,1)S(1)} collective-permute-done((bf16[176,1024]{1,0:T(8,128)(2,1)S(1)}, bf16[176,1024]{1,0:T(8,128)(2,1)S(1)}, u32[]{:S(2)}, u32[]{:S(2)}) %collective-permute-start.29) | collective-permute-done | bytes 360480 | tf_op jit(solution)/shard_map/ppermute | solution.py:62
  234.3 1.7 collective-permute-start.30
  239.4 9.3 %collective-permute-done.30 = bf16[288,1024]{1,0:T(8,128)(2,1)S(1)} collective-permute-done((bf16[288,1024]{1,0:T(8,128)(2,1)S(1)}, bf16[288,1024]{1,0:T(8,128)(2,1)S(1)}, u32[]{:S(2)}, u32[]{:S(2)}) %collective-permute-start.30) | collective-permute-done | bytes 589856 | tf_op jit(solution)/shard_map/ppermute | solution.py:62
  249.0 1.8 collective-permute-start.31
  250.8 1.8 fusion.2
  252.6 3.6 collective-permute-done.31
  260.5 3.7 all-to-all-start.2
  264.3 2.2 fusion.23
  268.8 6.1 %all-to-all-done.2.refs_5_ = bf16[16,72,128]{2,1,0:T(8,128)(2,1)S(1)} async-done(((bf16[16,72,128]{2,1,0:T(8,128)(2,1)}), bf16[16,72,128]{2,1,0:T(8,128)(2,1)S(1)}, u32[]{:S(2)}, u32[]{:S(2)}) %all-to-all-start.2) | async-done | bytes 294944 | tf_op jit(solution)/shard_map/all_to_all | solution.py:643
  279.5 14.6 %shard_map.291 = (bf16[8,2,72,192]{3,2,1,0:T(8,128)(2,1)S(1)}, bf16[8,2,72,192]{3,2,1,0:T(8,128)(2,1)S(1)}, f32[448,512]{1,0:T(8,128)S(1)}) custom-call(s32[1]{0:T(128)} %bitcast.refs_0_, s32[2,3]{1,0:T(2,128)S(1)} %copy-done.12, f32[448,512]{1,0:T(8,128)S(1)} %copy-done.1, bf16[8,2,72,192]{3,2,1,0:T(8,128)(2,1)S(1)} %bitcast.320, ...), custom_call_target="tpu_custom_call" | custom-call | flops 16777216 | bytes 1048576 | tf_op jit(solution)/shard_map/pallas_call | solution.py:664
  301.8 4.4 %all-to-all-start.3 = ((f32[32,32,88]{2,1,0:T(8,128)}), f32[32,32,88]{2,1,0:T(8,128)}, u32[]{:S(2)}, u32[]{:S(2)}) async-start(f32[32,32,88]{2,1,0:T(8,128)} %bitcast.155), calls=%async_computation.3 | async-start | bytes 1048576 | tf_op jit(solution)/shard_map/all_to_all | solution.py:683
  306.3 2.7 fusion.13
  309.0 1.7 convert_add_fusion.1
  310.9 1.7 convert_add_fusion
  312.8 1.8 collective-permute-start.46
  314.6 1.7 convert_add_fusion.2
  318.4 1.7 fusion.15
  320.5 1.7 fusion.14
  324.9 8.0 %collective-permute-done.37 = bf16[576,512]{1,0:T(8,128)(2,1)S(1)} collective-permute-done((bf16[576,512]{1,0:T(8,128)(2,1)S(1)}, bf16[576,512]{1,0:T(8,128)(2,1)S(1)}, u32[]{:S(2)}, u32[]{:S(2)}) %collective-permute-start.37) | collective-permute-done | bytes 589856 | tf_op jit(solution)/shard_map/ppermute | solution.py:62
  333.4 1.8 collective-permute-start.47
  340.4 9.8 %collective-permute-done.47 = bf16[288,512]{1,0:T(8,128)(2,1)S(1)} collective-permute-done((bf16[288,512]{1,0:T(8,128)(2,1)S(1)}, bf16[288,512]{1,0:T(8,128)(2,1)S(1)}, u32[]{:S(2)}, u32[]{:S(2)}) %collective-permute-start.47) | collective-permute-done | bytes 294944 | tf_op jit(solution)/shard_map/ppermute | solution.py:62
  353.6 2.2 collective-permute-done.48
  355.9 5.1 %collective-permute-done.44 = bf16[144,512]{1,0:T(8,128)(2,1)S(1)} collective-permute-done((bf16[144,512]{1,0:T(8,128)(2,1)S(1)}, bf16[144,512]{1,0:T(8,128)(2,1)S(1)}, u32[]{:S(2)}, u32[]{:S(2)}) %collective-permute-start.44) | collective-permute-done | bytes 147488 | tf_op jit(solution)/shard_map/ppermute | solution.py:62
  368.5 1.6 copy-done.14
  375.9 9.1 %collective-permute-done.50 = bf16[256,896]{1,0:T(8,128)(2,1)S(1)} collective-permute-done((bf16[256,896]{1,0:T(8,128)(2,1)S(1)}, bf16[256,896]{1,0:T(8,128)(2,1)S(1)}, u32[]{:S(2)}, u32[]{:S(2)}) %collective-permute-start.50) | collective-permute-done | bytes 458784 | tf_op jit(solution)/shard_map/ppermute | solution.py:62
  389.8 2.7 collective-permute-done.56
  396.1 6.2 %collective-permute-done.57 = bf16[64,2816]{1,0:T(8,128)(2,1)S(1)} collective-permute-done((bf16[64,2816]{1,0:T(8,128)(2,1)S(1)}, bf16[64,2816]{1,0:T(8,128)(2,1)S(1)}, u32[]{:S(2)}, u32[]{:S(2)}) %collective-permute-start.57) | collective-permute-done | bytes 360480 | tf_op jit(solution)/shard_map/ppermute | solution.py:62
  406.5 3.9 collective-permute-done.58
  (419 shorter events, 125.4 us)
Async XLA Ops:
  4.7 12.5 %collective-permute-start = (bf16[32,2816]{1,0:T(8,128)(2,1)S(1)}, bf16[32,2816]{1,0:T(8,128)(2,1)S(1)}, u32[]{:S(2)}, u32[]{:S(2)}) collective-permute-start(bf16[32,2816]{1,0:T(8,128)(2,1)S(1)} %bitcast.443), channel_id=1, source_target_pairs={{0,8},{1,9},{2,10},{3,11},{4,12},{5,13},{6,14},{7,15},{8,0},{9,1},... | collective-permute-start | bytes 540680 | tf_op jit(solution)/shard_map/ppermute | solution.py:62
  17.2 9.7 %collective-permute-start.1 = (bf16[64,2816]{1,0:T(8,128)(2,1)S(1)}, bf16[64,2816]{1,0:T(8,128)(2,1)S(1)}, u32[]{:S(2)}, u32[]{:S(2)}) collective-permute-start(bf16[64,2816]{1,0:T(8,128)(2,1)S(1)} %bitcast.431), channel_id=1, source_target_pairs={{0,4},{1,5},{2,6},{3,7},{4,0},{5,1},{6,2},{7,3},{8,12},{9,13},{10,... | collective-permute-start | bytes 1081352 | tf_op jit(solution)/shard_map/ppermute | solution.py:62
  27.1 8.7 %collective-permute-start.5 = (bf16[128,1408]{1,0:T(8,128)(2,1)S(1)}, bf16[128,1408]{1,0:T(8,128)(2,1)S(1)}, u32[]{:S(2)}, u32[]{:S(2)}) collective-permute-start(bf16[128,1408]{1,0:T(8,128)(2,1)S(1)} %get-tuple-element.220), channel_id=1, source_target_pairs={{0,16},{16,0},{1,17},{17,1},{2,18},{18,2},{3,19},{19,3},{4,20},{20... | collective-permute-start | bytes 1081352 | tf_op jit(solution)/shard_map/ppermute | solution.py:62
  28.5 8.4 %collective-permute-start.2 = (bf16[128,1408]{1,0:T(8,128)(2,1)S(1)}, bf16[128,1408]{1,0:T(8,128)(2,1)S(1)}, u32[]{:S(2)}, u32[]{:S(2)}) collective-permute-start(bf16[128,1408]{1,0:T(8,128)(2,1)S(1)} %get-tuple-element.221), channel_id=1, source_target_pairs={{0,2},{1,3},{2,0},{3,1},{4,6},{5,7},{6,4},{7,5},{8,10},{9,11},{10,... | collective-permute-start | bytes 1081352 | tf_op jit(solution)/shard_map/ppermute | solution.py:62
  37.1 15.3 %collective-permute-start.6 = (bf16[256,1408]{1,0:T(8,128)(2,1)S(1)}, bf16[256,1408]{1,0:T(8,128)(2,1)S(1)}, u32[]{:S(2)}, u32[]{:S(2)}) collective-permute-start(bf16[256,1408]{1,0:T(8,128)(2,1)S(1)} %bitcast.407), channel_id=1, source_target_pairs={{0,2},{1,3},{2,0},{3,1},{4,6},{5,7},{6,4},{7,5},{8,10},{9,11},{10,... | collective-permute-start | bytes 2162696 | tf_op jit(solution)/shard_map/ppermute | solution.py:62
  38.7 35.4 %copy-start.29 = (bf16[2,72,1024]{2,1,0:T(8,128)(2,1)}, bf16[2,72,1024]{2,1,0:T(8,128)(2,1)S(1)}, u32[]{:S(2)}) copy-start(bf16[2,72,1024]{2,1,0:T(8,128)(2,1)S(1)} %pad_maximum_fusion.31) | copy-start | bytes 884740
  38.7 7.4 %collective-permute-start.7 = (bf16[144,1024]{1,0:T(8,128)(2,1)S(1)}, bf16[144,1024]{1,0:T(8,128)(2,1)S(1)}, u32[]{:S(2)}, u32[]{:S(2)}) collective-permute-start(bf16[144,1024]{1,0:T(8,128)(2,1)S(1)} %bitcast.382), channel_id=1, source_target_pairs={{0,4},{1,5},{2,6},{3,7},{4,0},{5,1},{6,2},{7,3},{8,12},{9,13},{10,... | collective-permute-start | bytes 884744 | tf_op jit(solution)/shard_map/ppermute | solution.py:62
  46.2 15.2 %collective-permute-start.3 = (bf16[256,1408]{1,0:T(8,128)(2,1)S(1)}, bf16[256,1408]{1,0:T(8,128)(2,1)S(1)}, u32[]{:S(2)}, u32[]{:S(2)}) collective-permute-start(bf16[256,1408]{1,0:T(8,128)(2,1)S(1)} %bitcast.406), channel_id=1, source_target_pairs={{0,16},{16,0},{1,17},{17,1},{2,18},{18,2},{3,19},{19,3},{4,20},{20... | collective-permute-start | bytes 2162696 | tf_op jit(solution)/shard_map/ppermute | solution.py:62
  52.9 31.5 %collective-permute-start.8 = (bf16[512,1408]{1,0:T(8,128)(2,1)S(1)}, bf16[512,1408]{1,0:T(8,128)(2,1)}, u32[]{:S(2)}, u32[]{:S(2)}) collective-permute-start(bf16[512,1408]{1,0:T(8,128)(2,1)S(1)} %bitcast.369), channel_id=1, source_target_pairs={{0,1},{1,0},{2,3},{3,2},{4,5},{5,4},{6,7},{7,6},{8,9},{9,8},{10,11... | collective-permute-start | bytes 4325384 | tf_op jit(solution)/shard_map/ppermute | solution.py:62
  61.8 22.6 %collective-permute-start.4 = (bf16[512,1408]{1,0:T(8,128)(2,1)S(1)}, bf16[512,1408]{1,0:T(8,128)(2,1)}, u32[]{:S(2)}, u32[]{:S(2)}) collective-permute-start(bf16[512,1408]{1,0:T(8,128)(2,1)S(1)} %bitcast.371), channel_id=1, source_target_pairs={{0,1},{1,0},{2,3},{3,2},{4,5},{5,4},{6,7},{7,6},{8,9},{9,8},{10,11... | collective-permute-start | bytes 4325384 | tf_op jit(solution)/shard_map/ppermute | solution.py:62
  63.3 20.5 %collective-permute-start.9 = (bf16[88,2048]{1,0:T(8,128)(2,1)}, bf16[88,2048]{1,0:T(8,128)(2,1)}, u32[]{:S(2)}, u32[]{:S(2)}) collective-permute-start(bf16[88,2048]{1,0:T(8,128)(2,1)} %pad_maximum_fusion.30), channel_id=1, source_target_pairs={{0,8},{1,9},{2,10},{3,11},{4,12},{5,13},{6,14},{7,15},{8,0},{9,1},... | collective-permute-start | bytes 1081352 | tf_op jit(solution)/shard_map/ppermute | solution.py:62
  68.1 24.0 %collective-permute-start.10 = (bf16[96,1024]{1,0:T(8,128)(2,1)}, bf16[96,1024]{1,0:T(8,128)(2,1)}, u32[]{:S(2)}, u32[]{:S(2)}) collective-permute-start(bf16[96,1024]{1,0:T(8,128)(2,1)} %pad_maximum_fusion.34), channel_id=1, source_target_pairs={{0,0},{1,16},{2,2},{3,18},{4,4},{5,20},{6,6},{7,22},{8,8},{9,24},{... | collective-permute-start | bytes 589832 | tf_op jit(solution)/shard_map/ppermute | solution.py:451
  71.1 21.1 %collective-permute-start.11 = (bf16[96,1024]{1,0:T(8,128)(2,1)}, bf16[96,1024]{1,0:T(8,128)(2,1)}, u32[]{:S(2)}, u32[]{:S(2)}) collective-permute-start(bf16[96,1024]{1,0:T(8,128)(2,1)} %pad_maximum_fusion.34), channel_id=1, source_target_pairs={{0,16},{1,0},{2,18},{3,2},{4,20},{5,4},{6,22},{7,6},{8,24},{9,8},{... | collective-permute-start | bytes 589832 | tf_op jit(solution)/shard_map/ppermute | solution.py:451
  83.8 16.6 %collective-permute-start.12 = (bf16[288,1024]{1,0:T(8,128)(2,1)}, bf16[288,1024]{1,0:T(8,128)(2,1)}, u32[]{:S(2)}, u32[]{:S(2)}) collective-permute-start(bf16[288,1024]{1,0:T(8,128)(2,1)} %pad_maximum_fusion.20), channel_id=1, source_target_pairs={{0,2},{1,3},{2,0},{3,1},{4,6},{5,7},{6,4},{7,5},{8,10},{9,11},{10,... | collective-permute-start | bytes 1769480 | tf_op jit(solution)/shard_map/ppermute | solution.py:62
  92.2 9.2 %collective-permute-start.13 = (bf16[144,512]{1,0:T(8,128)(2,1)S(1)}, bf16[144,512]{1,0:T(8,128)(2,1)S(1)}, u32[]{:S(2)}, u32[]{:S(2)}) collective-permute-start(bf16[144,512]{1,0:T(8,128)(2,1)S(1)} %get-tuple-element.110), channel_id=1, source_target_pairs={{0,8},{1,9},{2,10},{3,11},{4,12},{5,13},{6,14},{7,15},{8,0},{9,1},... | collective-permute-start | bytes 442376 | tf_op jit(solution)/shard_map/ppermute | solution.py:62
  92.3 9.8 %collective-permute-start.16 = (bf16[144,512]{1,0:T(8,128)(2,1)S(1)}, bf16[144,512]{1,0:T(8,128)(2,1)S(1)}, u32[]{:S(2)}, u32[]{:S(2)}) collective-permute-start(bf16[144,512]{1,0:T(8,128)(2,1)S(1)} %get-tuple-element.238), channel_id=1, source_target_pairs={{0,2},{1,3},{2,0},{3,1},{4,6},{5,7},{6,4},{7,5},{8,10},{9,11},{10,... | collective-permute-start | bytes 442376 | tf_op jit(solution)/shard_map/ppermute | solution.py:62
  101.4 13.5 %collective-permute-start.14 = (bf16[288,512]{1,0:T(8,128)(2,1)S(1)}, bf16[288,512]{1,0:T(8,128)(2,1)S(1)}, u32[]{:S(2)}, u32[]{:S(2)}) collective-permute-start(bf16[288,512]{1,0:T(8,128)(2,1)S(1)} %bitcast.458), channel_id=1, source_target_pairs={{0,4},{1,5},{2,6},{3,7},{4,0},{5,1},{6,2},{7,3},{8,12},{9,13},{10,... | collective-permute-start | bytes 884744 | tf_op jit(solution)/shard_map/ppermute | solution.py:62
  102.1 15.4 %collective-permute-start.17 = (bf16[288,512]{1,0:T(8,128)(2,1)S(1)}, bf16[288,512]{1,0:T(8,128)(2,1)S(1)}, u32[]{:S(2)}, u32[]{:S(2)}) collective-permute-start(bf16[288,512]{1,0:T(8,128)(2,1)S(1)} %bitcast.436), channel_id=1, source_target_pairs={{0,8},{1,9},{2,10},{3,11},{4,12},{5,13},{6,14},{7,15},{8,0},{9,1},... | collective-permute-start | bytes 884744 | tf_op jit(solution)/shard_map/ppermute | solution.py:62
  115.1 14.2 %collective-permute-start.15 = (bf16[576,512]{1,0:T(8,128)(2,1)S(1)}, bf16[576,512]{1,0:T(8,128)(2,1)S(1)}, u32[]{:S(2)}, u32[]{:S(2)}) collective-permute-start(bf16[576,512]{1,0:T(8,128)(2,1)S(1)} %bitcast.422), channel_id=1, source_target_pairs={{0,2},{1,3},{2,0},{3,1},{4,6},{5,7},{6,4},{7,5},{8,10},{9,11},{10,... | collective-permute-start | bytes 1769480 | tf_op jit(solution)/shard_map/ppermute | solution.py:62
  117.6 13.2 %collective-permute-start.18 = (bf16[576,512]{1,0:T(8,128)(2,1)S(1)}, bf16[576,512]{1,0:T(8,128)(2,1)S(1)}, u32[]{:S(2)}, u32[]{:S(2)}) collective-permute-start(bf16[576,512]{1,0:T(8,128)(2,1)S(1)} %bitcast.449), channel_id=1, source_target_pairs={{0,4},{1,5},{2,6},{3,7},{4,0},{5,1},{6,2},{7,3},{8,12},{9,13},{10,... | collective-permute-start | bytes 1769480 | tf_op jit(solution)/shard_map/ppermute | solution.py:62
  130.9 15.0 %collective-permute-start.20 = (bf16[1152,512]{1,0:T(8,128)(2,1)S(1)}, bf16[1152,512]{1,0:T(8,128)(2,1)}, u32[]{:S(2)}, u32[]{:S(2)}) collective-permute-start(bf16[1152,512]{1,0:T(8,128)(2,1)S(1)} %bitcast.340), channel_id=1, source_target_pairs={{0,1},{1,0},{2,3},{3,2},{4,5},{5,4},{6,7},{7,6},{8,9},{9,8},{10,11... | collective-permute-start | bytes 3538952 | tf_op jit(solution)/shard_map/ppermute | solution.py:62
  133.5 16.6 %all-to-all-start = ((bf16[32,32,88]{2,1,0:T(8,128)(2,1)}), bf16[32,32,88]{2,1,0:T(8,128)(2,1)}, u32[]{:S(2)}, u32[]{:S(2)}) async-start(bf16[32,32,88]{2,1,0:T(8,128)(2,1)} %bitcast.308), calls=%async_computation | async-start | bytes 524288 | tf_op jit(solution)/shard_map/all_to_all | solution.py:431
  137.3 10.7 %collective-permute-start.19 = (bf16[1152,512]{1,0:T(8,128)(2,1)S(1)}, bf16[1152,512]{1,0:T(8,128)(2,1)}, u32[]{:S(2)}, u32[]{:S(2)}) collective-permute-start(bf16[1152,512]{1,0:T(8,128)(2,1)S(1)} %bitcast.337), channel_id=1, source_target_pairs={{0,1},{1,0},{2,3},{3,2},{4,5},{5,4},{6,7},{7,6},{8,9},{9,8},{10,11... | collective-permute-start | bytes 3538952 | tf_op jit(solution)/shard_map/ppermute | solution.py:62
  139.6 26.6 %collective-permute-start.21 = (bf16[176,2048]{1,0:T(8,128)(2,1)}, bf16[176,2048]{1,0:T(8,128)(2,1)}, u32[]{:S(2)}, u32[]{:S(2)}) collective-permute-start(bf16[176,2048]{1,0:T(8,128)(2,1)} %pad_maximum_fusion.15), channel_id=1, source_target_pairs={{0,16},{16,0},{1,17},{17,1},{2,18},{18,2},{3,19},{19,3},{4,20},{20... | collective-permute-start | bytes 2162696 | tf_op jit(solution)/shard_map/ppermute | solution.py:62
  150.1 16.1 %collective-permute-start.22 = (bf16[88,1024]{0,1:T(8,128)(2,1)}, bf16[88,1024]{0,1:T(8,128)(2,1)S(1)}, u32[]{:S(2)}, u32[]{:S(2)}) collective-permute-start(bf16[88,1024]{0,1:T(8,128)(2,1)} %bitcast.72), channel_id=1, source_target_pairs={{0,8},{1,9},{2,10},{3,11},{4,12},{5,13},{6,14},{7,15},{8,0},{9,1},... | collective-permute-start | bytes 540680 | tf_op jit(solution)/shard_map/ppermute | solution.py:62
  166.2 15.1 %all-to-all-start.1 = ((bf16[16,72,128]{2,1,0:T(8,128)(2,1)}), bf16[16,72,128]{2,1,0:T(8,128)(2,1)S(1)}, u32[]{:S(2)}, u32[]{:S(2)}) async-start(bf16[16,72,128]{2,1,0:T(8,128)(2,1)} %shard_map.289), calls=%async_computation.1 | async-start | bytes 589824 | tf_op jit(solution)/shard_map/all_to_all | solution.py:553
  184.7 8.8 %collective-permute-start.23 = (bf16[144,1024]{1,0:T(8,128)(2,1)S(1)}, bf16[144,1024]{1,0:T(8,128)(2,1)S(1)}, u32[]{:S(2)}, u32[]{:S(2)}) collective-permute-start(bf16[144,1024]{1,0:T(8,128)(2,1)S(1)} %get-tuple-element.121), channel_id=1, source_target_pairs={{0,4},{1,5},{2,6},{3,7},{4,0},{5,1},{6,2},{7,3},{8,12},{9,13},{10,... | collective-permute-start | bytes 884744 | tf_op jit(solution)/shard_map/ppermute | solution.py:62
  187.2 22.0 %collective-permute-start.27 = (bf16[576,1024]{1,0:T(8,128)(2,1)}, bf16[576,1024]{1,0:T(8,128)(2,1)}, u32[]{:S(2)}, u32[]{:S(2)}) collective-permute-start(bf16[576,1024]{1,0:T(8,128)(2,1)} %pad_maximum_fusion.9), channel_id=1, source_target_pairs={{0,1},{1,0},{2,3},{3,2},{4,5},{5,4},{6,7},{7,6},{8,9},{9,8},{10,11... | collective-permute-start | bytes 3538952 | tf_op jit(solution)/shard_map/ppermute | solution.py:62
  188.8 14.0 %collective-permute-start.24 = (bf16[176,1024]{0,1:T(8,128)(2,1)S(1)}, bf16[176,1024]{0,1:T(8,128)(2,1)S(1)}, u32[]{:S(2)}, u32[]{:S(2)}) collective-permute-start(bf16[176,1024]{0,1:T(8,128)(2,1)S(1)} %pad_maximum_fusion.24), channel_id=1, source_target_pairs={{0,16},{16,0},{1,17},{17,1},{2,18},{18,2},{3,19},{19,3},{4,20},{20... | collective-permute-start | bytes 1081352 | tf_op jit(solution)/shard_map/ppermute | solution.py:62
  193.5 14.4 %collective-permute-start.25 = (bf16[288,1024]{1,0:T(8,128)(2,1)S(1)}, bf16[288,1024]{1,0:T(8,128)(2,1)S(1)}, u32[]{:S(2)}, u32[]{:S(2)}) collective-permute-start(bf16[288,1024]{1,0:T(8,128)(2,1)S(1)} %constant_dynamic-update-slice_fusion), channel_id=1, source_target_pairs={{0,2},{1,3},{2,0},{3,1},{4,6},{5,7},{6,4},{7,5},{8,10},{9,11},{10,... | collective-permute-start | bytes 1769480 | tf_op jit(solution)/shard_map/ppermute | solution.py:62
  209.0 3.6 collective-permute-start.26
  220.7 5.5 %collective-permute-start.28 = (bf16[576,1024]{1,0:T(8,128)(2,1)S(1)}, bf16[576,1024]{1,0:T(8,128)(2,1)S(1)}, u32[]{:S(2)}, u32[]{:S(2)}) collective-permute-start(bf16[576,1024]{1,0:T(8,128)(2,1)S(1)} %fusion.11), channel_id=1, source_target_pairs={{0,1},{1,0},{2,3},{3,2},{4,5},{5,4},{6,7},{7,6},{8,9},{9,8},{10,11... | collective-permute-start | bytes 3538952 | tf_op jit(solution)/shard_map/ppermute | solution.py:62
  223.9 10.4 %collective-permute-start.29 = (bf16[176,1024]{1,0:T(8,128)(2,1)S(1)}, bf16[176,1024]{1,0:T(8,128)(2,1)S(1)}, u32[]{:S(2)}, u32[]{:S(2)}) collective-permute-start(bf16[176,1024]{1,0:T(8,128)(2,1)S(1)} %slice.338), channel_id=1, source_target_pairs={{0,16},{16,0},{1,17},{17,1},{2,18},{18,2},{3,19},{19,3},{4,20},{20... | collective-permute-start | bytes 1081352 | tf_op jit(solution)/shard_map/ppermute | solution.py:62
  226.2 24.6 %collective-permute-start.32 = (bf16[576,1024]{1,0:T(8,128)(2,1)S(1)}, bf16[576,1024]{1,0:T(8,128)(2,1)S(1)}, u32[]{:S(2)}, u32[]{:S(2)}) collective-permute-start(bf16[576,1024]{1,0:T(8,128)(2,1)S(1)} %fusion.12), channel_id=1, source_target_pairs={{0,1},{1,0},{2,3},{3,2},{4,5},{5,4},{6,7},{7,6},{8,9},{9,8},{10,11... | collective-permute-start | bytes 3538952 | tf_op jit(solution)/shard_map/ppermute | solution.py:62
  234.3 14.4 %collective-permute-start.30 = (bf16[288,1024]{1,0:T(8,128)(2,1)S(1)}, bf16[288,1024]{1,0:T(8,128)(2,1)S(1)}, u32[]{:S(2)}, u32[]{:S(2)}) collective-permute-start(bf16[288,1024]{1,0:T(8,128)(2,1)S(1)} %fusion.22), channel_id=1, source_target_pairs={{0,2},{1,3},{2,0},{3,1},{4,6},{5,7},{6,4},{7,5},{8,10},{9,11},{10,... | collective-permute-start | bytes 1769480 | tf_op jit(solution)/shard_map/ppermute | solution.py:62
  249.0 7.2 %collective-permute-start.31 = (bf16[144,1024]{1,0:T(8,128)(2,1)S(1)}, bf16[144,1024]{1,0:T(8,128)(2,1)S(1)}, u32[]{:S(2)}, u32[]{:S(2)}) collective-permute-start(bf16[144,1024]{1,0:T(8,128)(2,1)S(1)} %fusion.37), channel_id=1, source_target_pairs={{0,4},{1,5},{2,6},{3,7},{4,0},{5,1},{6,2},{7,3},{8,12},{9,13},{10,... | collective-permute-start | bytes 884744 | tf_op jit(solution)/shard_map/ppermute | solution.py:62
  260.5 14.3 %all-to-all-start.2 = ((bf16[16,72,128]{2,1,0:T(8,128)(2,1)}), bf16[16,72,128]{2,1,0:T(8,128)(2,1)S(1)}, u32[]{:S(2)}, u32[]{:S(2)}) async-start(bf16[16,72,128]{2,1,0:T(8,128)(2,1)} %bitcast.86), calls=%async_computation.2 | async-start | bytes 589824 | tf_op jit(solution)/shard_map/all_to_all | solution.py:643
  274.9 19.3 %collective-permute-start.34 = (bf16[288,1024]{1,0:T(8,128)(2,1)}, bf16[288,1024]{1,0:T(8,128)(2,1)S(1)}, u32[]{:S(2)}, u32[]{:S(2)}) collective-permute-start(bf16[288,1024]{1,0:T(8,128)(2,1)} %fusion.23), channel_id=1, source_target_pairs={{0,2},{1,3},{2,0},{3,1},{4,6},{5,7},{6,4},{7,5},{8,10},{9,11},{10,... | collective-permute-start | bytes 1769480 | tf_op jit(solution)/shard_map/ppermute | solution.py:62
  276.1 18.0 %collective-permute-start.33 = (bf16[88,1024]{1,0:T(8,128)(2,1)S(1)}, bf16[88,1024]{1,0:T(8,128)(2,1)S(1)}, u32[]{:S(2)}, u32[]{:S(2)}) collective-permute-start(bf16[88,1024]{1,0:T(8,128)(2,1)S(1)} %slice.521), channel_id=1, source_target_pairs={{0,8},{1,9},{2,10},{3,11},{4,12},{5,13},{6,14},{7,15},{8,0},{9,1},... | collective-permute-start | bytes 540680 | tf_op jit(solution)/shard_map/ppermute | solution.py:62
  297.2 11.8 %collective-permute-start.35 = (bf16[1152,512]{1,0:T(8,128)(2,1)}, bf16[1152,512]{1,0:T(8,128)(2,1)}, u32[]{:S(2)}, u32[]{:S(2)}) collective-permute-start(bf16[1152,512]{1,0:T(8,128)(2,1)} %convolution_convert_fusion.1), channel_id=1, source_target_pairs={{0,1},{1,0},{2,3},{3,2},{4,5},{5,4},{6,7},{7,6},{8,9},{9,8},{10,11... | collective-permute-start | bytes 3538952 | tf_op jit(solution)/shard_map/ppermute | solution.py:62
  298.0 37.3 %collective-permute-start.38 = (bf16[176,2048]{1,0:T(8,128)(2,1)}, bf16[176,2048]{1,0:T(8,128)(2,1)S(1)}, u32[]{:S(2)}, u32[]{:S(2)}) collective-permute-start(bf16[176,2048]{1,0:T(8,128)(2,1)} %fusion.19), channel_id=1, source_target_pairs={{0,16},{16,0},{1,17},{17,1},{2,18},{18,2},{3,19},{19,3},{4,20},{20... | collective-permute-start | bytes 2162696 | tf_op jit(solution)/shard_map/ppermute | solution.py:62
  298.5 16.1 %collective-permute-start.36 = (bf16[512,1024]{1,0:T(8,128)(2,1)}, bf16[512,1024]{1,0:T(8,128)(2,1)}, u32[]{:S(2)}, u32[]{:S(2)}) collective-permute-start(bf16[512,1024]{1,0:T(8,128)(2,1)} %bitcast.88), channel_id=1, source_target_pairs={{0,1},{1,0},{2,3},{3,2},{4,5},{5,4},{6,7},{7,6},{8,9},{9,8},{10,11... | collective-permute-start | bytes 3145736 | tf_op jit(solution)/shard_map/ppermute | solution.py:62
  300.1 10.8 %collective-permute-start.45 = (bf16[1152,512]{1,0:T(8,128)(2,1)}, bf16[1152,512]{1,0:T(8,128)(2,1)}, u32[]{:S(2)}, u32[]{:S(2)}) collective-permute-start(bf16[1152,512]{1,0:T(8,128)(2,1)} %convolution_convert_fusion), channel_id=1, source_target_pairs={{0,1},{1,0},{2,3},{3,2},{4,5},{5,4},{6,7},{7,6},{8,9},{9,8},{10,11... | collective-permute-start | bytes 3538952 | tf_op jit(solution)/shard_map/ppermute | solution.py:62
  301.8 94.3 %all-to-all-start.3 = ((f32[32,32,88]{2,1,0:T(8,128)}), f32[32,32,88]{2,1,0:T(8,128)}, u32[]{:S(2)}, u32[]{:S(2)}) async-start(f32[32,32,88]{2,1,0:T(8,128)} %bitcast.155), calls=%async_computation.3 | async-start | bytes 1048576 | tf_op jit(solution)/shard_map/all_to_all | solution.py:683
  312.8 20.4 %collective-permute-start.46 = (bf16[576,512]{1,0:T(8,128)(2,1)S(1)}, bf16[576,512]{1,0:T(8,128)(2,1)S(1)}, u32[]{:S(2)}, u32[]{:S(2)}) collective-permute-start(bf16[576,512]{1,0:T(8,128)(2,1)S(1)} %bitcast.450), channel_id=1, source_target_pairs={{0,4},{1,5},{2,6},{3,7},{4,0},{5,1},{6,2},{7,3},{8,12},{9,13},{10,... | collective-permute-start | bytes 1769480 | tf_op jit(solution)/shard_map/ppermute | solution.py:62
  316.8 16.0 %collective-permute-start.37 = (bf16[576,512]{1,0:T(8,128)(2,1)S(1)}, bf16[576,512]{1,0:T(8,128)(2,1)S(1)}, u32[]{:S(2)}, u32[]{:S(2)}) collective-permute-start(bf16[576,512]{1,0:T(8,128)(2,1)S(1)} %bitcast.451), channel_id=1, source_target_pairs={{0,2},{1,3},{2,0},{3,1},{4,6},{5,7},{6,4},{7,5},{8,10},{9,11},{10,... | collective-permute-start | bytes 1769480 | tf_op jit(solution)/shard_map/ppermute | solution.py:62
  322.4 13.9 %collective-permute-start.39 = (bf16[256,1024]{1,0:T(8,128)(2,1)S(1)}, bf16[256,1024]{1,0:T(8,128)(2,1)S(1)}, u32[]{:S(2)}, u32[]{:S(2)}) collective-permute-start(bf16[256,1024]{1,0:T(8,128)(2,1)S(1)} %fusion.30), channel_id=1, source_target_pairs={{0,16},{16,0},{1,17},{17,1},{2,18},{18,2},{3,19},{19,3},{4,20},{20... | collective-permute-start | bytes 1572872 | tf_op jit(solution)/shard_map/ppermute | solution.py:62
  324.0 27.7 %collective-permute-start.41 = (bf16[96,1024]{1,0:T(8,128)(2,1)S(1)}, bf16[96,1024]{1,0:T(8,128)(2,1)S(1)}, u32[]{:S(2)}, u32[]{:S(2)}) collective-permute-start(bf16[96,1024]{1,0:T(8,128)(2,1)S(1)} %bitcast.464), channel_id=1, source_target_pairs={{0,0},{16,1},{2,2},{18,3},{4,4},{20,5},{6,6},{22,7},{8,8},{24,9},{... | collective-permute-start | bytes 589832 | tf_op jit(solution)/shard_map/ppermute | solution.py:733
  332.9 18.8 %collective-permute-start.42 = (bf16[96,1024]{1,0:T(8,128)(2,1)S(1)}, bf16[96,1024]{1,0:T(8,128)(2,1)S(1)}, u32[]{:S(2)}, u32[]{:S(2)}) collective-permute-start(bf16[96,1024]{1,0:T(8,128)(2,1)S(1)} %bitcast.463), channel_id=1, source_target_pairs={{16,0},{0,1},{18,2},{2,3},{20,4},{4,5},{22,6},{6,7},{24,8},{8,9},{... | collective-permute-start | bytes 589832 | tf_op jit(solution)/shard_map/ppermute | solution.py:733
  333.4 16.8 %collective-permute-start.47 = (bf16[288,512]{1,0:T(8,128)(2,1)S(1)}, bf16[288,512]{1,0:T(8,128)(2,1)S(1)}, u32[]{:S(2)}, u32[]{:S(2)}) collective-permute-start(bf16[288,512]{1,0:T(8,128)(2,1)S(1)} %fusion.38), channel_id=1, source_target_pairs={{0,8},{1,9},{2,10},{3,11},{4,12},{5,13},{6,14},{7,15},{8,0},{9,1},... | collective-permute-start | bytes 884744 | tf_op jit(solution)/shard_map/ppermute | solution.py:62
  336.6 14.9 %collective-permute-start.40 = (bf16[288,512]{1,0:T(8,128)(2,1)S(1)}, bf16[288,512]{1,0:T(8,128)(2,1)S(1)}, u32[]{:S(2)}, u32[]{:S(2)}) collective-permute-start(bf16[288,512]{1,0:T(8,128)(2,1)S(1)} %bitcast.459), channel_id=1, source_target_pairs={{0,4},{1,5},{2,6},{3,7},{4,0},{5,1},{6,2},{7,3},{8,12},{9,13},{10,... | collective-permute-start | bytes 884744 | tf_op jit(solution)/shard_map/ppermute | solution.py:62
  337.7 14.0 %collective-permute-start.43 = (bf16[128,1024]{1,0:T(8,128)(2,1)S(1)}, bf16[128,1024]{1,0:T(8,128)(2,1)S(1)}, u32[]{:S(2)}, u32[]{:S(2)}) collective-permute-start(bf16[128,1024]{1,0:T(8,128)(2,1)S(1)} %bitcast.461), channel_id=1, source_target_pairs={{0,2},{1,3},{2,0},{3,1},{4,6},{5,7},{6,4},{7,5},{8,10},{9,11},{10,... | collective-permute-start | bytes 786440 | tf_op jit(solution)/shard_map/ppermute | solution.py:62
  350.3 5.6 %collective-permute-start.48 = (bf16[144,512]{1,0:T(8,128)(2,1)S(1)}, bf16[144,512]{1,0:T(8,128)(2,1)S(1)}, u32[]{:S(2)}, u32[]{:S(2)}) collective-permute-start(bf16[144,512]{1,0:T(8,128)(2,1)S(1)} %fusion.53), channel_id=1, source_target_pairs={{0,2},{1,3},{2,0},{3,1},{4,6},{5,7},{6,4},{7,5},{8,10},{9,11},{10,... | collective-permute-start | bytes 442376 | tf_op jit(solution)/shard_map/ppermute | solution.py:62
  351.7 9.3 %collective-permute-start.44 = (bf16[144,512]{1,0:T(8,128)(2,1)S(1)}, bf16[144,512]{1,0:T(8,128)(2,1)S(1)}, u32[]{:S(2)}, u32[]{:S(2)}) collective-permute-start(bf16[144,512]{1,0:T(8,128)(2,1)S(1)} %fusion.52), channel_id=1, source_target_pairs={{0,8},{1,9},{2,10},{3,11},{4,12},{5,13},{6,14},{7,15},{8,0},{9,1},... | collective-permute-start | bytes 442376 | tf_op jit(solution)/shard_map/ppermute | solution.py:62
  365.6 7.2 %collective-permute-start.49 = (bf16[512,896]{1,0:T(8,128)(2,1)S(1)}, bf16[512,896]{1,0:T(8,128)(2,1)S(1)}, u32[]{:S(2)}, u32[]{:S(2)}) collective-permute-start(bf16[512,896]{1,0:T(8,128)(2,1)S(1)} %bitcast.441), channel_id=1, source_target_pairs={{0,1},{1,0},{2,3},{3,2},{4,5},{5,4},{6,7},{7,6},{8,9},{9,8},{10,11... | collective-permute-start | bytes 2752520 | tf_op jit(solution)/shard_map/ppermute | solution.py:62
  366.4 18.8 %collective-permute-start.51 = (bf16[88,2048]{1,0:T(8,128)(2,1)S(1)}, bf16[88,2048]{1,0:T(8,128)(2,1)S(1)}, u32[]{:S(2)}, u32[]{:S(2)}) collective-permute-start(bf16[88,2048]{1,0:T(8,128)(2,1)S(1)} %copy-done.59), channel_id=1, source_target_pairs={{0,8},{1,9},{2,10},{3,11},{4,12},{5,13},{6,14},{7,15},{8,0},{9,1},... | collective-permute-start | bytes 1081352 | tf_op jit(solution)/shard_map/ppermute | solution.py:62
  366.9 22.9 %collective-permute-start.52 = (bf16[144,1024]{1,0:T(8,128)(2,1)S(1)}, bf16[144,1024]{1,0:T(8,128)(2,1)S(1)}, u32[]{:S(2)}, u32[]{:S(2)}) collective-permute-start(bf16[144,1024]{1,0:T(8,128)(2,1)S(1)} %fusion.39), channel_id=1, source_target_pairs={{0,4},{1,5},{2,6},{3,7},{4,0},{5,1},{6,2},{7,3},{8,12},{9,13},{10,... | collective-permute-start | bytes 884744 | tf_op jit(solution)/shard_map/ppermute | solution.py:62
  368.5 5.8 %collective-permute-start.54 = (bf16[512,896]{1,0:T(8,128)(2,1)S(1)}, bf16[512,896]{1,0:T(8,128)(2,1)S(1)}, u32[]{:S(2)}, u32[]{:S(2)}) collective-permute-start(bf16[512,896]{1,0:T(8,128)(2,1)S(1)} %bitcast.442), channel_id=1, source_target_pairs={{0,1},{1,0},{2,3},{3,2},{4,5},{5,4},{6,7},{7,6},{8,9},{9,8},{10,11... | collective-permute-start | bytes 2752520 | tf_op jit(solution)/shard_map/ppermute | solution.py:62
  373.1 11.9 %collective-permute-start.50 = (bf16[256,896]{1,0:T(8,128)(2,1)S(1)}, bf16[256,896]{1,0:T(8,128)(2,1)S(1)}, u32[]{:S(2)}, u32[]{:S(2)}) collective-permute-start(bf16[256,896]{1,0:T(8,128)(2,1)S(1)} %bitcast.455), channel_id=1, source_target_pairs={{0,2},{1,3},{2,0},{3,1},{4,6},{5,7},{6,4},{7,5},{8,10},{9,11},{10,... | collective-permute-start | bytes 1376264 | tf_op jit(solution)/shard_map/ppermute | solution.py:62
  374.6 11.7 %collective-permute-start.55 = (bf16[256,896]{1,0:T(8,128)(2,1)S(1)}, bf16[256,896]{1,0:T(8,128)(2,1)S(1)}, u32[]{:S(2)}, u32[]{:S(2)}) collective-permute-start(bf16[256,896]{1,0:T(8,128)(2,1)S(1)} %fusion.33), channel_id=1, source_target_pairs={{0,16},{16,0},{1,17},{17,1},{2,18},{18,2},{3,19},{19,3},{4,20},{20... | collective-permute-start | bytes 1376264 | tf_op jit(solution)/shard_map/ppermute | solution.py:62
  386.4 6.1 %collective-permute-start.56 = (bf16[128,896]{1,0:T(8,128)(2,1)S(1)}, bf16[128,896]{1,0:T(8,128)(2,1)S(1)}, u32[]{:S(2)}, u32[]{:S(2)}) collective-permute-start(bf16[128,896]{1,0:T(8,128)(2,1)S(1)} %bitcast.462), channel_id=1, source_target_pairs={{0,2},{1,3},{2,0},{3,1},{4,6},{5,7},{6,4},{7,5},{8,10},{9,11},{10,... | collective-permute-start | bytes 688136 | tf_op jit(solution)/shard_map/ppermute | solution.py:62
  387.5 6.0 %collective-permute-start.53 = (bf16[128,896]{1,0:T(8,128)(2,1)S(1)}, bf16[128,896]{1,0:T(8,128)(2,1)S(1)}, u32[]{:S(2)}, u32[]{:S(2)}) collective-permute-start(bf16[128,896]{1,0:T(8,128)(2,1)S(1)} %fusion.44), channel_id=1, source_target_pairs={{0,16},{16,0},{1,17},{17,1},{2,18},{18,2},{3,19},{19,3},{4,20},{20... | collective-permute-start | bytes 688136 | tf_op jit(solution)/shard_map/ppermute | solution.py:62
  393.7 8.6 %collective-permute-start.57 = (bf16[64,2816]{1,0:T(8,128)(2,1)S(1)}, bf16[64,2816]{1,0:T(8,128)(2,1)S(1)}, u32[]{:S(2)}, u32[]{:S(2)}) collective-permute-start(bf16[64,2816]{1,0:T(8,128)(2,1)S(1)} %bitcast.456), channel_id=1, source_target_pairs={{0,4},{1,5},{2,6},{3,7},{4,0},{5,1},{6,2},{7,3},{8,12},{9,13},{10,... | collective-permute-start | bytes 1081352 | tf_op jit(solution)/shard_map/ppermute | solution.py:62
  402.4 8.0 %collective-permute-start.58 = (bf16[32,2816]{1,0:T(8,128)(2,1)S(1)}, bf16[32,2816]{1,0:T(8,128)(2,1)S(1)}, u32[]{:S(2)}, u32[]{:S(2)}) collective-permute-start(bf16[32,2816]{1,0:T(8,128)(2,1)S(1)} %fusion.51), channel_id=1, source_target_pairs={{0,8},{1,9},{2,10},{3,11},{4,12},{5,13},{6,14},{7,15},{8,0},{9,1},... | collective-permute-start | bytes 540680 | tf_op jit(solution)/shard_map/ppermute | solution.py:62
  (71 other events, 404.8 us)
